TPU v7x, 256 devices: a whole 4x4x8 slice. The times are simulated.
256 devices in a mesh: gr: 16 (over x, y_hi, core), gc: 16 (over y_lo, z).
Axes of the slice: x: 4, y: 4 (y_hi: 2, y_lo: 2; y = y_hi * 2 + y_lo), z: 8, core: 2. Of those that a mesh axis runs over, the one named last changes fastest.
Arguments:
- border: bfloat16 [96, 768, 2048], P('gc', None, 'gr'), may hold values from -1 to 1
- row_scale: float32 [96, 768], P('gc'), may hold values from 0.1 to 10
- block_pick: int32 [96, 16], replicated, may hold values from 0 to 3
- given_diag: float32 [8192], replicated, may hold values from 0.5 to 4
Outputs:
- factored: float32 [8192, 8192], P('gr', 'gc')
All inputs are finite; a program needn't handle non-finite values.
Results may differ from a plain program's by a relative error of at most 0.00097.
Values may be sent and summed in bfloat16 or wider, within the bound.
No kernel may reach another device: no remote copies, remote signals or barrier semaphores. Data moves between devices by JAX's collectives and lax.ppermute only.
A program may use at most 128 MiB of HBM per device.

v0:
```python
import jax
import jax.numpy as jnp
from jax import lax
from jax.sharding import PartitionSpec as P

N = 8192
BLK = 128
NWIN = 16
PW = 256
PANELS = 2


def broadcast(x, axis, root):
    mine = lax.axis_index(axis) == root
    return lax.psum(jnp.where(mine, x, jnp.zeros_like(x)), axis)


def place_tiles(row_pick, col_pick, gram_tiles, span_count):
    positions = jnp.arange(span_count, dtype=jnp.int32)
    rows_hot = (row_pick[:, :, None] == positions[None, None, :]).astype(jnp.float32)
    cols_hot = (col_pick[:, :, None] == positions[None, None, :]).astype(jnp.float32)
    pair_hot = jnp.einsum("sam,sbn->sambn", rows_hot, cols_hot)
    return jnp.einsum("sambn,saxby->amxbny", pair_hot, gram_tiles, precision=lax.Precision.HIGHEST)


def body(border, row_scale, block_pick, given_diag):
    grid_rows = lax.axis_size("gr")
    grid_cols = lax.axis_size("gc")
    row_index = lax.axis_index("gr")
    col_index = lax.axis_index("gc")
    scen_here = border.shape[0]
    row_windows = NWIN // grid_rows
    col_windows = NWIN // grid_cols
    span_count = N // (BLK * NWIN)
    local_rows = N // grid_rows
    local_cols = N // grid_cols
    scaled = (jnp.sqrt(row_scale)[:, :, None] * border).astype(jnp.bfloat16)
    gram_rows = jnp.einsum(
        "srx,sry->sxy",
        scaled,
        lax.all_gather(scaled, "gr", axis=2, tiled=True),
        preferred_element_type=jnp.float32,
    )
    gram_tiles = gram_rows.reshape(scen_here, row_windows, BLK, NWIN, BLK)
    received = lax.all_to_all(gram_tiles, "gc", split_axis=3, concat_axis=0, tiled=True)
    row_pick = lax.dynamic_slice_in_dim(block_pick, row_index * row_windows, row_windows, 1)
    col_pick = lax.dynamic_slice_in_dim(block_pick, col_index * col_windows, col_windows, 1)
    placed = place_tiles(row_pick, col_pick, received, span_count)
    assembled = placed.reshape(local_rows, local_cols)
    row_global = row_index * local_rows + jnp.arange(local_rows, dtype=jnp.int32)
    col_global = col_index * local_cols + jnp.arange(local_cols, dtype=jnp.int32)
    diag_here = lax.dynamic_slice_in_dim(given_diag, row_index * local_rows, local_rows, 0)
    factored = assembled + jnp.where(
        row_global[:, None] == col_global[None, :], diag_here[:, None], 0.0
    )
    row_ratio = grid_rows // grid_cols
    for panel_index in range(PANELS):
        first_col = panel_index * PW
        past_col = first_col + PW
        corner = broadcast(factored[first_col:past_col, first_col:past_col], "gr", 0)
        chol_block = jnp.linalg.cholesky(corner)
        solved = jax.scipy.linalg.solve_triangular(
            chol_block, factored[:, first_col:past_col].T, lower=True
        ).T
        padded = jnp.zeros((local_rows, PW), jnp.float32).at[first_col:past_col].set(chol_block)
        row_inside = (row_global >= first_col) & (row_global < past_col)
        solved = jnp.where(
            (row_global >= past_col)[:, None], solved, jnp.where(row_inside[:, None], padded, 0.0)
        )
        panel_rows = broadcast(solved, "gc", 0)
        col_inside = (col_global >= first_col) & (col_global < past_col)
        pieces = broadcast(panel_rows, "gr", col_index * row_ratio + 0)
        product = jnp.dot(
            panel_rows,
            pieces.T,
            precision=lax.Precision.HIGHEST,
            preferred_element_type=jnp.float32,
        )
        trailing = (row_global >= past_col)[:, None] & (col_global >= past_col)[None, :]
        placed_cols = (
            jnp.zeros((local_rows, local_cols), jnp.float32)
            .at[:, first_col:past_col]
            .set(panel_rows)
        )
        factored = jnp.where(trailing, factored - product, factored)
        factored = jnp.where(col_inside[None, :], placed_cols, factored)
        factored = jnp.where(row_inside[:, None] & (col_global >= past_col)[None, :], 0.0, factored)
    return factored


def solution(mesh):
    in_specs = (P("gc", None, "gr"), P("gc", None), P(), P())
    out_specs = P("gr", "gc")
    return jax.shard_map(body, mesh=mesh, in_specs=in_specs, out_specs=out_specs, check_vma=False)
```

profile of v0, /device:TPU:66, one launch (start us, length us, event | category | flops | bytes accessed | tf_op | source)
XLA Modules:
  0.0 1317.6 jit_solution(5797193775737873356)
XLA Ops:
  6.5 0.7 sqrt.3
  7.3 2.7 multiply_convert_fusion
  10.0 140.2 %all-gather.2.cloned.1.call-done = bf16[6,768,2048]{2,1,0:T(8,128)(2,1)} async-done(((bf16[6,768,128]{2,1,0:T(8,128)(2,1)}), bf16[6,768,2048]{2,1,0:T(8,128)(2,1)}) %all-gather.2.cloned.1.call-update) | async-done | bytes 18874384 | tf_op jit(solution)/shard_map/all_gather | solution.py:41
  150.2 8.3 fusion.63
  158.5 1.5 copy.63
  160.0 4.6 copy.39
  164.6 7.4 all-to-all-start
  172.0 0.8 dynamic_slice.11
  172.8 0.8 fusion.59
  173.6 138.4 %all-to-all-done = f32[6,1,128,16,128]{4,2,0,1,3:T(8,128)} async-done(((f32[6,1,128,16,128]{4,2,0,1,3:T(8,128)}), f32[6,1,128,16,128]{4,2,0,1,3:T(8,128)}, u32[]{:S(2)}, u32[]{:S(2)}) %all-to-all-start) | async-done | bytes 6291488 | tf_op jit(solution)/shard_map/all_to_all | solution.py:45
  312.0 9.6 fusion.2
  321.7 0.5 copy.41
  322.4 0.7 slice_select_fusion.1
  323.1 0.2 all-reduce.14.cloned.1.call-start
  323.4 138.0 %all-reduce.12.cloned.1.call-done = f32[256,256]{0,1:T(8,128)} async-done(((f32[256,256]{0,1:T(8,128)}), f32[256,256]{0,1:T(8,128)}) %all-reduce.12.cloned.1.call-update) | async-done | bytes 262160 | tf_op jit(solution)/shard_map/psum | solution.py:15
  461.4 1.1 copy.42
  462.5 1.0 fusion.18
  463.5 11.7 cholesky.130
  475.4 9.8 custom-call.13
  485.2 0.2 fusion.31
  485.5 0.3 convolution_subtract_fusion.3
  485.8 11.7 cholesky.147
  497.6 0.6 compare_reduce_fusion.3
  498.2 0.7 compare_reduce_fusion.2
  500.5 4.6 while.8
  500.7 0.6 fusion.80
  501.3 1.4 dynamic-slice.50
  502.9 0.6 fusion.80
  503.5 1.4 dynamic-slice.50
  505.0 19.7 %custom-call.14 = f32[2,128,128]{1,2,0:T(8,128)S(1)} custom-call(f32[2,128,128]{2,1,0:T(8,128)S(1)} %get-tuple-element.69), custom_call_target="InvertDiagBlocksLowerTriangular" | custom-call | tf_op jit(solution)/shard_map/jit(_solve_triangular)/triangular_solve | solution.py:62
  524.7 0.4 fusion.15
  525.1 0.4 convolution_subtract_fusion.1
  525.6 0.4 fusion.30
  526.0 0.9 fusion.10
  527.0 0.7 compare_reduce_fusion.4
  527.7 141.6 %all-reduce.14.cloned.1.call-done = f32[512,256]{0,1:T(8,128)} async-done(((f32[512,256]{0,1:T(8,128)}), f32[512,256]{0,1:T(8,128)}) %all-reduce.14.cloned.1.call-update) | async-done | bytes 524304 | tf_op jit(solution)/shard_map/psum | solution.py:15
  669.3 2.7 broadcast_select_fusion.2
  672.0 137.6 %all-reduce.16.cloned.1.call-done = f32[512,256]{0,1:T(8,128)} async-done(((f32[512,256]{0,1:T(8,128)}), f32[512,256]{0,1:T(8,128)}) %all-reduce.16.cloned.1.call-update) | async-done | bytes 524304 | tf_op jit(solution)/shard_map/psum | solution.py:15
  809.6 2.5 fusion.8
  812.2 0.7 slice_select_fusion
  813.0 145.3 %all-reduce.18.cloned.1.call-done = f32[256,256]{0,1:T(8,128)} async-done(((f32[256,256]{0,1:T(8,128)}), f32[256,256]{0,1:T(8,128)}) %all-reduce.18.cloned.1.call-update) | async-done | bytes 262160 | tf_op jit(solution)/shard_map/psum | solution.py:15
  958.3 1.1 copy.48
  959.4 1.0 fusion.17
  960.4 11.7 cholesky.164
  972.2 9.8 custom-call.15
  982.4 0.3 convolution_subtract_fusion.2
  982.6 11.7 cholesky.181
  994.5 0.6 compare_reduce_fusion.1
  995.1 0.7 compare_reduce_fusion
  997.3 4.6 while.9
  997.6 0.6 fusion.81
  998.2 1.4 dynamic-slice.52
  999.7 0.6 fusion.81
  1000.3 1.4 dynamic-slice.52
  1001.9 19.7 %custom-call.16 = f32[2,128,128]{1,2,0:T(8,128)S(1)} custom-call(f32[2,128,128]{2,1,0:T(8,128)S(1)} %get-tuple-element.70), custom_call_target="InvertDiagBlocksLowerTriangular" | custom-call | tf_op jit(solution)/shard_map/jit(_solve_triangular)/triangular_solve | solution.py:62
  1021.6 0.4 fusion.13
  1022.0 0.4 convolution_subtract_fusion
  1022.4 0.4 fusion.26
  1022.9 0.9 fusion.12
  1023.8 142.3 %all-reduce.20.cloned.1.call-done = f32[512,256]{0,1:T(8,128)} async-done(((f32[512,256]{0,1:T(8,128)}), f32[512,256]{0,1:T(8,128)}) %all-reduce.20.cloned.1.call-update) | async-done | bytes 524304 | tf_op jit(solution)/shard_map/psum | solution.py:15
  1166.1 0.8 broadcast_select_fusion
  1167.0 139.3 %all-reduce.22.cloned.1.call-done = f32[512,256]{0,1:T(8,128)} async-done(((f32[512,256]{0,1:T(8,128)}), f32[512,256]{0,1:T(8,128)}) %all-reduce.22.cloned.1.call-update) | async-done | bytes 524304 | tf_op jit(solution)/shard_map/psum | solution.py:15
  1306.3 2.7 fusion.6
  1309.0 1.3 copy.54
  (63 shorter events, 2.2 us)
Async XLA Ops:
  6.5 143.7 %all-gather.2.cloned.1.call-start = ((), (), s32[]{:S(2)}) async-start(), calls=%async_computation.1 | async-start | bytes 20054016 | tf_op jit(solution)/shard_map/all_gather | solution.py:41
  164.6 147.5 %all-to-all-start = ((f32[6,1,128,16,128]{4,2,0,1,3:T(8,128)}), f32[6,1,128,16,128]{4,2,0,1,3:T(8,128)}, u32[]{:S(2)}, u32[]{:S(2)}) async-start(f32[6,1,128,16,128]{4,2,0,1,3:T(8,128)} %copy.39), calls=%async_computation | async-start | bytes 12582912 | tf_op jit(solution)/shard_map/all_to_all | solution.py:45
  172.0 289.4 %all-reduce.12.cloned.1.call-start = ((), (), s32[]{:S(2)}) async-start(), calls=%async_computation.2 | async-start | bytes 524288 | tf_op jit(solution)/shard_map/psum | solution.py:15
  323.1 346.2 %all-reduce.14.cloned.1.call-start = ((), (), s32[]{:S(2)}) async-start(), calls=%async_computation.3 | async-start | bytes 1048576 | tf_op jit(solution)/shard_map/psum | solution.py:15
  526.9 282.7 %all-reduce.16.cloned.1.call-start = ((), (), s32[]{:S(2)}) async-start(), calls=%async_computation.4 | async-start | bytes 1048576 | tf_op jit(solution)/shard_map/psum | solution.py:15
  671.9 286.4 %all-reduce.18.cloned.1.call-start = ((), (), s32[]{:S(2)}) async-start(), calls=%async_computation.5 | async-start | bytes 524288 | tf_op jit(solution)/shard_map/psum | solution.py:15
  812.9 353.2 %all-reduce.20.cloned.1.call-start = ((), (), s32[]{:S(2)}) async-start(), calls=%async_computation.6 | async-start | bytes 1048576 | tf_op jit(solution)/shard_map/psum | solution.py:15
  1023.8 282.6 %all-reduce.22.cloned.1.call-start = ((), (), s32[]{:S(2)}) async-start(), calls=%async_computation.7 | async-start | bytes 1048576 | tf_op jit(solution)/shard_map/psum | solution.py:15
Sparse Core Ops, SparseCore 0:
  10.1 140.0 all-gather.1
  323.2 138.1 all-reduce.11
  527.0 142.1 all-reduce.13
  672.1 137.5 all-reduce.15
  813.0 145.2 all-reduce.17
  1023.9 142.1 all-reduce.19
  1168.7 137.5 all-reduce.21
where the time goes:
time: 1330 us; the launch traced here: 1320 us
  waiting for transfers between devices  1120 us (84%)
  other arithmetic  121 us (9%)
  matrix products  26.5 us (2%)
  local copies, waits for them, and re-layouts  21.6 us (2%)
  between operations  17 us (1%)
    psum x6, waiting for transfers between devices, broadcast(): return lax.psum(jnp.where(mine, x, jnp.zeros_like(x)), axis)  844 us
    all_gather x1, waiting for transfers between devices, body(): lax.all_gather(scaled, 'gr', axis=2, tiled=True)  140 us
    all_to_all x1, waiting for transfers between devices, body(): lax.all_to_all(gram_tiles, 'gc', split_axis=3, concat_axis=0, tiled=True)  138 us
    another operation x14, other arithmetic, body(): chol_block = jnp.linalg.cholesky(corner)  69.3 us
    another operation x3, other arithmetic, body(): jax.scipy.linalg.solve_triangular(chol_block, factored[:, first_col:past_...  39.4 us
  transfers between devices with their start and end apart: 8, of which 8 were waited for; matrix products, arithmetic and copies ran while one was open for 0% of the time, Pallas kernels for 0%

commit v1 on v0

v1 whole, which is shorter than its diff:
```python
import jax
import jax.numpy as jnp
import numpy as np
from jax import lax
from jax.experimental import pallas as pl
from jax.experimental.pallas import tpu as pltpu
from jax.sharding import Mesh, PartitionSpec as P

N = 8192
BLK = 128
NWIN = 16
SPAN = 4
R = 768
GROUP = 6
HALF = 3
SLICE = 8
ROWS = HALF * BLK + GROUP * SLICE

AXES = ("x", "yh", "core", "yl", "z")
SIZES = (4, 2, 2, 2, 8)
GR = ("x", "yh", "core")
GC = ("yl", "z")
HIGH = lax.Precision.HIGHEST
CONTRACT_ROWS = (((0,), (0,)), ((), ()))
CONTRACT_COLS = (((1,), (1,)), ((), ()))


def gram_kernel(meta, first, mine, same, other, lead, out):
    q = pl.program_id(0)
    c = meta[1]
    at_same = 2 * q + c
    at_other = 2 * q + 1 - c
    for k in range(HALF):
        pair = jnp.concatenate([same[0, k], other[0, k]], axis=1)
        tiles = lax.dot_general(
            mine[k], pair, CONTRACT_ROWS, preferred_element_type=jnp.float32
        )
        out[at_same, k * BLK : (k + 1) * BLK, :] = tiles[:, :BLK]
        out[at_other, k * BLK : (k + 1) * BLK, :] = tiles[:, BLK:]

    @pl.when(q == 0)
    def _():
        for m in range(GROUP):
            if m < HALF:
                tile = lax.dot_general(
                    first[m], lead[m], CONTRACT_ROWS, preferred_element_type=jnp.float32
                )
            else:
                tile = out[0, (m - HALF) * BLK : (m - HALF + 1) * BLK, :]
            base = HALF * BLK + m * SLICE
            for j in range(NWIN):
                out[j, base : base + SLICE, :] = tile[j * SLICE : (j + 1) * SLICE, :]


def gram_slots(meta, scaled, same, other, lead):
    def pick_half(q, meta):
        return (jnp.where((q > meta[0]) | ((q == meta[0]) & (meta[1] == 0)), 0, 1), 0, 0)

    whole = (HALF, R, BLK)
    grid_spec = pltpu.PrefetchScalarGridSpec(
        num_scalar_prefetch=1,
        grid=(NWIN // 2,),
        in_specs=[
            pl.BlockSpec(whole, lambda q, meta: (0, 0, 0)),
            pl.BlockSpec(whole, pick_half),
            pl.BlockSpec((1,) + whole, lambda q, meta: (q, 0, 0, 0)),
            pl.BlockSpec((1,) + whole, lambda q, meta: (q, 0, 0, 0)),
            pl.BlockSpec(whole, lambda q, meta: (0, 0, 0)),
        ],
        out_specs=pl.BlockSpec((NWIN, ROWS, BLK), lambda q, meta: (0, 0, 0)),
    )
    return pl.pallas_call(
        gram_kernel,
        grid_spec=grid_spec,
        out_shape=jax.ShapeDtypeStruct((NWIN, ROWS, BLK), jnp.float32),
        name="gram_slots",
    )(meta, scaled, scaled, same, other, lead)


def place_kernel(meta, picks, slots, inverse, part, solved, panel):
    g = pl.program_id(0)
    i = meta[2]
    j = meta[3]

    @pl.when(g == 0)
    def _():
        part[...] = jnp.zeros_like(part)
        panel[...] = jnp.zeros_like(panel)

    base = g * GROUP + jnp.where(i < j, 0, HALF)
    for k in range(HALF):
        a = picks[base + k, i]
        b = picks[base + k, j]
        part[a, b] += slots[0, k * BLK : (k + 1) * BLK, :]
    for m in range(GROUP):
        a = picks[g * GROUP + m, i]
        b = picks[g * GROUP + m, 0]
        start = HALF * BLK + m * SLICE
        panel[b, a] += slots[0, start : start + SLICE, :]

    @pl.when(g == pl.num_programs(0) - 1)
    def _():
        for b in range(SPAN):
            rows = panel[b].reshape(SPAN * SLICE, BLK)
            done = lax.dot_general(
                rows,
                inverse[b],
                CONTRACT_COLS,
                precision=HIGH,
                preferred_element_type=jnp.float32,
            )
            solved[b] = done.reshape(SPAN, SLICE, BLK)


def place(meta, picks, slots, inverse):
    grid_spec = pltpu.PrefetchScalarGridSpec(
        num_scalar_prefetch=2,
        grid=(NWIN,),
        in_specs=[
            pl.BlockSpec((1, ROWS, BLK), lambda g, *_: (g, 0, 0)),
            pl.BlockSpec((SPAN, BLK, BLK), lambda g, *_: (0, 0, 0)),
        ],
        out_specs=[
            pl.BlockSpec((SPAN, SPAN, BLK, BLK), lambda g, *_: (0, 0, 0, 0)),
            pl.BlockSpec((SPAN, SPAN, SLICE, BLK), lambda g, *_: (0, 0, 0, 0)),
        ],
        scratch_shapes=[pltpu.VMEM((SPAN, SPAN, SLICE, BLK), jnp.float32)],
    )
    return pl.pallas_call(
        place_kernel,
        grid_spec=grid_spec,
        out_shape=[
            jax.ShapeDtypeStruct((SPAN, SPAN, BLK, BLK), jnp.float32),
            jax.ShapeDtypeStruct((SPAN, SPAN, SLICE, BLK), jnp.float32),
        ],
        name="place_tiles",
    )(meta, picks, slots, inverse)


def finish_kernel(meta, part, mirror, left, right, diag, chol, out):
    i = meta[2]
    j = meta[3]

    def block_rows(ref, a):
        return jnp.concatenate([ref[:, b, a].reshape(BLK, BLK) for b in range(SPAN)], axis=1)

    lefts = [block_rows(left, a) for a in range(SPAN)]
    inside = (i > 0) & (j > 0)

    @pl.when(inside & (i != j))
    def _():
        for a in range(SPAN):
            for b in range(SPAN):
                out[a * BLK : (a + 1) * BLK, b * BLK : (b + 1) * BLK] = part[a, b] + mirror[b, a].T

    @pl.when(inside & (i == j))
    def _():
        out[...] = jnp.zeros_like(out)
        for a in range(SPAN):
            out[a * BLK : (a + 1) * BLK, a * BLK : (a + 1) * BLK] = diag[a]

    @pl.when(inside)
    def _():
        for b in range(SPAN):
            rights = block_rows(right, b)
            for a in range(SPAN):
                spot = (slice(a * BLK, (a + 1) * BLK), slice(b * BLK, (b + 1) * BLK))
                out[spot] = out[spot] - lax.dot_general(
                    lefts[a],
                    rights,
                    CONTRACT_COLS,
                    precision=HIGH,
                    preferred_element_type=jnp.float32,
                )

    @pl.when((i == 0))
    def _():
        out[...] = jnp.zeros_like(out)

    @pl.when((i == 0) & (j == 0))
    def _():
        for a in range(SPAN):
            out[a * BLK : (a + 1) * BLK, a * BLK : (a + 1) * BLK] = chol[a]

    @pl.when((i > 0) & (j == 0))
    def _():
        for a in range(SPAN):
            out[a * BLK : (a + 1) * BLK, :] = lefts[a]


def finish(meta, part, mirror, left, right, diag, chol):
    def full(shape):
        zeros = (0,) * len(shape)
        return pl.BlockSpec(shape, lambda t, meta: zeros)

    blocks = (SPAN, SPAN, BLK, BLK)
    slices = (NWIN, SPAN, SPAN, SLICE, BLK)
    small = (SPAN, BLK, BLK)
    size = (SPAN * BLK, SPAN * BLK)
    grid_spec = pltpu.PrefetchScalarGridSpec(
        num_scalar_prefetch=1,
        grid=(1,),
        in_specs=[full(s) for s in (blocks, blocks, slices, slices, small, small)],
        out_specs=full(size),
    )
    return pl.pallas_call(
        finish_kernel,
        grid_spec=grid_spec,
        out_shape=jax.ShapeDtypeStruct(size, jnp.float32),
        name="finish",
    )(meta, part, mirror, left, right, diag, chol)


def swap_pairs(size, bit):
    return [(k, k ^ bit) for k in range(size)]


def spread_rows(v, steps):
    for step in steps:
        if step == "core":
            v = v + lax.ppermute(v, "core", [(0, 1)])
        elif step == "yh":
            v = v + lax.ppermute(v, "yh", [(0, 1)])
        else:
            up = lax.ppermute(v, "x", [(0, 1)])
            down = lax.ppermute(v, "x", [(0, 3)])
            v = v + up + down
            v = v + lax.ppermute(v, "x", [(1, 2)])
    return v


def body(border, row_scale, block_pick, given_diag):
    i = lax.axis_index(GR).astype(jnp.int32)
    j = lax.axis_index(GC).astype(jnp.int32)
    chip = i // 2
    core = i % 2
    meta = jnp.stack([chip, core, i, j])

    scaled = (jnp.sqrt(row_scale)[:, :, None] * border.astype(jnp.float32)).astype(jnp.bfloat16)

    peers = jnp.arange(8, dtype=jnp.int32)
    early = (peers < chip) | ((peers == chip) & (core == 1))
    slots = jnp.where(early[:, None, None, None], scaled[None, :HALF], scaled[None, HALF:])
    same = lax.all_to_all(slots, ("x", "yh"), 0, 0, tiled=True)
    other = lax.ppermute(same, "core", [(0, 1), (1, 0)])

    lead = spread_rows(
        jnp.where(i == 0, scaled[:HALF], jnp.zeros_like(scaled[:HALF])), ("yh", "x", "core")
    )

    own = jnp.einsum("srx,sry->sxy", scaled, scaled, preferred_element_type=jnp.float32)
    own_pick = lax.dynamic_slice(block_pick, (j * GROUP, i), (GROUP, 1))[:, 0]
    hot = own_pick[:, None] == jnp.arange(SPAN, dtype=jnp.int32)[None, :]
    diag = jnp.sum(jnp.where(hot[:, :, None, None], own[:, None], 0.0), axis=0)
    for bit in (1, 2, 4):
        diag = diag + lax.ppermute(diag, "z", swap_pairs(8, bit))
    diag = diag + lax.ppermute(diag, "yl", swap_pairs(2, 1))
    eye = jnp.eye(BLK, dtype=jnp.float32)
    given_here = lax.dynamic_slice(given_diag, (i * SPAN * BLK,), (SPAN * BLK,))
    diag = diag + given_here.reshape(SPAN, 1, BLK) * eye
    corner = spread_rows(jnp.where(i == 0, diag, 0.0), ("core", "yh", "x"))
    chol = jnp.linalg.cholesky(corner)
    inverse = lax.linalg.triangular_solve(
        chol, jnp.broadcast_to(eye, chol.shape), left_side=True, lower=True
    )

    tiles = gram_slots(meta, scaled, same, other, lead)
    tiles = lax.all_to_all(tiles, GC, 0, 0, tiled=True)
    part, solved = place(meta, block_pick, tiles, inverse)
    everywhere = [(r * NWIN + c, c * NWIN + r) for r in range(NWIN) for c in range(NWIN)]
    turned = lax.ppermute(solved, AXES, everywhere)
    mirror = lax.ppermute(part, AXES, everywhere)
    copies = (NWIN,) + solved.shape
    left = lax.all_to_all(jnp.broadcast_to(solved, copies), GC, 0, 0, tiled=True)
    right = lax.all_to_all(jnp.broadcast_to(turned, copies), GR, 0, 0, tiled=True)
    return finish(meta, part, mirror, left, right, diag, chol)


def solution(mesh):
    fine = Mesh(np.asarray(mesh.devices).reshape(SIZES), AXES)
    in_specs = (P(GC, None, GR), P(GC, None), P(), P())
    return jax.shard_map(
        body, mesh=fine, in_specs=in_specs, out_specs=P(GR, GC), check_vma=False
    )
```

time: 1330 us -> 544 us (0.41)
  waiting for transfers between devices: 1120 us -> 264 us
  blocking collectives: 0 us -> 84.6 us
  starting transfers between devices: 7.85 us -> 64.7 us
  Pallas kernels: 0 us -> 30.1 us
  other arithmetic: 121 us -> 93.1 us
  matrix products: 26.5 us -> 1.81 us
  local copies, waits for them, and re-layouts: 21.6 us -> 4.54 us
  between operations: 17 us -> 0.3 us
    psum x6 -> x0, waiting for transfers between devices: 844 us -> none  [broadcast(): return lax.psum(jnp.where(mine, x, jnp.zeros_like(x)), axis)]
    ppermute x0 -> x17, waiting for transfers between devices: none -> 264 us  [the longest x3 104 us: body(): diag = diag + lax.ppermute(diag, 'z', swap_pairs(8, bit))]
    all_gather x1 -> x0, waiting for transfers between devices: 140 us -> none  [body(): lax.all_gather(scaled, 'gr', axis=2, tiled=True)]
    all_to_all x1 -> x2, waiting for transfers between devices: 138 us -> 0.01 us  [the longest x1 0.01 us: body(): tiles = lax.all_to_all(tiles, GC, 0, 0, tiled=True)]
    all_to_all x0 -> x2, blocking collectives: none -> 84.6 us  [the longest x1 62.4 us: body(): same = lax.all_to_all(slots, ('x', 'yh'), 0, 0, tiled=True)]
    ppermute x0 -> x17, starting transfers between devices: none -> 42.1 us  [the longest x2 9.56 us: spread_rows(): v = v + lax.ppermute(v, 'yh', [(0, 1)])]
    pallas_call x0 -> x3, Pallas kernels: none -> 30.1 us  [the longest x1 11.4 us: place(): pl.pallas_call(place_kernel, grid_spec=grid_spec, out_shape=[jax.ShapeDty...]
    another operation x20 -> x8, other arithmetic: 112 us -> 87.9 us  [the longest x4 47.1 us: body(): chol = jnp.linalg.cholesky(corner)]
  transfers between devices with their start and end apart: 8 -> 19, of which waited for: 8 -> 14; matrix products, arithmetic and copies ran while one was open for 0% -> 17% of each run, Pallas kernels for 0% -> 0%
where the time goes in v1:
time: 544 us; the launch traced here: 543 us
  waiting for transfers between devices  264 us (49%)
  other arithmetic  93.1 us (17%)
  blocking collectives  84.6 us (16%)
  starting transfers between devices  64.7 us (12%)
  Pallas kernels  30.1 us (6%)
    ppermute x3, waiting for transfers between devices, body(): diag = diag + lax.ppermute(diag, 'z', swap_pairs(8, bit))  104 us
    ppermute x1, waiting for transfers between devices, body(): mirror = lax.ppermute(part, AXES, everywhere)  88.8 us
    all_to_all x1, blocking collectives, body(): same = lax.all_to_all(slots, ('x', 'yh'), 0, 0, tiled=True)  62.4 us
    another operation x4, other arithmetic, body(): chol = jnp.linalg.cholesky(corner)  47.1 us
    another operation x3, other arithmetic, body(): lax.linalg.triangular_solve(chol, jnp.broadcast_to(eye, chol.shape), left...  40.2 us
    ppermute x2, waiting for transfers between devices, spread_rows(): up = lax.ppermute(v, 'x', [(0, 1)])  25 us
    all_to_all x1, blocking collectives, body(): lax.all_to_all(jnp.broadcast_to(turned, copies), GR, 0, 0, tiled=True)  22.2 us
    ppermute x2, waiting for transfers between devices, spread_rows(): v = v + lax.ppermute(v, 'yh', [(0, 1)])  19.3 us
  transfers between devices with their start and end apart: 19, of which 14 were waited for; matrix products, arithmetic and copies ran while one was open for 17% of the time, Pallas kernels for 0%

profile of v1, /device:TPU:66, one launch (start us, length us, event | category | flops | bytes accessed | tf_op | source)
XLA Modules:
  0.0 543.0 jit_solution(9423665849499603378)
XLA Ops:
  0.0 0.8 sqrt.3
  0.8 1.9 multiply_convert_fusion.first.mine
  2.7 0.1 broadcast_select_fusion.1
  2.8 0.6 broadcast_select_fusion
  3.4 0.3 copy-done.1
  3.7 62.4 %all_to_all.20.same = bf16[8,3,768,128]{3,2,1,0:T(8,128)(2,1)} all-to-all(bf16[8,3,768,128]{3,2,1,0:T(8,128)(2,1)S(1)} %broadcast_select_fusion), channel_id=1, replica_groups=mesh['x'=4,'yh'=2,'core'=2,'yl'=2,'z'=8] {'x','yh'}, dimensions={0} | all-to-all | bytes 9437184 | tf_op jit(solution)/shard_map/all_to_all | solution.py:244
  66.1 3.5 collective-permute-start.1
  69.6 13.2 %collective-permute-done.1 = bf16[3,768,128]{2,1,0:T(8,128)(2,1)S(1)} collective-permute-done((bf16[3,768,128]{2,1,0:T(8,128)(2,1)S(1)}, bf16[3,768,128]{2,1,0:T(8,128)(2,1)S(1)}, u32[]{:S(2)}, u32[]{:S(2)}) %collective-permute-start.1) | collective-permute-done | bytes 589856 | tf_op jit(solution)/shard_map/ppermute | solution.py:223
  82.8 0.2 add.83
  83.0 0.7 collective-permute-start.3
  83.7 1.3 collective-permute-start.2
  85.0 16.7 %collective-permute-done.2 = bf16[3,768,128]{2,1,0:T(8,128)(2,1)S(1)} collective-permute-done((bf16[3,768,128]{2,1,0:T(8,128)(2,1)S(1)}, bf16[3,768,128]{2,1,0:T(8,128)(2,1)S(1)}, u32[]{:S(2)}, u32[]{:S(2)}) %collective-permute-start.2) | collective-permute-done | bytes 589856 | tf_op jit(solution)/shard_map/ppermute | solution.py:225
  101.7 0.1 add_add_fusion
  101.7 1.3 collective-permute-start.4
  103.1 11.8 %collective-permute-done.4 = bf16[3,768,128]{2,1,0:T(8,128)(2,1)S(1)} collective-permute-done((bf16[3,768,128]{2,1,0:T(8,128)(2,1)S(1)}, bf16[3,768,128]{2,1,0:T(8,128)(2,1)S(1)}, u32[]{:S(2)}, u32[]{:S(2)}) %collective-permute-start.4) | collective-permute-done | bytes 589856 | tf_op jit(solution)/shard_map/ppermute | solution.py:228
  114.8 0.2 add.86
  115.0 1.3 collective-permute-start.5
  116.3 0.7 pad_add_fusion.meta
  117.0 0.9 collective-permute-done.5
  117.9 1.0 add.87.lead
  118.9 10.9 %gram_slots.1 = f32[16,432,128]{2,1,0:T(8,128)} custom-call(s32[4]{0:T(128)} %pad_add_fusion.meta, bf16[6,768,128]{2,1,0:T(8,128)(2,1)} %copy-done.1, bf16[6,768,128]{2,1,0:T(8,128)(2,1)} %copy-done.1, bf16[8,3,768,128]{3,2,1,0:T(8,128)(2,1)} %all_to_all.20.same, bf16[8,3,768,128]{3,2,1,0:T(8,128)(2,1)} %collective-permute-done.other, ...), custom_call_target="tpu_custom_call" | custom-call | tf_op jit(solution)/shard_map/gram_slots/pallas_call | solution.py:72
  129.8 8.4 %all-to-all-start.1 = ((f32[16,432,128]{2,1,0:T(8,128)}), f32[16,432,128]{2,1,0:T(8,128)}, u32[]{:S(2)}, u32[]{:S(2)}) async-start(f32[16,432,128]{2,1,0:T(8,128)} %gram_slots.1), calls=%async_computation.1 | async-start | bytes 7077888 | tf_op jit(solution)/shard_map/all_to_all | solution.py:268
  138.2 0.1 dynamic-slice_bitcast_fusion.1
  138.3 0.1 iota_compare_fusion.2
  138.3 0.5 fusion.5
  138.9 0.2 select_reduce_fusion
  139.1 1.6 collective-permute-start.6
  140.6 84.0 %collective-permute-done.6 = f32[4,128,128]{2,1,0:T(8,128)S(1)} collective-permute-done((f32[4,128,128]{2,1,0:T(8,128)S(1)}, f32[4,128,128]{2,1,0:T(8,128)S(1)}, u32[]{:S(2)}, u32[]{:S(2)}) %collective-permute-start.6) | collective-permute-done | bytes 262176 | tf_op jit(solution)/shard_map/ppermute | solution.py:256
  224.7 0.1 collective-permute-start.7
  224.8 10.9 %collective-permute-done.7 = f32[4,128,128]{2,1,0:T(8,128)S(1)} collective-permute-done((f32[4,128,128]{2,1,0:T(8,128)S(1)}, f32[4,128,128]{2,1,0:T(8,128)S(1)}, u32[]{:S(2)}, u32[]{:S(2)}) %collective-permute-start.7) | collective-permute-done | bytes 262176 | tf_op jit(solution)/shard_map/ppermute | solution.py:256
  235.7 4.6 collective-permute-start.8
  240.3 9.0 %collective-permute-done.8 = f32[4,128,128]{2,1,0:T(8,128)S(1)} collective-permute-done((f32[4,128,128]{2,1,0:T(8,128)S(1)}, f32[4,128,128]{2,1,0:T(8,128)S(1)}, u32[]{:S(2)}, u32[]{:S(2)}) %collective-permute-start.8) | collective-permute-done | bytes 262176 | tf_op jit(solution)/shard_map/ppermute | solution.py:256
  249.3 1.5 collective-permute-start.9
  250.8 0.1 dynamic-slice_bitcast_fusion
  250.9 4.9 collective-permute-done.9
  255.8 0.8 broadcast_select_fusion.2
  256.6 1.3 collective-permute-start.10
  257.9 1.1 collective-permute-done.10
  259.0 6.0 %collective-permute-start.11 = (f32[4,128,128]{2,1,0:T(8,128)S(1)}, f32[4,128,128]{2,1,0:T(8,128)S(1)}, u32[]{:S(2)}, u32[]{:S(2)}) collective-permute-start(f32[4,128,128]{2,1,0:T(8,128)S(1)} %add.96), channel_id=1, source_target_pairs={{0,32},{1,33},{2,34},{3,35},{4,36},{5,37},{6,38},{7,39},{8,40},{9,... | collective-permute-start | bytes 786440 | tf_op jit(solution)/shard_map/ppermute | solution.py:223
  265.0 6.1 %collective-permute-done.11 = f32[4,128,128]{2,1,0:T(8,128)S(1)} collective-permute-done((f32[4,128,128]{2,1,0:T(8,128)S(1)}, f32[4,128,128]{2,1,0:T(8,128)S(1)}, u32[]{:S(2)}, u32[]{:S(2)}) %collective-permute-start.11) | collective-permute-done | bytes 262176 | tf_op jit(solution)/shard_map/ppermute | solution.py:223
  271.1 0.7 collective-permute-start.13
  271.8 1.3 collective-permute-start.12
  273.1 8.3 %collective-permute-done.12 = f32[4,128,128]{2,1,0:T(8,128)S(1)} collective-permute-done((f32[4,128,128]{2,1,0:T(8,128)S(1)}, f32[4,128,128]{2,1,0:T(8,128)S(1)}, u32[]{:S(2)}, u32[]{:S(2)}) %collective-permute-start.12) | collective-permute-done | bytes 262176 | tf_op jit(solution)/shard_map/ppermute | solution.py:225
  281.5 1.5 collective-permute-start.14
  283.0 0.7 copy.14.picks
  283.7 3.7 collective-permute-done.14
  287.5 0.1 copy.11
  287.7 46.9 %custom-call.7 = f32[4,128,128]{2,1,0:T(8,128)S(1)} custom-call(f32[4,128,128]{2,1,0:T(8,128)S(1)} %fusion.2), custom_call_target="Cholesky" | custom-call | tf_op jit(solution)/shard_map/jit(cholesky)/cholesky | solution.py:262
  334.6 0.1 compare_reduce_fusion
  334.7 0.8 select_bitcast_fusion
  335.6 39.3 %custom-call.8 = f32[4,1,128,128]{2,3,1,0:T(8,128)S(1)} custom-call(f32[4,1,128,128]{3,2,1,0:T(8,128)S(1)} %get-tuple-element.9), custom_call_target="InvertDiagBlocksLowerTriangular" | custom-call | tf_op jit(solution)/shard_map/triangular_solve | solution.py:263
  374.9 1.3 fusion.inverse
  376.2 11.4 %place_tiles.1 = (f32[4,4,128,128]{3,2,1,0:T(8,128)}, f32[4,4,8,128]{3,2,1,0:T(8,128)}) custom-call(s32[4]{0:T(128)} %pad_add_fusion.meta, s32[96,16]{1,0:T(8,128)} %copy.14.picks, f32[16,432,128]{2,1,0:T(8,128)} %all-to-all-done.1.slots, f32[4,128,128]{2,1,0:T(8,128)} %fusion.inverse), custom_call_target="tpu_custom_call" | custom-call | tf_op jit(solution)/shard_map/place_tiles/pallas_call | solution.py:129
  387.5 7.8 %collective-permute-start.16 = (f32[4,4,8,128]{3,2,1,0:T(8,128)}, f32[4,4,8,128]{3,2,1,0:T(8,128)S(1)}, u32[]{:S(2)}, u32[]{:S(2)}) collective-permute-start(f32[4,4,8,128]{3,2,1,0:T(8,128)} %get-tuple-element.8), channel_id=1, source_target_pairs={{0,0},{1,16},{2,32},{3,48},{4,64},{5,80},{6,96},{7,112},{8,128},{9... | collective-permute-start | bytes 196616 | tf_op jit(solution)/shard_map/ppermute | solution.py:271
  395.4 4.4 collective-permute-done.16
  399.7 0.1 broadcast_in_dim.79
  399.9 22.2 %all_to_all.21.right = f32[16,4,4,8,128]{4,3,2,1,0:T(8,128)} all-to-all(f32[16,4,4,8,128]{4,3,2,1,0:T(8,128)S(1)} %broadcast_in_dim.79), channel_id=1, replica_groups=mesh['x'=4,'yh'=2,'core'=2,'yl'=2,'z'=8] {'x','yh','core'}, dimensions={0} | all-to-all | bytes 2097152 | tf_op jit(solution)/shard_map/all_to_all | solution.py:275
  422.0 1.1 broadcast_in_dim.78
  423.1 14.2 %all-to-all-start.2 = ((f32[16,4,4,8,128]{4,3,2,1,0:T(8,128)}), f32[16,4,4,8,128]{4,3,2,1,0:T(8,128)S(1)}, u32[]{:S(2)}, u32[]{:S(2)}) async-start(f32[16,4,4,8,128]{4,3,2,1,0:T(8,128)} %broadcast_in_dim.78), calls=%async_computation.2 | async-start | bytes 2097152 | tf_op jit(solution)/shard_map/all_to_all | solution.py:274
  437.3 7.7 %collective-permute-start.15 = (f32[4,4,128,128]{3,2,1,0:T(8,128)S(1)}, f32[4,4,128,128]{3,2,1,0:T(8,128)S(1)}, u32[]{:S(2)}, u32[]{:S(2)}) collective-permute-start(f32[4,4,128,128]{3,2,1,0:T(8,128)S(1)} %copy-done.4), channel_id=1, source_target_pairs={{0,0},{1,16},{2,32},{3,48},{4,64},{5,80},{6,96},{7,112},{8,128},{9... | collective-permute-start | bytes 3145736 | tf_op jit(solution)/shard_map/ppermute | solution.py:272
  445.0 88.8 %collective-permute-done.15.mirror = f32[4,4,128,128]{3,2,1,0:T(8,128)S(1)} collective-permute-done((f32[4,4,128,128]{3,2,1,0:T(8,128)S(1)}, f32[4,4,128,128]{3,2,1,0:T(8,128)S(1)}, u32[]{:S(2)}, u32[]{:S(2)}) %collective-permute-start.15) | collective-permute-done | bytes 1048608 | tf_op jit(solution)/shard_map/ppermute | solution.py:272
  533.8 1.0 copy-done.5
  534.8 0.3 copy-done.3
  535.1 7.9 %finish.1 = f32[512,512]{1,0:T(8,128)} custom-call(s32[4]{0:T(128)} %pad_add_fusion.meta, f32[4,4,128,128]{3,2,1,0:T(8,128)} %get-tuple-element.7.part, f32[4,4,128,128]{3,2,1,0:T(8,128)} %copy-done.5, f32[16,4,4,8,128]{4,3,2,1,0:T(8,128)} %copy-done.3, f32[16,4,4,8,128]{4,3,2,1,0:T(8,128)} %all_to_all.21.right, f32[4,128,128]{2,1,0:T(8,128)} %get-tuple-element.12.diag, ...), custom_call_target="tpu_custom_call" | custom-call | tf_op jit(solution)/shard_map/finish/pallas_call | solution.py:206
  (32 shorter events, 0.4 us)
Async XLA Ops:
  0.0 250.8 %copy-start = (f32[8192]{0:T(1024)S(1)}, f32[8192]{0:T(1024)}, u32[]{:S(2)}) copy-start(f32[8192]{0:T(1024)} %param.7) | copy-start | bytes 98308
  2.6 1.0 copy-start.1
  66.1 52.8 %collective-permute-start = (bf16[8,3,768,128]{3,2,1,0:T(8,128)(2,1)}, bf16[8,3,768,128]{3,2,1,0:T(8,128)(2,1)}, u32[]{:S(2)}, u32[]{:S(2)}) collective-permute-start(bf16[8,3,768,128]{3,2,1,0:T(8,128)(2,1)} %all_to_all.20.same), channel_id=1, source_target_pairs={{0,16},{16,0},{1,17},{17,1},{2,18},{18,2},{3,19},{19,3},{4,20},{20... | collective-permute-start | bytes 14155784 | tf_op jit(solution)/shard_map/ppermute | solution.py:245
  66.1 16.8 %collective-permute-start.1 = (bf16[3,768,128]{2,1,0:T(8,128)(2,1)S(1)}, bf16[3,768,128]{2,1,0:T(8,128)(2,1)S(1)}, u32[]{:S(2)}, u32[]{:S(2)}) collective-permute-start(bf16[3,768,128]{2,1,0:T(8,128)(2,1)S(1)} %get-tuple-element.13), channel_id=1, source_target_pairs={{0,32},{1,33},{2,34},{3,35},{4,36},{5,37},{6,38},{7,39},{8,40},{9,... | collective-permute-start | bytes 1769480 | tf_op jit(solution)/shard_map/ppermute | solution.py:223
  83.0 2.0 collective-permute-start.3
  83.7 18.0 %collective-permute-start.2 = (bf16[3,768,128]{2,1,0:T(8,128)(2,1)S(1)}, bf16[3,768,128]{2,1,0:T(8,128)(2,1)S(1)}, u32[]{:S(2)}, u32[]{:S(2)}) collective-permute-start(bf16[3,768,128]{2,1,0:T(8,128)(2,1)S(1)} %add.83), channel_id=1, source_target_pairs={{0,64},{1,65},{2,66},{3,67},{4,68},{5,69},{6,70},{7,71},{8,72},{9,... | collective-permute-start | bytes 1769480 | tf_op jit(solution)/shard_map/ppermute | solution.py:225
  101.7 13.1 %collective-permute-start.4 = (bf16[3,768,128]{2,1,0:T(8,128)(2,1)S(1)}, bf16[3,768,128]{2,1,0:T(8,128)(2,1)S(1)}, u32[]{:S(2)}, u32[]{:S(2)}) collective-permute-start(bf16[3,768,128]{2,1,0:T(8,128)(2,1)S(1)} %add_add_fusion), channel_id=1, source_target_pairs={{64,128},{65,129},{66,130},{67,131},{68,132},{69,133},{70,134},{71... | collective-permute-start | bytes 1769480 | tf_op jit(solution)/shard_map/ppermute | solution.py:228
  115.0 2.9 collective-permute-start.5
  129.8 8.4 %copy-start.7 = (s32[96,16]{0,1:T(8,128)S(1)}, s32[96,16]{0,1:T(8,128)}, u32[]{:S(2)}) copy-start(s32[96,16]{0,1:T(8,128)} %param.6) | copy-start | bytes 18436
  129.8 8.5 %copy-start.2 = (bf16[6,768,128]{2,1,0:T(8,128)(2,1)S(1)}, bf16[6,768,128]{2,1,0:T(8,128)(2,1)}, u32[]{:S(2)}) copy-start(bf16[6,768,128]{2,1,0:T(8,128)(2,1)} %copy-done.1) | copy-start | bytes 3538948
  129.8 246.3 %all-to-all-start.1 = ((f32[16,432,128]{2,1,0:T(8,128)}), f32[16,432,128]{2,1,0:T(8,128)}, u32[]{:S(2)}, u32[]{:S(2)}) async-start(f32[16,432,128]{2,1,0:T(8,128)} %gram_slots.1), calls=%async_computation.1 | async-start | bytes 7077888 | tf_op jit(solution)/shard_map/all_to_all | solution.py:268
  139.1 85.6 %collective-permute-start.6 = (f32[4,128,128]{2,1,0:T(8,128)S(1)}, f32[4,128,128]{2,1,0:T(8,128)S(1)}, u32[]{:S(2)}, u32[]{:S(2)}) collective-permute-start(f32[4,128,128]{2,1,0:T(8,128)S(1)} %select_reduce_fusion), channel_id=1, source_target_pairs={{0,1},{1,0},{2,3},{3,2},{4,5},{5,4},{6,7},{7,6},{8,9},{9,8},{10,11... | collective-permute-start | bytes 786440 | tf_op jit(solution)/shard_map/ppermute | solution.py:256
  224.7 11.0 %collective-permute-start.7 = (f32[4,128,128]{2,1,0:T(8,128)S(1)}, f32[4,128,128]{2,1,0:T(8,128)S(1)}, u32[]{:S(2)}, u32[]{:S(2)}) collective-permute-start(f32[4,128,128]{2,1,0:T(8,128)S(1)} %add.90), channel_id=1, source_target_pairs={{0,2},{1,3},{2,0},{3,1},{4,6},{5,7},{6,4},{7,5},{8,10},{9,11},{10,... | collective-permute-start | bytes 786440 | tf_op jit(solution)/shard_map/ppermute | solution.py:256
  235.7 13.6 %collective-permute-start.8 = (f32[4,128,128]{2,1,0:T(8,128)S(1)}, f32[4,128,128]{2,1,0:T(8,128)S(1)}, u32[]{:S(2)}, u32[]{:S(2)}) collective-permute-start(f32[4,128,128]{2,1,0:T(8,128)S(1)} %add.91), channel_id=1, source_target_pairs={{0,4},{1,5},{2,6},{3,7},{4,0},{5,1},{6,2},{7,3},{8,12},{9,13},{10,... | collective-permute-start | bytes 786440 | tf_op jit(solution)/shard_map/ppermute | solution.py:256
  249.3 6.5 %collective-permute-start.9 = (f32[4,128,128]{2,1,0:T(8,128)S(1)}, f32[4,128,128]{2,1,0:T(8,128)S(1)}, u32[]{:S(2)}, u32[]{:S(2)}) collective-permute-start(f32[4,128,128]{2,1,0:T(8,128)S(1)} %add.92), channel_id=1, source_target_pairs={{0,8},{8,0},{1,9},{9,1},{2,10},{10,2},{3,11},{11,3},{4,12},{12,4},... | collective-permute-start | bytes 786440 | tf_op jit(solution)/shard_map/ppermute | solution.py:257
  256.6 2.4 collective-permute-start.10
  259.0 12.1 %collective-permute-start.11 = (f32[4,128,128]{2,1,0:T(8,128)S(1)}, f32[4,128,128]{2,1,0:T(8,128)S(1)}, u32[]{:S(2)}, u32[]{:S(2)}) collective-permute-start(f32[4,128,128]{2,1,0:T(8,128)S(1)} %add.96), channel_id=1, source_target_pairs={{0,32},{1,33},{2,34},{3,35},{4,36},{5,37},{6,38},{7,39},{8,40},{9,... | collective-permute-start | bytes 786440 | tf_op jit(solution)/shard_map/ppermute | solution.py:223
  271.1 2.0 collective-permute-start.13
  271.8 9.6 %collective-permute-start.12 = (f32[4,128,128]{2,1,0:T(8,128)S(1)}, f32[4,128,128]{2,1,0:T(8,128)S(1)}, u32[]{:S(2)}, u32[]{:S(2)}) collective-permute-start(f32[4,128,128]{2,1,0:T(8,128)S(1)} %add.97), channel_id=1, source_target_pairs={{0,64},{1,65},{2,66},{3,67},{4,68},{5,69},{6,70},{7,71},{8,72},{9,... | collective-permute-start | bytes 786440 | tf_op jit(solution)/shard_map/ppermute | solution.py:225
  281.5 6.0 %collective-permute-start.14 = (f32[4,128,128]{2,1,0:T(8,128)S(1)}, f32[4,128,128]{2,1,0:T(8,128)S(1)}, u32[]{:S(2)}, u32[]{:S(2)}) collective-permute-start(f32[4,128,128]{2,1,0:T(8,128)S(1)} %add_add_fusion.1), channel_id=1, source_target_pairs={{64,128},{65,129},{66,130},{67,131},{68,132},{69,133},{70,134},{71... | collective-permute-start | bytes 786440 | tf_op jit(solution)/shard_map/ppermute | solution.py:228
  387.5 34.5 %copy-start.6 = (f32[4,4,8,128]{3,2,1,0:T(8,128)S(1)}, f32[4,4,8,128]{3,2,1,0:T(8,128)}, u32[]{:S(2)}) copy-start(f32[4,4,8,128]{3,2,1,0:T(8,128)} %get-tuple-element.8) | copy-start | bytes 196612
  387.5 12.2 %collective-permute-start.16 = (f32[4,4,8,128]{3,2,1,0:T(8,128)}, f32[4,4,8,128]{3,2,1,0:T(8,128)S(1)}, u32[]{:S(2)}, u32[]{:S(2)}) collective-permute-start(f32[4,4,8,128]{3,2,1,0:T(8,128)} %get-tuple-element.8), channel_id=1, source_target_pairs={{0,0},{1,16},{2,32},{3,48},{4,64},{5,80},{6,96},{7,112},{8,128},{9... | collective-permute-start | bytes 196616 | tf_op jit(solution)/shard_map/ppermute | solution.py:271
  422.0 15.3 %copy-start.4 = (f32[4,4,128,128]{3,2,1,0:T(8,128)S(1)}, f32[4,4,128,128]{3,2,1,0:T(8,128)}, u32[]{:S(2)}) copy-start(f32[4,4,128,128]{3,2,1,0:T(8,128)} %get-tuple-element.7.part) | copy-start | bytes 3145732
  423.1 110.7 %all-to-all-start.2 = ((f32[16,4,4,8,128]{4,3,2,1,0:T(8,128)}), f32[16,4,4,8,128]{4,3,2,1,0:T(8,128)S(1)}, u32[]{:S(2)}, u32[]{:S(2)}) async-start(f32[16,4,4,8,128]{4,3,2,1,0:T(8,128)} %broadcast_in_dim.78), calls=%async_computation.2 | async-start | bytes 2097152 | tf_op jit(solution)/shard_map/all_to_all | solution.py:274
  437.3 96.5 %collective-permute-start.15 = (f32[4,4,128,128]{3,2,1,0:T(8,128)S(1)}, f32[4,4,128,128]{3,2,1,0:T(8,128)S(1)}, u32[]{:S(2)}, u32[]{:S(2)}) collective-permute-start(f32[4,4,128,128]{3,2,1,0:T(8,128)S(1)} %copy-done.4), channel_id=1, source_target_pairs={{0,0},{1,16},{2,32},{3,48},{4,64},{5,80},{6,96},{7,112},{8,128},{9... | collective-permute-start | bytes 3145736 | tf_op jit(solution)/shard_map/ppermute | solution.py:272
  533.8 1.0 copy-start.5
  533.8 1.3 copy-start.3

commit v2 on v1

v2 whole, which is shorter than its diff:
```python
import jax
import jax.numpy as jnp
import numpy as np
from jax import lax
from jax.experimental import pallas as pl
from jax.experimental.pallas import tpu as pltpu
from jax.sharding import Mesh, PartitionSpec as P

BLK = 128
NWIN = 16
SPAN = 4
R = 768
GROUP = 6
HALF = 3
SLICE = 8
ROWS = HALF * BLK + GROUP * SLICE
PLACE = 4

AXES = ("x", "yh", "core", "yl", "z")
SIZES = (4, 2, 2, 2, 8)
GR = ("x", "yh", "core")
GC = ("yl", "z")
HIGH = lax.Precision.HIGHEST
CONTRACT_ROWS = (((0,), (0,)), ((), ()))
CONTRACT_COLS = (((1,), (1,)), ((), ()))


def gram_kernel(meta, mine, same, other, out, late):
    q = pl.program_id(0)
    c = meta[1]
    at_same = 2 * q + c
    at_other = 2 * q + 1 - c
    for k in range(HALF):
        pair = jnp.concatenate([same[0, k], other[0, k]], axis=1)
        tiles = lax.dot_general(
            mine[k], pair, CONTRACT_ROWS, preferred_element_type=jnp.float32
        )
        out[at_same, k * BLK : (k + 1) * BLK, :] = tiles[:, :BLK]
        out[at_other, k * BLK : (k + 1) * BLK, :] = tiles[:, BLK:]

    @pl.when(q == 0)
    def _():
        late[...] = out[0, : HALF * BLK, :].reshape(HALF, BLK, BLK)
        out[:, HALF * BLK :, :] = jnp.zeros((NWIN, GROUP * SLICE, BLK), jnp.float32)


def gram_slots(meta, scaled, same, other):
    def pick_half(q, meta):
        return (jnp.where((q > meta[0]) | ((q == meta[0]) & (meta[1] == 0)), 0, 1), 0, 0)

    whole = (HALF, R, BLK)
    grid_spec = pltpu.PrefetchScalarGridSpec(
        num_scalar_prefetch=1,
        grid=(NWIN // 2,),
        in_specs=[
            pl.BlockSpec(whole, pick_half),
            pl.BlockSpec((1,) + whole, lambda q, meta: (q, 0, 0, 0)),
            pl.BlockSpec((1,) + whole, lambda q, meta: (q, 0, 0, 0)),
        ],
        out_specs=[
            pl.BlockSpec((NWIN, ROWS, BLK), lambda q, meta: (0, 0, 0)),
            pl.BlockSpec((HALF, BLK, BLK), lambda q, meta: (0, 0, 0)),
        ],
    )
    return pl.pallas_call(
        gram_kernel,
        grid_spec=grid_spec,
        out_shape=[
            jax.ShapeDtypeStruct((NWIN, ROWS, BLK), jnp.float32),
            jax.ShapeDtypeStruct((HALF, BLK, BLK), jnp.float32),
        ],
        name="gram_slots",
    )(meta, scaled, same, other)


def panel_kernel(first, lead, late, held, out):
    del held
    for m in range(GROUP):
        if m < HALF:
            tile = lax.dot_general(
                first[m], lead[m], CONTRACT_ROWS, preferred_element_type=jnp.float32
            )
        else:
            tile = late[m - HALF]
        for j in range(NWIN):
            out[j, m * SLICE : (m + 1) * SLICE, :] = tile[j * SLICE : (j + 1) * SLICE, :]


def panel_slots(scaled, lead, late, slots):
    whole = (HALF, R, BLK)
    rows = GROUP * SLICE
    return pl.pallas_call(
        panel_kernel,
        grid=(1,),
        in_specs=[
            pl.BlockSpec(whole, lambda t: (0, 0, 0)),
            pl.BlockSpec(whole, lambda t: (0, 0, 0)),
            pl.BlockSpec((HALF, BLK, BLK), lambda t: (0, 0, 0)),
            pl.BlockSpec(memory_space=pl.ANY),
        ],
        out_specs=pl.BlockSpec((NWIN, rows, BLK), lambda t: (0, HALF * BLK // rows, 0)),
        out_shape=jax.ShapeDtypeStruct(slots.shape, slots.dtype),
        input_output_aliases={3: 0},
        name="panel_slots",
    )(scaled, lead, late, slots)


def place_kernel(meta, picks, slots, part, panel):
    g = pl.program_id(0)
    i = meta[2]
    j = meta[3]

    @pl.when(g == 0)
    def _():
        part[...] = jnp.zeros_like(part)
        panel[...] = jnp.zeros_like(panel)

    for u in range(PLACE):
        group = g * PLACE + u
        base = group * GROUP + jnp.where(i < j, 0, HALF)
        for k in range(HALF):
            a = picks[base + k, i]
            b = picks[base + k, j]
            part[a, b] += slots[u, k * BLK : (k + 1) * BLK, :]
        for m in range(GROUP):
            a = picks[group * GROUP + m, i]
            b = picks[group * GROUP + m, 0]
            start = HALF * BLK + m * SLICE
            panel[b, a] += slots[u, start : start + SLICE, :]


def place(meta, picks, slots):
    grid_spec = pltpu.PrefetchScalarGridSpec(
        num_scalar_prefetch=2,
        grid=(NWIN // PLACE,),
        in_specs=[pl.BlockSpec((PLACE, ROWS, BLK), lambda g, *_: (g, 0, 0))],
        out_specs=[
            pl.BlockSpec((SPAN, SPAN, BLK, BLK), lambda g, *_: (0, 0, 0, 0)),
            pl.BlockSpec((SPAN, SPAN, SLICE, BLK), lambda g, *_: (0, 0, 0, 0)),
        ],
    )
    return pl.pallas_call(
        place_kernel,
        grid_spec=grid_spec,
        out_shape=[
            jax.ShapeDtypeStruct((SPAN, SPAN, BLK, BLK), jnp.float32),
            jax.ShapeDtypeStruct((SPAN, SPAN, SLICE, BLK), jnp.float32),
        ],
        name="place_tiles",
    )(meta, picks, slots)


def finish_kernel(meta, part, mirror, left, right, diag, chol, inverse, out):
    i = meta[2]
    j = meta[3]

    def block_rows(ref, a):
        solved = [
            lax.dot_general(
                ref[:, b, a].reshape(BLK, BLK),
                inverse[b],
                CONTRACT_COLS,
                precision=HIGH,
                preferred_element_type=jnp.float32,
            )
            for b in range(SPAN)
        ]
        return jnp.concatenate(solved, axis=1)

    lefts = [block_rows(left, a) for a in range(SPAN)]
    inside = (i > 0) & (j > 0)

    @pl.when(inside & (i != j))
    def _():
        for a in range(SPAN):
            for b in range(SPAN):
                out[a * BLK : (a + 1) * BLK, b * BLK : (b + 1) * BLK] = part[a, b] + mirror[b, a].T

    @pl.when(inside & (i == j))
    def _():
        out[...] = jnp.zeros_like(out)
        for a in range(SPAN):
            out[a * BLK : (a + 1) * BLK, a * BLK : (a + 1) * BLK] = diag[a]

    @pl.when(inside)
    def _():
        for b in range(SPAN):
            rights = block_rows(right, b)
            for a in range(SPAN):
                spot = (slice(a * BLK, (a + 1) * BLK), slice(b * BLK, (b + 1) * BLK))
                out[spot] = out[spot] - lax.dot_general(
                    lefts[a],
                    rights,
                    CONTRACT_COLS,
                    precision=HIGH,
                    preferred_element_type=jnp.float32,
                )

    @pl.when((i == 0))
    def _():
        out[...] = jnp.zeros_like(out)

    @pl.when((i == 0) & (j == 0))
    def _():
        for a in range(SPAN):
            out[a * BLK : (a + 1) * BLK, a * BLK : (a + 1) * BLK] = chol[a]

    @pl.when((i > 0) & (j == 0))
    def _():
        for a in range(SPAN):
            out[a * BLK : (a + 1) * BLK, :] = lefts[a]


def finish(meta, part, mirror, left, right, diag, chol, inverse):
    def full(shape):
        zeros = (0,) * len(shape)
        return pl.BlockSpec(shape, lambda t, meta: zeros)

    blocks = (SPAN, SPAN, BLK, BLK)
    slices = (NWIN, SPAN, SPAN, SLICE, BLK)
    small = (SPAN, BLK, BLK)
    size = (SPAN * BLK, SPAN * BLK)
    grid_spec = pltpu.PrefetchScalarGridSpec(
        num_scalar_prefetch=1,
        grid=(1,),
        in_specs=[full(s) for s in (blocks, blocks, slices, slices, small, small, small)],
        out_specs=full(size),
    )
    return pl.pallas_call(
        finish_kernel,
        grid_spec=grid_spec,
        out_shape=jax.ShapeDtypeStruct(size, jnp.float32),
        name="finish",
    )(meta, part, mirror, left, right, diag, chol, inverse)


def swap_pairs(size, bit):
    return [(k, k ^ bit) for k in range(size)]


def spread_rows(v, steps):
    for step in steps:
        if step == "core":
            v = v + lax.ppermute(v, "core", [(0, 1)])
        elif step == "yh":
            v = v + lax.ppermute(v, "yh", [(0, 1)])
        else:
            up = lax.ppermute(v, "x", [(0, 1)])
            down = lax.ppermute(v, "x", [(0, 3)])
            v = v + up + down
            v = v + lax.ppermute(v, "x", [(1, 2)])
    return v


def body(border, row_scale, block_pick, given_diag):
    i = lax.axis_index(GR).astype(jnp.int32)
    j = lax.axis_index(GC).astype(jnp.int32)
    chip = i // 2
    core = i % 2
    meta = jnp.stack([chip, core, i, j])

    scaled = (jnp.sqrt(row_scale)[:, :, None] * border.astype(jnp.float32)).astype(jnp.bfloat16)

    own = jnp.einsum("srx,sry->sxy", scaled, scaled, preferred_element_type=jnp.float32)
    own_pick = lax.dynamic_slice(block_pick, (j * GROUP, i), (GROUP, 1))[:, 0]
    hot = own_pick[:, None] == jnp.arange(SPAN, dtype=jnp.int32)[None, :]
    diag = jnp.sum(jnp.where(hot[:, :, None, None], own[:, None], 0.0), axis=0)
    for bit in (1, 2, 4):
        diag = diag + lax.ppermute(diag, "z", swap_pairs(8, bit))

    peers = jnp.arange(8, dtype=jnp.int32)
    early = (peers < chip) | ((peers == chip) & (core == 1))
    slots = jnp.where(early[:, None, None, None], scaled[None, :HALF], scaled[None, HALF:])
    same = lax.all_to_all(slots, ("x", "yh"), 0, 0, tiled=True)
    same, diag = lax.optimization_barrier((same, diag))
    other = lax.ppermute(same, "core", [(0, 1), (1, 0)])

    cut = R // 2
    rootly = jnp.where(i == 0, scaled[:HALF], jnp.zeros_like(scaled[:HALF]))
    piece = rootly[:, :cut] + lax.ppermute(rootly[:, cut:], "core", [(0, 1)])
    piece = spread_rows(piece, ("yh", "x"))
    tiles, late = gram_slots(meta, scaled, same, other)
    piece, late = lax.optimization_barrier((piece, late))
    twin = lax.ppermute(piece, "core", [(0, 1), (1, 0)])
    lead = jnp.concatenate(
        [jnp.where(core == 0, piece, twin), jnp.where(core == 0, twin, piece)], axis=1
    )

    diag = diag + lax.ppermute(diag, "yl", swap_pairs(2, 1))
    eye = jnp.eye(BLK, dtype=jnp.float32)
    given_here = lax.dynamic_slice(given_diag, (i * SPAN * BLK,), (SPAN * BLK,))
    diag = diag + given_here.reshape(SPAN, 1, BLK) * eye
    corner = spread_rows(jnp.where(i == 0, diag, 0.0), ("core", "x", "yh"))

    tiles = panel_slots(scaled, lead, late, tiles)
    tiles, corner = lax.optimization_barrier((tiles, corner))
    tiles = lax.all_to_all(tiles, GC, 0, 0, tiled=True)
    chol = jnp.linalg.cholesky(corner)
    tiles, chol = lax.optimization_barrier((tiles, chol))
    inverse = lax.linalg.triangular_solve(
        chol, jnp.broadcast_to(eye, chol.shape), left_side=True, lower=True
    )

    part, strip = place(meta, block_pick, tiles)
    everywhere = [(r * NWIN + c, c * NWIN + r) for r in range(NWIN) for c in range(NWIN)]
    copies = (NWIN,) + strip.shape
    turned = lax.ppermute(strip, AXES, everywhere)
    mirror = lax.ppermute(part, AXES, everywhere)
    left = lax.all_to_all(jnp.broadcast_to(strip, copies), GC, 0, 0, tiled=True)
    right = lax.all_to_all(jnp.broadcast_to(turned, copies), GR, 0, 0, tiled=True)
    return finish(meta, part, mirror, left, right, diag, chol, inverse)


def solution(mesh):
    fine = Mesh(np.asarray(mesh.devices).reshape(SIZES), AXES)
    in_specs = (P(GC, None, GR), P(GC, None), P(), P())
    return jax.shard_map(body, mesh=fine, in_specs=in_specs, out_specs=P(GR, GC), check_vma=False)
```

time: 544 us -> 395 us (0.73)
  waiting for transfers between devices: 264 us -> 175 us
  blocking collectives: 84.6 us -> 21.1 us
    ppermute x3, waiting for transfers between devices: 104 us -> 24.9 us  [body(): diag = diag + lax.ppermute(diag, 'z', swap_pairs(8, bit))]
    all_to_all x1 -> x0, blocking collectives: 62.4 us -> none  [body(): same = lax.all_to_all(slots, ('x', 'yh'), 0, 0, tiled=True)]
    ppermute x1, waiting for transfers between devices: 88.8 us -> 46.7 us  [body(): mirror = lax.ppermute(part, AXES, everywhere)]
    all_to_all x1, waiting for transfers between devices: 0.01 us -> 31.1 us  [body(): tiles = lax.all_to_all(tiles, GC, 0, 0, tiled=True)]
    all_to_all x1 -> x2, waiting for transfers between devices: 0.01 us -> 29.4 us  [the longest x1 29.4 us: body(): same = lax.all_to_all(slots, ('x', 'yh'), 0, 0, tiled=True)]
    ppermute x2, waiting for transfers between devices: 15.5 us -> 0.01 us  [spread_rows(): v = v + lax.ppermute(v, 'x', [(1, 2)])]
    ppermute x2, waiting for transfers between devices: 25 us -> 11.5 us  [spread_rows(): up = lax.ppermute(v, 'x', [(0, 1)])]
    ppermute x1 -> x3, waiting for transfers between devices: 4.37 us -> 13.1 us  [the longest x1 7.36 us: body(): turned = lax.ppermute(strip, AXES, everywhere)]
  transfers between devices with their start and end apart: 19 -> 21, of which waited for: 14 -> 14; matrix products, arithmetic and copies ran while one was open for 17% -> 24% of each run, Pallas kernels for 0% -> 3%
where the time goes in v2:
time: 395 us; the launch traced here: 393 us
  waiting for transfers between devices  175 us (44%)
  other arithmetic  95.9 us (24%)
  starting transfers between devices  65 us (16%)
  Pallas kernels  30.4 us (8%)
  blocking collectives  21.1 us (5%)
  local copies, waits for them, and re-layouts  4.29 us (1%)
    another operation x3, other arithmetic, body(): chol = jnp.linalg.cholesky(corner)  47.1 us
    ppermute x1, waiting for transfers between devices, body(): mirror = lax.ppermute(part, AXES, everywhere)  46.7 us
    another operation x2, other arithmetic, body(): lax.linalg.triangular_solve(chol, jnp.broadcast_to(eye, chol.shape), left...  40.8 us
    all_to_all x1, waiting for transfers between devices, body(): tiles = lax.all_to_all(tiles, GC, 0, 0, tiled=True)  31.1 us
    all_to_all x1, waiting for transfers between devices, body(): same = lax.all_to_all(slots, ('x', 'yh'), 0, 0, tiled=True)  29.4 us
    ppermute x3, waiting for transfers between devices, body(): diag = diag + lax.ppermute(diag, 'z', swap_pairs(8, bit))  24.9 us
    all_to_all x1, blocking collectives, body(): lax.all_to_all(jnp.broadcast_to(turned, copies), GR, 0, 0, tiled=True)  21.1 us
    ppermute x2, waiting for transfers between devices, spread_rows(): v = v + lax.ppermute(v, 'yh', [(0, 1)])  12.7 us
  transfers between devices with their start and end apart: 21, of which 14 were waited for; matrix products, arithmetic and copies ran while one was open for 24% of the time, Pallas kernels for 3%

profile of v2, /device:TPU:66, one launch (start us, length us, event | category | flops | bytes accessed | tf_op | source)
XLA Modules:
  0.0 393.4 jit_solution(16171739482918405588)
XLA Ops:
  0.0 0.8 sqrt.3
  0.8 1.9 multiply_convert_fusion.mine.first
  2.7 0.1 fusion.5
  2.8 2.8 broadcast_select_fusion
  5.6 7.6 %all-to-all-start = ((bf16[8,3,768,128]{3,2,1,0:T(8,128)(2,1)}), bf16[8,3,768,128]{3,2,1,0:T(8,128)(2,1)}, u32[]{:S(2)}, u32[]{:S(2)}) async-start(bf16[8,3,768,128]{3,2,1,0:T(8,128)(2,1)} %broadcast_select_fusion), calls=%async_computation | async-start | bytes 9437184 | tf_op jit(solution)/shard_map/all_to_all | solution.py:274
  13.2 0.1 dynamic-slice_bitcast_fusion.1
  13.3 0.1 iota_compare_fusion.2
  13.3 0.5 fusion.6
  13.8 0.2 select_reduce_fusion
  14.0 2.0 collective-permute-start.5
  16.0 5.7 %collective-permute-done.5 = f32[4,128,128]{2,1,0:T(8,128)S(1)} collective-permute-done((f32[4,128,128]{2,1,0:T(8,128)S(1)}, f32[4,128,128]{2,1,0:T(8,128)S(1)}, u32[]{:S(2)}, u32[]{:S(2)}) %collective-permute-start.5) | collective-permute-done | bytes 262176 | tf_op jit(solution)/shard_map/ppermute | solution.py:269
  21.8 0.1 collective-permute-start.6
  21.9 10.3 %collective-permute-done.6 = f32[4,128,128]{2,1,0:T(8,128)S(1)} collective-permute-done((f32[4,128,128]{2,1,0:T(8,128)S(1)}, f32[4,128,128]{2,1,0:T(8,128)S(1)}, u32[]{:S(2)}, u32[]{:S(2)}) %collective-permute-start.6) | collective-permute-done | bytes 262176 | tf_op jit(solution)/shard_map/ppermute | solution.py:269
  32.3 6.3 %collective-permute-start.7 = (f32[4,128,128]{2,1,0:T(8,128)S(1)}, f32[4,128,128]{2,1,0:T(8,128)S(1)}, u32[]{:S(2)}, u32[]{:S(2)}) collective-permute-start(f32[4,128,128]{2,1,0:T(8,128)S(1)} %add.91), channel_id=1, source_target_pairs={{0,4},{1,5},{2,6},{3,7},{4,0},{5,1},{6,2},{7,3},{8,12},{9,13},{10,... | collective-permute-start | bytes 786440 | tf_op jit(solution)/shard_map/ppermute | solution.py:269
  38.6 8.8 %collective-permute-done.7 = f32[4,128,128]{2,1,0:T(8,128)S(1)} collective-permute-done((f32[4,128,128]{2,1,0:T(8,128)S(1)}, f32[4,128,128]{2,1,0:T(8,128)S(1)}, u32[]{:S(2)}, u32[]{:S(2)}) %collective-permute-start.7) | collective-permute-done | bytes 262176 | tf_op jit(solution)/shard_map/ppermute | solution.py:269
  47.4 29.4 %all-to-all-done.same = bf16[8,3,768,128]{3,2,1,0:T(8,128)(2,1)} async-done(((bf16[8,3,768,128]{3,2,1,0:T(8,128)(2,1)}), bf16[8,3,768,128]{3,2,1,0:T(8,128)(2,1)}, u32[]{:S(2)}, u32[]{:S(2)}) %all-to-all-start) | async-done | bytes 4718624 | tf_op jit(solution)/shard_map/all_to_all | solution.py:274
  76.9 2.4 collective-permute-start
  79.3 5.7 %collective-permute-done = bf16[3,384,128]{2,1,0:T(8,128)(2,1)S(1)} collective-permute-done((bf16[3,384,128]{2,1,0:T(8,128)(2,1)S(1)}, bf16[3,384,128]{2,1,0:T(8,128)(2,1)S(1)}, u32[]{:S(2)}, u32[]{:S(2)}) %collective-permute-start) | collective-permute-done | bytes 294944 | tf_op jit(solution)/shard_map/ppermute | solution.py:280
  85.1 4.1 %collective-permute-start.1 = (bf16[3,384,128]{2,1,0:T(8,128)(2,1)S(1)}, bf16[3,384,128]{2,1,0:T(8,128)(2,1)S(1)}, u32[]{:S(2)}, u32[]{:S(2)}) collective-permute-start(bf16[3,384,128]{2,1,0:T(8,128)(2,1)S(1)} %slice_add_fusion), channel_id=1, source_target_pairs={{0,32},{1,33},{2,34},{3,35},{4,36},{5,37},{6,38},{7,39},{8,40},{9,... | collective-permute-start | bytes 884744 | tf_op jit(solution)/shard_map/ppermute | solution.py:246
  89.2 0.8 collective-permute-start.10
  89.9 0.1 dynamic-slice_bitcast_fusion
  90.0 6.5 %collective-permute-done.1 = bf16[3,384,128]{2,1,0:T(8,128)(2,1)S(1)} collective-permute-done((bf16[3,384,128]{2,1,0:T(8,128)(2,1)S(1)}, bf16[3,384,128]{2,1,0:T(8,128)(2,1)S(1)}, u32[]{:S(2)}, u32[]{:S(2)}) %collective-permute-start.1) | collective-permute-done | bytes 294944 | tf_op jit(solution)/shard_map/ppermute | solution.py:246
  96.5 0.1 add.84
  96.6 0.7 collective-permute-start.3
  97.3 1.3 collective-permute-start.2
  98.6 4.1 %collective-permute-done.10 = f32[4,128,128]{2,1,0:T(8,128)S(1)} collective-permute-done((f32[4,128,128]{2,1,0:T(8,128)S(1)}, f32[4,128,128]{2,1,0:T(8,128)S(1)}, u32[]{:S(2)}, u32[]{:S(2)}) %collective-permute-start.10) | collective-permute-done | bytes 262176 | tf_op jit(solution)/shard_map/ppermute | solution.py:289
  102.7 0.8 broadcast_select_fusion.4
  103.4 1.4 collective-permute-start.11
  104.9 1.1 collective-permute-done.11
  106.0 0.7 collective-permute-start.13
  106.7 1.3 collective-permute-start.12
  108.0 2.8 collective-permute-done.2
  110.8 1.3 collective-permute-start.4
  112.2 8.8 %collective-permute-done.12 = f32[4,128,128]{2,1,0:T(8,128)S(1)} collective-permute-done((f32[4,128,128]{2,1,0:T(8,128)S(1)}, f32[4,128,128]{2,1,0:T(8,128)S(1)}, u32[]{:S(2)}, u32[]{:S(2)}) %collective-permute-start.12) | collective-permute-done | bytes 262176 | tf_op jit(solution)/shard_map/ppermute | solution.py:248
  121.0 1.3 collective-permute-start.14
  122.3 0.6 pad_add_fusion.meta
  123.0 0.1 add.87
  123.0 10.2 %gram_slots.1 = (f32[16,432,128]{2,1,0:T(8,128)}, f32[3,128,128]{2,1,0:T(8,128)}) custom-call(s32[4]{0:T(128)} %pad_add_fusion.meta, bf16[6,768,128]{2,1,0:T(8,128)(2,1)} %copy-done.1, bf16[8,3,768,128]{3,2,1,0:T(8,128)(2,1)} %all-to-all-done.same, bf16[8,3,768,128]{3,2,1,0:T(8,128)(2,1)} %collective-permute-done.8.other), custom_call_target="tpu_custom_call" | custom-call | tf_op jit(solution)/shard_map/gram_slots/pallas_call | solution.py:65
  133.3 2.7 collective-permute-start.15
  135.9 6.2 %collective-permute-done.15 = f32[4,128,128]{2,1,0:T(8,128)S(1)} collective-permute-done((f32[4,128,128]{2,1,0:T(8,128)S(1)}, f32[4,128,128]{2,1,0:T(8,128)S(1)}, u32[]{:S(2)}, u32[]{:S(2)}) %collective-permute-start.15) | collective-permute-done | bytes 262176 | tf_op jit(solution)/shard_map/ppermute | solution.py:246
  142.2 0.9 pad_maximum_fusion.lead
  143.1 2.4 panel_slots.1
  145.5 8.2 %all-to-all-start.1 = ((f32[16,432,128]{2,1,0:T(8,128)}), f32[16,432,128]{2,1,0:T(8,128)}, u32[]{:S(2)}, u32[]{:S(2)}) async-start(f32[16,432,128]{2,1,0:T(8,128)} %panel_slots.1), calls=%async_computation.1 | async-start | bytes 7077888 | tf_op jit(solution)/shard_map/all_to_all | solution.py:297
  153.8 0.7 copy.13.picks
  154.5 0.1 copy.12
  154.7 46.9 %custom-call.7 = f32[4,128,128]{2,1,0:T(8,128)S(1)} custom-call(f32[4,128,128]{2,1,0:T(8,128)S(1)} %fusion.2), custom_call_target="Cholesky" | custom-call | tf_op jit(solution)/shard_map/jit(cholesky)/cholesky | solution.py:298
  201.6 0.1 compare_reduce_fusion
  201.7 0.1 select_select_fusion.chol
  201.9 31.1 %all-to-all-done.1.slots = f32[16,432,128]{2,1,0:T(8,128)} async-done(((f32[16,432,128]{2,1,0:T(8,128)}), f32[16,432,128]{2,1,0:T(8,128)}, u32[]{:S(2)}, u32[]{:S(2)}) %all-to-all-start.1) | async-done | bytes 3538976 | tf_op jit(solution)/shard_map/all_to_all | solution.py:297
  232.9 5.4 %place_tiles.1 = (f32[4,4,128,128]{3,2,1,0:T(8,128)}, f32[4,4,8,128]{3,2,1,0:T(8,128)}) custom-call(s32[4]{0:T(128)} %pad_add_fusion.meta, s32[96,16]{1,0:T(8,128)} %copy.13.picks, f32[16,432,128]{2,1,0:T(8,128)} %all-to-all-done.1.slots), custom_call_target="tpu_custom_call" | custom-call | tf_op jit(solution)/shard_map/place_tiles/pallas_call | solution.py:142
  238.4 7.2 %collective-permute-start.17 = (f32[4,4,8,128]{3,2,1,0:T(8,128)}, f32[4,4,8,128]{3,2,1,0:T(8,128)S(1)}, u32[]{:S(2)}, u32[]{:S(2)}) collective-permute-start(f32[4,4,8,128]{3,2,1,0:T(8,128)} %get-tuple-element.27), channel_id=1, source_target_pairs={{0,0},{1,16},{2,32},{3,48},{4,64},{5,80},{6,96},{7,112},{8,128},{9... | collective-permute-start | bytes 196616 | tf_op jit(solution)/shard_map/ppermute | solution.py:307
  245.6 7.4 %collective-permute-done.17 = f32[4,4,8,128]{3,2,1,0:T(8,128)S(1)} collective-permute-done((f32[4,4,8,128]{3,2,1,0:T(8,128)}, f32[4,4,8,128]{3,2,1,0:T(8,128)S(1)}, u32[]{:S(2)}, u32[]{:S(2)}) %collective-permute-start.17) | collective-permute-done | bytes 65568 | tf_op jit(solution)/shard_map/ppermute | solution.py:307
  252.9 0.1 broadcast_in_dim.84
  253.1 21.1 %all_to_all.20.right = f32[16,4,4,8,128]{4,3,2,1,0:T(8,128)} all-to-all(f32[16,4,4,8,128]{4,3,2,1,0:T(8,128)S(1)} %broadcast_in_dim.84), channel_id=1, replica_groups=mesh['x'=4,'yh'=2,'core'=2,'yl'=2,'z'=8] {'x','yh','core'}, dimensions={0} | all-to-all | bytes 2097152 | tf_op jit(solution)/shard_map/all_to_all | solution.py:310
  274.1 1.1 broadcast_in_dim.83
  275.2 8.0 %all-to-all-start.2 = ((f32[16,4,4,8,128]{4,3,2,1,0:T(8,128)}), f32[16,4,4,8,128]{4,3,2,1,0:T(8,128)S(1)}, u32[]{:S(2)}, u32[]{:S(2)}) async-start(f32[16,4,4,8,128]{4,3,2,1,0:T(8,128)} %broadcast_in_dim.83), calls=%async_computation.2 | async-start | bytes 2097152 | tf_op jit(solution)/shard_map/all_to_all | solution.py:309
  283.2 7.7 %collective-permute-start.16 = (f32[4,4,128,128]{3,2,1,0:T(8,128)S(1)}, f32[4,4,128,128]{3,2,1,0:T(8,128)S(1)}, u32[]{:S(2)}, u32[]{:S(2)}) collective-permute-start(f32[4,4,128,128]{3,2,1,0:T(8,128)S(1)} %copy-done.4), channel_id=1, source_target_pairs={{0,0},{1,16},{2,32},{3,48},{4,64},{5,80},{6,96},{7,112},{8,128},{9... | collective-permute-start | bytes 3145736 | tf_op jit(solution)/shard_map/ppermute | solution.py:308
  290.9 0.7 select_bitcast_fusion
  291.6 40.1 %custom-call.8 = f32[4,1,128,128]{2,3,1,0:T(8,128)S(1)} custom-call(f32[4,1,128,128]{3,2,1,0:T(8,128)} %select_bitcast_fusion), custom_call_target="InvertDiagBlocksLowerTriangular" | custom-call | tf_op jit(solution)/shard_map/triangular_solve | solution.py:300
  331.8 1.3 fusion.inverse
  333.1 46.7 %collective-permute-done.16.mirror = f32[4,4,128,128]{3,2,1,0:T(8,128)S(1)} collective-permute-done((f32[4,4,128,128]{3,2,1,0:T(8,128)S(1)}, f32[4,4,128,128]{3,2,1,0:T(8,128)S(1)}, u32[]{:S(2)}, u32[]{:S(2)}) %collective-permute-start.16) | collective-permute-done | bytes 1048608 | tf_op jit(solution)/shard_map/ppermute | solution.py:308
  379.8 1.0 copy-done.5
  380.7 0.3 copy-done.2
  381.1 12.4 %finish.1 = f32[512,512]{1,0:T(8,128)} custom-call(s32[4]{0:T(128)} %pad_add_fusion.meta, f32[4,4,128,128]{3,2,1,0:T(8,128)} %get-tuple-element.26.part, f32[4,4,128,128]{3,2,1,0:T(8,128)} %copy-done.5, f32[16,4,4,8,128]{4,3,2,1,0:T(8,128)} %copy-done.2, f32[16,4,4,8,128]{4,3,2,1,0:T(8,128)} %all_to_all.20.right, f32[4,128,128]{2,1,0:T(8,128)} %get-tuple-element.30.diag, ...), custom_call_target="tpu_custom_call" | custom-call | tf_op jit(solution)/shard_map/finish/pallas_call | solution.py:229
  (40 shorter events, 0.6 us)
Async XLA Ops:
  0.0 89.9 %copy-start = (f32[8192]{0:T(1024)S(1)}, f32[8192]{0:T(1024)}, u32[]{:S(2)}) copy-start(f32[8192]{0:T(1024)} %param.7) | copy-start | bytes 98308
  2.6 10.7 %copy-start.1 = (bf16[6,768,128]{2,1,0:T(8,128)(2,1)}, bf16[6,768,128]{2,1,0:T(8,128)(2,1)S(1)}, u32[]{:S(2)}) copy-start(bf16[6,768,128]{2,1,0:T(8,128)(2,1)S(1)} %multiply_convert_fusion.mine.first) | copy-start | bytes 3538948
  5.6 7.6 %copy-start.7 = (s32[96,16]{0,1:T(8,128)S(1)}, s32[96,16]{0,1:T(8,128)}, u32[]{:S(2)}) copy-start(s32[96,16]{0,1:T(8,128)} %param.6) | copy-start | bytes 18436
  5.6 71.3 %all-to-all-start = ((bf16[8,3,768,128]{3,2,1,0:T(8,128)(2,1)}), bf16[8,3,768,128]{3,2,1,0:T(8,128)(2,1)}, u32[]{:S(2)}, u32[]{:S(2)}) async-start(bf16[8,3,768,128]{3,2,1,0:T(8,128)(2,1)} %broadcast_select_fusion), calls=%async_computation | async-start | bytes 9437184 | tf_op jit(solution)/shard_map/all_to_all | solution.py:274
  14.0 7.8 %collective-permute-start.5 = (f32[4,128,128]{2,1,0:T(8,128)S(1)}, f32[4,128,128]{2,1,0:T(8,128)S(1)}, u32[]{:S(2)}, u32[]{:S(2)}) collective-permute-start(f32[4,128,128]{2,1,0:T(8,128)S(1)} %select_reduce_fusion), channel_id=1, source_target_pairs={{0,1},{1,0},{2,3},{3,2},{4,5},{5,4},{6,7},{7,6},{8,9},{9,8},{10,11... | collective-permute-start | bytes 786440 | tf_op jit(solution)/shard_map/ppermute | solution.py:269
  21.8 10.4 %collective-permute-start.6 = (f32[4,128,128]{2,1,0:T(8,128)S(1)}, f32[4,128,128]{2,1,0:T(8,128)S(1)}, u32[]{:S(2)}, u32[]{:S(2)}) collective-permute-start(f32[4,128,128]{2,1,0:T(8,128)S(1)} %add.90), channel_id=1, source_target_pairs={{0,2},{1,3},{2,0},{3,1},{4,6},{5,7},{6,4},{7,5},{8,10},{9,11},{10,... | collective-permute-start | bytes 786440 | tf_op jit(solution)/shard_map/ppermute | solution.py:269
  32.3 15.1 %collective-permute-start.7 = (f32[4,128,128]{2,1,0:T(8,128)S(1)}, f32[4,128,128]{2,1,0:T(8,128)S(1)}, u32[]{:S(2)}, u32[]{:S(2)}) collective-permute-start(f32[4,128,128]{2,1,0:T(8,128)S(1)} %add.91), channel_id=1, source_target_pairs={{0,4},{1,5},{2,6},{3,7},{4,0},{5,1},{6,2},{7,3},{8,12},{9,13},{10,... | collective-permute-start | bytes 786440 | tf_op jit(solution)/shard_map/ppermute | solution.py:269
  76.9 46.2 %collective-permute-start.8 = (bf16[8,3,768,128]{3,2,1,0:T(8,128)(2,1)}, bf16[8,3,768,128]{3,2,1,0:T(8,128)(2,1)}, u32[]{:S(2)}, u32[]{:S(2)}) collective-permute-start(bf16[8,3,768,128]{3,2,1,0:T(8,128)(2,1)} %all-to-all-done.same), channel_id=1, source_target_pairs={{0,16},{16,0},{1,17},{17,1},{2,18},{18,2},{3,19},{19,3},{4,20},{20... | collective-permute-start | bytes 14155784 | tf_op jit(solution)/shard_map/ppermute | solution.py:276
  76.9 8.1 %collective-permute-start = (bf16[3,384,128]{2,1,0:T(8,128)(2,1)S(1)}, bf16[3,384,128]{2,1,0:T(8,128)(2,1)S(1)}, u32[]{:S(2)}, u32[]{:S(2)}) collective-permute-start(bf16[3,384,128]{2,1,0:T(8,128)(2,1)S(1)} %slice.29), channel_id=1, source_target_pairs={{0,16},{1,17},{2,18},{3,19},{4,20},{5,21},{6,22},{7,23},{8,24},{9,... | collective-permute-start | bytes 884744 | tf_op jit(solution)/shard_map/ppermute | solution.py:280
  85.1 11.5 %collective-permute-start.1 = (bf16[3,384,128]{2,1,0:T(8,128)(2,1)S(1)}, bf16[3,384,128]{2,1,0:T(8,128)(2,1)S(1)}, u32[]{:S(2)}, u32[]{:S(2)}) collective-permute-start(bf16[3,384,128]{2,1,0:T(8,128)(2,1)S(1)} %slice_add_fusion), channel_id=1, source_target_pairs={{0,32},{1,33},{2,34},{3,35},{4,36},{5,37},{6,38},{7,39},{8,40},{9,... | collective-permute-start | bytes 884744 | tf_op jit(solution)/shard_map/ppermute | solution.py:246
  89.2 13.5 %collective-permute-start.10 = (f32[4,128,128]{2,1,0:T(8,128)S(1)}, f32[4,128,128]{2,1,0:T(8,128)S(1)}, u32[]{:S(2)}, u32[]{:S(2)}) collective-permute-start(f32[4,128,128]{2,1,0:T(8,128)S(1)} %add.92), channel_id=1, source_target_pairs={{0,8},{8,0},{1,9},{9,1},{2,10},{10,2},{3,11},{11,3},{4,12},{12,4},... | collective-permute-start | bytes 786440 | tf_op jit(solution)/shard_map/ppermute | solution.py:289
  96.6 11.4 %collective-permute-start.3 = (bf16[3,384,128]{2,1,0:T(8,128)(2,1)S(1)}, bf16[3,384,128]{2,1,0:T(8,128)(2,1)S(1)}, u32[]{:S(2)}, u32[]{:S(2)}) collective-permute-start(bf16[3,384,128]{2,1,0:T(8,128)(2,1)S(1)} %add.84), channel_id=1, source_target_pairs={{0,192},{1,193},{2,194},{3,195},{4,196},{5,197},{6,198},{7,199},{8... | collective-permute-start | bytes 884744 | tf_op jit(solution)/shard_map/ppermute | solution.py:249
  97.3 13.5 %collective-permute-start.2 = (bf16[3,384,128]{2,1,0:T(8,128)(2,1)S(1)}, bf16[3,384,128]{2,1,0:T(8,128)(2,1)S(1)}, u32[]{:S(2)}, u32[]{:S(2)}) collective-permute-start(bf16[3,384,128]{2,1,0:T(8,128)(2,1)S(1)} %add.84), channel_id=1, source_target_pairs={{0,64},{1,65},{2,66},{3,67},{4,68},{5,69},{6,70},{7,71},{8,72},{9,... | collective-permute-start | bytes 884744 | tf_op jit(solution)/shard_map/ppermute | solution.py:248
  103.4 2.6 collective-permute-start.11
  106.0 6.1 %collective-permute-start.13 = (f32[4,128,128]{2,1,0:T(8,128)S(1)}, f32[4,128,128]{2,1,0:T(8,128)S(1)}, u32[]{:S(2)}, u32[]{:S(2)}) collective-permute-start(f32[4,128,128]{2,1,0:T(8,128)S(1)} %add.96), channel_id=1, source_target_pairs={{0,192},{1,193},{2,194},{3,195},{4,196},{5,197},{6,198},{7,199},{8... | collective-permute-start | bytes 786440 | tf_op jit(solution)/shard_map/ppermute | solution.py:249
  106.7 14.2 %collective-permute-start.12 = (f32[4,128,128]{2,1,0:T(8,128)S(1)}, f32[4,128,128]{2,1,0:T(8,128)S(1)}, u32[]{:S(2)}, u32[]{:S(2)}) collective-permute-start(f32[4,128,128]{2,1,0:T(8,128)S(1)} %add.96), channel_id=1, source_target_pairs={{0,64},{1,65},{2,66},{3,67},{4,68},{5,69},{6,70},{7,71},{8,72},{9,... | collective-permute-start | bytes 786440 | tf_op jit(solution)/shard_map/ppermute | solution.py:248
  110.8 12.1 %collective-permute-start.4 = (bf16[3,384,128]{2,1,0:T(8,128)(2,1)S(1)}, bf16[3,384,128]{2,1,0:T(8,128)(2,1)S(1)}, u32[]{:S(2)}, u32[]{:S(2)}) collective-permute-start(bf16[3,384,128]{2,1,0:T(8,128)(2,1)S(1)} %add_add_fusion), channel_id=1, source_target_pairs={{64,128},{65,129},{66,130},{67,131},{68,132},{69,133},{70,134},{71... | collective-permute-start | bytes 884744 | tf_op jit(solution)/shard_map/ppermute | solution.py:251
  121.0 12.2 %collective-permute-start.14 = (f32[4,128,128]{2,1,0:T(8,128)S(1)}, f32[4,128,128]{2,1,0:T(8,128)S(1)}, u32[]{:S(2)}, u32[]{:S(2)}) collective-permute-start(f32[4,128,128]{2,1,0:T(8,128)S(1)} %add_add_fusion.1), channel_id=1, source_target_pairs={{64,128},{65,129},{66,130},{67,131},{68,132},{69,133},{70,134},{71... | collective-permute-start | bytes 786440 | tf_op jit(solution)/shard_map/ppermute | solution.py:251
  133.2 9.0 %collective-permute-start.9 = (bf16[3,384,128]{2,1,0:T(8,128)(2,1)S(1)}, bf16[3,384,128]{2,1,0:T(8,128)(2,1)S(1)}, u32[]{:S(2)}, u32[]{:S(2)}) collective-permute-start(bf16[3,384,128]{2,1,0:T(8,128)(2,1)S(1)} %add.87), channel_id=1, source_target_pairs={{0,16},{16,0},{1,17},{17,1},{2,18},{18,2},{3,19},{19,3},{4,20},{20... | collective-permute-start | bytes 884744 | tf_op jit(solution)/shard_map/ppermute | solution.py:284
  133.3 8.9 %collective-permute-start.15 = (f32[4,128,128]{2,1,0:T(8,128)S(1)}, f32[4,128,128]{2,1,0:T(8,128)S(1)}, u32[]{:S(2)}, u32[]{:S(2)}) collective-permute-start(f32[4,128,128]{2,1,0:T(8,128)S(1)} %add.99), channel_id=1, source_target_pairs={{0,32},{1,33},{2,34},{3,35},{4,36},{5,37},{6,38},{7,39},{8,40},{9,... | collective-permute-start | bytes 786440 | tf_op jit(solution)/shard_map/ppermute | solution.py:246
  145.5 87.4 %all-to-all-start.1 = ((f32[16,432,128]{2,1,0:T(8,128)}), f32[16,432,128]{2,1,0:T(8,128)}, u32[]{:S(2)}, u32[]{:S(2)}) async-start(f32[16,432,128]{2,1,0:T(8,128)} %panel_slots.1), calls=%async_computation.1 | async-start | bytes 7077888 | tf_op jit(solution)/shard_map/all_to_all | solution.py:297
  201.8 89.1 %copy-start.3 = (f32[4,128,128]{2,1,0:T(8,128)}, f32[4,128,128]{2,1,0:T(8,128)S(1)}, u32[]{:S(2)}) copy-start(f32[4,128,128]{2,1,0:T(8,128)S(1)} %select_select_fusion.chol) | copy-start | bytes 786436
  238.4 35.8 %copy-start.6 = (f32[4,4,8,128]{3,2,1,0:T(8,128)S(1)}, f32[4,4,8,128]{3,2,1,0:T(8,128)}, u32[]{:S(2)}) copy-start(f32[4,4,8,128]{3,2,1,0:T(8,128)} %get-tuple-element.27) | copy-start | bytes 196612
  238.4 14.6 %collective-permute-start.17 = (f32[4,4,8,128]{3,2,1,0:T(8,128)}, f32[4,4,8,128]{3,2,1,0:T(8,128)S(1)}, u32[]{:S(2)}, u32[]{:S(2)}) collective-permute-start(f32[4,4,8,128]{3,2,1,0:T(8,128)} %get-tuple-element.27), channel_id=1, source_target_pairs={{0,0},{1,16},{2,32},{3,48},{4,64},{5,80},{6,96},{7,112},{8,128},{9... | collective-permute-start | bytes 196616 | tf_op jit(solution)/shard_map/ppermute | solution.py:307
  274.1 9.1 %copy-start.4 = (f32[4,4,128,128]{3,2,1,0:T(8,128)S(1)}, f32[4,4,128,128]{3,2,1,0:T(8,128)}, u32[]{:S(2)}) copy-start(f32[4,4,128,128]{3,2,1,0:T(8,128)} %get-tuple-element.26.part) | copy-start | bytes 3145732
  275.2 104.5 %all-to-all-start.2 = ((f32[16,4,4,8,128]{4,3,2,1,0:T(8,128)}), f32[16,4,4,8,128]{4,3,2,1,0:T(8,128)S(1)}, u32[]{:S(2)}, u32[]{:S(2)}) async-start(f32[16,4,4,8,128]{4,3,2,1,0:T(8,128)} %broadcast_in_dim.83), calls=%async_computation.2 | async-start | bytes 2097152 | tf_op jit(solution)/shard_map/all_to_all | solution.py:309
  283.2 96.5 %collective-permute-start.16 = (f32[4,4,128,128]{3,2,1,0:T(8,128)S(1)}, f32[4,4,128,128]{3,2,1,0:T(8,128)S(1)}, u32[]{:S(2)}, u32[]{:S(2)}) collective-permute-start(f32[4,4,128,128]{3,2,1,0:T(8,128)S(1)} %copy-done.4), channel_id=1, source_target_pairs={{0,0},{1,16},{2,32},{3,48},{4,64},{5,80},{6,96},{7,112},{8,128},{9... | collective-permute-start | bytes 3145736 | tf_op jit(solution)/shard_map/ppermute | solution.py:308
  379.8 1.0 copy-start.5
  379.8 1.3 copy-start.2

commit v3 on v2

--- a/solution.py
+++ b/solution.py
@@ -13,7 +13,7 @@
 GROUP = 6
 HALF = 3
 SLICE = 8
-ROWS = HALF * BLK + GROUP * SLICE
+ROWS = HALF * BLK
 PLACE = 4
 
 AXES = ("x", "yh", "core", "yl", "z")
@@ -40,8 +40,7 @@
 
     @pl.when(q == 0)
     def _():
-        late[...] = out[0, : HALF * BLK, :].reshape(HALF, BLK, BLK)
-        out[:, HALF * BLK :, :] = jnp.zeros((NWIN, GROUP * SLICE, BLK), jnp.float32)
+        late[...] = out[0].reshape(HALF, BLK, BLK)
 
 
 def gram_slots(meta, scaled, same, other):
@@ -73,8 +72,7 @@
     )(meta, scaled, same, other)
 
 
-def panel_kernel(first, lead, late, held, out):
-    del held
+def panel_kernel(first, lead, late, out):
     for m in range(GROUP):
         if m < HALF:
             tile = lax.dot_general(
@@ -86,9 +84,9 @@
             out[j, m * SLICE : (m + 1) * SLICE, :] = tile[j * SLICE : (j + 1) * SLICE, :]
 
 
-def panel_slots(scaled, lead, late, slots):
+def panel_slots(scaled, lead, late):
     whole = (HALF, R, BLK)
-    rows = GROUP * SLICE
+    shape = (NWIN, GROUP * SLICE, BLK)
     return pl.pallas_call(
         panel_kernel,
         grid=(1,),
@@ -96,16 +94,14 @@
             pl.BlockSpec(whole, lambda t: (0, 0, 0)),
             pl.BlockSpec(whole, lambda t: (0, 0, 0)),
             pl.BlockSpec((HALF, BLK, BLK), lambda t: (0, 0, 0)),
-            pl.BlockSpec(memory_space=pl.ANY),
         ],
-        out_specs=pl.BlockSpec((NWIN, rows, BLK), lambda t: (0, HALF * BLK // rows, 0)),
-        out_shape=jax.ShapeDtypeStruct(slots.shape, slots.dtype),
-        input_output_aliases={3: 0},
+        out_specs=pl.BlockSpec(shape, lambda t: (0, 0, 0)),
+        out_shape=jax.ShapeDtypeStruct(shape, jnp.float32),
         name="panel_slots",
-    )(scaled, lead, late, slots)
-
-
-def place_kernel(meta, picks, slots, part, panel):
+    )(scaled, lead, late)
+
+
+def place_kernel(meta, picks, slots, part):
     g = pl.program_id(0)
     i = meta[2]
     j = meta[3]
@@ -113,20 +109,13 @@
     @pl.when(g == 0)
     def _():
         part[...] = jnp.zeros_like(part)
-        panel[...] = jnp.zeros_like(panel)
 
     for u in range(PLACE):
-        group = g * PLACE + u
-        base = group * GROUP + jnp.where(i < j, 0, HALF)
+        base = (g * PLACE + u) * GROUP + jnp.where(i < j, 0, HALF)
         for k in range(HALF):
             a = picks[base + k, i]
             b = picks[base + k, j]
             part[a, b] += slots[u, k * BLK : (k + 1) * BLK, :]
-        for m in range(GROUP):
-            a = picks[group * GROUP + m, i]
-            b = picks[group * GROUP + m, 0]
-            start = HALF * BLK + m * SLICE
-            panel[b, a] += slots[u, start : start + SLICE, :]
 
 
 def place(meta, picks, slots):
@@ -134,19 +123,39 @@
         num_scalar_prefetch=2,
         grid=(NWIN // PLACE,),
         in_specs=[pl.BlockSpec((PLACE, ROWS, BLK), lambda g, *_: (g, 0, 0))],
-        out_specs=[
-            pl.BlockSpec((SPAN, SPAN, BLK, BLK), lambda g, *_: (0, 0, 0, 0)),
-            pl.BlockSpec((SPAN, SPAN, SLICE, BLK), lambda g, *_: (0, 0, 0, 0)),
-        ],
+        out_specs=pl.BlockSpec((SPAN, SPAN, BLK, BLK), lambda g, *_: (0, 0, 0, 0)),
     )
     return pl.pallas_call(
         place_kernel,
         grid_spec=grid_spec,
-        out_shape=[
-            jax.ShapeDtypeStruct((SPAN, SPAN, BLK, BLK), jnp.float32),
-            jax.ShapeDtypeStruct((SPAN, SPAN, SLICE, BLK), jnp.float32),
-        ],
+        out_shape=jax.ShapeDtypeStruct((SPAN, SPAN, BLK, BLK), jnp.float32),
         name="place_tiles",
+    )(meta, picks, slots)
+
+
+def strip_kernel(meta, picks, slots, strip):
+    i = meta[2]
+    strip[...] = jnp.zeros_like(strip)
+    for g in range(NWIN):
+        for m in range(GROUP):
+            a = picks[g * GROUP + m, i]
+            b = picks[g * GROUP + m, 0]
+            strip[b, a] += slots[g, m * SLICE : (m + 1) * SLICE, :]
+
+
+def place_strip(meta, picks, slots):
+    shape = (SPAN, SPAN, SLICE, BLK)
+    grid_spec = pltpu.PrefetchScalarGridSpec(
+        num_scalar_prefetch=2,
+        grid=(1,),
+        in_specs=[pl.BlockSpec(slots.shape, lambda t, *_: (0, 0, 0))],
+        out_specs=pl.BlockSpec(shape, lambda t, *_: (0, 0, 0, 0)),
+    )
+    return pl.pallas_call(
+        strip_kernel,
+        grid_spec=grid_spec,
+        out_shape=jax.ShapeDtypeStruct(shape, jnp.float32),
+        name="place_strip",
     )(meta, picks, slots)
 
 
@@ -238,18 +247,11 @@
     return [(k, k ^ bit) for k in range(size)]
 
 
-def spread_rows(v, steps):
-    for step in steps:
-        if step == "core":
-            v = v + lax.ppermute(v, "core", [(0, 1)])
-        elif step == "yh":
-            v = v + lax.ppermute(v, "yh", [(0, 1)])
-        else:
-            up = lax.ppermute(v, "x", [(0, 1)])
-            down = lax.ppermute(v, "x", [(0, 3)])
-            v = v + up + down
-            v = v + lax.ppermute(v, "x", [(1, 2)])
-    return v
+def spread(v, step):
+    if step != "x":
+        return v + lax.ppermute(v, step, [(0, 1)])
+    v = v + lax.ppermute(v, "x", [(0, 1)]) + lax.ppermute(v, "x", [(0, 3)])
+    return v + lax.ppermute(v, "x", [(1, 2)])
 
 
 def body(border, row_scale, block_pick, given_diag):
@@ -272,41 +274,44 @@
     early = (peers < chip) | ((peers == chip) & (core == 1))
     slots = jnp.where(early[:, None, None, None], scaled[None, :HALF], scaled[None, HALF:])
     same = lax.all_to_all(slots, ("x", "yh"), 0, 0, tiled=True)
-    same, diag = lax.optimization_barrier((same, diag))
-    other = lax.ppermute(same, "core", [(0, 1), (1, 0)])
-
     cut = R // 2
     rootly = jnp.where(i == 0, scaled[:HALF], jnp.zeros_like(scaled[:HALF]))
     piece = rootly[:, :cut] + lax.ppermute(rootly[:, cut:], "core", [(0, 1)])
-    piece = spread_rows(piece, ("yh", "x"))
-    tiles, late = gram_slots(meta, scaled, same, other)
-    piece, late = lax.optimization_barrier((piece, late))
-    twin = lax.ppermute(piece, "core", [(0, 1), (1, 0)])
-    lead = jnp.concatenate(
-        [jnp.where(core == 0, piece, twin), jnp.where(core == 0, twin, piece)], axis=1
-    )
-
+    same, diag, piece = lax.optimization_barrier((same, diag, piece))
+
+    other = lax.ppermute(same, "core", [(0, 1), (1, 0)])
     diag = diag + lax.ppermute(diag, "yl", swap_pairs(2, 1))
     eye = jnp.eye(BLK, dtype=jnp.float32)
     given_here = lax.dynamic_slice(given_diag, (i * SPAN * BLK,), (SPAN * BLK,))
     diag = diag + given_here.reshape(SPAN, 1, BLK) * eye
-    corner = spread_rows(jnp.where(i == 0, diag, 0.0), ("core", "x", "yh"))
-
-    tiles = panel_slots(scaled, lead, late, tiles)
-    tiles, corner = lax.optimization_barrier((tiles, corner))
+    corner = spread(spread(jnp.where(i == 0, diag, 0.0), "core"), "yh")
+    piece = spread(piece, "yh")
+    tiles, late = gram_slots(meta, scaled, same, other)
+    tiles, late, corner, piece = lax.optimization_barrier((tiles, late, corner, piece))
+
     tiles = lax.all_to_all(tiles, GC, 0, 0, tiled=True)
-    chol = jnp.linalg.cholesky(corner)
-    tiles, chol = lax.optimization_barrier((tiles, chol))
+    chol = jnp.linalg.cholesky(spread(corner, "x"))
+    piece = spread(piece, "x")
+    twin = lax.ppermute(piece, "core", [(0, 1), (1, 0)])
+    lead = jnp.concatenate(
+        [jnp.where(core == 0, piece, twin), jnp.where(core == 0, twin, piece)], axis=1
+    )
+    slices = panel_slots(scaled, lead, late)
+    tiles, slices, chol = lax.optimization_barrier((tiles, slices, chol))
+
+    part = place(meta, block_pick, tiles)
+    slices = lax.all_to_all(slices, GC, 0, 0, tiled=True)
+    everywhere = [(r * NWIN + c, c * NWIN + r) for r in range(NWIN) for c in range(NWIN)]
+    mirror = lax.ppermute(part, AXES, everywhere)
+    slices, chol = lax.optimization_barrier((slices, chol))
     inverse = lax.linalg.triangular_solve(
         chol, jnp.broadcast_to(eye, chol.shape), left_side=True, lower=True
     )
-
-    part, strip = place(meta, block_pick, tiles)
-    everywhere = [(r * NWIN + c, c * NWIN + r) for r in range(NWIN) for c in range(NWIN)]
+    strip = place_strip(meta, block_pick, slices)
     copies = (NWIN,) + strip.shape
     turned = lax.ppermute(strip, AXES, everywhere)
-    mirror = lax.ppermute(part, AXES, everywhere)
     left = lax.all_to_all(jnp.broadcast_to(strip, copies), GC, 0, 0, tiled=True)
+    turned, inverse = lax.optimization_barrier((turned, inverse))
     right = lax.all_to_all(jnp.broadcast_to(turned, copies), GR, 0, 0, tiled=True)
     return finish(meta, part, mirror, left, right, diag, chol, inverse)
 

time: 395 us -> 418 us (1.058)
  other arithmetic: 95.9 us -> 106 us
  starting transfers between devices: 65 us -> 70.4 us
    ppermute x1, waiting for transfers between devices: 46.7 us -> 83.5 us  [body(): mirror = lax.ppermute(part, AXES, everywhere)]
    all_to_all x1, waiting for transfers between devices: 31.1 us -> 0.01 us  [body(): tiles = lax.all_to_all(tiles, GC, 0, 0, tiled=True)]
    all_to_all x0 -> x1, waiting for transfers between devices: none -> 11.5 us  [body(): slices = lax.all_to_all(slices, GC, 0, 0, tiled=True)]
    all_to_all x0 -> x1, starting transfers between devices: none -> 8.13 us  [body(): slices = lax.all_to_all(slices, GC, 0, 0, tiled=True)]
    ppermute x1, waiting for transfers between devices: 7.36 us -> 0.01 us  [body(): turned = lax.ppermute(strip, AXES, everywhere)]
    add x7, other arithmetic: 0.35 us -> 6.6 us  [the longest x2 3.52 us: spread(): v = v + lax.ppermute(v, 'x', [(0, 1)]) + lax.ppermute(v, 'x', [(0, 3)])]
    ppermute x9, waiting for transfers between devices: 25.4 us -> 19.5 us  [the longest x4 10.2 us: spread(): v = v + lax.ppermute(v, 'x', [(0, 1)]) + lax.ppermute(v, 'x', [(0, 3)])]
    ppermute x1, waiting for transfers between devices: 5.71 us -> 0.01 us  [body(): piece = rootly[:, :cut] + lax.ppermute(rootly[:, cut:], 'core', [(0, 1)])]
  transfers between devices with their start and end apart: 21 -> 22, of which waited for: 14 -> 12; matrix products, arithmetic and copies ran while one was open for 24% -> 25% of each run, Pallas kernels for 3% -> 2%
where the time goes in v3:
time: 418 us; the launch traced here: 416 us
  waiting for transfers between devices  175 us (42%)
  other arithmetic  106 us (25%)
  starting transfers between devices  70.4 us (17%)
  Pallas kernels  33.4 us (8%)
  blocking collectives  22.6 us (5%)
  local copies, waits for them, and re-layouts  6.61 us (2%)
    ppermute x1, waiting for transfers between devices, body(): mirror = lax.ppermute(part, AXES, everywhere)  83.5 us
    another operation x3, other arithmetic, body(): chol = jnp.linalg.cholesky(spread(corner, 'x'))  47.9 us
    another operation x2, other arithmetic, body(): lax.linalg.triangular_solve(chol, jnp.broadcast_to(eye, chol.shape), left...  40.8 us
    all_to_all x1, waiting for transfers between devices, body(): same = lax.all_to_all(slots, ('x', 'yh'), 0, 0, tiled=True)  28.7 us
    ppermute x3, waiting for transfers between devices, body(): diag = diag + lax.ppermute(diag, 'z', swap_pairs(8, bit))  23.5 us
    all_to_all x1, blocking collectives, body(): lax.all_to_all(jnp.broadcast_to(turned, copies), GR, 0, 0, tiled=True)  22.6 us
    pallas_call x1, Pallas kernels, finish(): pl.pallas_call(finish_kernel, grid_spec=grid_spec, out_shape=jax.ShapeDty...  12.2 us
    all_to_all x1, waiting for transfers between devices, body(): slices = lax.all_to_all(slices, GC, 0, 0, tiled=True)  11.5 us
  transfers between devices with their start and end apart: 22, of which 12 were waited for; matrix products, arithmetic and copies ran while one was open for 25% of the time, Pallas kernels for 2%

profile of v3, /device:TPU:66, one launch (start us, length us, event | category | flops | bytes accessed | tf_op | source)
XLA Modules:
  0.0 416.4 jit_solution(10808157133121052564)
XLA Ops:
  0.0 0.8 sqrt.3
  0.8 1.9 multiply_convert_fusion.mine.first
  2.8 2.8 broadcast_select_fusion
  5.6 7.5 %all-to-all-start = ((bf16[8,3,768,128]{3,2,1,0:T(8,128)(2,1)}), bf16[8,3,768,128]{3,2,1,0:T(8,128)(2,1)}, u32[]{:S(2)}, u32[]{:S(2)}) async-start(bf16[8,3,768,128]{3,2,1,0:T(8,128)(2,1)} %broadcast_select_fusion), calls=%async_computation | async-start | bytes 9437184 | tf_op jit(solution)/shard_map/all_to_all | solution.py:276
  13.0 0.8 dynamic-slice_bitcast_fusion.1
  13.9 0.5 fusion.5
  14.6 2.0 collective-permute-start
  16.6 1.3 collective-permute-start.3
  17.9 4.4 %collective-permute-done = f32[4,128,128]{2,1,0:T(8,128)S(1)} collective-permute-done((f32[4,128,128]{2,1,0:T(8,128)S(1)}, f32[4,128,128]{2,1,0:T(8,128)S(1)}, u32[]{:S(2)}, u32[]{:S(2)}) %collective-permute-start) | collective-permute-done | bytes 262176 | tf_op jit(solution)/shard_map/ppermute | solution.py:271
  22.5 10.3 %collective-permute-done.1 = f32[4,128,128]{2,1,0:T(8,128)S(1)} collective-permute-done((f32[4,128,128]{2,1,0:T(8,128)S(1)}, f32[4,128,128]{2,1,0:T(8,128)S(1)}, u32[]{:S(2)}, u32[]{:S(2)}) %collective-permute-start.1) | collective-permute-done | bytes 262176 | tf_op jit(solution)/shard_map/ppermute | solution.py:271
  32.8 6.3 %collective-permute-start.2 = (f32[4,128,128]{2,1,0:T(8,128)S(1)}, f32[4,128,128]{2,1,0:T(8,128)S(1)}, u32[]{:S(2)}, u32[]{:S(2)}) collective-permute-start(f32[4,128,128]{2,1,0:T(8,128)S(1)} %add.86), channel_id=1, source_target_pairs={{0,4},{1,5},{2,6},{3,7},{4,0},{5,1},{6,2},{7,3},{8,12},{9,13},{10,... | collective-permute-start | bytes 786440 | tf_op jit(solution)/shard_map/ppermute | solution.py:271
  39.2 8.8 %collective-permute-done.2 = f32[4,128,128]{2,1,0:T(8,128)S(1)} collective-permute-done((f32[4,128,128]{2,1,0:T(8,128)S(1)}, f32[4,128,128]{2,1,0:T(8,128)S(1)}, u32[]{:S(2)}, u32[]{:S(2)}) %collective-permute-start.2) | collective-permute-done | bytes 262176 | tf_op jit(solution)/shard_map/ppermute | solution.py:271
  48.0 28.7 %all-to-all-done.same = bf16[8,3,768,128]{3,2,1,0:T(8,128)(2,1)} async-done(((bf16[8,3,768,128]{3,2,1,0:T(8,128)(2,1)}), bf16[8,3,768,128]{3,2,1,0:T(8,128)(2,1)}, u32[]{:S(2)}, u32[]{:S(2)}) %all-to-all-start) | async-done | bytes 4718624 | tf_op jit(solution)/shard_map/all_to_all | solution.py:276
  76.7 0.7 collective-permute-start.5
  77.5 8.0 %collective-permute-done.5 = f32[4,128,128]{2,1,0:T(8,128)S(1)} collective-permute-done((f32[4,128,128]{2,1,0:T(8,128)S(1)}, f32[4,128,128]{2,1,0:T(8,128)S(1)}, u32[]{:S(2)}, u32[]{:S(2)}) %collective-permute-start.5) | collective-permute-done | bytes 262176 | tf_op jit(solution)/shard_map/ppermute | solution.py:283
  85.4 0.7 broadcast_select_fusion.4
  86.2 1.6 collective-permute-start.6
  87.7 4.1 collective-permute-start.8
  91.9 1.3 collective-permute-start.7
  93.2 0.7 pad_add_fusion.meta
  93.8 5.3 %collective-permute-done.8 = bf16[3,384,128]{2,1,0:T(8,128)(2,1)S(1)} collective-permute-done((bf16[3,384,128]{2,1,0:T(8,128)(2,1)S(1)}, bf16[3,384,128]{2,1,0:T(8,128)(2,1)S(1)}, u32[]{:S(2)}, u32[]{:S(2)}) %collective-permute-start.8) | collective-permute-done | bytes 294944 | tf_op jit(solution)/shard_map/ppermute | solution.py:252
  99.3 3.9 collective-permute-done.7
  103.2 0.7 add.93
  103.9 9.9 %gram_slots.1 = (f32[16,384,128]{2,1,0:T(8,128)}, f32[3,128,128]{2,1,0:T(8,128)}) custom-call(s32[4]{0:T(128)} %pad_add_fusion.meta, bf16[6,768,128]{2,1,0:T(8,128)(2,1)} %copy-done.1, bf16[8,3,768,128]{3,2,1,0:T(8,128)(2,1)} %all-to-all-done.same, bf16[8,3,768,128]{3,2,1,0:T(8,128)(2,1)} %collective-permute-done.4.other), custom_call_target="tpu_custom_call" | custom-call | tf_op jit(solution)/shard_map/gram_slots/pallas_call | solution.py:64
  113.9 8.2 %all-to-all-start.1 = ((f32[16,384,128]{2,1,0:T(8,128)}), f32[16,384,128]{2,1,0:T(8,128)S(1)}, u32[]{:S(2)}, u32[]{:S(2)}) async-start(f32[16,384,128]{2,1,0:T(8,128)} %get-tuple-element.26), calls=%async_computation.1 | async-start | bytes 6291456 | tf_op jit(solution)/shard_map/all_to_all | solution.py:292
  122.1 0.7 collective-permute-start.14
  122.8 1.3 collective-permute-start.13
  124.1 0.6 iota_compare_fusion.1
  124.7 1.4 collective-permute-start.10
  126.1 1.3 collective-permute-start.9
  127.4 9.5 %collective-permute-done.13 = f32[4,128,128]{2,1,0:T(8,128)S(1)} collective-permute-done((f32[4,128,128]{2,1,0:T(8,128)}, f32[4,128,128]{2,1,0:T(8,128)S(1)}, u32[]{:S(2)}, u32[]{:S(2)}) %collective-permute-start.13) | collective-permute-done | bytes 262176 | tf_op jit(solution)/shard_map/ppermute | solution.py:253
  136.9 1.7 add_add_fusion.1
  138.6 2.0 collective-permute-start.15
  140.7 0.7 collective-permute-done.9
  141.3 1.8 add_add_fusion
  143.1 2.1 collective-permute-start.11
  145.3 1.1 add.100
  146.3 0.8 copy.12
  147.2 1.7 fusion.2
  148.9 47.7 %custom-call.7 = f32[4,128,128]{2,1,0:T(8,128)S(1)} custom-call(f32[4,128,128]{2,1,0:T(8,128)} %fusion.2), custom_call_target="Cholesky" | custom-call | tf_op jit(solution)/shard_map/jit(cholesky)/cholesky | solution.py:293
  196.6 1.2 add.97
  197.8 0.3 collective-permute-start.12
  198.2 1.0 select_select_fusion.chol
  199.3 0.4 collective-permute-done.12
  199.7 0.9 pad_maximum_fusion.lead
  200.6 2.4 panel_slots.1
  203.0 8.1 %all-to-all-start.2 = ((f32[16,48,128]{2,1,0:T(8,128)}), f32[16,48,128]{2,1,0:T(8,128)}, u32[]{:S(2)}, u32[]{:S(2)}) async-start(f32[16,48,128]{2,1,0:T(8,128)} %panel_slots.1), calls=%async_computation.2 | async-start | bytes 786432 | tf_op jit(solution)/shard_map/all_to_all | solution.py:303
  211.1 0.7 copy.13.picks
  211.8 11.5 %all-to-all-done.2.slots = f32[16,48,128]{2,1,0:T(8,128)} async-done(((f32[16,48,128]{2,1,0:T(8,128)}), f32[16,48,128]{2,1,0:T(8,128)}, u32[]{:S(2)}, u32[]{:S(2)}) %all-to-all-start.2) | async-done | bytes 393248 | tf_op jit(solution)/shard_map/all_to_all | solution.py:303
  223.4 3.6 place_strip.1
  226.9 5.5 %collective-permute-start.17 = (f32[4,4,8,128]{3,2,1,0:T(8,128)}, f32[4,4,8,128]{3,2,1,0:T(8,128)}, u32[]{:S(2)}, u32[]{:S(2)}) collective-permute-start(f32[4,4,8,128]{3,2,1,0:T(8,128)} %place_strip.1), channel_id=1, source_target_pairs={{0,0},{1,16},{2,32},{3,48},{4,64},{5,80},{6,96},{7,112},{8,128},{9... | collective-permute-start | bytes 196616 | tf_op jit(solution)/shard_map/ppermute | solution.py:312
  232.4 0.7 select_bitcast_fusion
  233.1 40.1 %custom-call.8 = f32[4,1,128,128]{2,3,1,0:T(8,128)S(1)} custom-call(f32[4,1,128,128]{3,2,1,0:T(8,128)} %select_bitcast_fusion), custom_call_target="InvertDiagBlocksLowerTriangular" | custom-call | tf_op jit(solution)/shard_map/triangular_solve | solution.py:307
  273.3 1.3 fusion.inverse
  274.6 1.0 broadcast_in_dim.84
  275.6 22.6 %all_to_all.25.right = f32[16,4,4,8,128]{4,3,2,1,0:T(8,128)} all-to-all(f32[16,4,4,8,128]{4,3,2,1,0:T(8,128)S(1)} %broadcast_in_dim.84), channel_id=1, replica_groups=mesh['x'=4,'yh'=2,'core'=2,'yl'=2,'z'=8] {'x','yh','core'}, dimensions={0} | all-to-all | bytes 2097152 | tf_op jit(solution)/shard_map/all_to_all | solution.py:315
  298.2 1.1 broadcast_in_dim.83
  299.3 7.4 %all-to-all-start.3 = ((f32[16,4,4,8,128]{4,3,2,1,0:T(8,128)}), f32[16,4,4,8,128]{4,3,2,1,0:T(8,128)S(1)}, u32[]{:S(2)}, u32[]{:S(2)}) async-start(f32[16,4,4,8,128]{4,3,2,1,0:T(8,128)} %broadcast_in_dim.83), calls=%async_computation.3 | async-start | bytes 2097152 | tf_op jit(solution)/shard_map/all_to_all | solution.py:313
  306.7 5.3 %place_tiles.1.part = f32[4,4,128,128]{3,2,1,0:T(8,128)} custom-call(s32[4]{0:T(128)} %pad_add_fusion.meta, s32[96,16]{1,0:T(8,128)} %copy.13.picks, f32[16,384,128]{2,1,0:T(8,128)} %copy-done.2), custom_call_target="tpu_custom_call" | custom-call | tf_op jit(solution)/shard_map/place_tiles/pallas_call | solution.py:128
  312.0 7.4 %collective-permute-start.16 = (f32[4,4,128,128]{3,2,1,0:T(8,128)}, f32[4,4,128,128]{3,2,1,0:T(8,128)S(1)}, u32[]{:S(2)}, u32[]{:S(2)}) collective-permute-start(f32[4,4,128,128]{3,2,1,0:T(8,128)} %place_tiles.1.part), channel_id=1, source_target_pairs={{0,0},{1,16},{2,32},{3,48},{4,64},{5,80},{6,96},{7,112},{8,128},{9... | collective-permute-start | bytes 3145736 | tf_op jit(solution)/shard_map/ppermute | solution.py:305
  319.4 83.5 %collective-permute-done.16.mirror = f32[4,4,128,128]{3,2,1,0:T(8,128)S(1)} collective-permute-done((f32[4,4,128,128]{3,2,1,0:T(8,128)}, f32[4,4,128,128]{3,2,1,0:T(8,128)S(1)}, u32[]{:S(2)}, u32[]{:S(2)}) %collective-permute-start.16) | collective-permute-done | bytes 1048608 | tf_op jit(solution)/shard_map/ppermute | solution.py:305
  402.9 1.0 copy-done.6
  403.9 0.4 copy-done.3
  404.3 12.2 %finish.1 = f32[512,512]{1,0:T(8,128)} custom-call(s32[4]{0:T(128)} %pad_add_fusion.meta, f32[4,4,128,128]{3,2,1,0:T(8,128)} %place_tiles.1.part, f32[4,4,128,128]{3,2,1,0:T(8,128)} %copy-done.6, f32[16,4,4,8,128]{4,3,2,1,0:T(8,128)} %copy-done.3, f32[16,4,4,8,128]{4,3,2,1,0:T(8,128)} %all_to_all.25.right, f32[4,128,128]{2,1,0:T(8,128)} %get-tuple-element.38.diag, ...), custom_call_target="tpu_custom_call" | custom-call | tf_op jit(solution)/shard_map/finish/pallas_call | solution.py:238
  (47 shorter events, 1.1 us)
Async XLA Ops:
  0.0 77.4 %copy-start = (f32[8192]{0:T(1024)S(1)}, f32[8192]{0:T(1024)}, u32[]{:S(2)}) copy-start(f32[8192]{0:T(1024)} %param.7) | copy-start | bytes 98308
  2.6 11.2 %copy-start.1 = (bf16[6,768,128]{2,1,0:T(8,128)(2,1)}, bf16[6,768,128]{2,1,0:T(8,128)(2,1)S(1)}, u32[]{:S(2)}) copy-start(bf16[6,768,128]{2,1,0:T(8,128)(2,1)S(1)} %multiply_convert_fusion.mine.first) | copy-start | bytes 3538948
  5.6 71.1 %all-to-all-start = ((bf16[8,3,768,128]{3,2,1,0:T(8,128)(2,1)}), bf16[8,3,768,128]{3,2,1,0:T(8,128)(2,1)}, u32[]{:S(2)}, u32[]{:S(2)}) async-start(bf16[8,3,768,128]{3,2,1,0:T(8,128)(2,1)} %broadcast_select_fusion), calls=%async_computation | async-start | bytes 9437184 | tf_op jit(solution)/shard_map/all_to_all | solution.py:276
  14.6 7.7 %collective-permute-start = (f32[4,128,128]{2,1,0:T(8,128)S(1)}, f32[4,128,128]{2,1,0:T(8,128)S(1)}, u32[]{:S(2)}, u32[]{:S(2)}) collective-permute-start(f32[4,128,128]{2,1,0:T(8,128)S(1)} %select_reduce_fusion), channel_id=1, source_target_pairs={{0,1},{1,0},{2,3},{3,2},{4,5},{5,4},{6,7},{7,6},{8,9},{9,8},{10,11... | collective-permute-start | bytes 786440 | tf_op jit(solution)/shard_map/ppermute | solution.py:271
  16.6 22.5 %collective-permute-start.3 = (bf16[3,384,128]{2,1,0:T(8,128)(2,1)S(1)}, bf16[3,384,128]{2,1,0:T(8,128)(2,1)S(1)}, u32[]{:S(2)}, u32[]{:S(2)}) collective-permute-start(bf16[3,384,128]{2,1,0:T(8,128)(2,1)S(1)} %slice.30), channel_id=1, source_target_pairs={{0,16},{1,17},{2,18},{3,19},{4,20},{5,21},{6,22},{7,23},{8,24},{9,... | collective-permute-start | bytes 884744 | tf_op jit(solution)/shard_map/ppermute | solution.py:279
  22.4 10.4 %collective-permute-start.1 = (f32[4,128,128]{2,1,0:T(8,128)S(1)}, f32[4,128,128]{2,1,0:T(8,128)S(1)}, u32[]{:S(2)}, u32[]{:S(2)}) collective-permute-start(f32[4,128,128]{2,1,0:T(8,128)S(1)} %add.85), channel_id=1, source_target_pairs={{0,2},{1,3},{2,0},{3,1},{4,6},{5,7},{6,4},{7,5},{8,10},{9,11},{10,... | collective-permute-start | bytes 786440 | tf_op jit(solution)/shard_map/ppermute | solution.py:271
  32.8 15.1 %collective-permute-start.2 = (f32[4,128,128]{2,1,0:T(8,128)S(1)}, f32[4,128,128]{2,1,0:T(8,128)S(1)}, u32[]{:S(2)}, u32[]{:S(2)}) collective-permute-start(f32[4,128,128]{2,1,0:T(8,128)S(1)} %add.86), channel_id=1, source_target_pairs={{0,4},{1,5},{2,6},{3,7},{4,0},{5,1},{6,2},{7,3},{8,12},{9,13},{10,... | collective-permute-start | bytes 786440 | tf_op jit(solution)/shard_map/ppermute | solution.py:271
  76.7 27.2 %collective-permute-start.4 = (bf16[8,3,768,128]{3,2,1,0:T(8,128)(2,1)}, bf16[8,3,768,128]{3,2,1,0:T(8,128)(2,1)}, u32[]{:S(2)}, u32[]{:S(2)}) collective-permute-start(bf16[8,3,768,128]{3,2,1,0:T(8,128)(2,1)} %all-to-all-done.same), channel_id=1, source_target_pairs={{0,16},{16,0},{1,17},{17,1},{2,18},{18,2},{3,19},{19,3},{4,20},{20... | collective-permute-start | bytes 14155784 | tf_op jit(solution)/shard_map/ppermute | solution.py:282
  76.7 8.7 %collective-permute-start.5 = (f32[4,128,128]{2,1,0:T(8,128)S(1)}, f32[4,128,128]{2,1,0:T(8,128)S(1)}, u32[]{:S(2)}, u32[]{:S(2)}) collective-permute-start(f32[4,128,128]{2,1,0:T(8,128)S(1)} %add.87), channel_id=1, source_target_pairs={{0,8},{8,0},{1,9},{9,1},{2,10},{10,2},{3,11},{11,3},{4,12},{12,4},... | collective-permute-start | bytes 786440 | tf_op jit(solution)/shard_map/ppermute | solution.py:283
  86.2 5.7 %collective-permute-start.6 = (f32[4,128,128]{2,1,0:T(8,128)S(1)}, f32[4,128,128]{2,1,0:T(8,128)S(1)}, u32[]{:S(2)}, u32[]{:S(2)}) collective-permute-start(f32[4,128,128]{2,1,0:T(8,128)S(1)} %get-tuple-element.37), channel_id=1, source_target_pairs={{0,16},{1,17},{2,18},{3,19},{4,20},{5,21},{6,22},{7,23},{8,24},{9,... | collective-permute-start | bytes 786440 | tf_op jit(solution)/shard_map/ppermute | solution.py:252
  87.7 11.5 %collective-permute-start.8 = (bf16[3,384,128]{2,1,0:T(8,128)(2,1)S(1)}, bf16[3,384,128]{2,1,0:T(8,128)(2,1)S(1)}, u32[]{:S(2)}, u32[]{:S(2)}) collective-permute-start(bf16[3,384,128]{2,1,0:T(8,128)(2,1)S(1)} %slice_add_fusion), channel_id=1, source_target_pairs={{0,32},{1,33},{2,34},{3,35},{4,36},{5,37},{6,38},{7,39},{8,40},{9,... | collective-permute-start | bytes 884744 | tf_op jit(solution)/shard_map/ppermute | solution.py:252
  91.9 11.3 %collective-permute-start.7 = (f32[4,128,128]{2,1,0:T(8,128)S(1)}, f32[4,128,128]{2,1,0:T(8,128)S(1)}, u32[]{:S(2)}, u32[]{:S(2)}) collective-permute-start(f32[4,128,128]{2,1,0:T(8,128)S(1)} %add.92), channel_id=1, source_target_pairs={{0,32},{1,33},{2,34},{3,35},{4,36},{5,37},{6,38},{7,39},{8,40},{9,... | collective-permute-start | bytes 786440 | tf_op jit(solution)/shard_map/ppermute | solution.py:252
  113.9 89.1 %all-to-all-start.1 = ((f32[16,384,128]{2,1,0:T(8,128)}), f32[16,384,128]{2,1,0:T(8,128)S(1)}, u32[]{:S(2)}, u32[]{:S(2)}) async-start(f32[16,384,128]{2,1,0:T(8,128)} %get-tuple-element.26), calls=%async_computation.1 | async-start | bytes 6291456 | tf_op jit(solution)/shard_map/all_to_all | solution.py:292
  122.1 5.2 %collective-permute-start.14 = (f32[4,128,128]{2,1,0:T(8,128)}, f32[4,128,128]{2,1,0:T(8,128)S(1)}, u32[]{:S(2)}, u32[]{:S(2)}) collective-permute-start(f32[4,128,128]{2,1,0:T(8,128)} %add.93), channel_id=1, source_target_pairs={{0,192},{1,193},{2,194},{3,195},{4,196},{5,197},{6,198},{7,199},{8... | collective-permute-start | bytes 786440 | tf_op jit(solution)/shard_map/ppermute | solution.py:253
  122.8 14.1 %collective-permute-start.13 = (f32[4,128,128]{2,1,0:T(8,128)}, f32[4,128,128]{2,1,0:T(8,128)S(1)}, u32[]{:S(2)}, u32[]{:S(2)}) collective-permute-start(f32[4,128,128]{2,1,0:T(8,128)} %add.93), channel_id=1, source_target_pairs={{0,64},{1,65},{2,66},{3,67},{4,68},{5,69},{6,70},{7,71},{8,72},{9,... | collective-permute-start | bytes 786440 | tf_op jit(solution)/shard_map/ppermute | solution.py:253
  124.7 15.9 %collective-permute-start.10 = (bf16[3,384,128]{2,1,0:T(8,128)(2,1)S(1)}, bf16[3,384,128]{2,1,0:T(8,128)(2,1)}, u32[]{:S(2)}, u32[]{:S(2)}) collective-permute-start(bf16[3,384,128]{2,1,0:T(8,128)(2,1)S(1)} %add.94), channel_id=1, source_target_pairs={{0,192},{1,193},{2,194},{3,195},{4,196},{5,197},{6,198},{7,199},{8... | collective-permute-start | bytes 884744 | tf_op jit(solution)/shard_map/ppermute | solution.py:253
  126.1 15.3 %collective-permute-start.9 = (bf16[3,384,128]{2,1,0:T(8,128)(2,1)S(1)}, bf16[3,384,128]{2,1,0:T(8,128)(2,1)}, u32[]{:S(2)}, u32[]{:S(2)}) collective-permute-start(bf16[3,384,128]{2,1,0:T(8,128)(2,1)S(1)} %add.94), channel_id=1, source_target_pairs={{0,64},{1,65},{2,66},{3,67},{4,68},{5,69},{6,70},{7,71},{8,72},{9,... | collective-permute-start | bytes 884744 | tf_op jit(solution)/shard_map/ppermute | solution.py:253
  138.6 6.7 %collective-permute-start.15 = (f32[4,128,128]{2,1,0:T(8,128)}, f32[4,128,128]{2,1,0:T(8,128)}, u32[]{:S(2)}, u32[]{:S(2)}) collective-permute-start(f32[4,128,128]{2,1,0:T(8,128)} %add_add_fusion.1), channel_id=1, source_target_pairs={{64,128},{65,129},{66,130},{67,131},{68,132},{69,133},{70,134},{71... | collective-permute-start | bytes 786440 | tf_op jit(solution)/shard_map/ppermute | solution.py:254
  143.1 53.4 %copy-start.8 = (pred[128,128]{1,0:T(8,128)(4,1)S(1)}, pred[128,128]{1,0:T(8,128)(4,1)}, u32[]{:S(2)}) copy-start(pred[128,128]{1,0:T(8,128)(4,1)} %iota_compare_fusion.1) | copy-start | bytes 49156
  143.1 53.5 %collective-permute-start.11 = (bf16[3,384,128]{2,1,0:T(8,128)(2,1)}, bf16[3,384,128]{2,1,0:T(8,128)(2,1)}, u32[]{:S(2)}, u32[]{:S(2)}) collective-permute-start(bf16[3,384,128]{2,1,0:T(8,128)(2,1)} %add_add_fusion), channel_id=1, source_target_pairs={{64,128},{65,129},{66,130},{67,131},{68,132},{69,133},{70,134},{71... | collective-permute-start | bytes 884744 | tf_op jit(solution)/shard_map/ppermute | solution.py:254
  196.6 1.5 copy-start.5
  197.8 1.9 collective-permute-start.12
  199.3 33.1 %copy-start.4 = (f32[4,128,128]{2,1,0:T(8,128)}, f32[4,128,128]{2,1,0:T(8,128)S(1)}, u32[]{:S(2)}) copy-start(f32[4,128,128]{2,1,0:T(8,128)S(1)} %select_select_fusion.chol) | copy-start | bytes 786436
  200.6 10.5 %copy-start.9 = (s32[96,16]{0,1:T(8,128)S(1)}, s32[96,16]{0,1:T(8,128)}, u32[]{:S(2)}) copy-start(s32[96,16]{0,1:T(8,128)} %param.6) | copy-start | bytes 18436
  203.0 72.6 %copy-start.2 = (f32[16,384,128]{2,1,0:T(8,128)}, f32[16,384,128]{2,1,0:T(8,128)S(1)}, u32[]{:S(2)}) copy-start(f32[16,384,128]{2,1,0:T(8,128)S(1)} %all-to-all-done.1.slots) | copy-start | bytes 9437188
  203.0 20.4 %all-to-all-start.2 = ((f32[16,48,128]{2,1,0:T(8,128)}), f32[16,48,128]{2,1,0:T(8,128)}, u32[]{:S(2)}, u32[]{:S(2)}) async-start(f32[16,48,128]{2,1,0:T(8,128)} %panel_slots.1), calls=%async_computation.2 | async-start | bytes 786432 | tf_op jit(solution)/shard_map/all_to_all | solution.py:303
  226.9 47.6 %collective-permute-start.17 = (f32[4,4,8,128]{3,2,1,0:T(8,128)}, f32[4,4,8,128]{3,2,1,0:T(8,128)}, u32[]{:S(2)}, u32[]{:S(2)}) collective-permute-start(f32[4,4,8,128]{3,2,1,0:T(8,128)} %place_strip.1), channel_id=1, source_target_pairs={{0,0},{1,16},{2,32},{3,48},{4,64},{5,80},{6,96},{7,112},{8,128},{9... | collective-permute-start | bytes 196616 | tf_op jit(solution)/shard_map/ppermute | solution.py:312
  274.6 23.6 %copy-start.7 = (f32[4,4,8,128]{3,2,1,0:T(8,128)S(1)}, f32[4,4,8,128]{3,2,1,0:T(8,128)}, u32[]{:S(2)}) copy-start(f32[4,4,8,128]{3,2,1,0:T(8,128)} %place_strip.1) | copy-start | bytes 196612
  299.3 103.6 %all-to-all-start.3 = ((f32[16,4,4,8,128]{4,3,2,1,0:T(8,128)}), f32[16,4,4,8,128]{4,3,2,1,0:T(8,128)S(1)}, u32[]{:S(2)}, u32[]{:S(2)}) async-start(f32[16,4,4,8,128]{4,3,2,1,0:T(8,128)} %broadcast_in_dim.83), calls=%async_computation.3 | async-start | bytes 2097152 | tf_op jit(solution)/shard_map/all_to_all | solution.py:313
  312.0 90.9 %collective-permute-start.16 = (f32[4,4,128,128]{3,2,1,0:T(8,128)}, f32[4,4,128,128]{3,2,1,0:T(8,128)S(1)}, u32[]{:S(2)}, u32[]{:S(2)}) collective-permute-start(f32[4,4,128,128]{3,2,1,0:T(8,128)} %place_tiles.1.part), channel_id=1, source_target_pairs={{0,0},{1,16},{2,32},{3,48},{4,64},{5,80},{6,96},{7,112},{8,128},{9... | collective-permute-start | bytes 3145736 | tf_op jit(solution)/shard_map/ppermute | solution.py:305
  402.9 1.0 copy-start.6
  402.9 1.3 copy-start.3

commit v4 on v3

--- a/solution.py
+++ b/solution.py
@@ -21,8 +21,24 @@
 GR = ("x", "yh", "core")
 GC = ("yl", "z")
 HIGH = lax.Precision.HIGHEST
+CONTRACT_INNER = (((1,), (0,)), ((), ()))
 CONTRACT_ROWS = (((0,), (0,)), ((), ()))
 CONTRACT_COLS = (((1,), (1,)), ((), ()))
+
+
+def flip_kernel(scaled, out):
+    out[0] = scaled[0].T
+
+
+def flip(scaled):
+    return pl.pallas_call(
+        flip_kernel,
+        grid=(GROUP,),
+        in_specs=[pl.BlockSpec((1, R, BLK), lambda s: (s, 0, 0))],
+        out_specs=pl.BlockSpec((1, BLK, R), lambda s: (s, 0, 0)),
+        out_shape=jax.ShapeDtypeStruct((GROUP, BLK, R), scaled.dtype),
+        name="flip",
+    )(scaled)
 
 
 def gram_kernel(meta, mine, same, other, out, late):
@@ -33,7 +49,7 @@
     for k in range(HALF):
         pair = jnp.concatenate([same[0, k], other[0, k]], axis=1)
         tiles = lax.dot_general(
-            mine[k], pair, CONTRACT_ROWS, preferred_element_type=jnp.float32
+            mine[k], pair, CONTRACT_INNER, preferred_element_type=jnp.float32
         )
         out[at_same, k * BLK : (k + 1) * BLK, :] = tiles[:, :BLK]
         out[at_other, k * BLK : (k + 1) * BLK, :] = tiles[:, BLK:]
@@ -43,7 +59,7 @@
         late[...] = out[0].reshape(HALF, BLK, BLK)
 
 
-def gram_slots(meta, scaled, same, other):
+def gram_slots(meta, flipped, same, other):
     def pick_half(q, meta):
         return (jnp.where((q > meta[0]) | ((q == meta[0]) & (meta[1] == 0)), 0, 1), 0, 0)
 
@@ -52,7 +68,7 @@
         num_scalar_prefetch=1,
         grid=(NWIN // 2,),
         in_specs=[
-            pl.BlockSpec(whole, pick_half),
+            pl.BlockSpec((HALF, BLK, R), pick_half),
             pl.BlockSpec((1,) + whole, lambda q, meta: (q, 0, 0, 0)),
             pl.BlockSpec((1,) + whole, lambda q, meta: (q, 0, 0, 0)),
         ],
@@ -69,7 +85,7 @@
             jax.ShapeDtypeStruct((HALF, BLK, BLK), jnp.float32),
         ],
         name="gram_slots",
-    )(meta, scaled, same, other)
+    )(meta, flipped, same, other)
 
 
 def panel_kernel(first, lead, late, out):
@@ -159,45 +175,71 @@
     )(meta, picks, slots)
 
 
-def finish_kernel(meta, part, mirror, left, right, diag, chol, inverse, out):
+def solve_block(ref, inverse, a):
+    solved = [
+        lax.dot_general(
+            ref[:, b, a].reshape(BLK, BLK),
+            inverse[b],
+            CONTRACT_COLS,
+            precision=HIGH,
+            preferred_element_type=jnp.float32,
+        )
+        for b in range(SPAN)
+    ]
+    return jnp.concatenate(solved, axis=1)
+
+
+def full_spec(shape):
+    zeros = (0,) * len(shape)
+    return pl.BlockSpec(shape, lambda *_: zeros)
+
+
+def solve_kernel(left, inverse, out):
+    for a in range(SPAN):
+        out[a] = solve_block(left, inverse, a)
+
+
+def solve_rows(left, inverse):
+    shape = (SPAN, BLK, SPAN * BLK)
+    return pl.pallas_call(
+        solve_kernel,
+        grid=(1,),
+        in_specs=[full_spec(left.shape), full_spec(inverse.shape)],
+        out_specs=full_spec(shape),
+        out_shape=jax.ShapeDtypeStruct(shape, jnp.float32),
+        name="solve_rows",
+    )(left, inverse)
+
+
+def update_kernel(meta, part, lefts, right, diag, chol, inverse, out):
     i = meta[2]
     j = meta[3]
-
-    def block_rows(ref, a):
-        solved = [
-            lax.dot_general(
-                ref[:, b, a].reshape(BLK, BLK),
-                inverse[b],
-                CONTRACT_COLS,
-                precision=HIGH,
-                preferred_element_type=jnp.float32,
-            )
-            for b in range(SPAN)
-        ]
-        return jnp.concatenate(solved, axis=1)
-
-    lefts = [block_rows(left, a) for a in range(SPAN)]
     inside = (i > 0) & (j > 0)
+
+    def spot(a, b):
+        return (slice(a * BLK, (a + 1) * BLK), slice(b * BLK, (b + 1) * BLK))
 
     @pl.when(inside & (i != j))
     def _():
         for a in range(SPAN):
             for b in range(SPAN):
-                out[a * BLK : (a + 1) * BLK, b * BLK : (b + 1) * BLK] = part[a, b] + mirror[b, a].T
+                out[spot(a, b)] = part[a, b]
+
+    @pl.when(jnp.logical_not(inside) | (i == j))
+    def _():
+        out[...] = jnp.zeros_like(out)
 
     @pl.when(inside & (i == j))
     def _():
-        out[...] = jnp.zeros_like(out)
         for a in range(SPAN):
-            out[a * BLK : (a + 1) * BLK, a * BLK : (a + 1) * BLK] = diag[a]
+            out[spot(a, a)] = diag[a]
 
     @pl.when(inside)
     def _():
         for b in range(SPAN):
-            rights = block_rows(right, b)
+            rights = solve_block(right, inverse, b)
             for a in range(SPAN):
-                spot = (slice(a * BLK, (a + 1) * BLK), slice(b * BLK, (b + 1) * BLK))
-                out[spot] = out[spot] - lax.dot_general(
+                out[spot(a, b)] = out[spot(a, b)] - lax.dot_general(
                     lefts[a],
                     rights,
                     CONTRACT_COLS,
@@ -205,14 +247,10 @@
                     preferred_element_type=jnp.float32,
                 )
 
-    @pl.when((i == 0))
-    def _():
-        out[...] = jnp.zeros_like(out)
-
     @pl.when((i == 0) & (j == 0))
     def _():
         for a in range(SPAN):
-            out[a * BLK : (a + 1) * BLK, a * BLK : (a + 1) * BLK] = chol[a]
+            out[spot(a, a)] = chol[a]
 
     @pl.when((i > 0) & (j == 0))
     def _():
@@ -220,27 +258,52 @@
             out[a * BLK : (a + 1) * BLK, :] = lefts[a]
 
 
-def finish(meta, part, mirror, left, right, diag, chol, inverse):
-    def full(shape):
-        zeros = (0,) * len(shape)
-        return pl.BlockSpec(shape, lambda t, meta: zeros)
-
-    blocks = (SPAN, SPAN, BLK, BLK)
-    slices = (NWIN, SPAN, SPAN, SLICE, BLK)
-    small = (SPAN, BLK, BLK)
+def update(meta, part, lefts, right, diag, chol, inverse):
     size = (SPAN * BLK, SPAN * BLK)
     grid_spec = pltpu.PrefetchScalarGridSpec(
         num_scalar_prefetch=1,
         grid=(1,),
-        in_specs=[full(s) for s in (blocks, blocks, slices, slices, small, small, small)],
-        out_specs=full(size),
+        in_specs=[full_spec(v.shape) for v in (part, lefts, right, diag, chol, inverse)],
+        out_specs=full_spec(size),
+    )
+    return pl.pallas_call(
+        update_kernel,
+        grid_spec=grid_spec,
+        out_shape=jax.ShapeDtypeStruct(size, jnp.float32),
+        name="update",
+    )(meta, part, lefts, right, diag, chol, inverse)
+
+
+def finish_kernel(meta, base, mirror, out):
+    i = meta[2]
+    j = meta[3]
+    both = (i > 0) & (j > 0) & (i != j)
+
+    @pl.when(both)
+    def _():
+        for b in range(SPAN):
+            out[:, b * BLK : (b + 1) * BLK] = base[:, b * BLK : (b + 1) * BLK] + mirror[b, 0].T
+
+    @pl.when(jnp.logical_not(both))
+    def _():
+        out[...] = base[...]
+
+
+def finish(meta, base, mirror):
+    size = (SPAN * BLK, SPAN * BLK)
+    rows = pl.BlockSpec((BLK, SPAN * BLK), lambda a, meta: (a, 0))
+    grid_spec = pltpu.PrefetchScalarGridSpec(
+        num_scalar_prefetch=1,
+        grid=(SPAN,),
+        in_specs=[rows, pl.BlockSpec((SPAN, 1, BLK, BLK), lambda a, meta: (0, a, 0, 0))],
+        out_specs=rows,
     )
     return pl.pallas_call(
         finish_kernel,
         grid_spec=grid_spec,
         out_shape=jax.ShapeDtypeStruct(size, jnp.float32),
         name="finish",
-    )(meta, part, mirror, left, right, diag, chol, inverse)
+    )(meta, base, mirror)
 
 
 def swap_pairs(size, bit):
@@ -277,17 +340,18 @@
     cut = R // 2
     rootly = jnp.where(i == 0, scaled[:HALF], jnp.zeros_like(scaled[:HALF]))
     piece = rootly[:, :cut] + lax.ppermute(rootly[:, cut:], "core", [(0, 1)])
-    same, diag, piece = lax.optimization_barrier((same, diag, piece))
+    flipped = flip(scaled)
+    same, diag, piece, flipped = lax.optimization_barrier((same, diag, piece, flipped))
 
     other = lax.ppermute(same, "core", [(0, 1), (1, 0)])
     diag = diag + lax.ppermute(diag, "yl", swap_pairs(2, 1))
     eye = jnp.eye(BLK, dtype=jnp.float32)
     given_here = lax.dynamic_slice(given_diag, (i * SPAN * BLK,), (SPAN * BLK,))
     diag = diag + given_here.reshape(SPAN, 1, BLK) * eye
-    corner = spread(spread(jnp.where(i == 0, diag, 0.0), "core"), "yh")
+    corner = spread(jnp.where(i == 0, diag, 0.0), "core")
+    corner = spread(corner, "yh")
     piece = spread(piece, "yh")
-    tiles, late = gram_slots(meta, scaled, same, other)
-    tiles, late, corner, piece = lax.optimization_barrier((tiles, late, corner, piece))
+    tiles, late = gram_slots(meta, flipped, same, other)
 
     tiles = lax.all_to_all(tiles, GC, 0, 0, tiled=True)
     chol = jnp.linalg.cholesky(spread(corner, "x"))
@@ -313,7 +377,9 @@
     left = lax.all_to_all(jnp.broadcast_to(strip, copies), GC, 0, 0, tiled=True)
     turned, inverse = lax.optimization_barrier((turned, inverse))
     right = lax.all_to_all(jnp.broadcast_to(turned, copies), GR, 0, 0, tiled=True)
-    return finish(meta, part, mirror, left, right, diag, chol, inverse)
+    lefts = solve_rows(left, inverse)
+    base = update(meta, part, lefts, right, diag, chol, inverse)
+    return finish(meta, base, mirror)
 
 
 def solution(mesh):

time: 418 us -> 410 us (0.981); the launches traced: 416 us -> 403 us
  blocking collectives: 22.6 us -> 0 us
  Pallas kernels: 33.4 us -> 44.6 us
    ppermute x1, waiting for transfers between devices: 83.5 us -> 0.01 us  [body(): mirror = lax.ppermute(part, AXES, everywhere)]
    ppermute x1, waiting for transfers between devices: 0.01 us -> 40.5 us  [body(): turned = lax.ppermute(strip, AXES, everywhere)]
    ppermute x3, waiting for transfers between devices: 9.28 us -> 37 us  [spread(): return v + lax.ppermute(v, step, [(0, 1)])]
    all_to_all x1 -> x0, blocking collectives: 22.6 us -> none  [body(): lax.all_to_all(jnp.broadcast_to(turned, copies), GR, 0, 0, tiled=True)]
    pallas_call x0 -> x3, Pallas kernels: none -> 18.9 us  [the longest x1 9.68 us: update(): pl.pallas_call(update_kernel, grid_spec=grid_spec, out_shape=jax.ShapeDty...]
    all_to_all x0 -> x1, waiting for transfers between devices: none -> 11.3 us  [body(): lax.all_to_all(jnp.broadcast_to(turned, copies), GR, 0, 0, tiled=True)]
    pallas_call x1, Pallas kernels: 12.2 us -> 4.45 us  [finish(): pl.pallas_call(finish_kernel, grid_spec=grid_spec, out_shape=jax.ShapeDty...]
    ppermute x1, waiting for transfers between devices: 0.01 us -> 7.6 us  [body(): other = lax.ppermute(same, 'core', [(0, 1), (1, 0)])]
  transfers between devices with their start and end apart: 22 -> 23, of which waited for: 12 -> 15; matrix products, arithmetic and copies ran while one was open for 25% -> 26% of each run, Pallas kernels for 2% -> 7%
where the time goes in v4:
time: 410 us; the launch traced here: 403 us
  waiting for transfers between devices  172 us (42%)
  other arithmetic  104 us (25%)
  starting transfers between devices  71.6 us (17%)
  Pallas kernels  44.6 us (11%)
  local copies, waits for them, and re-layouts  8.93 us (2%)
    another operation x4, other arithmetic, body(): chol = jnp.linalg.cholesky(spread(corner, 'x'))  48.5 us
    ppermute x1, waiting for transfers between devices, body(): turned = lax.ppermute(strip, AXES, everywhere)  40.5 us
    another operation x2, other arithmetic, body(): lax.linalg.triangular_solve(chol, jnp.broadcast_to(eye, chol.shape), left...  39.3 us
    ppermute x3, waiting for transfers between devices, spread(): return v + lax.ppermute(v, step, [(0, 1)])  37 us
    all_to_all x1, waiting for transfers between devices, body(): same = lax.all_to_all(slots, ('x', 'yh'), 0, 0, tiled=True)  28 us
    ppermute x3, waiting for transfers between devices, body(): diag = diag + lax.ppermute(diag, 'z', swap_pairs(8, bit))  18.9 us
    ppermute x4, waiting for transfers between devices, spread(): v = v + lax.ppermute(v, 'x', [(0, 1)]) + lax.ppermute(v, 'x', [(0, 3)])  12.2 us
    all_to_all x1, waiting for transfers between devices, body(): lax.all_to_all(jnp.broadcast_to(turned, copies), GR, 0, 0, tiled=True)  11.3 us
  transfers between devices with their start and end apart: 23, of which 15 were waited for; matrix products, arithmetic and copies ran while one was open for 26% of the time, Pallas kernels for 7%

profile of v4, /device:TPU:66, one launch (start us, length us, event | category | flops | bytes accessed | tf_op | source)
XLA Modules:
  0.0 402.9 jit_solution(4754280879460146309)
XLA Ops:
  0.0 0.8 sqrt.3
  0.8 1.9 multiply_convert_fusion.scaled.first
  2.8 2.8 broadcast_select_fusion
  5.6 7.5 %all-to-all-start = ((bf16[8,3,768,128]{3,2,1,0:T(8,128)(2,1)}), bf16[8,3,768,128]{3,2,1,0:T(8,128)(2,1)}, u32[]{:S(2)}, u32[]{:S(2)}) async-start(bf16[8,3,768,128]{3,2,1,0:T(8,128)(2,1)} %broadcast_select_fusion), calls=%async_computation | async-start | bytes 9437184 | tf_op jit(solution)/shard_map/all_to_all | solution.py:339
  13.0 0.8 dynamic-slice_bitcast_fusion.1
  14.6 2.0 collective-permute-start
  16.6 1.3 collective-permute-start.3
  17.9 4.4 %collective-permute-done = f32[4,128,128]{2,1,0:T(8,128)S(1)} collective-permute-done((f32[4,128,128]{2,1,0:T(8,128)S(1)}, f32[4,128,128]{2,1,0:T(8,128)S(1)}, u32[]{:S(2)}, u32[]{:S(2)}) %collective-permute-start) | collective-permute-done | bytes 262176 | tf_op jit(solution)/shard_map/ppermute | solution.py:334
  22.5 10.3 %collective-permute-done.1 = f32[4,128,128]{2,1,0:T(8,128)S(1)} collective-permute-done((f32[4,128,128]{2,1,0:T(8,128)S(1)}, f32[4,128,128]{2,1,0:T(8,128)S(1)}, u32[]{:S(2)}, u32[]{:S(2)}) %collective-permute-start.1) | collective-permute-done | bytes 262176 | tf_op jit(solution)/shard_map/ppermute | solution.py:334
  32.8 6.3 %collective-permute-start.2 = (f32[4,128,128]{2,1,0:T(8,128)S(1)}, f32[4,128,128]{2,1,0:T(8,128)S(1)}, u32[]{:S(2)}, u32[]{:S(2)}) collective-permute-start(f32[4,128,128]{2,1,0:T(8,128)S(1)} %add.86), channel_id=1, source_target_pairs={{0,4},{1,5},{2,6},{3,7},{4,0},{5,1},{6,2},{7,3},{8,12},{9,13},{10,... | collective-permute-start | bytes 786440 | tf_op jit(solution)/shard_map/ppermute | solution.py:334
  39.1 4.6 %flip.1.mine = bf16[6,128,768]{2,1,0:T(8,128)(2,1)} custom-call(bf16[6,768,128]{2,1,0:T(8,128)(2,1)} %copy-done.1), custom_call_target="tpu_custom_call" | custom-call | tf_op jit(solution)/shard_map/flip/pallas_call | solution.py:34
  43.8 4.1 %collective-permute-done.2 = f32[4,128,128]{2,1,0:T(8,128)S(1)} collective-permute-done((f32[4,128,128]{2,1,0:T(8,128)S(1)}, f32[4,128,128]{2,1,0:T(8,128)S(1)}, u32[]{:S(2)}, u32[]{:S(2)}) %collective-permute-start.2) | collective-permute-done | bytes 262176 | tf_op jit(solution)/shard_map/ppermute | solution.py:334
  47.9 0.7 add.87
  48.7 28.0 %all-to-all-done.same = bf16[8,3,768,128]{3,2,1,0:T(8,128)(2,1)} async-done(((bf16[8,3,768,128]{3,2,1,0:T(8,128)(2,1)}), bf16[8,3,768,128]{3,2,1,0:T(8,128)(2,1)}, u32[]{:S(2)}, u32[]{:S(2)}) %all-to-all-start) | async-done | bytes 4718624 | tf_op jit(solution)/shard_map/all_to_all | solution.py:339
  77.4 7.6 %collective-permute-done.4.other = bf16[8,3,768,128]{3,2,1,0:T(8,128)(2,1)} collective-permute-done((bf16[8,3,768,128]{3,2,1,0:T(8,128)(2,1)}, bf16[8,3,768,128]{3,2,1,0:T(8,128)(2,1)}, u32[]{:S(2)}, u32[]{:S(2)}) %collective-permute-start.4) | collective-permute-done | bytes 4718624 | tf_op jit(solution)/shard_map/ppermute | solution.py:346
  85.0 9.8 %gram_slots.1 = (f32[16,384,128]{2,1,0:T(8,128)}, f32[3,128,128]{2,1,0:T(8,128)}) custom-call(s32[4]{0:T(128)} %pad_add_fusion.meta, bf16[6,128,768]{2,1,0:T(8,128)(2,1)} %flip.1.mine, bf16[8,3,768,128]{3,2,1,0:T(8,128)(2,1)} %all-to-all-done.same, bf16[8,3,768,128]{3,2,1,0:T(8,128)(2,1)} %collective-permute-done.4.other), custom_call_target="tpu_custom_call" | custom-call | tf_op jit(solution)/shard_map/gram_slots/pallas_call | solution.py:80
  94.8 8.2 %all-to-all-start.1 = ((f32[16,384,128]{2,1,0:T(8,128)}), f32[16,384,128]{2,1,0:T(8,128)S(1)}, u32[]{:S(2)}, u32[]{:S(2)}) async-start(f32[16,384,128]{2,1,0:T(8,128)} %get-tuple-element.20), calls=%async_computation.1 | async-start | bytes 6291456 | tf_op jit(solution)/shard_map/all_to_all | solution.py:356
  103.0 5.4 %collective-permute-start.5 = (bf16[3,384,128]{2,1,0:T(8,128)(2,1)S(1)}, bf16[3,384,128]{2,1,0:T(8,128)(2,1)}, u32[]{:S(2)}, u32[]{:S(2)}) collective-permute-start(bf16[3,384,128]{2,1,0:T(8,128)(2,1)S(1)} %slice_add_fusion), channel_id=1, source_target_pairs={{0,32},{1,33},{2,34},{3,35},{4,36},{5,37},{6,38},{7,39},{8,40},{9,... | collective-permute-start | bytes 884744 | tf_op jit(solution)/shard_map/ppermute | solution.py:315
  108.4 0.9 collective-permute-start.10
  109.4 18.0 %collective-permute-done.5 = bf16[3,384,128]{2,1,0:T(8,128)(2,1)} collective-permute-done((bf16[3,384,128]{2,1,0:T(8,128)(2,1)S(1)}, bf16[3,384,128]{2,1,0:T(8,128)(2,1)}, u32[]{:S(2)}, u32[]{:S(2)}) %collective-permute-start.5) | collective-permute-done | bytes 294944 | tf_op jit(solution)/shard_map/ppermute | solution.py:315
  127.4 1.0 add.89
  128.4 0.7 collective-permute-start.7
  129.1 1.3 collective-permute-start.6
  130.4 3.6 collective-permute-done.10
  134.0 1.8 broadcast_select_fusion.4
  135.8 1.3 collective-permute-start.11
  137.1 1.1 collective-permute-done.11
  138.3 2.4 collective-permute-start.12
  141.4 1.8 collective-permute-start.8
  143.2 17.8 %collective-permute-done.12 = f32[4,128,128]{2,1,0:T(8,128)S(1)} collective-permute-done((f32[4,128,128]{2,1,0:T(8,128)S(1)}, f32[4,128,128]{2,1,0:T(8,128)S(1)}, u32[]{:S(2)}, u32[]{:S(2)}) %collective-permute-start.12) | collective-permute-done | bytes 262176 | tf_op jit(solution)/shard_map/ppermute | solution.py:315
  161.0 0.7 add.97
  161.7 1.4 collective-permute-start.14
  163.1 1.3 collective-permute-start.13
  165.2 11.6 %collective-permute-done.13 = f32[4,128,128]{2,1,0:T(8,128)} collective-permute-done((f32[4,128,128]{2,1,0:T(8,128)}, f32[4,128,128]{2,1,0:T(8,128)}, u32[]{:S(2)}, u32[]{:S(2)}) %collective-permute-start.13) | collective-permute-done | bytes 262176 | tf_op jit(solution)/shard_map/ppermute | solution.py:316
  176.8 1.1 add_add_fusion.1
  178.0 1.5 collective-permute-start.15
  179.5 1.0 broadcast_select_fusion.3
  180.5 0.9 pad_maximum_fusion.lead
  181.3 3.0 collective-permute-done.15
  184.4 0.9 copy.12
  185.3 1.7 fusion.2
  187.0 47.7 %custom-call.7 = f32[4,128,128]{2,1,0:T(8,128)S(1)} custom-call(f32[4,128,128]{2,1,0:T(8,128)} %fusion.2), custom_call_target="Cholesky" | custom-call | tf_op jit(solution)/shard_map/jit(cholesky)/cholesky | solution.py:357
  235.5 1.0 select_select_fusion.chol
  236.6 2.5 panel_slots.1
  239.1 6.8 %all-to-all-start.2 = ((f32[16,48,128]{2,1,0:T(8,128)}), f32[16,48,128]{2,1,0:T(8,128)}, u32[]{:S(2)}, u32[]{:S(2)}) async-start(f32[16,48,128]{2,1,0:T(8,128)} %panel_slots.1), calls=%async_computation.2 | async-start | bytes 786432 | tf_op jit(solution)/shard_map/all_to_all | solution.py:367
  245.9 0.7 copy.13.picks
  246.6 9.6 %all-to-all-done.2.slots = f32[16,48,128]{2,1,0:T(8,128)} async-done(((f32[16,48,128]{2,1,0:T(8,128)}), f32[16,48,128]{2,1,0:T(8,128)}, u32[]{:S(2)}, u32[]{:S(2)}) %all-to-all-start.2) | async-done | bytes 393248 | tf_op jit(solution)/shard_map/all_to_all | solution.py:367
  256.3 3.6 place_strip.1
  259.8 2.0 broadcast_in_dim.83
  261.8 5.6 %all-to-all-start.3 = ((f32[16,4,4,8,128]{4,3,2,1,0:T(8,128)}), f32[16,4,4,8,128]{4,3,2,1,0:T(8,128)}, u32[]{:S(2)}, u32[]{:S(2)}) async-start(f32[16,4,4,8,128]{4,3,2,1,0:T(8,128)} %broadcast_in_dim.83), calls=%async_computation.3 | async-start | bytes 2097152 | tf_op jit(solution)/shard_map/all_to_all | solution.py:377
  267.5 5.4 %place_tiles.1.part = f32[4,4,128,128]{3,2,1,0:T(8,128)} custom-call(s32[4]{0:T(128)} %pad_add_fusion.meta, s32[96,16]{1,0:T(8,128)} %copy.13.picks, f32[16,384,128]{2,1,0:T(8,128)} %copy-done.2), custom_call_target="tpu_custom_call" | custom-call | tf_op jit(solution)/shard_map/place_tiles/pallas_call | solution.py:144
  272.9 6.1 %collective-permute-start.17 = (f32[4,4,128,128]{3,2,1,0:T(8,128)}, f32[4,4,128,128]{3,2,1,0:T(8,128)S(1)}, u32[]{:S(2)}, u32[]{:S(2)}) collective-permute-start(f32[4,4,128,128]{3,2,1,0:T(8,128)} %place_tiles.1.part), channel_id=1, source_target_pairs={{0,0},{1,16},{2,32},{3,48},{4,64},{5,80},{6,96},{7,112},{8,128},{9... | collective-permute-start | bytes 3145736 | tf_op jit(solution)/shard_map/ppermute | solution.py:369
  279.0 5.2 %collective-permute-start.16 = (f32[4,4,8,128]{3,2,1,0:T(8,128)S(1)}, f32[4,4,8,128]{3,2,1,0:T(8,128)S(1)}, u32[]{:S(2)}, u32[]{:S(2)}) collective-permute-start(f32[4,4,8,128]{3,2,1,0:T(8,128)S(1)} %copy-done.7), channel_id=1, source_target_pairs={{0,0},{1,16},{2,32},{3,48},{4,64},{5,80},{6,96},{7,112},{8,128},{9... | collective-permute-start | bytes 196616 | tf_op jit(solution)/shard_map/ppermute | solution.py:376
  284.2 39.3 %custom-call.8 = f32[4,1,128,128]{2,3,1,0:T(8,128)S(1)} custom-call(f32[4,1,128,128]{3,2,1,0:T(8,128)S(1)} %select_bitcast_fusion), custom_call_target="InvertDiagBlocksLowerTriangular" | custom-call | tf_op jit(solution)/shard_map/triangular_solve | solution.py:371
  323.5 1.3 fusion.inverse
  324.8 40.5 %collective-permute-done.16 = f32[4,4,8,128]{3,2,1,0:T(8,128)S(1)} collective-permute-done((f32[4,4,8,128]{3,2,1,0:T(8,128)S(1)}, f32[4,4,8,128]{3,2,1,0:T(8,128)S(1)}, u32[]{:S(2)}, u32[]{:S(2)}) %collective-permute-start.16) | collective-permute-done | bytes 65568 | tf_op jit(solution)/shard_map/ppermute | solution.py:376
  365.3 1.1 broadcast_in_dim.84
  366.4 4.5 %all-to-all-start.4 = ((f32[16,4,4,8,128]{4,3,2,1,0:T(8,128)}), f32[16,4,4,8,128]{4,3,2,1,0:T(8,128)S(1)}, u32[]{:S(2)}, u32[]{:S(2)}) async-start(f32[16,4,4,8,128]{4,3,2,1,0:T(8,128)} %broadcast_in_dim.84), calls=%async_computation.4 | async-start | bytes 2097152 | tf_op jit(solution)/shard_map/all_to_all | solution.py:379
  370.9 4.5 %solve_rows.1.lefts = f32[4,128,512]{2,1,0:T(8,128)} custom-call(f32[16,4,4,8,128]{4,3,2,1,0:T(8,128)} %all-to-all-done.3.left, f32[4,128,128]{2,1,0:T(8,128)} %fusion.inverse), custom_call_target="tpu_custom_call" | custom-call | tf_op jit(solution)/shard_map/solve_rows/pallas_call | solution.py:204
  375.5 11.3 %all-to-all-done.4.right = f32[16,4,4,8,128]{4,3,2,1,0:T(8,128)S(1)} async-done(((f32[16,4,4,8,128]{4,3,2,1,0:T(8,128)}), f32[16,4,4,8,128]{4,3,2,1,0:T(8,128)S(1)}, u32[]{:S(2)}, u32[]{:S(2)}) %all-to-all-start.4) | async-done | bytes 1048608 | tf_op jit(solution)/shard_map/all_to_all | solution.py:379
  386.8 1.0 copy-done.3
  387.8 9.7 %update.1.base = f32[512,512]{1,0:T(8,128)} custom-call(s32[4]{0:T(128)} %pad_add_fusion.meta, f32[4,4,128,128]{3,2,1,0:T(8,128)} %place_tiles.1.part, f32[4,128,512]{2,1,0:T(8,128)} %solve_rows.1.lefts, f32[16,4,4,8,128]{4,3,2,1,0:T(8,128)} %copy-done.3, f32[4,128,128]{2,1,0:T(8,128)} %get-tuple-element.32.diag, f32[4,128,128]{2,1,0:T(8,128)} %copy-done.4, ...), custom_call_target="tpu_custom_call" | custom-call | tf_op jit(solution)/shard_map/update/pallas_call | solution.py:269
  397.5 1.0 copy-done.6
  398.4 4.4 %finish.1 = f32[512,512]{1,0:T(8,128)} custom-call(s32[4]{0:T(128)} %pad_add_fusion.meta, f32[512,512]{1,0:T(8,128)} %update.1.base, f32[4,4,128,128]{3,2,1,0:T(8,128)} %copy-done.6), custom_call_target="tpu_custom_call" | custom-call | tf_op jit(solution)/shard_map/finish/pallas_call | solution.py:301
  (51 shorter events, 4.3 us)
Async XLA Ops:
  0.0 109.3 %copy-start = (f32[8192]{0:T(1024)S(1)}, f32[8192]{0:T(1024)}, u32[]{:S(2)}) copy-start(f32[8192]{0:T(1024)} %param.7) | copy-start | bytes 98308
  2.6 11.2 %copy-start.1 = (bf16[6,768,128]{2,1,0:T(8,128)(2,1)}, bf16[6,768,128]{2,1,0:T(8,128)(2,1)S(1)}, u32[]{:S(2)}) copy-start(bf16[6,768,128]{2,1,0:T(8,128)(2,1)S(1)} %multiply_convert_fusion.scaled.first) | copy-start | bytes 3538948
  5.6 71.1 %all-to-all-start = ((bf16[8,3,768,128]{3,2,1,0:T(8,128)(2,1)}), bf16[8,3,768,128]{3,2,1,0:T(8,128)(2,1)}, u32[]{:S(2)}, u32[]{:S(2)}) async-start(bf16[8,3,768,128]{3,2,1,0:T(8,128)(2,1)} %broadcast_select_fusion), calls=%async_computation | async-start | bytes 9437184 | tf_op jit(solution)/shard_map/all_to_all | solution.py:339
  14.6 7.7 %collective-permute-start = (f32[4,128,128]{2,1,0:T(8,128)S(1)}, f32[4,128,128]{2,1,0:T(8,128)S(1)}, u32[]{:S(2)}, u32[]{:S(2)}) collective-permute-start(f32[4,128,128]{2,1,0:T(8,128)S(1)} %select_reduce_fusion), channel_id=1, source_target_pairs={{0,1},{1,0},{2,3},{3,2},{4,5},{5,4},{6,7},{7,6},{8,9},{9,8},{10,11... | collective-permute-start | bytes 786440 | tf_op jit(solution)/shard_map/ppermute | solution.py:334
  16.6 27.2 %collective-permute-start.3 = (bf16[3,384,128]{2,1,0:T(8,128)(2,1)S(1)}, bf16[3,384,128]{2,1,0:T(8,128)(2,1)S(1)}, u32[]{:S(2)}, u32[]{:S(2)}) collective-permute-start(bf16[3,384,128]{2,1,0:T(8,128)(2,1)S(1)} %slice.30), channel_id=1, source_target_pairs={{0,16},{1,17},{2,18},{3,19},{4,20},{5,21},{6,22},{7,23},{8,24},{9,... | collective-permute-start | bytes 884744 | tf_op jit(solution)/shard_map/ppermute | solution.py:342
  22.4 10.4 %collective-permute-start.1 = (f32[4,128,128]{2,1,0:T(8,128)S(1)}, f32[4,128,128]{2,1,0:T(8,128)S(1)}, u32[]{:S(2)}, u32[]{:S(2)}) collective-permute-start(f32[4,128,128]{2,1,0:T(8,128)S(1)} %add.85), channel_id=1, source_target_pairs={{0,2},{1,3},{2,0},{3,1},{4,6},{5,7},{6,4},{7,5},{8,10},{9,11},{10,... | collective-permute-start | bytes 786440 | tf_op jit(solution)/shard_map/ppermute | solution.py:334
  32.8 15.1 %collective-permute-start.2 = (f32[4,128,128]{2,1,0:T(8,128)S(1)}, f32[4,128,128]{2,1,0:T(8,128)S(1)}, u32[]{:S(2)}, u32[]{:S(2)}) collective-permute-start(f32[4,128,128]{2,1,0:T(8,128)S(1)} %add.86), channel_id=1, source_target_pairs={{0,4},{1,5},{2,6},{3,7},{4,0},{5,1},{6,2},{7,3},{8,12},{9,13},{10,... | collective-permute-start | bytes 786440 | tf_op jit(solution)/shard_map/ppermute | solution.py:334
  76.7 8.3 %collective-permute-start.4 = (bf16[8,3,768,128]{3,2,1,0:T(8,128)(2,1)}, bf16[8,3,768,128]{3,2,1,0:T(8,128)(2,1)}, u32[]{:S(2)}, u32[]{:S(2)}) collective-permute-start(bf16[8,3,768,128]{3,2,1,0:T(8,128)(2,1)} %all-to-all-done.same), channel_id=1, source_target_pairs={{0,16},{16,0},{1,17},{17,1},{2,18},{18,2},{3,19},{19,3},{4,20},{20... | collective-permute-start | bytes 14155784 | tf_op jit(solution)/shard_map/ppermute | solution.py:346
  94.8 144.3 %all-to-all-start.1 = ((f32[16,384,128]{2,1,0:T(8,128)}), f32[16,384,128]{2,1,0:T(8,128)S(1)}, u32[]{:S(2)}, u32[]{:S(2)}) async-start(f32[16,384,128]{2,1,0:T(8,128)} %get-tuple-element.20), calls=%async_computation.1 | async-start | bytes 6291456 | tf_op jit(solution)/shard_map/all_to_all | solution.py:356
  103.0 24.4 %collective-permute-start.5 = (bf16[3,384,128]{2,1,0:T(8,128)(2,1)S(1)}, bf16[3,384,128]{2,1,0:T(8,128)(2,1)}, u32[]{:S(2)}, u32[]{:S(2)}) collective-permute-start(bf16[3,384,128]{2,1,0:T(8,128)(2,1)S(1)} %slice_add_fusion), channel_id=1, source_target_pairs={{0,32},{1,33},{2,34},{3,35},{4,36},{5,37},{6,38},{7,39},{8,40},{9,... | collective-permute-start | bytes 884744 | tf_op jit(solution)/shard_map/ppermute | solution.py:315
  108.4 25.6 %collective-permute-start.10 = (f32[4,128,128]{2,1,0:T(8,128)}, f32[4,128,128]{2,1,0:T(8,128)}, u32[]{:S(2)}, u32[]{:S(2)}) collective-permute-start(f32[4,128,128]{2,1,0:T(8,128)} %add.87), channel_id=1, source_target_pairs={{0,8},{8,0},{1,9},{9,1},{2,10},{10,2},{3,11},{11,3},{4,12},{12,4},... | collective-permute-start | bytes 786440 | tf_op jit(solution)/shard_map/ppermute | solution.py:347
  128.4 12.3 %collective-permute-start.7 = (bf16[3,384,128]{2,1,0:T(8,128)(2,1)S(1)}, bf16[3,384,128]{2,1,0:T(8,128)(2,1)S(1)}, u32[]{:S(2)}, u32[]{:S(2)}) collective-permute-start(bf16[3,384,128]{2,1,0:T(8,128)(2,1)S(1)} %add.89), channel_id=1, source_target_pairs={{0,192},{1,193},{2,194},{3,195},{4,196},{5,197},{6,198},{7,199},{8... | collective-permute-start | bytes 884744 | tf_op jit(solution)/shard_map/ppermute | solution.py:316
  129.1 12.2 %collective-permute-start.6 = (bf16[3,384,128]{2,1,0:T(8,128)(2,1)S(1)}, bf16[3,384,128]{2,1,0:T(8,128)(2,1)S(1)}, u32[]{:S(2)}, u32[]{:S(2)}) collective-permute-start(bf16[3,384,128]{2,1,0:T(8,128)(2,1)S(1)} %add.89), channel_id=1, source_target_pairs={{0,64},{1,65},{2,66},{3,67},{4,68},{5,69},{6,70},{7,71},{8,72},{9,... | collective-permute-start | bytes 884744 | tf_op jit(solution)/shard_map/ppermute | solution.py:316
  135.8 2.4 collective-permute-start.11
  138.3 22.7 %collective-permute-start.12 = (f32[4,128,128]{2,1,0:T(8,128)S(1)}, f32[4,128,128]{2,1,0:T(8,128)S(1)}, u32[]{:S(2)}, u32[]{:S(2)}) collective-permute-start(f32[4,128,128]{2,1,0:T(8,128)S(1)} %add.96), channel_id=1, source_target_pairs={{0,32},{1,33},{2,34},{3,35},{4,36},{5,37},{6,38},{7,39},{8,40},{9,... | collective-permute-start | bytes 786440 | tf_op jit(solution)/shard_map/ppermute | solution.py:315
  141.4 23.6 %collective-permute-start.8 = (bf16[3,384,128]{2,1,0:T(8,128)(2,1)S(1)}, bf16[3,384,128]{2,1,0:T(8,128)(2,1)S(1)}, u32[]{:S(2)}, u32[]{:S(2)}) collective-permute-start(bf16[3,384,128]{2,1,0:T(8,128)(2,1)S(1)} %add_add_fusion), channel_id=1, source_target_pairs={{64,128},{65,129},{66,130},{67,131},{68,132},{69,133},{70,134},{71... | collective-permute-start | bytes 884744 | tf_op jit(solution)/shard_map/ppermute | solution.py:317
  161.7 3.5 collective-permute-start.14
  163.1 13.7 %collective-permute-start.13 = (f32[4,128,128]{2,1,0:T(8,128)}, f32[4,128,128]{2,1,0:T(8,128)}, u32[]{:S(2)}, u32[]{:S(2)}) collective-permute-start(f32[4,128,128]{2,1,0:T(8,128)} %add.97), channel_id=1, source_target_pairs={{0,64},{1,65},{2,66},{3,67},{4,68},{5,69},{6,70},{7,71},{8,72},{9,... | collective-permute-start | bytes 786440 | tf_op jit(solution)/shard_map/ppermute | solution.py:316
  165.1 14.4 %collective-permute-start.9 = (bf16[3,384,128]{2,1,0:T(8,128)(2,1)S(1)}, bf16[3,384,128]{2,1,0:T(8,128)(2,1)}, u32[]{:S(2)}, u32[]{:S(2)}) collective-permute-start(bf16[3,384,128]{2,1,0:T(8,128)(2,1)S(1)} %add.92), channel_id=1, source_target_pairs={{0,16},{16,0},{1,17},{17,1},{2,18},{18,2},{3,19},{19,3},{4,20},{20... | collective-permute-start | bytes 884744 | tf_op jit(solution)/shard_map/ppermute | solution.py:359
  178.0 6.4 %collective-permute-start.15 = (f32[4,128,128]{2,1,0:T(8,128)S(1)}, f32[4,128,128]{2,1,0:T(8,128)S(1)}, u32[]{:S(2)}, u32[]{:S(2)}) collective-permute-start(f32[4,128,128]{2,1,0:T(8,128)S(1)} %add_add_fusion.1), channel_id=1, source_target_pairs={{64,128},{65,129},{66,130},{67,131},{68,132},{69,133},{70,134},{71... | collective-permute-start | bytes 786440 | tf_op jit(solution)/shard_map/ppermute | solution.py:317
  180.5 54.2 %copy-start.8 = (pred[128,128]{1,0:T(8,128)(4,1)S(1)}, pred[128,128]{1,0:T(8,128)(4,1)}, u32[]{:S(2)}) copy-start(pred[128,128]{1,0:T(8,128)(4,1)} %iota_compare_fusion) | copy-start | bytes 49156
  234.7 0.7 copy-start.5
  236.6 47.6 %copy-start.4 = (f32[4,128,128]{2,1,0:T(8,128)}, f32[4,128,128]{2,1,0:T(8,128)S(1)}, u32[]{:S(2)}) copy-start(f32[4,128,128]{2,1,0:T(8,128)S(1)} %select_select_fusion.chol) | copy-start | bytes 786436
  236.6 9.3 %copy-start.9 = (s32[96,16]{0,1:T(8,128)S(1)}, s32[96,16]{0,1:T(8,128)}, u32[]{:S(2)}) copy-start(s32[96,16]{0,1:T(8,128)} %param.6) | copy-start | bytes 18436
  239.1 22.8 %copy-start.2 = (f32[16,384,128]{2,1,0:T(8,128)}, f32[16,384,128]{2,1,0:T(8,128)S(1)}, u32[]{:S(2)}) copy-start(f32[16,384,128]{2,1,0:T(8,128)S(1)} %all-to-all-done.1.slots) | copy-start | bytes 9437188
  239.1 17.2 %all-to-all-start.2 = ((f32[16,48,128]{2,1,0:T(8,128)}), f32[16,48,128]{2,1,0:T(8,128)}, u32[]{:S(2)}, u32[]{:S(2)}) async-start(f32[16,48,128]{2,1,0:T(8,128)} %panel_slots.1), calls=%async_computation.2 | async-start | bytes 786432 | tf_op jit(solution)/shard_map/all_to_all | solution.py:367
  261.8 103.5 %all-to-all-start.3 = ((f32[16,4,4,8,128]{4,3,2,1,0:T(8,128)}), f32[16,4,4,8,128]{4,3,2,1,0:T(8,128)}, u32[]{:S(2)}, u32[]{:S(2)}) async-start(f32[16,4,4,8,128]{4,3,2,1,0:T(8,128)} %broadcast_in_dim.83), calls=%async_computation.3 | async-start | bytes 2097152 | tf_op jit(solution)/shard_map/all_to_all | solution.py:377
  267.5 11.5 %copy-start.7 = (f32[4,4,8,128]{3,2,1,0:T(8,128)S(1)}, f32[4,4,8,128]{3,2,1,0:T(8,128)}, u32[]{:S(2)}) copy-start(f32[4,4,8,128]{3,2,1,0:T(8,128)} %place_strip.1) | copy-start | bytes 196612
  272.9 124.6 %collective-permute-start.17 = (f32[4,4,128,128]{3,2,1,0:T(8,128)}, f32[4,4,128,128]{3,2,1,0:T(8,128)S(1)}, u32[]{:S(2)}, u32[]{:S(2)}) collective-permute-start(f32[4,4,128,128]{3,2,1,0:T(8,128)} %place_tiles.1.part), channel_id=1, source_target_pairs={{0,0},{1,16},{2,32},{3,48},{4,64},{5,80},{6,96},{7,112},{8,128},{9... | collective-permute-start | bytes 3145736 | tf_op jit(solution)/shard_map/ppermute | solution.py:369
  279.0 86.3 %collective-permute-start.16 = (f32[4,4,8,128]{3,2,1,0:T(8,128)S(1)}, f32[4,4,8,128]{3,2,1,0:T(8,128)S(1)}, u32[]{:S(2)}, u32[]{:S(2)}) collective-permute-start(f32[4,4,8,128]{3,2,1,0:T(8,128)S(1)} %copy-done.7), channel_id=1, source_target_pairs={{0,0},{1,16},{2,32},{3,48},{4,64},{5,80},{6,96},{7,112},{8,128},{9... | collective-permute-start | bytes 196616 | tf_op jit(solution)/shard_map/ppermute | solution.py:376
  366.4 20.4 %all-to-all-start.4 = ((f32[16,4,4,8,128]{4,3,2,1,0:T(8,128)}), f32[16,4,4,8,128]{4,3,2,1,0:T(8,128)S(1)}, u32[]{:S(2)}, u32[]{:S(2)}) async-start(f32[16,4,4,8,128]{4,3,2,1,0:T(8,128)} %broadcast_in_dim.84), calls=%async_computation.4 | async-start | bytes 2097152 | tf_op jit(solution)/shard_map/all_to_all | solution.py:379
  386.8 1.0 copy-start.3
  397.5 1.0 copy-start.6

commit v5 on v4

--- a/solution.py
+++ b/solution.py
@@ -14,7 +14,6 @@
 HALF = 3
 SLICE = 8
 ROWS = HALF * BLK
-PLACE = 4
 
 AXES = ("x", "yh", "core", "yl", "z")
 SIZES = (4, 2, 2, 2, 8)
@@ -24,6 +23,57 @@
 CONTRACT_INNER = (((1,), (0,)), ((), ()))
 CONTRACT_ROWS = (((0,), (0,)), ((), ()))
 CONTRACT_COLS = (((1,), (1,)), ((), ()))
+
+
+LOCAL = pl.BlockSpec(memory_space=pltpu.VMEM)
+
+
+def factor_kernel(corner, chol, inverse, work):
+    row = lax.broadcasted_iota(jnp.int32, (BLK, BLK), 0)
+    lane = lax.broadcasted_iota(jnp.int32, (BLK, BLK), 1)
+    strip_row = lax.broadcasted_iota(jnp.int32, (8, 1), 0)
+    for b in range(SPAN):
+        work[b, :, :BLK] = corner[b]
+        work[b, :, BLK:] = jnp.where(row == lane, 1.0, 0.0)
+    for t in range(BLK // 8):
+        top = 8 * t
+        for b in range(SPAN):
+            panel = work[b, top : top + 8, :]
+            scale = jnp.ones((8, 1), jnp.float32)
+            for s in range(8):
+                column = panel[:, top + s : top + s + 1]
+                pivot = 1.0 / column[s : s + 1, :]
+                scale = jnp.where(strip_row == s, pivot, scale)
+                factor = jnp.where(strip_row > s, column * pivot, 0.0)
+                panel = panel - factor * panel[s : s + 1, :]
+            work[b, top : top + 8, :] = panel
+            if t < BLK // 8 - 1:
+                change = lax.dot_general(
+                    panel[:, :BLK] * scale,
+                    panel,
+                    CONTRACT_ROWS,
+                    precision=HIGH,
+                    preferred_element_type=jnp.float32,
+                )
+                work[b, top + 8 :, :] = work[b, top + 8 :, :] - change[top + 8 :, :]
+    for b in range(SPAN):
+        upper = work[b, :, :BLK]
+        pivots = jnp.sum(jnp.where(row == lane, upper, 0.0), axis=1, keepdims=True)
+        root = 1.0 / jnp.sqrt(pivots)
+        chol[b] = jnp.where(lane >= row, upper * root, 0.0).T
+        inverse[b] = work[b, :, BLK:] * root
+
+
+def factor(corner):
+    shape = (SPAN, BLK, BLK)
+    return pl.pallas_call(
+        factor_kernel,
+        in_specs=[LOCAL],
+        out_specs=[LOCAL] * 2,
+        out_shape=[jax.ShapeDtypeStruct(shape, jnp.float32)] * 2,
+        scratch_shapes=[pltpu.VMEM((SPAN, BLK, 2 * BLK), jnp.float32)],
+        name="factor",
+    )(corner)
 
 
 def flip_kernel(scaled, out):
@@ -118,35 +168,15 @@
 
 
 def place_kernel(meta, picks, slots, part):
-    g = pl.program_id(0)
     i = meta[2]
     j = meta[3]
-
-    @pl.when(g == 0)
-    def _():
-        part[...] = jnp.zeros_like(part)
-
-    for u in range(PLACE):
-        base = (g * PLACE + u) * GROUP + jnp.where(i < j, 0, HALF)
+    part[...] = jnp.zeros_like(part)
+    for g in range(NWIN):
+        base = g * GROUP + jnp.where(i < j, 0, HALF)
         for k in range(HALF):
             a = picks[base + k, i]
             b = picks[base + k, j]
-            part[a, b] += slots[u, k * BLK : (k + 1) * BLK, :]
-
-
-def place(meta, picks, slots):
-    grid_spec = pltpu.PrefetchScalarGridSpec(
-        num_scalar_prefetch=2,
-        grid=(NWIN // PLACE,),
-        in_specs=[pl.BlockSpec((PLACE, ROWS, BLK), lambda g, *_: (g, 0, 0))],
-        out_specs=pl.BlockSpec((SPAN, SPAN, BLK, BLK), lambda g, *_: (0, 0, 0, 0)),
-    )
-    return pl.pallas_call(
-        place_kernel,
-        grid_spec=grid_spec,
-        out_shape=jax.ShapeDtypeStruct((SPAN, SPAN, BLK, BLK), jnp.float32),
-        name="place_tiles",
-    )(meta, picks, slots)
+            part[a, b] += slots[g, k * BLK : (k + 1) * BLK, :]
 
 
 def strip_kernel(meta, picks, slots, strip):
@@ -159,59 +189,42 @@
             strip[b, a] += slots[g, m * SLICE : (m + 1) * SLICE, :]
 
 
-def place_strip(meta, picks, slots):
-    shape = (SPAN, SPAN, SLICE, BLK)
+def place(kernel, meta, picks, slots, shape):
     grid_spec = pltpu.PrefetchScalarGridSpec(
-        num_scalar_prefetch=2,
-        grid=(1,),
-        in_specs=[pl.BlockSpec(slots.shape, lambda t, *_: (0, 0, 0))],
-        out_specs=pl.BlockSpec(shape, lambda t, *_: (0, 0, 0, 0)),
-    )
-    return pl.pallas_call(
-        strip_kernel,
-        grid_spec=grid_spec,
-        out_shape=jax.ShapeDtypeStruct(shape, jnp.float32),
-        name="place_strip",
+        num_scalar_prefetch=2, grid=(1,), in_specs=[LOCAL], out_specs=LOCAL
+    )
+    return pl.pallas_call(
+        kernel, grid_spec=grid_spec, out_shape=jax.ShapeDtypeStruct(shape, jnp.float32)
     )(meta, picks, slots)
 
 
-def solve_block(ref, inverse, a):
-    solved = [
-        lax.dot_general(
-            ref[:, b, a].reshape(BLK, BLK),
-            inverse[b],
-            CONTRACT_COLS,
-            precision=HIGH,
-            preferred_element_type=jnp.float32,
-        )
-        for b in range(SPAN)
-    ]
-    return jnp.concatenate(solved, axis=1)
-
-
-def full_spec(shape):
-    zeros = (0,) * len(shape)
-    return pl.BlockSpec(shape, lambda *_: zeros)
-
-
-def solve_kernel(left, inverse, out):
-    for a in range(SPAN):
-        out[a] = solve_block(left, inverse, a)
+def solve_part(ref, inverse, b):
+    rows = jnp.concatenate([ref[:, b, a].reshape(BLK, BLK) for a in range(SPAN)], axis=0)
+    solved = lax.dot_general(
+        rows, inverse[b], CONTRACT_COLS, precision=HIGH, preferred_element_type=jnp.float32
+    )
+    high = solved.astype(jnp.bfloat16)
+    return solved, high, (solved - high.astype(jnp.float32)).astype(jnp.bfloat16)
+
+
+def solve_kernel(left, inverse, out, high, low):
+    for b in range(SPAN):
+        cols = slice(b * BLK, (b + 1) * BLK)
+        out[:, cols], high[:, cols], low[:, cols] = solve_part(left, inverse, b)
 
 
 def solve_rows(left, inverse):
-    shape = (SPAN, BLK, SPAN * BLK)
+    size = (SPAN * BLK, SPAN * BLK)
     return pl.pallas_call(
         solve_kernel,
-        grid=(1,),
-        in_specs=[full_spec(left.shape), full_spec(inverse.shape)],
-        out_specs=full_spec(shape),
-        out_shape=jax.ShapeDtypeStruct(shape, jnp.float32),
+        in_specs=[LOCAL] * 2,
+        out_specs=[LOCAL] * 3,
+        out_shape=[jax.ShapeDtypeStruct(size, t) for t in (jnp.float32, jnp.bfloat16, jnp.bfloat16)],
         name="solve_rows",
     )(left, inverse)
 
 
-def update_kernel(meta, part, lefts, right, diag, chol, inverse, out):
+def update_kernel(meta, part, lefts, high, low, right, diag, chol, inverse, out):
     i = meta[2]
     j = meta[3]
     inside = (i > 0) & (j > 0)
@@ -236,16 +249,15 @@
 
     @pl.when(inside)
     def _():
-        for b in range(SPAN):
-            rights = solve_block(right, inverse, b)
-            for a in range(SPAN):
-                out[spot(a, b)] = out[spot(a, b)] - lax.dot_general(
-                    lefts[a],
-                    rights,
-                    CONTRACT_COLS,
-                    precision=HIGH,
-                    preferred_element_type=jnp.float32,
-                )
+        parts = [solve_part(right, inverse, b) for b in range(SPAN)]
+        other_high = jnp.concatenate([p[1] for p in parts], axis=1)
+        other_low = jnp.concatenate([p[2] for p in parts], axis=1)
+
+        def times(x, y):
+            return lax.dot_general(x, y, CONTRACT_COLS, preferred_element_type=jnp.float32)
+
+        small = times(low[...], other_high) + times(high[...], other_low)
+        out[...] = out[...] - (times(high[...], other_high) + small)
 
     @pl.when((i == 0) & (j == 0))
     def _():
@@ -254,24 +266,20 @@
 
     @pl.when((i > 0) & (j == 0))
     def _():
-        for a in range(SPAN):
-            out[a * BLK : (a + 1) * BLK, :] = lefts[a]
-
-
-def update(meta, part, lefts, right, diag, chol, inverse):
+        out[...] = lefts[...]
+
+
+def update(meta, *operands):
     size = (SPAN * BLK, SPAN * BLK)
     grid_spec = pltpu.PrefetchScalarGridSpec(
-        num_scalar_prefetch=1,
-        grid=(1,),
-        in_specs=[full_spec(v.shape) for v in (part, lefts, right, diag, chol, inverse)],
-        out_specs=full_spec(size),
+        num_scalar_prefetch=1, grid=(1,), in_specs=[LOCAL] * len(operands), out_specs=LOCAL
     )
     return pl.pallas_call(
         update_kernel,
         grid_spec=grid_spec,
         out_shape=jax.ShapeDtypeStruct(size, jnp.float32),
         name="update",
-    )(meta, part, lefts, right, diag, chol, inverse)
+    )(meta, *operands)
 
 
 def finish_kernel(meta, base, mirror, out):
@@ -354,31 +362,26 @@
     tiles, late = gram_slots(meta, flipped, same, other)
 
     tiles = lax.all_to_all(tiles, GC, 0, 0, tiled=True)
-    chol = jnp.linalg.cholesky(spread(corner, "x"))
+    chol, inverse = factor(spread(corner, "x"))
     piece = spread(piece, "x")
     twin = lax.ppermute(piece, "core", [(0, 1), (1, 0)])
     lead = jnp.concatenate(
         [jnp.where(core == 0, piece, twin), jnp.where(core == 0, twin, piece)], axis=1
     )
     slices = panel_slots(scaled, lead, late)
-    tiles, slices, chol = lax.optimization_barrier((tiles, slices, chol))
-
-    part = place(meta, block_pick, tiles)
+    tiles, slices, chol, inverse = lax.optimization_barrier((tiles, slices, chol, inverse))
+
+    part = place(place_kernel, meta, block_pick, tiles, (SPAN, SPAN, BLK, BLK))
     slices = lax.all_to_all(slices, GC, 0, 0, tiled=True)
     everywhere = [(r * NWIN + c, c * NWIN + r) for r in range(NWIN) for c in range(NWIN)]
     mirror = lax.ppermute(part, AXES, everywhere)
-    slices, chol = lax.optimization_barrier((slices, chol))
-    inverse = lax.linalg.triangular_solve(
-        chol, jnp.broadcast_to(eye, chol.shape), left_side=True, lower=True
-    )
-    strip = place_strip(meta, block_pick, slices)
+    strip = place(strip_kernel, meta, block_pick, slices, (SPAN, SPAN, SLICE, BLK))
     copies = (NWIN,) + strip.shape
     turned = lax.ppermute(strip, AXES, everywhere)
     left = lax.all_to_all(jnp.broadcast_to(strip, copies), GC, 0, 0, tiled=True)
-    turned, inverse = lax.optimization_barrier((turned, inverse))
     right = lax.all_to_all(jnp.broadcast_to(turned, copies), GR, 0, 0, tiled=True)
-    lefts = solve_rows(left, inverse)
-    base = update(meta, part, lefts, right, diag, chol, inverse)
+    lefts, high, low = solve_rows(left, inverse)
+    base = update(meta, part, lefts, high, low, right, diag, chol, inverse)
     return finish(meta, base, mirror)
 
 

time: 410 us -> 361 us (0.88)
  other arithmetic: 104 us -> 13.9 us
  waiting for transfers between devices: 172 us -> 201 us
  Pallas kernels: 44.6 us -> 60.4 us
    another operation x6 -> x0, other arithmetic: 87.8 us -> none  [the longest x4 48.5 us: body(): chol = jnp.linalg.cholesky(spread(corner, 'x'))]
    ppermute x1, waiting for transfers between devices: 40.5 us -> 60.3 us  [body(): turned = lax.ppermute(strip, AXES, everywhere)]
    pallas_call x3 -> x4, Pallas kernels: 13.5 us -> 33.1 us  [the longest x1 21 us: factor(): pl.pallas_call(factor_kernel, in_specs=[LOCAL], out_specs=[LOCAL] * 2, ou...]
    all_to_all x1, waiting for transfers between devices: 11.3 us -> 19.8 us  [body(): lax.all_to_all(jnp.broadcast_to(turned, copies), GR, 0, 0, tiled=True)]
  transfers between devices with their start and end apart: 23 -> 23, of which waited for: 15 -> 15; matrix products, arithmetic and copies ran while one was open for 26% -> 3% of each run, Pallas kernels for 7% -> 12%
where the time goes in v5:
time: 361 us; the launch traced here: 355 us
  waiting for transfers between devices  201 us (56%)
  starting transfers between devices  72 us (20%)
  Pallas kernels  60.4 us (17%)
  other arithmetic  13.9 us (4%)
  local copies, waits for them, and re-layouts  6.77 us (2%)
    ppermute x1, waiting for transfers between devices, body(): turned = lax.ppermute(strip, AXES, everywhere)  60.3 us
    ppermute x3, waiting for transfers between devices, spread(): return v + lax.ppermute(v, step, [(0, 1)])  36.9 us
    all_to_all x1, waiting for transfers between devices, body(): same = lax.all_to_all(slots, ('x', 'yh'), 0, 0, tiled=True)  28.7 us
    pallas_call x1, Pallas kernels, factor(): pl.pallas_call(factor_kernel, in_specs=[LOCAL], out_specs=[LOCAL] * 2, ou...  21 us
    all_to_all x1, waiting for transfers between devices, body(): lax.all_to_all(jnp.broadcast_to(turned, copies), GR, 0, 0, tiled=True)  19.8 us
    ppermute x3, waiting for transfers between devices, body(): diag = diag + lax.ppermute(diag, 'z', swap_pairs(8, bit))  18.8 us
    ppermute x4, waiting for transfers between devices, spread(): v = v + lax.ppermute(v, 'x', [(0, 1)]) + lax.ppermute(v, 'x', [(0, 3)])  12.9 us
    pallas_call x1, Pallas kernels, gram_slots(): pl.pallas_call(gram_kernel, grid_spec=grid_spec, out_shape=[jax.ShapeDtyp...  9.8 us
  transfers between devices with their start and end apart: 23, of which 15 were waited for; matrix products, arithmetic and copies ran while one was open for 3% of the time, Pallas kernels for 12%

profile of v5, /device:TPU:66, one launch (start us, length us, event | category | flops | bytes accessed | tf_op | source)
XLA Modules:
  0.0 355.3 jit_solution(3748849525282827782)
XLA Ops:
  0.0 0.8 sqrt.3
  0.8 1.9 multiply_convert_fusion.scaled.first
  2.7 0.1 broadcast_select_fusion.1
  2.8 2.8 broadcast_select_fusion
  5.6 7.6 %all-to-all-start = ((bf16[8,3,768,128]{3,2,1,0:T(8,128)(2,1)}), bf16[8,3,768,128]{3,2,1,0:T(8,128)(2,1)}, u32[]{:S(2)}, u32[]{:S(2)}) async-start(bf16[8,3,768,128]{3,2,1,0:T(8,128)(2,1)} %broadcast_select_fusion), calls=%async_computation | async-start | bytes 9437184 | tf_op jit(solution)/shard_map/all_to_all | solution.py:347
  13.3 0.5 fusion.1
  13.8 0.2 select_reduce_fusion
  14.0 2.0 collective-permute-start
  16.0 1.3 collective-permute-start.3
  17.4 4.4 %collective-permute-done = f32[4,128,128]{2,1,0:T(8,128)S(1)} collective-permute-done((f32[4,128,128]{2,1,0:T(8,128)S(1)}, f32[4,128,128]{2,1,0:T(8,128)S(1)}, u32[]{:S(2)}, u32[]{:S(2)}) %collective-permute-start) | collective-permute-done | bytes 262176 | tf_op jit(solution)/shard_map/ppermute | solution.py:342
  21.9 10.3 %collective-permute-done.1 = f32[4,128,128]{2,1,0:T(8,128)S(1)} collective-permute-done((f32[4,128,128]{2,1,0:T(8,128)S(1)}, f32[4,128,128]{2,1,0:T(8,128)S(1)}, u32[]{:S(2)}, u32[]{:S(2)}) %collective-permute-start.1) | collective-permute-done | bytes 262176 | tf_op jit(solution)/shard_map/ppermute | solution.py:342
  32.3 6.3 %collective-permute-start.2 = (f32[4,128,128]{2,1,0:T(8,128)S(1)}, f32[4,128,128]{2,1,0:T(8,128)S(1)}, u32[]{:S(2)}, u32[]{:S(2)}) collective-permute-start(f32[4,128,128]{2,1,0:T(8,128)S(1)} %add.75), channel_id=1, source_target_pairs={{0,4},{1,5},{2,6},{3,7},{4,0},{5,1},{6,2},{7,3},{8,12},{9,13},{10,... | collective-permute-start | bytes 786440 | tf_op jit(solution)/shard_map/ppermute | solution.py:342
  38.6 4.6 %flip.1.mine = bf16[6,128,768]{2,1,0:T(8,128)(2,1)} custom-call(bf16[6,768,128]{2,1,0:T(8,128)(2,1)} %copy-done.1), custom_call_target="tpu_custom_call" | custom-call | tf_op jit(solution)/shard_map/flip/pallas_call | solution.py:84
  43.3 4.1 %collective-permute-done.2 = f32[4,128,128]{2,1,0:T(8,128)S(1)} collective-permute-done((f32[4,128,128]{2,1,0:T(8,128)S(1)}, f32[4,128,128]{2,1,0:T(8,128)S(1)}, u32[]{:S(2)}, u32[]{:S(2)}) %collective-permute-start.2) | collective-permute-done | bytes 262176 | tf_op jit(solution)/shard_map/ppermute | solution.py:342
  47.4 0.7 add.76
  48.1 28.7 %all-to-all-done.same = bf16[8,3,768,128]{3,2,1,0:T(8,128)(2,1)} async-done(((bf16[8,3,768,128]{3,2,1,0:T(8,128)(2,1)}), bf16[8,3,768,128]{3,2,1,0:T(8,128)(2,1)}, u32[]{:S(2)}, u32[]{:S(2)}) %all-to-all-start) | async-done | bytes 4718624 | tf_op jit(solution)/shard_map/all_to_all | solution.py:347
  76.8 0.6 pad_add_fusion.meta
  77.4 7.7 %collective-permute-done.4.other = bf16[8,3,768,128]{3,2,1,0:T(8,128)(2,1)} collective-permute-done((bf16[8,3,768,128]{3,2,1,0:T(8,128)(2,1)}, bf16[8,3,768,128]{3,2,1,0:T(8,128)(2,1)}, u32[]{:S(2)}, u32[]{:S(2)}) %collective-permute-start.4) | collective-permute-done | bytes 4718624 | tf_op jit(solution)/shard_map/ppermute | solution.py:354
  85.1 9.8 %gram_slots.1 = (f32[16,384,128]{2,1,0:T(8,128)}, f32[3,128,128]{2,1,0:T(8,128)}) custom-call(s32[4]{0:T(128)} %pad_add_fusion.meta, bf16[6,128,768]{2,1,0:T(8,128)(2,1)} %flip.1.mine, bf16[8,3,768,128]{3,2,1,0:T(8,128)(2,1)} %all-to-all-done.same, bf16[8,3,768,128]{3,2,1,0:T(8,128)(2,1)} %collective-permute-done.4.other), custom_call_target="tpu_custom_call" | custom-call | tf_op jit(solution)/shard_map/gram_slots/pallas_call | solution.py:130
  94.9 8.2 %all-to-all-start.1 = ((f32[16,384,128]{2,1,0:T(8,128)}), f32[16,384,128]{2,1,0:T(8,128)S(1)}, u32[]{:S(2)}, u32[]{:S(2)}) async-start(f32[16,384,128]{2,1,0:T(8,128)} %get-tuple-element.22), calls=%async_computation.1 | async-start | bytes 6291456 | tf_op jit(solution)/shard_map/all_to_all | solution.py:364
  103.1 5.4 %collective-permute-start.5 = (bf16[3,384,128]{2,1,0:T(8,128)(2,1)S(1)}, bf16[3,384,128]{2,1,0:T(8,128)(2,1)}, u32[]{:S(2)}, u32[]{:S(2)}) collective-permute-start(bf16[3,384,128]{2,1,0:T(8,128)(2,1)S(1)} %slice_add_fusion), channel_id=1, source_target_pairs={{0,32},{1,33},{2,34},{3,35},{4,36},{5,37},{6,38},{7,39},{8,40},{9,... | collective-permute-start | bytes 884744 | tf_op jit(solution)/shard_map/ppermute | solution.py:323
  108.5 0.9 collective-permute-start.10
  109.5 18.0 %collective-permute-done.5 = bf16[3,384,128]{2,1,0:T(8,128)(2,1)} collective-permute-done((bf16[3,384,128]{2,1,0:T(8,128)(2,1)S(1)}, bf16[3,384,128]{2,1,0:T(8,128)(2,1)}, u32[]{:S(2)}, u32[]{:S(2)}) %collective-permute-start.5) | collective-permute-done | bytes 294944 | tf_op jit(solution)/shard_map/ppermute | solution.py:323
  127.5 1.0 add.78
  128.5 0.7 collective-permute-start.7
  129.2 1.3 collective-permute-start.6
  130.5 3.6 %collective-permute-done.10 = f32[4,128,128]{2,1,0:T(8,128)} collective-permute-done((f32[4,128,128]{2,1,0:T(8,128)}, f32[4,128,128]{2,1,0:T(8,128)}, u32[]{:S(2)}, u32[]{:S(2)}) %collective-permute-start.10) | collective-permute-done | bytes 262176 | tf_op jit(solution)/shard_map/ppermute | solution.py:355
  134.1 1.8 broadcast_select_fusion.4
  135.9 1.3 collective-permute-start.11
  137.2 1.1 collective-permute-done.11
  138.4 2.4 collective-permute-start.12
  140.8 0.7 collective-permute-done.6
  141.5 1.8 collective-permute-start.8
  143.3 17.8 %collective-permute-done.12 = f32[4,128,128]{2,1,0:T(8,128)S(1)} collective-permute-done((f32[4,128,128]{2,1,0:T(8,128)S(1)}, f32[4,128,128]{2,1,0:T(8,128)S(1)}, u32[]{:S(2)}, u32[]{:S(2)}) %collective-permute-start.12) | collective-permute-done | bytes 262176 | tf_op jit(solution)/shard_map/ppermute | solution.py:323
  161.1 0.7 add.86
  161.8 1.3 collective-permute-start.14
  163.2 1.3 collective-permute-start.13
  164.7 12.2 %collective-permute-done.13 = f32[4,128,128]{2,1,0:T(8,128)} collective-permute-done((f32[4,128,128]{2,1,0:T(8,128)}, f32[4,128,128]{2,1,0:T(8,128)}, u32[]{:S(2)}, u32[]{:S(2)}) %collective-permute-start.13) | collective-permute-done | bytes 262176 | tf_op jit(solution)/shard_map/ppermute | solution.py:324
  176.9 1.1 add_add_fusion.1
  178.0 1.5 collective-permute-start.15
  179.5 1.0 broadcast_select_fusion.3
  180.6 0.9 pad_maximum_fusion.lead
  181.4 3.0 collective-permute-done.15
  184.5 0.8 add.89.corner
  185.2 21.0 %factor.1 = (f32[4,128,128]{2,1,0:T(8,128)}, f32[4,128,128]{2,1,0:T(8,128)}) custom-call(f32[4,128,128]{2,1,0:T(8,128)} %add.89.corner), custom_call_target="tpu_custom_call" | custom-call | tf_op jit(solution)/shard_map/factor/pallas_call | solution.py:69
  206.2 2.4 panel_slots.1
  208.6 6.9 %all-to-all-start.2 = ((f32[16,48,128]{2,1,0:T(8,128)}), f32[16,48,128]{2,1,0:T(8,128)}, u32[]{:S(2)}, u32[]{:S(2)}) async-start(f32[16,48,128]{2,1,0:T(8,128)} %panel_slots.1), calls=%async_computation.2 | async-start | bytes 786432 | tf_op jit(solution)/shard_map/all_to_all | solution.py:375
  215.5 0.7 copy.9.picks
  216.2 9.6 %all-to-all-done.2.slots = f32[16,48,128]{2,1,0:T(8,128)} async-done(((f32[16,48,128]{2,1,0:T(8,128)}), f32[16,48,128]{2,1,0:T(8,128)}, u32[]{:S(2)}, u32[]{:S(2)}) %all-to-all-start.2) | async-done | bytes 393248 | tf_op jit(solution)/shard_map/all_to_all | solution.py:375
  225.8 3.6 %shard_map.47 = f32[4,4,8,128]{3,2,1,0:T(8,128)} custom-call(s32[4]{0:T(128)} %pad_add_fusion.meta, s32[96,16]{1,0:T(8,128)} %copy.9.picks, f32[16,48,128]{2,1,0:T(8,128)} %all-to-all-done.2.slots), custom_call_target="tpu_custom_call" | custom-call | tf_op jit(solution)/shard_map/pallas_call | solution.py:196
  229.4 2.1 broadcast_in_dim.73
  231.5 5.9 %all-to-all-start.3 = ((f32[16,4,4,8,128]{4,3,2,1,0:T(8,128)}), f32[16,4,4,8,128]{4,3,2,1,0:T(8,128)}, u32[]{:S(2)}, u32[]{:S(2)}) async-start(f32[16,4,4,8,128]{4,3,2,1,0:T(8,128)} %broadcast_in_dim.73), calls=%async_computation.3 | async-start | bytes 2097152 | tf_op jit(solution)/shard_map/all_to_all | solution.py:381
  237.3 6.1 %collective-permute-start.16 = (f32[4,4,8,128]{3,2,1,0:T(8,128)S(1)}, f32[4,4,8,128]{3,2,1,0:T(8,128)S(1)}, u32[]{:S(2)}, u32[]{:S(2)}) collective-permute-start(f32[4,4,8,128]{3,2,1,0:T(8,128)S(1)} %copy-done.5), channel_id=1, source_target_pairs={{0,0},{1,16},{2,32},{3,48},{4,64},{5,80},{6,96},{7,112},{8,128},{9... | collective-permute-start | bytes 196616 | tf_op jit(solution)/shard_map/ppermute | solution.py:380
  243.4 4.8 %shard_map.46.part = f32[4,4,128,128]{3,2,1,0:T(8,128)} custom-call(s32[4]{0:T(128)} %pad_add_fusion.meta, s32[96,16]{1,0:T(8,128)} %copy.9.picks, f32[16,384,128]{2,1,0:T(8,128)} %copy-done.2), custom_call_target="tpu_custom_call" | custom-call | tf_op jit(solution)/shard_map/pallas_call | solution.py:196
  248.3 5.2 %collective-permute-start.17 = (f32[4,4,128,128]{3,2,1,0:T(8,128)}, f32[4,4,128,128]{3,2,1,0:T(8,128)S(1)}, u32[]{:S(2)}, u32[]{:S(2)}) collective-permute-start(f32[4,4,128,128]{3,2,1,0:T(8,128)} %shard_map.46.part), channel_id=1, source_target_pairs={{0,0},{1,16},{2,32},{3,48},{4,64},{5,80},{6,96},{7,112},{8,128},{9... | collective-permute-start | bytes 3145736 | tf_op jit(solution)/shard_map/ppermute | solution.py:377
  253.4 60.3 %collective-permute-done.16 = f32[4,4,8,128]{3,2,1,0:T(8,128)S(1)} collective-permute-done((f32[4,4,8,128]{3,2,1,0:T(8,128)S(1)}, f32[4,4,8,128]{3,2,1,0:T(8,128)S(1)}, u32[]{:S(2)}, u32[]{:S(2)}) %collective-permute-start.16) | collective-permute-done | bytes 65568 | tf_op jit(solution)/shard_map/ppermute | solution.py:380
  313.7 1.1 broadcast_in_dim.74
  314.8 4.5 %all-to-all-start.4 = ((f32[16,4,4,8,128]{4,3,2,1,0:T(8,128)}), f32[16,4,4,8,128]{4,3,2,1,0:T(8,128)S(1)}, u32[]{:S(2)}, u32[]{:S(2)}) async-start(f32[16,4,4,8,128]{4,3,2,1,0:T(8,128)} %broadcast_in_dim.74), calls=%async_computation.4 | async-start | bytes 2097152 | tf_op jit(solution)/shard_map/all_to_all | solution.py:382
  319.4 3.7 %solve_rows.1 = (f32[512,512]{1,0:T(8,128)}, bf16[512,512]{1,0:T(8,128)(2,1)}, bf16[512,512]{1,0:T(8,128)(2,1)}) custom-call(f32[16,4,4,8,128]{4,3,2,1,0:T(8,128)} %all-to-all-done.3.left, f32[4,128,128]{2,1,0:T(8,128)} %get-tuple-element.30.inverse), custom_call_target="tpu_custom_call" | custom-call | tf_op jit(solution)/shard_map/solve_rows/pallas_call | solution.py:218
  323.0 19.8 %all-to-all-done.4.right = f32[16,4,4,8,128]{4,3,2,1,0:T(8,128)S(1)} async-done(((f32[16,4,4,8,128]{4,3,2,1,0:T(8,128)}), f32[16,4,4,8,128]{4,3,2,1,0:T(8,128)S(1)}, u32[]{:S(2)}, u32[]{:S(2)}) %all-to-all-start.4) | async-done | bytes 1048608 | tf_op jit(solution)/shard_map/all_to_all | solution.py:382
  342.9 1.0 copy-done.3
  343.9 6.0 %update.1.base = f32[512,512]{1,0:T(8,128)} custom-call(s32[4]{0:T(128)} %pad_add_fusion.meta, f32[4,4,128,128]{3,2,1,0:T(8,128)} %shard_map.46.part, f32[512,512]{1,0:T(8,128)} %get-tuple-element.31.lefts, bf16[512,512]{1,0:T(8,128)(2,1)} %get-tuple-element.32.high, bf16[512,512]{1,0:T(8,128)(2,1)} %get-tuple-element.33.low, ...), custom_call_target="tpu_custom_call" | custom-call | tf_op jit(solution)/shard_map/update/pallas_call | solution.py:277
  349.8 1.0 copy-done.4
  350.8 4.4 %finish.1 = f32[512,512]{1,0:T(8,128)} custom-call(s32[4]{0:T(128)} %pad_add_fusion.meta, f32[512,512]{1,0:T(8,128)} %update.1.base, f32[4,4,128,128]{3,2,1,0:T(8,128)} %copy-done.4), custom_call_target="tpu_custom_call" | custom-call | tf_op jit(solution)/shard_map/finish/pallas_call | solution.py:309
  (35 shorter events, 0.8 us)
Async XLA Ops:
  0.0 109.4 %copy-start = (f32[8192]{0:T(1024)S(1)}, f32[8192]{0:T(1024)}, u32[]{:S(2)}) copy-start(f32[8192]{0:T(1024)} %param.7) | copy-start | bytes 98308
  2.6 10.7 %copy-start.1 = (bf16[6,768,128]{2,1,0:T(8,128)(2,1)}, bf16[6,768,128]{2,1,0:T(8,128)(2,1)S(1)}, u32[]{:S(2)}) copy-start(bf16[6,768,128]{2,1,0:T(8,128)(2,1)S(1)} %multiply_convert_fusion.scaled.first) | copy-start | bytes 3538948
  5.6 7.6 %copy-start.6 = (s32[96,16]{0,1:T(8,128)S(1)}, s32[96,16]{0,1:T(8,128)}, u32[]{:S(2)}) copy-start(s32[96,16]{0,1:T(8,128)} %param.6) | copy-start | bytes 18436
  5.6 71.3 %all-to-all-start = ((bf16[8,3,768,128]{3,2,1,0:T(8,128)(2,1)}), bf16[8,3,768,128]{3,2,1,0:T(8,128)(2,1)}, u32[]{:S(2)}, u32[]{:S(2)}) async-start(bf16[8,3,768,128]{3,2,1,0:T(8,128)(2,1)} %broadcast_select_fusion), calls=%async_computation | async-start | bytes 9437184 | tf_op jit(solution)/shard_map/all_to_all | solution.py:347
  14.0 7.7 %collective-permute-start = (f32[4,128,128]{2,1,0:T(8,128)S(1)}, f32[4,128,128]{2,1,0:T(8,128)S(1)}, u32[]{:S(2)}, u32[]{:S(2)}) collective-permute-start(f32[4,128,128]{2,1,0:T(8,128)S(1)} %select_reduce_fusion), channel_id=1, source_target_pairs={{0,1},{1,0},{2,3},{3,2},{4,5},{5,4},{6,7},{7,6},{8,9},{9,8},{10,11... | collective-permute-start | bytes 786440 | tf_op jit(solution)/shard_map/ppermute | solution.py:342
  16.0 27.2 %collective-permute-start.3 = (bf16[3,384,128]{2,1,0:T(8,128)(2,1)S(1)}, bf16[3,384,128]{2,1,0:T(8,128)(2,1)S(1)}, u32[]{:S(2)}, u32[]{:S(2)}) collective-permute-start(bf16[3,384,128]{2,1,0:T(8,128)(2,1)S(1)} %slice.20), channel_id=1, source_target_pairs={{0,16},{1,17},{2,18},{3,19},{4,20},{5,21},{6,22},{7,23},{8,24},{9,... | collective-permute-start | bytes 884744 | tf_op jit(solution)/shard_map/ppermute | solution.py:350
  21.8 10.4 %collective-permute-start.1 = (f32[4,128,128]{2,1,0:T(8,128)S(1)}, f32[4,128,128]{2,1,0:T(8,128)S(1)}, u32[]{:S(2)}, u32[]{:S(2)}) collective-permute-start(f32[4,128,128]{2,1,0:T(8,128)S(1)} %add.74), channel_id=1, source_target_pairs={{0,2},{1,3},{2,0},{3,1},{4,6},{5,7},{6,4},{7,5},{8,10},{9,11},{10,... | collective-permute-start | bytes 786440 | tf_op jit(solution)/shard_map/ppermute | solution.py:342
  32.3 15.1 %collective-permute-start.2 = (f32[4,128,128]{2,1,0:T(8,128)S(1)}, f32[4,128,128]{2,1,0:T(8,128)S(1)}, u32[]{:S(2)}, u32[]{:S(2)}) collective-permute-start(f32[4,128,128]{2,1,0:T(8,128)S(1)} %add.75), channel_id=1, source_target_pairs={{0,4},{1,5},{2,6},{3,7},{4,0},{5,1},{6,2},{7,3},{8,12},{9,13},{10,... | collective-permute-start | bytes 786440 | tf_op jit(solution)/shard_map/ppermute | solution.py:342
  76.8 8.3 %collective-permute-start.4 = (bf16[8,3,768,128]{3,2,1,0:T(8,128)(2,1)}, bf16[8,3,768,128]{3,2,1,0:T(8,128)(2,1)}, u32[]{:S(2)}, u32[]{:S(2)}) collective-permute-start(bf16[8,3,768,128]{3,2,1,0:T(8,128)(2,1)} %all-to-all-done.same), channel_id=1, source_target_pairs={{0,16},{16,0},{1,17},{17,1},{2,18},{18,2},{3,19},{19,3},{4,20},{20... | collective-permute-start | bytes 14155784 | tf_op jit(solution)/shard_map/ppermute | solution.py:354
  94.9 113.7 %all-to-all-start.1 = ((f32[16,384,128]{2,1,0:T(8,128)}), f32[16,384,128]{2,1,0:T(8,128)S(1)}, u32[]{:S(2)}, u32[]{:S(2)}) async-start(f32[16,384,128]{2,1,0:T(8,128)} %get-tuple-element.22), calls=%async_computation.1 | async-start | bytes 6291456 | tf_op jit(solution)/shard_map/all_to_all | solution.py:364
  103.1 24.4 %collective-permute-start.5 = (bf16[3,384,128]{2,1,0:T(8,128)(2,1)S(1)}, bf16[3,384,128]{2,1,0:T(8,128)(2,1)}, u32[]{:S(2)}, u32[]{:S(2)}) collective-permute-start(bf16[3,384,128]{2,1,0:T(8,128)(2,1)S(1)} %slice_add_fusion), channel_id=1, source_target_pairs={{0,32},{1,33},{2,34},{3,35},{4,36},{5,37},{6,38},{7,39},{8,40},{9,... | collective-permute-start | bytes 884744 | tf_op jit(solution)/shard_map/ppermute | solution.py:323
  108.5 25.6 %collective-permute-start.10 = (f32[4,128,128]{2,1,0:T(8,128)}, f32[4,128,128]{2,1,0:T(8,128)}, u32[]{:S(2)}, u32[]{:S(2)}) collective-permute-start(f32[4,128,128]{2,1,0:T(8,128)} %add.76), channel_id=1, source_target_pairs={{0,8},{8,0},{1,9},{9,1},{2,10},{10,2},{3,11},{11,3},{4,12},{12,4},... | collective-permute-start | bytes 786440 | tf_op jit(solution)/shard_map/ppermute | solution.py:355
  128.5 12.3 %collective-permute-start.7 = (bf16[3,384,128]{2,1,0:T(8,128)(2,1)S(1)}, bf16[3,384,128]{2,1,0:T(8,128)(2,1)S(1)}, u32[]{:S(2)}, u32[]{:S(2)}) collective-permute-start(bf16[3,384,128]{2,1,0:T(8,128)(2,1)S(1)} %add.78), channel_id=1, source_target_pairs={{0,192},{1,193},{2,194},{3,195},{4,196},{5,197},{6,198},{7,199},{8... | collective-permute-start | bytes 884744 | tf_op jit(solution)/shard_map/ppermute | solution.py:324
  129.2 12.2 %collective-permute-start.6 = (bf16[3,384,128]{2,1,0:T(8,128)(2,1)S(1)}, bf16[3,384,128]{2,1,0:T(8,128)(2,1)S(1)}, u32[]{:S(2)}, u32[]{:S(2)}) collective-permute-start(bf16[3,384,128]{2,1,0:T(8,128)(2,1)S(1)} %add.78), channel_id=1, source_target_pairs={{0,64},{1,65},{2,66},{3,67},{4,68},{5,69},{6,70},{7,71},{8,72},{9,... | collective-permute-start | bytes 884744 | tf_op jit(solution)/shard_map/ppermute | solution.py:324
  135.9 2.4 collective-permute-start.11
  138.4 22.7 %collective-permute-start.12 = (f32[4,128,128]{2,1,0:T(8,128)S(1)}, f32[4,128,128]{2,1,0:T(8,128)S(1)}, u32[]{:S(2)}, u32[]{:S(2)}) collective-permute-start(f32[4,128,128]{2,1,0:T(8,128)S(1)} %add.85), channel_id=1, source_target_pairs={{0,32},{1,33},{2,34},{3,35},{4,36},{5,37},{6,38},{7,39},{8,40},{9,... | collective-permute-start | bytes 786440 | tf_op jit(solution)/shard_map/ppermute | solution.py:323
  141.5 23.0 %collective-permute-start.8 = (bf16[3,384,128]{2,1,0:T(8,128)(2,1)S(1)}, bf16[3,384,128]{2,1,0:T(8,128)(2,1)S(1)}, u32[]{:S(2)}, u32[]{:S(2)}) collective-permute-start(bf16[3,384,128]{2,1,0:T(8,128)(2,1)S(1)} %add_add_fusion), channel_id=1, source_target_pairs={{64,128},{65,129},{66,130},{67,131},{68,132},{69,133},{70,134},{71... | collective-permute-start | bytes 884744 | tf_op jit(solution)/shard_map/ppermute | solution.py:325
  161.8 2.8 collective-permute-start.14
  163.2 13.7 %collective-permute-start.13 = (f32[4,128,128]{2,1,0:T(8,128)}, f32[4,128,128]{2,1,0:T(8,128)}, u32[]{:S(2)}, u32[]{:S(2)}) collective-permute-start(f32[4,128,128]{2,1,0:T(8,128)} %add.86), channel_id=1, source_target_pairs={{0,64},{1,65},{2,66},{3,67},{4,68},{5,69},{6,70},{7,71},{8,72},{9,... | collective-permute-start | bytes 786440 | tf_op jit(solution)/shard_map/ppermute | solution.py:324
  164.6 15.0 %collective-permute-start.9 = (bf16[3,384,128]{2,1,0:T(8,128)(2,1)S(1)}, bf16[3,384,128]{2,1,0:T(8,128)(2,1)}, u32[]{:S(2)}, u32[]{:S(2)}) collective-permute-start(bf16[3,384,128]{2,1,0:T(8,128)(2,1)S(1)} %add.81), channel_id=1, source_target_pairs={{0,16},{16,0},{1,17},{17,1},{2,18},{18,2},{3,19},{19,3},{4,20},{20... | collective-permute-start | bytes 884744 | tf_op jit(solution)/shard_map/ppermute | solution.py:367
  178.0 6.4 %collective-permute-start.15 = (f32[4,128,128]{2,1,0:T(8,128)S(1)}, f32[4,128,128]{2,1,0:T(8,128)S(1)}, u32[]{:S(2)}, u32[]{:S(2)}) collective-permute-start(f32[4,128,128]{2,1,0:T(8,128)S(1)} %add_add_fusion.1), channel_id=1, source_target_pairs={{64,128},{65,129},{66,130},{67,131},{68,132},{69,133},{70,134},{71... | collective-permute-start | bytes 786440 | tf_op jit(solution)/shard_map/ppermute | solution.py:325
  208.6 22.8 %copy-start.2 = (f32[16,384,128]{2,1,0:T(8,128)}, f32[16,384,128]{2,1,0:T(8,128)S(1)}, u32[]{:S(2)}) copy-start(f32[16,384,128]{2,1,0:T(8,128)S(1)} %all-to-all-done.1.slots) | copy-start | bytes 9437188
  208.6 17.2 %all-to-all-start.2 = ((f32[16,48,128]{2,1,0:T(8,128)}), f32[16,48,128]{2,1,0:T(8,128)}, u32[]{:S(2)}, u32[]{:S(2)}) async-start(f32[16,48,128]{2,1,0:T(8,128)} %panel_slots.1), calls=%async_computation.2 | async-start | bytes 786432 | tf_op jit(solution)/shard_map/all_to_all | solution.py:375
  229.4 7.9 %copy-start.5 = (f32[4,4,8,128]{3,2,1,0:T(8,128)S(1)}, f32[4,4,8,128]{3,2,1,0:T(8,128)}, u32[]{:S(2)}) copy-start(f32[4,4,8,128]{3,2,1,0:T(8,128)} %shard_map.47) | copy-start | bytes 196612
  231.5 82.3 %all-to-all-start.3 = ((f32[16,4,4,8,128]{4,3,2,1,0:T(8,128)}), f32[16,4,4,8,128]{4,3,2,1,0:T(8,128)}, u32[]{:S(2)}, u32[]{:S(2)}) async-start(f32[16,4,4,8,128]{4,3,2,1,0:T(8,128)} %broadcast_in_dim.73), calls=%async_computation.3 | async-start | bytes 2097152 | tf_op jit(solution)/shard_map/all_to_all | solution.py:381
  237.3 76.4 %collective-permute-start.16 = (f32[4,4,8,128]{3,2,1,0:T(8,128)S(1)}, f32[4,4,8,128]{3,2,1,0:T(8,128)S(1)}, u32[]{:S(2)}, u32[]{:S(2)}) collective-permute-start(f32[4,4,8,128]{3,2,1,0:T(8,128)S(1)} %copy-done.5), channel_id=1, source_target_pairs={{0,0},{1,16},{2,32},{3,48},{4,64},{5,80},{6,96},{7,112},{8,128},{9... | collective-permute-start | bytes 196616 | tf_op jit(solution)/shard_map/ppermute | solution.py:380
  248.3 101.6 %collective-permute-start.17 = (f32[4,4,128,128]{3,2,1,0:T(8,128)}, f32[4,4,128,128]{3,2,1,0:T(8,128)S(1)}, u32[]{:S(2)}, u32[]{:S(2)}) collective-permute-start(f32[4,4,128,128]{3,2,1,0:T(8,128)} %shard_map.46.part), channel_id=1, source_target_pairs={{0,0},{1,16},{2,32},{3,48},{4,64},{5,80},{6,96},{7,112},{8,128},{9... | collective-permute-start | bytes 3145736 | tf_op jit(solution)/shard_map/ppermute | solution.py:377
  314.8 28.0 %all-to-all-start.4 = ((f32[16,4,4,8,128]{4,3,2,1,0:T(8,128)}), f32[16,4,4,8,128]{4,3,2,1,0:T(8,128)S(1)}, u32[]{:S(2)}, u32[]{:S(2)}) async-start(f32[16,4,4,8,128]{4,3,2,1,0:T(8,128)} %broadcast_in_dim.74), calls=%async_computation.4 | async-start | bytes 2097152 | tf_op jit(solution)/shard_map/all_to_all | solution.py:382
  342.9 1.0 copy-start.3
  349.8 1.0 copy-start.4

commit v6 on v5

--- a/solution.py
+++ b/solution.py
@@ -167,7 +167,7 @@
     )(scaled, lead, late)
 
 
-def place_kernel(meta, picks, slots, part):
+def place_kernel(meta, picks, slots, upper, lower, part):
     i = meta[2]
     j = meta[3]
     part[...] = jnp.zeros_like(part)
@@ -177,6 +177,25 @@
             a = picks[base + k, i]
             b = picks[base + k, j]
             part[a, b] += slots[g, k * BLK : (k + 1) * BLK, :]
+    upper[...] = part[: SPAN // 2]
+    lower[...] = part[SPAN // 2 :]
+
+
+def place_tiles(meta, picks, slots):
+    shape = (SPAN // 2, SPAN, BLK, BLK)
+    grid_spec = pltpu.PrefetchScalarGridSpec(
+        num_scalar_prefetch=2,
+        grid=(1,),
+        in_specs=[LOCAL],
+        out_specs=[LOCAL] * 2,
+        scratch_shapes=[pltpu.VMEM((SPAN, SPAN, BLK, BLK), jnp.float32)],
+    )
+    return pl.pallas_call(
+        place_kernel,
+        grid_spec=grid_spec,
+        out_shape=[jax.ShapeDtypeStruct(shape, jnp.float32)] * 2,
+        name="place_tiles",
+    )(meta, picks, slots)
 
 
 def strip_kernel(meta, picks, slots, strip):
@@ -189,17 +208,22 @@
             strip[b, a] += slots[g, m * SLICE : (m + 1) * SLICE, :]
 
 
-def place(kernel, meta, picks, slots, shape):
+def place_strip(meta, picks, slots):
     grid_spec = pltpu.PrefetchScalarGridSpec(
         num_scalar_prefetch=2, grid=(1,), in_specs=[LOCAL], out_specs=LOCAL
     )
     return pl.pallas_call(
-        kernel, grid_spec=grid_spec, out_shape=jax.ShapeDtypeStruct(shape, jnp.float32)
+        strip_kernel,
+        grid_spec=grid_spec,
+        out_shape=jax.ShapeDtypeStruct((SPAN, SPAN, SLICE, BLK), jnp.float32),
+        name="place_strip",
     )(meta, picks, slots)
 
 
-def solve_part(ref, inverse, b):
-    rows = jnp.concatenate([ref[:, b, a].reshape(BLK, BLK) for a in range(SPAN)], axis=0)
+def solve_part(ref, inverse, b, order):
+    rows = jnp.concatenate(
+        [ref[order[k], b, a] for a in range(SPAN) for k in range(NWIN)], axis=0
+    )
     solved = lax.dot_general(
         rows, inverse[b], CONTRACT_COLS, precision=HIGH, preferred_element_type=jnp.float32
     )
@@ -210,7 +234,7 @@
 def solve_kernel(left, inverse, out, high, low):
     for b in range(SPAN):
         cols = slice(b * BLK, (b + 1) * BLK)
-        out[:, cols], high[:, cols], low[:, cols] = solve_part(left, inverse, b)
+        out[:, cols], high[:, cols], low[:, cols] = solve_part(left, inverse, b, range(NWIN))
 
 
 def solve_rows(left, inverse):
@@ -224,7 +248,7 @@
     )(left, inverse)
 
 
-def update_kernel(meta, part, lefts, high, low, right, diag, chol, inverse, out):
+def update_kernel(meta, upper, lower, lefts, high, low, right, diag, chol, inverse, out):
     i = meta[2]
     j = meta[3]
     inside = (i > 0) & (j > 0)
@@ -236,7 +260,8 @@
     def _():
         for a in range(SPAN):
             for b in range(SPAN):
-                out[spot(a, b)] = part[a, b]
+                half = upper if a < SPAN // 2 else lower
+                out[spot(a, b)] = half[a % (SPAN // 2), b]
 
     @pl.when(jnp.logical_not(inside) | (i == j))
     def _():
@@ -249,7 +274,12 @@
 
     @pl.when(inside)
     def _():
-        parts = [solve_part(right, inverse, b) for b in range(SPAN)]
+        gaps = [k ^ i for k in range(NWIN)]
+        order = [
+            ((d >> 1) & 1) | ((((d >> 2) ^ (d >> 3)) & 1) << 1) | ((d >> 3) << 2) | ((d & 1) << 3)
+            for d in gaps
+        ]
+        parts = [solve_part(right, inverse, b, order) for b in range(SPAN)]
         other_high = jnp.concatenate([p[1] for p in parts], axis=1)
         other_low = jnp.concatenate([p[2] for p in parts], axis=1)
 
@@ -282,7 +312,7 @@
     )(meta, *operands)
 
 
-def finish_kernel(meta, base, mirror, out):
+def finish_kernel(meta, base, upper, lower, out):
     i = meta[2]
     j = meta[3]
     both = (i > 0) & (j > 0) & (i != j)
@@ -290,28 +320,28 @@
     @pl.when(both)
     def _():
         for b in range(SPAN):
-            out[:, b * BLK : (b + 1) * BLK] = base[:, b * BLK : (b + 1) * BLK] + mirror[b, 0].T
+            half = upper if b < SPAN // 2 else lower
+            cols = slice(b * BLK, (b + 1) * BLK)
+            out[:, cols] = base[:, cols] + half[b % (SPAN // 2), 0].T
 
     @pl.when(jnp.logical_not(both))
     def _():
         out[...] = base[...]
 
 
-def finish(meta, base, mirror):
+def finish(meta, base, upper, lower):
     size = (SPAN * BLK, SPAN * BLK)
     rows = pl.BlockSpec((BLK, SPAN * BLK), lambda a, meta: (a, 0))
+    tall = pl.BlockSpec((SPAN // 2, 1, BLK, BLK), lambda a, meta: (0, a, 0, 0))
     grid_spec = pltpu.PrefetchScalarGridSpec(
-        num_scalar_prefetch=1,
-        grid=(SPAN,),
-        in_specs=[rows, pl.BlockSpec((SPAN, 1, BLK, BLK), lambda a, meta: (0, a, 0, 0))],
-        out_specs=rows,
+        num_scalar_prefetch=1, grid=(SPAN,), in_specs=[rows, tall, tall], out_specs=rows
     )
     return pl.pallas_call(
         finish_kernel,
         grid_spec=grid_spec,
         out_shape=jax.ShapeDtypeStruct(size, jnp.float32),
         name="finish",
-    )(meta, base, mirror)
+    )(meta, base, upper, lower)
 
 
 def swap_pairs(size, bit):
@@ -352,14 +382,16 @@
     same, diag, piece, flipped = lax.optimization_barrier((same, diag, piece, flipped))
 
     other = lax.ppermute(same, "core", [(0, 1), (1, 0)])
-    diag = diag + lax.ppermute(diag, "yl", swap_pairs(2, 1))
+    across = lax.ppermute(diag, "yl", swap_pairs(2, 1))
+    tiles, late = gram_slots(meta, flipped, same, other)
+    across, late = lax.optimization_barrier((across, late))
+    diag = diag + across
     eye = jnp.eye(BLK, dtype=jnp.float32)
     given_here = lax.dynamic_slice(given_diag, (i * SPAN * BLK,), (SPAN * BLK,))
     diag = diag + given_here.reshape(SPAN, 1, BLK) * eye
     corner = spread(jnp.where(i == 0, diag, 0.0), "core")
     corner = spread(corner, "yh")
     piece = spread(piece, "yh")
-    tiles, late = gram_slots(meta, flipped, same, other)
 
     tiles = lax.all_to_all(tiles, GC, 0, 0, tiled=True)
     chol, inverse = factor(spread(corner, "x"))
@@ -371,18 +403,25 @@
     slices = panel_slots(scaled, lead, late)
     tiles, slices, chol, inverse = lax.optimization_barrier((tiles, slices, chol, inverse))
 
-    part = place(place_kernel, meta, block_pick, tiles, (SPAN, SPAN, BLK, BLK))
+    upper, lower = place_tiles(meta, block_pick, tiles)
     slices = lax.all_to_all(slices, GC, 0, 0, tiled=True)
     everywhere = [(r * NWIN + c, c * NWIN + r) for r in range(NWIN) for c in range(NWIN)]
-    mirror = lax.ppermute(part, AXES, everywhere)
-    strip = place(strip_kernel, meta, block_pick, slices, (SPAN, SPAN, SLICE, BLK))
-    copies = (NWIN,) + strip.shape
-    turned = lax.ppermute(strip, AXES, everywhere)
-    left = lax.all_to_all(jnp.broadcast_to(strip, copies), GC, 0, 0, tiled=True)
-    right = lax.all_to_all(jnp.broadcast_to(turned, copies), GR, 0, 0, tiled=True)
+    strip = place_strip(meta, block_pick, slices)
+    right = lax.ppermute(strip, AXES, everywhere)[None]
+    copies = jnp.broadcast_to(strip, (NWIN,) + strip.shape)
+    left = lax.all_to_all(copies, GC, 0, 0, tiled=True)
+    mirror_a = lax.ppermute(upper, AXES, everywhere)
+    mirror_b = lax.ppermute(lower, AXES, everywhere)
+    for axis, pairs in (
+        ("yh", swap_pairs(2, 1)),
+        ("x", swap_pairs(4, 1)),
+        ("x", swap_pairs(4, 3)),
+        ("core", swap_pairs(2, 1)),
+    ):
+        right = jnp.concatenate([right, lax.ppermute(right, axis, pairs)], axis=0)
     lefts, high, low = solve_rows(left, inverse)
-    base = update(meta, part, lefts, high, low, right, diag, chol, inverse)
-    return finish(meta, base, mirror)
+    base = update(meta, upper, lower, lefts, high, low, right, diag, chol, inverse)
+    return finish(meta, base, mirror_a, mirror_b)
 
 
 def solution(mesh):

time: 361 us -> 365 us (1.011); the launches traced: 355 us -> 364 us
  starting transfers between devices: 72 us -> 80.6 us
    ppermute x3 -> x8, waiting for transfers between devices: 63.9 us -> 89.8 us  [the longest x1 38.2 us: body(): mirror_a = lax.ppermute(upper, AXES, everywhere)]
    all_to_all x2 -> x1, waiting for transfers between devices: 19.8 us -> 0.01 us  [body(): left = lax.all_to_all(copies, GC, 0, 0, tiled=True)]
    ppermute x3 -> x8, starting transfers between devices: 12.1 us -> 23.6 us  [the longest x1 10.6 us: body(): right = lax.ppermute(strip, AXES, everywhere)[None]]
    all_to_all x2 -> x1, starting transfers between devices: 10.4 us -> 5.83 us  [body(): left = lax.all_to_all(copies, GC, 0, 0, tiled=True)]
    ppermute x4, waiting for transfers between devices: 12.9 us -> 8.43 us  [spread(): v = v + lax.ppermute(v, 'x', [(0, 1)]) + lax.ppermute(v, 'x', [(0, 3)])]
  transfers between devices with their start and end apart: 23 -> 27, of which waited for: 15 -> 18; matrix products, arithmetic and copies ran while one was open for 3% -> 3% of each run, Pallas kernels for 12% -> 12%
where the time goes in v6:
time: 365 us; the launch traced here: 364 us
  waiting for transfers between devices  201 us (55%)
  starting transfers between devices  80.6 us (22%)
  Pallas kernels  60.8 us (17%)
  other arithmetic  15.7 us (4%)
  local copies, waits for them, and re-layouts  4.54 us (1%)
    ppermute x1, waiting for transfers between devices, body(): mirror_a = lax.ppermute(upper, AXES, everywhere)  38.2 us
    ppermute x3, waiting for transfers between devices, spread(): return v + lax.ppermute(v, step, [(0, 1)])  37 us
    all_to_all x1, waiting for transfers between devices, body(): same = lax.all_to_all(slots, ('x', 'yh'), 0, 0, tiled=True)  28.7 us
    ppermute x1, waiting for transfers between devices, body(): right = lax.ppermute(strip, AXES, everywhere)[None]  24.3 us
    pallas_call x1, Pallas kernels, factor(): pl.pallas_call(factor_kernel, in_specs=[LOCAL], out_specs=[LOCAL] * 2, ou...  21 us
    ppermute x3, waiting for transfers between devices, body(): diag = diag + lax.ppermute(diag, 'z', swap_pairs(8, bit))  18.9 us
    ppermute x4, waiting for transfers between devices, body(): right = jnp.concatenate([right, lax.ppermute(right, axis, pairs)], axis=0)  12.5 us
    ppermute x1, waiting for transfers between devices, body(): mirror_b = lax.ppermute(lower, AXES, everywhere)  11.1 us
  transfers between devices with their start and end apart: 27, of which 18 were waited for; matrix products, arithmetic and copies ran while one was open for 3% of the time, Pallas kernels for 12%

profile of v6, /device:TPU:66, one launch (start us, length us, event | category | flops | bytes accessed | tf_op | source)
XLA Modules:
  0.0 363.8 jit_solution(10551162499807097372)
XLA Ops:
  0.0 0.8 sqrt.3
  0.8 1.9 multiply_convert_fusion.scaled.first
  2.8 2.8 broadcast_select_fusion
  5.6 7.6 %all-to-all-start = ((bf16[8,3,768,128]{3,2,1,0:T(8,128)(2,1)}), bf16[8,3,768,128]{3,2,1,0:T(8,128)(2,1)}, u32[]{:S(2)}, u32[]{:S(2)}) async-start(bf16[8,3,768,128]{3,2,1,0:T(8,128)(2,1)} %broadcast_select_fusion), calls=%async_computation | async-start | bytes 9437184 | tf_op jit(solution)/shard_map/all_to_all | solution.py:377
  13.3 0.5 fusion.1
  14.0 2.0 collective-permute-start
  16.0 1.3 collective-permute-start.3
  17.4 4.4 %collective-permute-done = f32[4,128,128]{2,1,0:T(8,128)S(1)} collective-permute-done((f32[4,128,128]{2,1,0:T(8,128)S(1)}, f32[4,128,128]{2,1,0:T(8,128)S(1)}, u32[]{:S(2)}, u32[]{:S(2)}) %collective-permute-start) | collective-permute-done | bytes 262176 | tf_op jit(solution)/shard_map/ppermute | solution.py:372
  21.9 10.3 %collective-permute-done.1 = f32[4,128,128]{2,1,0:T(8,128)S(1)} collective-permute-done((f32[4,128,128]{2,1,0:T(8,128)S(1)}, f32[4,128,128]{2,1,0:T(8,128)S(1)}, u32[]{:S(2)}, u32[]{:S(2)}) %collective-permute-start.1) | collective-permute-done | bytes 262176 | tf_op jit(solution)/shard_map/ppermute | solution.py:372
  32.3 6.3 %collective-permute-start.2 = (f32[4,128,128]{2,1,0:T(8,128)S(1)}, f32[4,128,128]{2,1,0:T(8,128)S(1)}, u32[]{:S(2)}, u32[]{:S(2)}) collective-permute-start(f32[4,128,128]{2,1,0:T(8,128)S(1)} %add.75), channel_id=1, source_target_pairs={{0,4},{1,5},{2,6},{3,7},{4,0},{5,1},{6,2},{7,3},{8,12},{9,13},{10,... | collective-permute-start | bytes 786440 | tf_op jit(solution)/shard_map/ppermute | solution.py:372
  38.5 4.6 %flip.1.mine = bf16[6,128,768]{2,1,0:T(8,128)(2,1)} custom-call(bf16[6,768,128]{2,1,0:T(8,128)(2,1)} %copy-done.1), custom_call_target="tpu_custom_call" | custom-call | tf_op jit(solution)/shard_map/flip/pallas_call | solution.py:84
  43.2 4.2 %collective-permute-done.2 = f32[4,128,128]{2,1,0:T(8,128)S(1)} collective-permute-done((f32[4,128,128]{2,1,0:T(8,128)S(1)}, f32[4,128,128]{2,1,0:T(8,128)S(1)}, u32[]{:S(2)}, u32[]{:S(2)}) %collective-permute-start.2) | collective-permute-done | bytes 262176 | tf_op jit(solution)/shard_map/ppermute | solution.py:372
  47.4 0.7 add.76
  48.1 28.7 %all-to-all-done.same = bf16[8,3,768,128]{3,2,1,0:T(8,128)(2,1)} async-done(((bf16[8,3,768,128]{3,2,1,0:T(8,128)(2,1)}), bf16[8,3,768,128]{3,2,1,0:T(8,128)(2,1)}, u32[]{:S(2)}, u32[]{:S(2)}) %all-to-all-start) | async-done | bytes 4718624 | tf_op jit(solution)/shard_map/all_to_all | solution.py:377
  76.8 0.6 pad_add_fusion.meta
  77.4 7.6 %collective-permute-done.4.other = bf16[8,3,768,128]{3,2,1,0:T(8,128)(2,1)} collective-permute-done((bf16[8,3,768,128]{3,2,1,0:T(8,128)(2,1)}, bf16[8,3,768,128]{3,2,1,0:T(8,128)(2,1)}, u32[]{:S(2)}, u32[]{:S(2)}) %collective-permute-start.4) | collective-permute-done | bytes 4718624 | tf_op jit(solution)/shard_map/ppermute | solution.py:384
  85.1 9.8 %gram_slots.1 = (f32[16,384,128]{2,1,0:T(8,128)}, f32[3,128,128]{2,1,0:T(8,128)}) custom-call(s32[4]{0:T(128)} %pad_add_fusion.meta, bf16[6,128,768]{2,1,0:T(8,128)(2,1)} %flip.1.mine, bf16[8,3,768,128]{3,2,1,0:T(8,128)(2,1)} %all-to-all-done.same, bf16[8,3,768,128]{3,2,1,0:T(8,128)(2,1)} %collective-permute-done.4.other), custom_call_target="tpu_custom_call" | custom-call | tf_op jit(solution)/shard_map/gram_slots/pallas_call | solution.py:130
  94.9 8.2 %all-to-all-start.1 = ((f32[16,384,128]{2,1,0:T(8,128)}), f32[16,384,128]{2,1,0:T(8,128)S(1)}, u32[]{:S(2)}, u32[]{:S(2)}) async-start(f32[16,384,128]{2,1,0:T(8,128)} %get-tuple-element.26), calls=%async_computation.1 | async-start | bytes 6291456 | tf_op jit(solution)/shard_map/all_to_all | solution.py:396
  103.2 5.4 %collective-permute-start.5 = (bf16[3,384,128]{2,1,0:T(8,128)(2,1)S(1)}, bf16[3,384,128]{2,1,0:T(8,128)(2,1)}, u32[]{:S(2)}, u32[]{:S(2)}) collective-permute-start(bf16[3,384,128]{2,1,0:T(8,128)(2,1)S(1)} %slice_add_fusion), channel_id=1, source_target_pairs={{0,32},{1,33},{2,34},{3,35},{4,36},{5,37},{6,38},{7,39},{8,40},{9,... | collective-permute-start | bytes 884744 | tf_op jit(solution)/shard_map/ppermute | solution.py:353
  108.6 0.9 collective-permute-start.10
  109.5 18.0 %collective-permute-done.5 = bf16[3,384,128]{2,1,0:T(8,128)(2,1)} collective-permute-done((bf16[3,384,128]{2,1,0:T(8,128)(2,1)S(1)}, bf16[3,384,128]{2,1,0:T(8,128)(2,1)}, u32[]{:S(2)}, u32[]{:S(2)}) %collective-permute-start.5) | collective-permute-done | bytes 294944 | tf_op jit(solution)/shard_map/ppermute | solution.py:353
  127.5 1.0 add.78
  128.6 1.3 collective-permute-start.6
  129.9 0.7 collective-permute-start.7
  130.6 3.6 collective-permute-done.10
  134.2 1.8 broadcast_select_fusion.4
  136.0 1.3 collective-permute-start.11
  137.3 1.1 collective-permute-done.11
  138.4 2.4 collective-permute-start.12
  140.9 2.4 collective-permute-start.8
  143.3 17.8 %collective-permute-done.12 = f32[4,128,128]{2,1,0:T(8,128)S(1)} collective-permute-done((f32[4,128,128]{2,1,0:T(8,128)S(1)}, f32[4,128,128]{2,1,0:T(8,128)S(1)}, u32[]{:S(2)}, u32[]{:S(2)}) %collective-permute-start.12) | collective-permute-done | bytes 262176 | tf_op jit(solution)/shard_map/ppermute | solution.py:353
  161.1 0.7 add.86
  161.9 1.3 collective-permute-start.13
  163.2 1.4 collective-permute-start.14
  164.7 8.4 %collective-permute-done.13 = f32[4,128,128]{2,1,0:T(8,128)} collective-permute-done((f32[4,128,128]{2,1,0:T(8,128)}, f32[4,128,128]{2,1,0:T(8,128)}, u32[]{:S(2)}, u32[]{:S(2)}) %collective-permute-start.13) | collective-permute-done | bytes 262176 | tf_op jit(solution)/shard_map/ppermute | solution.py:354
  173.2 1.8 add_add_fusion.1
  175.0 2.0 collective-permute-start.15
  177.0 1.0 broadcast_select_fusion.3
  178.0 0.9 pad_maximum_fusion.lead
  178.9 2.4 panel_slots.1
  181.3 0.8 collective-permute-done.15
  182.1 1.8 add.89.corner
  183.8 21.0 %factor.1 = (f32[4,128,128]{2,1,0:T(8,128)}, f32[4,128,128]{2,1,0:T(8,128)}) custom-call(f32[4,128,128]{2,1,0:T(8,128)} %add.89.corner), custom_call_target="tpu_custom_call" | custom-call | tf_op jit(solution)/shard_map/factor/pallas_call | solution.py:69
  204.8 7.4 %all-to-all-start.2 = ((f32[16,48,128]{2,1,0:T(8,128)}), f32[16,48,128]{2,1,0:T(8,128)}, u32[]{:S(2)}, u32[]{:S(2)}) async-start(f32[16,48,128]{2,1,0:T(8,128)} %panel_slots.1), calls=%async_computation.2 | async-start | bytes 786432 | tf_op jit(solution)/shard_map/all_to_all | solution.py:407
  212.2 0.7 copy.9.picks
  212.9 10.0 %all-to-all-done.2.slots = f32[16,48,128]{2,1,0:T(8,128)} async-done(((f32[16,48,128]{2,1,0:T(8,128)}), f32[16,48,128]{2,1,0:T(8,128)}, u32[]{:S(2)}, u32[]{:S(2)}) %all-to-all-start.2) | async-done | bytes 393248 | tf_op jit(solution)/shard_map/all_to_all | solution.py:407
  222.9 3.6 place_strip.1
  226.5 2.0 broadcast_in_dim.73
  228.5 5.8 %all-to-all-start.3 = ((f32[16,4,4,8,128]{4,3,2,1,0:T(8,128)}), f32[16,4,4,8,128]{4,3,2,1,0:T(8,128)}, u32[]{:S(2)}, u32[]{:S(2)}) async-start(f32[16,4,4,8,128]{4,3,2,1,0:T(8,128)} %broadcast_in_dim.73), calls=%async_computation.3 | async-start | bytes 2097152 | tf_op jit(solution)/shard_map/all_to_all | solution.py:412
  234.3 10.6 %collective-permute-start.16 = (f32[4,4,8,128]{3,2,1,0:T(8,128)S(1)}, f32[4,4,8,128]{3,2,1,0:T(8,128)S(1)}, u32[]{:S(2)}, u32[]{:S(2)}) collective-permute-start(f32[4,4,8,128]{3,2,1,0:T(8,128)S(1)} %copy-done.6), channel_id=1, source_target_pairs={{0,0},{1,16},{2,32},{3,48},{4,64},{5,80},{6,96},{7,112},{8,128},{9... | collective-permute-start | bytes 196616 | tf_op jit(solution)/shard_map/ppermute | solution.py:410
  245.0 24.3 %collective-permute-done.16 = f32[4,4,8,128]{3,2,1,0:T(8,128)S(1)} collective-permute-done((f32[4,4,8,128]{3,2,1,0:T(8,128)S(1)}, f32[4,4,8,128]{3,2,1,0:T(8,128)S(1)}, u32[]{:S(2)}, u32[]{:S(2)}) %collective-permute-start.16) | collective-permute-done | bytes 65568 | tf_op jit(solution)/shard_map/ppermute | solution.py:410
  269.3 5.8 %collective-permute-done.17 = f32[1,4,4,8,128]{4,3,2,1,0:T(8,128)S(1)} collective-permute-done((f32[1,4,4,8,128]{4,3,2,1,0:T(8,128)S(1)}, f32[1,4,4,8,128]{4,3,2,1,0:T(8,128)S(1)}, u32[]{:S(2)}, u32[]{:S(2)}) %collective-permute-start.17) | collective-permute-done | bytes 65568 | tf_op jit(solution)/shard_map/ppermute | solution.py:421
  275.2 5.0 %collective-permute-done.18 = f32[2,4,4,8,128]{4,3,2,1,0:T(8,128)S(1)} collective-permute-done((f32[2,4,4,8,128]{4,3,2,1,0:T(8,128)S(1)}, f32[2,4,4,8,128]{4,3,2,1,0:T(8,128)S(1)}, u32[]{:S(2)}, u32[]{:S(2)}) %collective-permute-start.18) | collective-permute-done | bytes 131104 | tf_op jit(solution)/shard_map/ppermute | solution.py:421
  280.1 0.7 collective-permute-start.19
  280.8 4.9 %place_tiles.1 = (f32[2,4,128,128]{3,2,1,0:T(8,128)}, f32[2,4,128,128]{3,2,1,0:T(8,128)}) custom-call(s32[4]{0:T(128)} %pad_add_fusion.meta, s32[96,16]{1,0:T(8,128)} %copy.9.picks, f32[16,384,128]{2,1,0:T(8,128)} %copy-done.2), custom_call_target="tpu_custom_call" | custom-call | tf_op jit(solution)/shard_map/place_tiles/pallas_call | solution.py:193
  285.8 3.1 collective-permute-start.21
  288.9 8.1 %collective-permute-start.22 = (f32[2,4,128,128]{3,2,1,0:T(8,128)}, f32[2,4,128,128]{3,2,1,0:T(8,128)S(1)}, u32[]{:S(2)}, u32[]{:S(2)}) collective-permute-start(f32[2,4,128,128]{3,2,1,0:T(8,128)} %get-tuple-element.36.lower), channel_id=1, source_target_pairs={{0,0},{1,16},{2,32},{3,48},{4,64},{5,80},{6,96},{7,112},{8,128},{9... | collective-permute-start | bytes 1572872 | tf_op jit(solution)/shard_map/ppermute | solution.py:414
  297.2 1.8 collective-permute-done.20
  299.1 4.0 %solve_rows.1 = (f32[512,512]{1,0:T(8,128)}, bf16[512,512]{1,0:T(8,128)(2,1)}, bf16[512,512]{1,0:T(8,128)(2,1)}) custom-call(f32[16,4,4,8,128]{4,3,2,1,0:T(8,128)} %all-to-all-done.3.left, f32[4,128,128]{2,1,0:T(8,128)} %get-tuple-element.38.inverse), custom_call_target="tpu_custom_call" | custom-call | tf_op jit(solution)/shard_map/solve_rows/pallas_call | solution.py:242
  303.2 6.0 %update.1.base = f32[512,512]{1,0:T(8,128)} custom-call(s32[4]{0:T(128)} %pad_add_fusion.meta, f32[2,4,128,128]{3,2,1,0:T(8,128)} %get-tuple-element.35.upper, f32[2,4,128,128]{3,2,1,0:T(8,128)} %get-tuple-element.36.lower, f32[512,512]{1,0:T(8,128)} %get-tuple-element.39.lefts, bf16[512,512]{1,0:T(8,128)(2,1)} %get-tuple-element.40.high, ...), custom_call_target="tpu_custom_call" | custom-call | tf_op jit(solution)/shard_map/update/pallas_call | solution.py:307
  309.2 38.2 %collective-permute-done.21.upper = f32[2,4,128,128]{3,2,1,0:T(8,128)S(1)} collective-permute-done((f32[2,4,128,128]{3,2,1,0:T(8,128)}, f32[2,4,128,128]{3,2,1,0:T(8,128)S(1)}, u32[]{:S(2)}, u32[]{:S(2)}) %collective-permute-start.21) | collective-permute-done | bytes 524320 | tf_op jit(solution)/shard_map/ppermute | solution.py:413
  347.4 11.1 %collective-permute-done.22.lower = f32[2,4,128,128]{3,2,1,0:T(8,128)S(1)} collective-permute-done((f32[2,4,128,128]{3,2,1,0:T(8,128)}, f32[2,4,128,128]{3,2,1,0:T(8,128)S(1)}, u32[]{:S(2)}, u32[]{:S(2)}) %collective-permute-start.22) | collective-permute-done | bytes 524320 | tf_op jit(solution)/shard_map/ppermute | solution.py:414
  358.5 0.8 copy-done.5
  359.3 4.5 %finish.1 = f32[512,512]{1,0:T(8,128)} custom-call(s32[4]{0:T(128)} %pad_add_fusion.meta, f32[512,512]{1,0:T(8,128)} %update.1.base, f32[2,4,128,128]{3,2,1,0:T(8,128)} %copy-done.4, f32[2,4,128,128]{3,2,1,0:T(8,128)} %copy-done.5), custom_call_target="tpu_custom_call" | custom-call | tf_op jit(solution)/shard_map/finish/pallas_call | solution.py:339
  (52 shorter events, 1.4 us)
Async XLA Ops:
  0.0 109.4 %copy-start = (f32[8192]{0:T(1024)S(1)}, f32[8192]{0:T(1024)}, u32[]{:S(2)}) copy-start(f32[8192]{0:T(1024)} %param.7) | copy-start | bytes 98308
  2.6 10.7 %copy-start.1 = (bf16[6,768,128]{2,1,0:T(8,128)(2,1)}, bf16[6,768,128]{2,1,0:T(8,128)(2,1)S(1)}, u32[]{:S(2)}) copy-start(bf16[6,768,128]{2,1,0:T(8,128)(2,1)S(1)} %multiply_convert_fusion.scaled.first) | copy-start | bytes 3538948
  5.6 7.6 %copy-start.7 = (s32[96,16]{0,1:T(8,128)S(1)}, s32[96,16]{0,1:T(8,128)}, u32[]{:S(2)}) copy-start(s32[96,16]{0,1:T(8,128)} %param.6) | copy-start | bytes 18436
  5.6 71.3 %all-to-all-start = ((bf16[8,3,768,128]{3,2,1,0:T(8,128)(2,1)}), bf16[8,3,768,128]{3,2,1,0:T(8,128)(2,1)}, u32[]{:S(2)}, u32[]{:S(2)}) async-start(bf16[8,3,768,128]{3,2,1,0:T(8,128)(2,1)} %broadcast_select_fusion), calls=%async_computation | async-start | bytes 9437184 | tf_op jit(solution)/shard_map/all_to_all | solution.py:377
  14.0 7.7 %collective-permute-start = (f32[4,128,128]{2,1,0:T(8,128)S(1)}, f32[4,128,128]{2,1,0:T(8,128)S(1)}, u32[]{:S(2)}, u32[]{:S(2)}) collective-permute-start(f32[4,128,128]{2,1,0:T(8,128)S(1)} %select_reduce_fusion), channel_id=1, source_target_pairs={{0,1},{1,0},{2,3},{3,2},{4,5},{5,4},{6,7},{7,6},{8,9},{9,8},{10,11... | collective-permute-start | bytes 786440 | tf_op jit(solution)/shard_map/ppermute | solution.py:372
  16.0 27.1 %collective-permute-start.3 = (bf16[3,384,128]{2,1,0:T(8,128)(2,1)S(1)}, bf16[3,384,128]{2,1,0:T(8,128)(2,1)S(1)}, u32[]{:S(2)}, u32[]{:S(2)}) collective-permute-start(bf16[3,384,128]{2,1,0:T(8,128)(2,1)S(1)} %slice.20), channel_id=1, source_target_pairs={{0,16},{1,17},{2,18},{3,19},{4,20},{5,21},{6,22},{7,23},{8,24},{9,... | collective-permute-start | bytes 884744 | tf_op jit(solution)/shard_map/ppermute | solution.py:380
  21.8 10.4 %collective-permute-start.1 = (f32[4,128,128]{2,1,0:T(8,128)S(1)}, f32[4,128,128]{2,1,0:T(8,128)S(1)}, u32[]{:S(2)}, u32[]{:S(2)}) collective-permute-start(f32[4,128,128]{2,1,0:T(8,128)S(1)} %add.74), channel_id=1, source_target_pairs={{0,2},{1,3},{2,0},{3,1},{4,6},{5,7},{6,4},{7,5},{8,10},{9,11},{10,... | collective-permute-start | bytes 786440 | tf_op jit(solution)/shard_map/ppermute | solution.py:372
  32.3 15.1 %collective-permute-start.2 = (f32[4,128,128]{2,1,0:T(8,128)S(1)}, f32[4,128,128]{2,1,0:T(8,128)S(1)}, u32[]{:S(2)}, u32[]{:S(2)}) collective-permute-start(f32[4,128,128]{2,1,0:T(8,128)S(1)} %add.75), channel_id=1, source_target_pairs={{0,4},{1,5},{2,6},{3,7},{4,0},{5,1},{6,2},{7,3},{8,12},{9,13},{10,... | collective-permute-start | bytes 786440 | tf_op jit(solution)/shard_map/ppermute | solution.py:372
  76.8 8.3 %collective-permute-start.4 = (bf16[8,3,768,128]{3,2,1,0:T(8,128)(2,1)}, bf16[8,3,768,128]{3,2,1,0:T(8,128)(2,1)}, u32[]{:S(2)}, u32[]{:S(2)}) collective-permute-start(bf16[8,3,768,128]{3,2,1,0:T(8,128)(2,1)} %all-to-all-done.same), channel_id=1, source_target_pairs={{0,16},{16,0},{1,17},{17,1},{2,18},{18,2},{3,19},{19,3},{4,20},{20... | collective-permute-start | bytes 14155784 | tf_op jit(solution)/shard_map/ppermute | solution.py:384
  94.9 109.9 %all-to-all-start.1 = ((f32[16,384,128]{2,1,0:T(8,128)}), f32[16,384,128]{2,1,0:T(8,128)S(1)}, u32[]{:S(2)}, u32[]{:S(2)}) async-start(f32[16,384,128]{2,1,0:T(8,128)} %get-tuple-element.26), calls=%async_computation.1 | async-start | bytes 6291456 | tf_op jit(solution)/shard_map/all_to_all | solution.py:396
  103.2 24.4 %collective-permute-start.5 = (bf16[3,384,128]{2,1,0:T(8,128)(2,1)S(1)}, bf16[3,384,128]{2,1,0:T(8,128)(2,1)}, u32[]{:S(2)}, u32[]{:S(2)}) collective-permute-start(bf16[3,384,128]{2,1,0:T(8,128)(2,1)S(1)} %slice_add_fusion), channel_id=1, source_target_pairs={{0,32},{1,33},{2,34},{3,35},{4,36},{5,37},{6,38},{7,39},{8,40},{9,... | collective-permute-start | bytes 884744 | tf_op jit(solution)/shard_map/ppermute | solution.py:353
  108.6 25.6 %collective-permute-start.10 = (f32[4,128,128]{2,1,0:T(8,128)}, f32[4,128,128]{2,1,0:T(8,128)}, u32[]{:S(2)}, u32[]{:S(2)}) collective-permute-start(f32[4,128,128]{2,1,0:T(8,128)} %add.76), channel_id=1, source_target_pairs={{0,8},{8,0},{1,9},{9,1},{2,10},{10,2},{3,11},{11,3},{4,12},{12,4},... | collective-permute-start | bytes 786440 | tf_op jit(solution)/shard_map/ppermute | solution.py:385
  128.6 12.3 %collective-permute-start.6 = (bf16[3,384,128]{2,1,0:T(8,128)(2,1)S(1)}, bf16[3,384,128]{2,1,0:T(8,128)(2,1)S(1)}, u32[]{:S(2)}, u32[]{:S(2)}) collective-permute-start(bf16[3,384,128]{2,1,0:T(8,128)(2,1)S(1)} %add.78), channel_id=1, source_target_pairs={{0,64},{1,65},{2,66},{3,67},{4,68},{5,69},{6,70},{7,71},{8,72},{9,... | collective-permute-start | bytes 884744 | tf_op jit(solution)/shard_map/ppermute | solution.py:354
  129.9 11.0 %collective-permute-start.7 = (bf16[3,384,128]{2,1,0:T(8,128)(2,1)S(1)}, bf16[3,384,128]{2,1,0:T(8,128)(2,1)S(1)}, u32[]{:S(2)}, u32[]{:S(2)}) collective-permute-start(bf16[3,384,128]{2,1,0:T(8,128)(2,1)S(1)} %add.78), channel_id=1, source_target_pairs={{0,192},{1,193},{2,194},{3,195},{4,196},{5,197},{6,198},{7,199},{8... | collective-permute-start | bytes 884744 | tf_op jit(solution)/shard_map/ppermute | solution.py:354
  136.0 2.4 collective-permute-start.11
  138.4 22.7 %collective-permute-start.12 = (f32[4,128,128]{2,1,0:T(8,128)S(1)}, f32[4,128,128]{2,1,0:T(8,128)S(1)}, u32[]{:S(2)}, u32[]{:S(2)}) collective-permute-start(f32[4,128,128]{2,1,0:T(8,128)S(1)} %add.85), channel_id=1, source_target_pairs={{0,32},{1,33},{2,34},{3,35},{4,36},{5,37},{6,38},{7,39},{8,40},{9,... | collective-permute-start | bytes 786440 | tf_op jit(solution)/shard_map/ppermute | solution.py:353
  140.9 23.6 %collective-permute-start.8 = (bf16[3,384,128]{2,1,0:T(8,128)(2,1)S(1)}, bf16[3,384,128]{2,1,0:T(8,128)(2,1)S(1)}, u32[]{:S(2)}, u32[]{:S(2)}) collective-permute-start(bf16[3,384,128]{2,1,0:T(8,128)(2,1)S(1)} %add_add_fusion), channel_id=1, source_target_pairs={{64,128},{65,129},{66,130},{67,131},{68,132},{69,133},{70,134},{71... | collective-permute-start | bytes 884744 | tf_op jit(solution)/shard_map/ppermute | solution.py:355
  161.9 11.3 %collective-permute-start.13 = (f32[4,128,128]{2,1,0:T(8,128)}, f32[4,128,128]{2,1,0:T(8,128)}, u32[]{:S(2)}, u32[]{:S(2)}) collective-permute-start(f32[4,128,128]{2,1,0:T(8,128)} %add.86), channel_id=1, source_target_pairs={{0,64},{1,65},{2,66},{3,67},{4,68},{5,69},{6,70},{7,71},{8,72},{9,... | collective-permute-start | bytes 786440 | tf_op jit(solution)/shard_map/ppermute | solution.py:354
  163.2 10.0 %collective-permute-start.14 = (f32[4,128,128]{2,1,0:T(8,128)}, f32[4,128,128]{2,1,0:T(8,128)}, u32[]{:S(2)}, u32[]{:S(2)}) collective-permute-start(f32[4,128,128]{2,1,0:T(8,128)} %add.86), channel_id=1, source_target_pairs={{0,192},{1,193},{2,194},{3,195},{4,196},{5,197},{6,198},{7,199},{8... | collective-permute-start | bytes 786440 | tf_op jit(solution)/shard_map/ppermute | solution.py:354
  164.6 12.4 %collective-permute-start.9 = (bf16[3,384,128]{2,1,0:T(8,128)(2,1)S(1)}, bf16[3,384,128]{2,1,0:T(8,128)(2,1)}, u32[]{:S(2)}, u32[]{:S(2)}) collective-permute-start(bf16[3,384,128]{2,1,0:T(8,128)(2,1)S(1)} %add.81), channel_id=1, source_target_pairs={{0,16},{16,0},{1,17},{17,1},{2,18},{18,2},{3,19},{19,3},{4,20},{20... | collective-permute-start | bytes 884744 | tf_op jit(solution)/shard_map/ppermute | solution.py:399
  175.0 7.0 %collective-permute-start.15 = (f32[4,128,128]{2,1,0:T(8,128)}, f32[4,128,128]{2,1,0:T(8,128)}, u32[]{:S(2)}, u32[]{:S(2)}) collective-permute-start(f32[4,128,128]{2,1,0:T(8,128)} %add_add_fusion.1), channel_id=1, source_target_pairs={{64,128},{65,129},{66,130},{67,131},{68,132},{69,133},{70,134},{71... | collective-permute-start | bytes 786440 | tf_op jit(solution)/shard_map/ppermute | solution.py:355
  204.8 23.7 %copy-start.2 = (f32[16,384,128]{2,1,0:T(8,128)}, f32[16,384,128]{2,1,0:T(8,128)S(1)}, u32[]{:S(2)}) copy-start(f32[16,384,128]{2,1,0:T(8,128)S(1)} %all-to-all-done.1.slots) | copy-start | bytes 9437188
  204.8 18.1 %all-to-all-start.2 = ((f32[16,48,128]{2,1,0:T(8,128)}), f32[16,48,128]{2,1,0:T(8,128)}, u32[]{:S(2)}, u32[]{:S(2)}) async-start(f32[16,48,128]{2,1,0:T(8,128)} %panel_slots.1), calls=%async_computation.2 | async-start | bytes 786432 | tf_op jit(solution)/shard_map/all_to_all | solution.py:407
  226.5 7.8 %copy-start.6 = (f32[4,4,8,128]{3,2,1,0:T(8,128)S(1)}, f32[4,4,8,128]{3,2,1,0:T(8,128)}, u32[]{:S(2)}) copy-start(f32[4,4,8,128]{3,2,1,0:T(8,128)} %place_strip.1) | copy-start | bytes 196612
  228.5 70.6 %all-to-all-start.3 = ((f32[16,4,4,8,128]{4,3,2,1,0:T(8,128)}), f32[16,4,4,8,128]{4,3,2,1,0:T(8,128)}, u32[]{:S(2)}, u32[]{:S(2)}) async-start(f32[16,4,4,8,128]{4,3,2,1,0:T(8,128)} %broadcast_in_dim.73), calls=%async_computation.3 | async-start | bytes 2097152 | tf_op jit(solution)/shard_map/all_to_all | solution.py:412
  234.3 35.0 %collective-permute-start.16 = (f32[4,4,8,128]{3,2,1,0:T(8,128)S(1)}, f32[4,4,8,128]{3,2,1,0:T(8,128)S(1)}, u32[]{:S(2)}, u32[]{:S(2)}) collective-permute-start(f32[4,4,8,128]{3,2,1,0:T(8,128)S(1)} %copy-done.6), channel_id=1, source_target_pairs={{0,0},{1,16},{2,32},{3,48},{4,64},{5,80},{6,96},{7,112},{8,128},{9... | collective-permute-start | bytes 196616 | tf_op jit(solution)/shard_map/ppermute | solution.py:410
  269.3 5.8 %collective-permute-start.17 = (f32[1,4,4,8,128]{4,3,2,1,0:T(8,128)S(1)}, f32[1,4,4,8,128]{4,3,2,1,0:T(8,128)S(1)}, u32[]{:S(2)}, u32[]{:S(2)}) collective-permute-start(f32[1,4,4,8,128]{4,3,2,1,0:T(8,128)S(1)} %bitcast.12), channel_id=1, source_target_pairs={{0,32},{32,0},{1,33},{33,1},{2,34},{34,2},{3,35},{35,3},{4,36},{36... | collective-permute-start | bytes 196616 | tf_op jit(solution)/shard_map/ppermute | solution.py:421
  275.1 5.1 %collective-permute-start.18 = (f32[2,4,4,8,128]{4,3,2,1,0:T(8,128)S(1)}, f32[2,4,4,8,128]{4,3,2,1,0:T(8,128)S(1)}, u32[]{:S(2)}, u32[]{:S(2)}) collective-permute-start(f32[2,4,4,8,128]{4,3,2,1,0:T(8,128)S(1)} %pad_maximum_fusion.3), channel_id=1, source_target_pairs={{0,64},{64,0},{128,192},{192,128},{1,65},{65,1},{129,193},{193,129... | collective-permute-start | bytes 393224 | tf_op jit(solution)/shard_map/ppermute | solution.py:421
  280.1 16.9 %collective-permute-start.19 = (f32[4,4,4,8,128]{4,3,2,1,0:T(8,128)S(1)}, f32[4,4,4,8,128]{4,3,2,1,0:T(8,128)S(1)}, u32[]{:S(2)}, u32[]{:S(2)}) collective-permute-start(f32[4,4,4,8,128]{4,3,2,1,0:T(8,128)S(1)} %pad_maximum_fusion.2), channel_id=1, source_target_pairs={{0,192},{64,128},{128,64},{192,0},{1,193},{65,129},{129,65},{193,1... | collective-permute-start | bytes 786440 | tf_op jit(solution)/shard_map/ppermute | solution.py:421
  285.8 61.6 %collective-permute-start.21 = (f32[2,4,128,128]{3,2,1,0:T(8,128)}, f32[2,4,128,128]{3,2,1,0:T(8,128)S(1)}, u32[]{:S(2)}, u32[]{:S(2)}) collective-permute-start(f32[2,4,128,128]{3,2,1,0:T(8,128)} %get-tuple-element.35.upper), channel_id=1, source_target_pairs={{0,0},{1,16},{2,32},{3,48},{4,64},{5,80},{6,96},{7,112},{8,128},{9... | collective-permute-start | bytes 1572872 | tf_op jit(solution)/shard_map/ppermute | solution.py:413
  288.9 69.6 %collective-permute-start.22 = (f32[2,4,128,128]{3,2,1,0:T(8,128)}, f32[2,4,128,128]{3,2,1,0:T(8,128)S(1)}, u32[]{:S(2)}, u32[]{:S(2)}) collective-permute-start(f32[2,4,128,128]{3,2,1,0:T(8,128)} %get-tuple-element.36.lower), channel_id=1, source_target_pairs={{0,0},{1,16},{2,32},{3,48},{4,64},{5,80},{6,96},{7,112},{8,128},{9... | collective-permute-start | bytes 1572872 | tf_op jit(solution)/shard_map/ppermute | solution.py:414
  297.1 2.0 collective-permute-start.20
  299.1 4.1 %copy-start.3 = (f32[16,4,4,8,128]{4,3,2,1,0:T(8,128)}, f32[16,4,4,8,128]{4,3,2,1,0:T(8,128)S(1)}, u32[]{:S(2)}) copy-start(f32[16,4,4,8,128]{4,3,2,1,0:T(8,128)S(1)} %constant_dynamic-update-slice_fusion.right) | copy-start | bytes 3145732
  347.4 11.1 %copy-start.4 = (f32[2,4,128,128]{3,2,1,0:T(8,128)}, f32[2,4,128,128]{3,2,1,0:T(8,128)S(1)}, u32[]{:S(2)}) copy-start(f32[2,4,128,128]{3,2,1,0:T(8,128)S(1)} %collective-permute-done.21.upper) | copy-start | bytes 1572868
  358.5 0.8 copy-start.5

commit v7 on v6

--- a/solution.py
+++ b/solution.py
@@ -14,6 +14,27 @@
 HALF = 3
 SLICE = 8
 ROWS = HALF * BLK
+
+LANDING = (
+    (0, 1, 2, 3, 4, 5, 6, 7, 8, 9, 10, 11, 12, 13, 14, 15),
+    (14, 5, 0, 13, 6, 9, 12, 10, 2, 1, 8, 4, 3, 7, 11, 15),
+    (5, 12, 0, 3, 4, 13, 14, 7, 15, 10, 2, 1, 11, 8, 6, 9),
+    (8, 0, 9, 6, 3, 7, 4, 10, 5, 11, 2, 12, 1, 13, 14, 15),
+    (0, 10, 2, 5, 8, 6, 14, 3, 7, 1, 15, 12, 4, 13, 11, 9),
+    (2, 1, 7, 3, 4, 8, 13, 15, 6, 10, 9, 11, 12, 5, 14, 0),
+    (10, 1, 2, 5, 12, 15, 11, 0, 8, 4, 14, 3, 9, 13, 6, 7),
+    (6, 3, 7, 9, 10, 13, 4, 14, 0, 1, 2, 11, 12, 15, 5, 8),
+    (3, 8, 0, 12, 10, 14, 4, 15, 6, 9, 2, 5, 11, 1, 13, 7),
+    (10, 2, 1, 5, 3, 0, 14, 7, 8, 13, 9, 11, 12, 6, 4, 15),
+    (12, 8, 9, 10, 3, 5, 0, 1, 15, 2, 14, 11, 4, 7, 6, 13),
+    (0, 7, 12, 11, 4, 6, 5, 13, 15, 9, 10, 8, 3, 14, 2, 1),
+    (0, 6, 15, 4, 10, 5, 12, 2, 7, 11, 1, 3, 8, 13, 14, 9),
+    (9, 10, 11, 13, 3, 15, 6, 7, 14, 2, 0, 12, 4, 1, 5, 8),
+    (0, 1, 7, 11, 4, 13, 14, 15, 8, 2, 6, 12, 3, 5, 10, 9),
+    (5, 3, 10, 4, 2, 13, 6, 15, 8, 9, 0, 11, 12, 7, 14, 1),
+)
+BLOCK_AT = tuple(tuple(row.index(m) for m in range(NWIN)) for row in LANDING)
+INNER = [(r, c) for r in range(1, NWIN) for c in range(1, NWIN) if r != c]
 
 AXES = ("x", "yh", "core", "yl", "z")
 SIZES = (4, 2, 2, 2, 8)
@@ -91,11 +112,12 @@
     )(scaled)
 
 
-def gram_kernel(meta, mine, same, other, out, late):
+def gram_kernel(meta, landing, mine, same, other, out, late):
     q = pl.program_id(0)
     c = meta[1]
-    at_same = 2 * q + c
-    at_other = 2 * q + 1 - c
+    i = meta[2]
+    at_same = landing[i, 2 * q + c]
+    at_other = landing[i, 2 * q + 1 - c]
     for k in range(HALF):
         pair = jnp.concatenate([same[0, k], other[0, k]], axis=1)
         tiles = lax.dot_general(
@@ -106,25 +128,25 @@
 
     @pl.when(q == 0)
     def _():
-        late[...] = out[0].reshape(HALF, BLK, BLK)
+        late[...] = out[landing[i, 0]].reshape(HALF, BLK, BLK)
 
 
 def gram_slots(meta, flipped, same, other):
-    def pick_half(q, meta):
+    def pick_half(q, meta, landing):
         return (jnp.where((q > meta[0]) | ((q == meta[0]) & (meta[1] == 0)), 0, 1), 0, 0)
 
     whole = (HALF, R, BLK)
     grid_spec = pltpu.PrefetchScalarGridSpec(
-        num_scalar_prefetch=1,
+        num_scalar_prefetch=2,
         grid=(NWIN // 2,),
         in_specs=[
             pl.BlockSpec((HALF, BLK, R), pick_half),
-            pl.BlockSpec((1,) + whole, lambda q, meta: (q, 0, 0, 0)),
-            pl.BlockSpec((1,) + whole, lambda q, meta: (q, 0, 0, 0)),
+            pl.BlockSpec((1,) + whole, lambda q, *_: (q, 0, 0, 0)),
+            pl.BlockSpec((1,) + whole, lambda q, *_: (q, 0, 0, 0)),
         ],
         out_specs=[
-            pl.BlockSpec((NWIN, ROWS, BLK), lambda q, meta: (0, 0, 0)),
-            pl.BlockSpec((HALF, BLK, BLK), lambda q, meta: (0, 0, 0)),
+            pl.BlockSpec((NWIN, ROWS, BLK), lambda q, *_: (0, 0, 0)),
+            pl.BlockSpec((HALF, BLK, BLK), lambda q, *_: (0, 0, 0)),
         ],
     )
     return pl.pallas_call(
@@ -135,7 +157,7 @@
             jax.ShapeDtypeStruct((HALF, BLK, BLK), jnp.float32),
         ],
         name="gram_slots",
-    )(meta, flipped, same, other)
+    )(meta, jnp.array(LANDING, jnp.int32), flipped, same, other)
 
 
 def panel_kernel(first, lead, late, out):
@@ -167,9 +189,9 @@
     )(scaled, lead, late)
 
 
-def place_kernel(meta, picks, slots, upper, lower, part):
+def place_kernel(meta, picks, block_at, slots, upper, lower, part):
     i = meta[2]
-    j = meta[3]
+    j = block_at[i, meta[3]]
     part[...] = jnp.zeros_like(part)
     for g in range(NWIN):
         base = g * GROUP + jnp.where(i < j, 0, HALF)
@@ -184,7 +206,7 @@
 def place_tiles(meta, picks, slots):
     shape = (SPAN // 2, SPAN, BLK, BLK)
     grid_spec = pltpu.PrefetchScalarGridSpec(
-        num_scalar_prefetch=2,
+        num_scalar_prefetch=3,
         grid=(1,),
         in_specs=[LOCAL],
         out_specs=[LOCAL] * 2,
@@ -195,7 +217,7 @@
         grid_spec=grid_spec,
         out_shape=[jax.ShapeDtypeStruct(shape, jnp.float32)] * 2,
         name="place_tiles",
-    )(meta, picks, slots)
+    )(meta, picks, jnp.array(BLOCK_AT, jnp.int32), slots)
 
 
 def strip_kernel(meta, picks, slots, strip):
@@ -248,7 +270,7 @@
     )(left, inverse)
 
 
-def update_kernel(meta, upper, lower, lefts, high, low, right, diag, chol, inverse, out):
+def update_kernel(meta, lefts, high, low, right, diag, chol, inverse, out):
     i = meta[2]
     j = meta[3]
     inside = (i > 0) & (j > 0)
@@ -256,16 +278,7 @@
     def spot(a, b):
         return (slice(a * BLK, (a + 1) * BLK), slice(b * BLK, (b + 1) * BLK))
 
-    @pl.when(inside & (i != j))
-    def _():
-        for a in range(SPAN):
-            for b in range(SPAN):
-                half = upper if a < SPAN // 2 else lower
-                out[spot(a, b)] = half[a % (SPAN // 2), b]
-
-    @pl.when(jnp.logical_not(inside) | (i == j))
-    def _():
-        out[...] = jnp.zeros_like(out)
+    out[...] = jnp.zeros_like(out)
 
     @pl.when(inside & (i == j))
     def _():
@@ -312,36 +325,48 @@
     )(meta, *operands)
 
 
-def finish_kernel(meta, base, upper, lower, out):
+def finish_kernel(meta, base, upper, lower, turned_upper, turned_lower, out):
+    a = pl.program_id(0)
     i = meta[2]
     j = meta[3]
     both = (i > 0) & (j > 0) & (i != j)
 
-    @pl.when(both)
-    def _():
+    def add(near):
         for b in range(SPAN):
-            half = upper if b < SPAN // 2 else lower
+            far = turned_upper if b < SPAN // 2 else turned_lower
             cols = slice(b * BLK, (b + 1) * BLK)
-            out[:, cols] = base[:, cols] + half[b % (SPAN // 2), 0].T
+            out[:, cols] = base[:, cols] + (near[0, b] + far[b % (SPAN // 2), 0].T)
+
+    @pl.when(both & (a < SPAN // 2))
+    def _():
+        add(upper)
+
+    @pl.when(both & (a >= SPAN // 2))
+    def _():
+        add(lower)
 
     @pl.when(jnp.logical_not(both))
     def _():
         out[...] = base[...]
 
 
-def finish(meta, base, upper, lower):
+def finish(meta, *operands):
     size = (SPAN * BLK, SPAN * BLK)
     rows = pl.BlockSpec((BLK, SPAN * BLK), lambda a, meta: (a, 0))
+    wide = pl.BlockSpec((1, SPAN, BLK, BLK), lambda a, meta: (a % (SPAN // 2), 0, 0, 0))
     tall = pl.BlockSpec((SPAN // 2, 1, BLK, BLK), lambda a, meta: (0, a, 0, 0))
     grid_spec = pltpu.PrefetchScalarGridSpec(
-        num_scalar_prefetch=1, grid=(SPAN,), in_specs=[rows, tall, tall], out_specs=rows
+        num_scalar_prefetch=1,
+        grid=(SPAN,),
+        in_specs=[rows, wide, wide, tall, tall],
+        out_specs=rows,
     )
     return pl.pallas_call(
         finish_kernel,
         grid_spec=grid_spec,
         out_shape=jax.ShapeDtypeStruct(size, jnp.float32),
         name="finish",
-    )(meta, base, upper, lower)
+    )(meta, *operands)
 
 
 def swap_pairs(size, bit):
@@ -410,8 +435,10 @@
     right = lax.ppermute(strip, AXES, everywhere)[None]
     copies = jnp.broadcast_to(strip, (NWIN,) + strip.shape)
     left = lax.all_to_all(copies, GC, 0, 0, tiled=True)
-    mirror_a = lax.ppermute(upper, AXES, everywhere)
-    mirror_b = lax.ppermute(lower, AXES, everywhere)
+    home = [(r * NWIN + LANDING[r][c], r * NWIN + c) for r, c in INNER]
+    across = [(r * NWIN + LANDING[r][c], c * NWIN + r) for r, c in INNER]
+    sums_a = [lax.ppermute(upper, AXES, pairs) for pairs in (across, home)]
+    sums_b = [lax.ppermute(lower, AXES, pairs) for pairs in (across, home)]
     for axis, pairs in (
         ("yh", swap_pairs(2, 1)),
         ("x", swap_pairs(4, 1)),
@@ -420,8 +447,8 @@
     ):
         right = jnp.concatenate([right, lax.ppermute(right, axis, pairs)], axis=0)
     lefts, high, low = solve_rows(left, inverse)
-    base = update(meta, upper, lower, lefts, high, low, right, diag, chol, inverse)
-    return finish(meta, base, mirror_a, mirror_b)
+    base = update(meta, lefts, high, low, right, diag, chol, inverse)
+    return finish(meta, base, sums_a[1], sums_b[1], sums_a[0], sums_b[0])
 
 
 def solution(mesh):

time: 365 us -> 386 us (1.058)
  the two profiles are of different devices: /device:TPU:66 before, /device:TPU:65 now
where the time goes in v7:
time: 386 us; the launch traced here: 384 us
  waiting for transfers between devices  207 us (54%)
  starting transfers between devices  95.2 us (25%)
  Pallas kernels  61.2 us (16%)
  other arithmetic  15.6 us (4%)
    ppermute x3, waiting for transfers between devices, spread(): return v + lax.ppermute(v, step, [(0, 1)])  36.8 us
    ppermute x2, waiting for transfers between devices, body(): sums_b = [lax.ppermute(lower, AXES, pairs) for pairs in (across, home)]  33 us
    ppermute x2, waiting for transfers between devices, body(): sums_a = [lax.ppermute(upper, AXES, pairs) for pairs in (across, home)]  32.6 us
    all_to_all x1, waiting for transfers between devices, body(): same = lax.all_to_all(slots, ('x', 'yh'), 0, 0, tiled=True)  30.7 us
    ppermute x1, waiting for transfers between devices, body(): right = lax.ppermute(strip, AXES, everywhere)[None]  23.7 us
    pallas_call x1, Pallas kernels, factor(): pl.pallas_call(factor_kernel, in_specs=[LOCAL], out_specs=[LOCAL] * 2, ou...  21 us
    ppermute x3, waiting for transfers between devices, body(): diag = diag + lax.ppermute(diag, 'z', swap_pairs(8, bit))  19.2 us
    ppermute x3, starting transfers between devices, spread(): return v + lax.ppermute(v, step, [(0, 1)])  11 us
  transfers between devices with their start and end apart: 29, of which 20 were waited for; matrix products, arithmetic and copies ran while one was open for 3% of the time, Pallas kernels for 11%

profile of v7, /device:TPU:65, one launch (start us, length us, event | category | flops | bytes accessed | tf_op | source)
XLA Modules:
  0.0 383.7 jit_solution(2679327256364942086)
XLA Ops:
  0.0 0.8 sqrt.3
  0.8 1.9 multiply_convert_fusion.scaled.first
  2.8 2.8 broadcast_select_fusion
  5.6 6.8 %all-to-all-start = ((bf16[8,3,768,128]{3,2,1,0:T(8,128)(2,1)}), bf16[8,3,768,128]{3,2,1,0:T(8,128)(2,1)}, u32[]{:S(2)}, u32[]{:S(2)}) async-start(bf16[8,3,768,128]{3,2,1,0:T(8,128)(2,1)} %broadcast_select_fusion), calls=%async_computation | async-start | bytes 9437184 | tf_op jit(solution)/shard_map/all_to_all | solution.py:402
  13.2 1.7 collective-permute-start
  15.0 1.3 collective-permute-start.3
  16.3 4.4 %collective-permute-done = f32[4,128,128]{2,1,0:T(8,128)S(1)} collective-permute-done((f32[4,128,128]{2,1,0:T(8,128)S(1)}, f32[4,128,128]{2,1,0:T(8,128)S(1)}, u32[]{:S(2)}, u32[]{:S(2)}) %collective-permute-start) | collective-permute-done | bytes 262176 | tf_op jit(solution)/shard_map/ppermute | solution.py:397
  20.8 10.6 %collective-permute-done.1 = f32[4,128,128]{2,1,0:T(8,128)S(1)} collective-permute-done((f32[4,128,128]{2,1,0:T(8,128)S(1)}, f32[4,128,128]{2,1,0:T(8,128)S(1)}, u32[]{:S(2)}, u32[]{:S(2)}) %collective-permute-start.1) | collective-permute-done | bytes 262176 | tf_op jit(solution)/shard_map/ppermute | solution.py:397
  31.5 6.6 %collective-permute-start.2 = (f32[4,128,128]{2,1,0:T(8,128)S(1)}, f32[4,128,128]{2,1,0:T(8,128)S(1)}, u32[]{:S(2)}, u32[]{:S(2)}) collective-permute-start(f32[4,128,128]{2,1,0:T(8,128)S(1)} %add.75), channel_id=1, source_target_pairs={{0,4},{1,5},{2,6},{3,7},{4,0},{5,1},{6,2},{7,3},{8,12},{9,13},{10,... | collective-permute-start | bytes 786440 | tf_op jit(solution)/shard_map/ppermute | solution.py:397
  38.1 4.6 %flip.1.mine = bf16[6,128,768]{2,1,0:T(8,128)(2,1)} custom-call(bf16[6,768,128]{2,1,0:T(8,128)(2,1)} %copy-done.1), custom_call_target="tpu_custom_call" | custom-call | tf_op jit(solution)/shard_map/flip/pallas_call | solution.py:105
  42.7 4.2 %collective-permute-done.2 = f32[4,128,128]{2,1,0:T(8,128)S(1)} collective-permute-done((f32[4,128,128]{2,1,0:T(8,128)S(1)}, f32[4,128,128]{2,1,0:T(8,128)S(1)}, u32[]{:S(2)}, u32[]{:S(2)}) %collective-permute-start.2) | collective-permute-done | bytes 262176 | tf_op jit(solution)/shard_map/ppermute | solution.py:397
  46.9 0.7 add.76
  47.7 30.7 %all-to-all-done.same = bf16[8,3,768,128]{3,2,1,0:T(8,128)(2,1)} async-done(((bf16[8,3,768,128]{3,2,1,0:T(8,128)(2,1)}), bf16[8,3,768,128]{3,2,1,0:T(8,128)(2,1)}, u32[]{:S(2)}, u32[]{:S(2)}) %all-to-all-start) | async-done | bytes 4718624 | tf_op jit(solution)/shard_map/all_to_all | solution.py:402
  78.4 1.6 collective-permute-start.4
  80.5 7.3 %collective-permute-done.4.other = bf16[8,3,768,128]{3,2,1,0:T(8,128)(2,1)} collective-permute-done((bf16[8,3,768,128]{3,2,1,0:T(8,128)(2,1)}, bf16[8,3,768,128]{3,2,1,0:T(8,128)(2,1)}, u32[]{:S(2)}, u32[]{:S(2)}) %collective-permute-start.4) | collective-permute-done | bytes 4718624 | tf_op jit(solution)/shard_map/ppermute | solution.py:409
  87.8 10.0 %gram_slots.1 = (f32[16,384,128]{2,1,0:T(8,128)}, f32[3,128,128]{2,1,0:T(8,128)}) custom-call(s32[4]{0:T(128)} %pad_add_fusion.meta, s32[16,16]{1,0:T(8,128)} %constant.71.clone.landing, bf16[6,128,768]{2,1,0:T(8,128)(2,1)} %flip.1.mine, bf16[8,3,768,128]{3,2,1,0:T(8,128)(2,1)} %all-to-all-done.same, bf16[8,3,768,128]{3,2,1,0:T(8,128)(2,1)} %collective-permute-done.4.other), custom_call_target="tpu_custom_call" | custom-call | tf_op jit(solution)/shard_map/gram_slots/pallas_call | solution.py:152
  97.8 7.7 %all-to-all-start.1 = ((f32[16,384,128]{2,1,0:T(8,128)}), f32[16,384,128]{2,1,0:T(8,128)S(1)}, u32[]{:S(2)}, u32[]{:S(2)}) async-start(f32[16,384,128]{2,1,0:T(8,128)} %get-tuple-element.26), calls=%async_computation.1 | async-start | bytes 6291456 | tf_op jit(solution)/shard_map/all_to_all | solution.py:421
  105.5 5.2 %collective-permute-start.5 = (bf16[3,384,128]{2,1,0:T(8,128)(2,1)S(1)}, bf16[3,384,128]{2,1,0:T(8,128)(2,1)}, u32[]{:S(2)}, u32[]{:S(2)}) collective-permute-start(bf16[3,384,128]{2,1,0:T(8,128)(2,1)S(1)} %slice_add_fusion), channel_id=1, source_target_pairs={{0,32},{1,33},{2,34},{3,35},{4,36},{5,37},{6,38},{7,39},{8,40},{9,... | collective-permute-start | bytes 884744 | tf_op jit(solution)/shard_map/ppermute | solution.py:378
  111.4 17.0 %collective-permute-done.5 = bf16[3,384,128]{2,1,0:T(8,128)(2,1)} collective-permute-done((bf16[3,384,128]{2,1,0:T(8,128)(2,1)S(1)}, bf16[3,384,128]{2,1,0:T(8,128)(2,1)}, u32[]{:S(2)}, u32[]{:S(2)}) %collective-permute-start.5) | collective-permute-done | bytes 294944 | tf_op jit(solution)/shard_map/ppermute | solution.py:378
  128.4 1.0 add.78
  129.4 1.3 collective-permute-start.6
  130.8 2.8 collective-permute-start.7
  133.6 2.5 collective-permute-done.10
  136.0 1.8 broadcast_select_fusion.4
  137.8 1.3 collective-permute-start.11
  139.1 2.4 collective-permute-done.11
  141.5 4.5 %collective-permute-start.12 = (f32[4,128,128]{2,1,0:T(8,128)S(1)}, f32[4,128,128]{2,1,0:T(8,128)S(1)}, u32[]{:S(2)}, u32[]{:S(2)}) collective-permute-start(f32[4,128,128]{2,1,0:T(8,128)S(1)} %add.85), channel_id=1, source_target_pairs={{0,32},{1,33},{2,34},{3,35},{4,36},{5,37},{6,38},{7,39},{8,40},{9,... | collective-permute-start | bytes 786440 | tf_op jit(solution)/shard_map/ppermute | solution.py:378
  146.8 17.4 %collective-permute-done.12 = f32[4,128,128]{2,1,0:T(8,128)S(1)} collective-permute-done((f32[4,128,128]{2,1,0:T(8,128)S(1)}, f32[4,128,128]{2,1,0:T(8,128)S(1)}, u32[]{:S(2)}, u32[]{:S(2)}) %collective-permute-start.12) | collective-permute-done | bytes 262176 | tf_op jit(solution)/shard_map/ppermute | solution.py:378
  164.9 2.0 collective-permute-start.13
  166.9 3.2 collective-permute-start.14
  170.2 0.9 collective-permute-start.9
  171.1 0.9 collective-permute-done.13
  172.0 2.8 collective-permute-done.14
  174.8 1.9 add_add_fusion.1
  176.7 1.4 collective-permute-start.15
  178.0 1.0 broadcast_select_fusion.3
  179.0 0.9 pad_maximum_fusion.lead
  179.9 2.4 panel_slots.1
  182.3 1.8 add.89.corner
  184.1 21.0 %factor.1 = (f32[4,128,128]{2,1,0:T(8,128)}, f32[4,128,128]{2,1,0:T(8,128)}) custom-call(f32[4,128,128]{2,1,0:T(8,128)} %add.89.corner), custom_call_target="tpu_custom_call" | custom-call | tf_op jit(solution)/shard_map/factor/pallas_call | solution.py:90
  205.1 6.3 %all-to-all-start.2 = ((f32[16,48,128]{2,1,0:T(8,128)}), f32[16,48,128]{2,1,0:T(8,128)}, u32[]{:S(2)}, u32[]{:S(2)}) async-start(f32[16,48,128]{2,1,0:T(8,128)} %panel_slots.1), calls=%async_computation.2 | async-start | bytes 786432 | tf_op jit(solution)/shard_map/all_to_all | solution.py:432
  212.1 8.6 %all-to-all-done.2.slots = f32[16,48,128]{2,1,0:T(8,128)} async-done(((f32[16,48,128]{2,1,0:T(8,128)}), f32[16,48,128]{2,1,0:T(8,128)}, u32[]{:S(2)}, u32[]{:S(2)}) %all-to-all-start.2) | async-done | bytes 393248 | tf_op jit(solution)/shard_map/all_to_all | solution.py:432
  220.7 3.6 place_strip.1
  224.3 2.0 broadcast_in_dim.73
  226.3 7.7 %all-to-all-start.3 = ((f32[16,4,4,8,128]{4,3,2,1,0:T(8,128)}), f32[16,4,4,8,128]{4,3,2,1,0:T(8,128)}, u32[]{:S(2)}, u32[]{:S(2)}) async-start(f32[16,4,4,8,128]{4,3,2,1,0:T(8,128)} %broadcast_in_dim.73), calls=%async_computation.3 | async-start | bytes 2097152 | tf_op jit(solution)/shard_map/all_to_all | solution.py:437
  234.0 8.6 %collective-permute-start.16 = (f32[4,4,8,128]{3,2,1,0:T(8,128)S(1)}, f32[4,4,8,128]{3,2,1,0:T(8,128)S(1)}, u32[]{:S(2)}, u32[]{:S(2)}) collective-permute-start(f32[4,4,8,128]{3,2,1,0:T(8,128)S(1)} %copy-done.7), channel_id=1, source_target_pairs={{0,0},{1,16},{2,32},{3,48},{4,64},{5,80},{6,96},{7,112},{8,128},{9... | collective-permute-start | bytes 196616 | tf_op jit(solution)/shard_map/ppermute | solution.py:435
  242.5 23.7 %collective-permute-done.16 = f32[4,4,8,128]{3,2,1,0:T(8,128)S(1)} collective-permute-done((f32[4,4,8,128]{3,2,1,0:T(8,128)S(1)}, f32[4,4,8,128]{3,2,1,0:T(8,128)S(1)}, u32[]{:S(2)}, u32[]{:S(2)}) %collective-permute-start.16) | collective-permute-done | bytes 65568 | tf_op jit(solution)/shard_map/ppermute | solution.py:435
  266.3 4.6 %collective-permute-done.17 = f32[1,4,4,8,128]{4,3,2,1,0:T(8,128)S(1)} collective-permute-done((f32[1,4,4,8,128]{4,3,2,1,0:T(8,128)S(1)}, f32[1,4,4,8,128]{4,3,2,1,0:T(8,128)S(1)}, u32[]{:S(2)}, u32[]{:S(2)}) %collective-permute-start.17) | collective-permute-done | bytes 65568 | tf_op jit(solution)/shard_map/ppermute | solution.py:448
  270.9 3.2 collective-permute-start.18
  274.1 2.4 collective-permute-done.18
  276.4 2.8 collective-permute-start.19
  279.2 5.1 %place_tiles.1 = (f32[2,4,128,128]{3,2,1,0:T(8,128)}, f32[2,4,128,128]{3,2,1,0:T(8,128)}) custom-call(s32[4]{0:T(128)} %pad_add_fusion.meta, s32[96,16]{1,0:T(8,128)} %copy.11.picks, s32[16,16]{1,0:T(8,128)} %constant.72.clone.block_at, f32[16,384,128]{2,1,0:T(8,128)} %copy-done.2), custom_call_target="tpu_custom_call" | custom-call | tf_op jit(solution)/shard_map/place_tiles/pallas_call | solution.py:215
  284.3 1.9 collective-permute-start.21
  286.2 5.6 %collective-permute-start.23 = (f32[2,4,128,128]{3,2,1,0:T(8,128)}, f32[2,4,128,128]{3,2,1,0:T(8,128)S(1)}, u32[]{:S(2)}, u32[]{:S(2)}) collective-permute-start(f32[2,4,128,128]{3,2,1,0:T(8,128)} %get-tuple-element.41), channel_id=1, source_target_pairs={{16,33},{29,49},{22,65},{25,81},{28,97},{26,113},{18,129},{17,145}... | collective-permute-start | bytes 1572872 | tf_op jit(solution)/shard_map/ppermute | solution.py:440
  291.8 1.9 collective-permute-start.22
  293.7 7.7 %collective-permute-start.24 = (f32[2,4,128,128]{3,2,1,0:T(8,128)}, f32[2,4,128,128]{3,2,1,0:T(8,128)}, u32[]{:S(2)}, u32[]{:S(2)}) collective-permute-start(f32[2,4,128,128]{3,2,1,0:T(8,128)} %get-tuple-element.42), channel_id=1, source_target_pairs={{16,33},{29,49},{22,65},{25,81},{28,97},{26,113},{18,129},{17,145}... | collective-permute-start | bytes 1572872 | tf_op jit(solution)/shard_map/ppermute | solution.py:441
  301.7 1.8 collective-permute-done.20
  303.6 4.0 %solve_rows.1 = (f32[512,512]{1,0:T(8,128)}, bf16[512,512]{1,0:T(8,128)(2,1)}, bf16[512,512]{1,0:T(8,128)(2,1)}) custom-call(f32[16,4,4,8,128]{4,3,2,1,0:T(8,128)} %all-to-all-done.3.left, f32[4,128,128]{2,1,0:T(8,128)} %get-tuple-element.35.inverse), custom_call_target="tpu_custom_call" | custom-call | tf_op jit(solution)/shard_map/solve_rows/pallas_call | solution.py:264
  307.6 5.7 %update.1.base = f32[512,512]{1,0:T(8,128)} custom-call(s32[4]{0:T(128)} %pad_add_fusion.meta, f32[512,512]{1,0:T(8,128)} %get-tuple-element.36.lefts, bf16[512,512]{1,0:T(8,128)(2,1)} %get-tuple-element.37.high, bf16[512,512]{1,0:T(8,128)(2,1)} %get-tuple-element.38.low, f32[16,4,4,8,128]{4,3,2,1,0:T(8,128)} %copy-done.3, ...), custom_call_target="tpu_custom_call" | custom-call | tf_op jit(solution)/shard_map/update/pallas_call | solution.py:320
  313.3 4.5 %collective-permute-done.21.upper = f32[2,4,128,128]{3,2,1,0:T(8,128)S(1)} collective-permute-done((f32[2,4,128,128]{3,2,1,0:T(8,128)}, f32[2,4,128,128]{3,2,1,0:T(8,128)S(1)}, u32[]{:S(2)}, u32[]{:S(2)}) %collective-permute-start.21) | collective-permute-done | bytes 524320 | tf_op jit(solution)/shard_map/ppermute | solution.py:440
  317.8 13.6 %collective-permute-done.22.lower = f32[2,4,128,128]{3,2,1,0:T(8,128)S(1)} collective-permute-done((f32[2,4,128,128]{3,2,1,0:T(8,128)}, f32[2,4,128,128]{3,2,1,0:T(8,128)S(1)}, u32[]{:S(2)}, u32[]{:S(2)}) %collective-permute-start.22) | collective-permute-done | bytes 524320 | tf_op jit(solution)/shard_map/ppermute | solution.py:441
  331.3 28.1 %collective-permute-done.23.turned_upper = f32[2,4,128,128]{3,2,1,0:T(8,128)S(1)} collective-permute-done((f32[2,4,128,128]{3,2,1,0:T(8,128)}, f32[2,4,128,128]{3,2,1,0:T(8,128)S(1)}, u32[]{:S(2)}, u32[]{:S(2)}) %collective-permute-start.23) | collective-permute-done | bytes 524320 | tf_op jit(solution)/shard_map/ppermute | solution.py:440
  359.5 19.4 %collective-permute-done.24.turned_lower = f32[2,4,128,128]{3,2,1,0:T(8,128)} collective-permute-done((f32[2,4,128,128]{3,2,1,0:T(8,128)}, f32[2,4,128,128]{3,2,1,0:T(8,128)}, u32[]{:S(2)}, u32[]{:S(2)}) %collective-permute-start.24) | collective-permute-done | bytes 524320 | tf_op jit(solution)/shard_map/ppermute | solution.py:441
  378.9 4.8 %finish.1 = f32[512,512]{1,0:T(8,128)} custom-call(s32[4]{0:T(128)} %pad_add_fusion.meta, f32[512,512]{1,0:T(8,128)} %update.1.base, f32[2,4,128,128]{3,2,1,0:T(8,128)} %copy-done.4, f32[2,4,128,128]{3,2,1,0:T(8,128)} %copy-done.6, f32[2,4,128,128]{3,2,1,0:T(8,128)} %copy-done.5, f32[2,4,128,128]{3,2,1,0:T(8,128)} %collective-permute-done.24.turned_lower), custom_call_target="tpu_custom_call" | custom-call | tf_op jit(solution)/shard_map/finish/pallas_call | solution.py:364
  (58 shorter events, 5.0 us)
Async XLA Ops:
  0.0 111.3 %copy-start = (f32[8192]{0:T(1024)S(1)}, f32[8192]{0:T(1024)}, u32[]{:S(2)}) copy-start(f32[8192]{0:T(1024)} %param.9) | copy-start | bytes 98308
  2.6 9.9 %copy-start.1 = (bf16[6,768,128]{2,1,0:T(8,128)(2,1)}, bf16[6,768,128]{2,1,0:T(8,128)(2,1)S(1)}, u32[]{:S(2)}) copy-start(bf16[6,768,128]{2,1,0:T(8,128)(2,1)S(1)} %multiply_convert_fusion.scaled.first) | copy-start | bytes 3538948
  5.6 6.8 %copy-start.8 = (s32[96,16]{0,1:T(8,128)S(1)}, s32[96,16]{0,1:T(8,128)}, u32[]{:S(2)}) copy-start(s32[96,16]{0,1:T(8,128)} %param.8) | copy-start | bytes 18436
  5.6 72.8 %all-to-all-start = ((bf16[8,3,768,128]{3,2,1,0:T(8,128)(2,1)}), bf16[8,3,768,128]{3,2,1,0:T(8,128)(2,1)}, u32[]{:S(2)}, u32[]{:S(2)}) async-start(bf16[8,3,768,128]{3,2,1,0:T(8,128)(2,1)} %broadcast_select_fusion), calls=%async_computation | async-start | bytes 9437184 | tf_op jit(solution)/shard_map/all_to_all | solution.py:402
  13.2 7.5 %collective-permute-start = (f32[4,128,128]{2,1,0:T(8,128)S(1)}, f32[4,128,128]{2,1,0:T(8,128)S(1)}, u32[]{:S(2)}, u32[]{:S(2)}) collective-permute-start(f32[4,128,128]{2,1,0:T(8,128)S(1)} %select_reduce_fusion), channel_id=1, source_target_pairs={{0,1},{1,0},{2,3},{3,2},{4,5},{5,4},{6,7},{7,6},{8,9},{9,8},{10,11... | collective-permute-start | bytes 786440 | tf_op jit(solution)/shard_map/ppermute | solution.py:397
  15.0 27.7 %collective-permute-start.3 = (bf16[3,384,128]{2,1,0:T(8,128)(2,1)S(1)}, bf16[3,384,128]{2,1,0:T(8,128)(2,1)S(1)}, u32[]{:S(2)}, u32[]{:S(2)}) collective-permute-start(bf16[3,384,128]{2,1,0:T(8,128)(2,1)S(1)} %slice.20), channel_id=1, source_target_pairs={{0,16},{1,17},{2,18},{3,19},{4,20},{5,21},{6,22},{7,23},{8,24},{9,... | collective-permute-start | bytes 884744 | tf_op jit(solution)/shard_map/ppermute | solution.py:405
  20.7 10.7 %collective-permute-start.1 = (f32[4,128,128]{2,1,0:T(8,128)S(1)}, f32[4,128,128]{2,1,0:T(8,128)S(1)}, u32[]{:S(2)}, u32[]{:S(2)}) collective-permute-start(f32[4,128,128]{2,1,0:T(8,128)S(1)} %add.74), channel_id=1, source_target_pairs={{0,2},{1,3},{2,0},{3,1},{4,6},{5,7},{6,4},{7,5},{8,10},{9,11},{10,... | collective-permute-start | bytes 786440 | tf_op jit(solution)/shard_map/ppermute | solution.py:397
  31.5 15.4 %collective-permute-start.2 = (f32[4,128,128]{2,1,0:T(8,128)S(1)}, f32[4,128,128]{2,1,0:T(8,128)S(1)}, u32[]{:S(2)}, u32[]{:S(2)}) collective-permute-start(f32[4,128,128]{2,1,0:T(8,128)S(1)} %add.75), channel_id=1, source_target_pairs={{0,4},{1,5},{2,6},{3,7},{4,0},{5,1},{6,2},{7,3},{8,12},{9,13},{10,... | collective-permute-start | bytes 786440 | tf_op jit(solution)/shard_map/ppermute | solution.py:397
  78.4 9.4 %collective-permute-start.4 = (bf16[8,3,768,128]{3,2,1,0:T(8,128)(2,1)}, bf16[8,3,768,128]{3,2,1,0:T(8,128)(2,1)}, u32[]{:S(2)}, u32[]{:S(2)}) collective-permute-start(bf16[8,3,768,128]{3,2,1,0:T(8,128)(2,1)} %all-to-all-done.same), channel_id=1, source_target_pairs={{0,16},{16,0},{1,17},{17,1},{2,18},{18,2},{3,19},{19,3},{4,20},{20... | collective-permute-start | bytes 14155784 | tf_op jit(solution)/shard_map/ppermute | solution.py:409
  97.8 107.3 %all-to-all-start.1 = ((f32[16,384,128]{2,1,0:T(8,128)}), f32[16,384,128]{2,1,0:T(8,128)S(1)}, u32[]{:S(2)}, u32[]{:S(2)}) async-start(f32[16,384,128]{2,1,0:T(8,128)} %get-tuple-element.26), calls=%async_computation.1 | async-start | bytes 6291456 | tf_op jit(solution)/shard_map/all_to_all | solution.py:421
  105.5 22.9 %collective-permute-start.5 = (bf16[3,384,128]{2,1,0:T(8,128)(2,1)S(1)}, bf16[3,384,128]{2,1,0:T(8,128)(2,1)}, u32[]{:S(2)}, u32[]{:S(2)}) collective-permute-start(bf16[3,384,128]{2,1,0:T(8,128)(2,1)S(1)} %slice_add_fusion), channel_id=1, source_target_pairs={{0,32},{1,33},{2,34},{3,35},{4,36},{5,37},{6,38},{7,39},{8,40},{9,... | collective-permute-start | bytes 884744 | tf_op jit(solution)/shard_map/ppermute | solution.py:378
  110.7 25.4 %collective-permute-start.10 = (f32[4,128,128]{2,1,0:T(8,128)}, f32[4,128,128]{2,1,0:T(8,128)}, u32[]{:S(2)}, u32[]{:S(2)}) collective-permute-start(f32[4,128,128]{2,1,0:T(8,128)} %add.76), channel_id=1, source_target_pairs={{0,8},{8,0},{1,9},{9,1},{2,10},{10,2},{3,11},{11,3},{4,12},{12,4},... | collective-permute-start | bytes 786440 | tf_op jit(solution)/shard_map/ppermute | solution.py:410
  129.4 16.6 %collective-permute-start.6 = (bf16[3,384,128]{2,1,0:T(8,128)(2,1)S(1)}, bf16[3,384,128]{2,1,0:T(8,128)(2,1)S(1)}, u32[]{:S(2)}, u32[]{:S(2)}) collective-permute-start(bf16[3,384,128]{2,1,0:T(8,128)(2,1)S(1)} %add.78), channel_id=1, source_target_pairs={{0,64},{1,65},{2,66},{3,67},{4,68},{5,69},{6,70},{7,71},{8,72},{9,... | collective-permute-start | bytes 884744 | tf_op jit(solution)/shard_map/ppermute | solution.py:379
  130.8 15.3 %collective-permute-start.7 = (bf16[3,384,128]{2,1,0:T(8,128)(2,1)S(1)}, bf16[3,384,128]{2,1,0:T(8,128)(2,1)S(1)}, u32[]{:S(2)}, u32[]{:S(2)}) collective-permute-start(bf16[3,384,128]{2,1,0:T(8,128)(2,1)S(1)} %add.78), channel_id=1, source_target_pairs={{0,192},{1,193},{2,194},{3,195},{4,196},{5,197},{6,198},{7,199},{8... | collective-permute-start | bytes 884744 | tf_op jit(solution)/shard_map/ppermute | solution.py:379
  137.8 3.7 collective-permute-start.11
  141.5 22.7 %collective-permute-start.12 = (f32[4,128,128]{2,1,0:T(8,128)S(1)}, f32[4,128,128]{2,1,0:T(8,128)S(1)}, u32[]{:S(2)}, u32[]{:S(2)}) collective-permute-start(f32[4,128,128]{2,1,0:T(8,128)S(1)} %add.85), channel_id=1, source_target_pairs={{0,32},{1,33},{2,34},{3,35},{4,36},{5,37},{6,38},{7,39},{8,40},{9,... | collective-permute-start | bytes 786440 | tf_op jit(solution)/shard_map/ppermute | solution.py:378
  146.1 24.0 %collective-permute-start.8 = (bf16[3,384,128]{2,1,0:T(8,128)(2,1)S(1)}, bf16[3,384,128]{2,1,0:T(8,128)(2,1)S(1)}, u32[]{:S(2)}, u32[]{:S(2)}) collective-permute-start(bf16[3,384,128]{2,1,0:T(8,128)(2,1)S(1)} %add_add_fusion), channel_id=1, source_target_pairs={{64,128},{65,129},{66,130},{67,131},{68,132},{69,133},{70,134},{71... | collective-permute-start | bytes 884744 | tf_op jit(solution)/shard_map/ppermute | solution.py:380
  164.9 7.0 %collective-permute-start.13 = (f32[4,128,128]{2,1,0:T(8,128)}, f32[4,128,128]{2,1,0:T(8,128)}, u32[]{:S(2)}, u32[]{:S(2)}) collective-permute-start(f32[4,128,128]{2,1,0:T(8,128)} %add.86), channel_id=1, source_target_pairs={{0,64},{1,65},{2,66},{3,67},{4,68},{5,69},{6,70},{7,71},{8,72},{9,... | collective-permute-start | bytes 786440 | tf_op jit(solution)/shard_map/ppermute | solution.py:379
  166.9 7.9 %collective-permute-start.14 = (f32[4,128,128]{2,1,0:T(8,128)}, f32[4,128,128]{2,1,0:T(8,128)}, u32[]{:S(2)}, u32[]{:S(2)}) collective-permute-start(f32[4,128,128]{2,1,0:T(8,128)} %add.86), channel_id=1, source_target_pairs={{0,192},{1,193},{2,194},{3,195},{4,196},{5,197},{6,198},{7,199},{8... | collective-permute-start | bytes 786440 | tf_op jit(solution)/shard_map/ppermute | solution.py:379
  170.2 7.9 %collective-permute-start.9 = (bf16[3,384,128]{2,1,0:T(8,128)(2,1)S(1)}, bf16[3,384,128]{2,1,0:T(8,128)(2,1)}, u32[]{:S(2)}, u32[]{:S(2)}) collective-permute-start(bf16[3,384,128]{2,1,0:T(8,128)(2,1)S(1)} %add.81), channel_id=1, source_target_pairs={{0,16},{16,0},{1,17},{17,1},{2,18},{18,2},{3,19},{19,3},{4,20},{20... | collective-permute-start | bytes 884744 | tf_op jit(solution)/shard_map/ppermute | solution.py:424
  176.7 5.6 %collective-permute-start.15 = (f32[4,128,128]{2,1,0:T(8,128)}, f32[4,128,128]{2,1,0:T(8,128)}, u32[]{:S(2)}, u32[]{:S(2)}) collective-permute-start(f32[4,128,128]{2,1,0:T(8,128)} %add_add_fusion.1), channel_id=1, source_target_pairs={{64,128},{65,129},{66,130},{67,131},{68,132},{69,133},{70,134},{71... | collective-permute-start | bytes 786440 | tf_op jit(solution)/shard_map/ppermute | solution.py:380
  205.1 21.2 %copy-start.2 = (f32[16,384,128]{2,1,0:T(8,128)}, f32[16,384,128]{2,1,0:T(8,128)S(1)}, u32[]{:S(2)}) copy-start(f32[16,384,128]{2,1,0:T(8,128)S(1)} %all-to-all-done.1.slots) | copy-start | bytes 9437188
  205.1 15.6 %all-to-all-start.2 = ((f32[16,48,128]{2,1,0:T(8,128)}), f32[16,48,128]{2,1,0:T(8,128)}, u32[]{:S(2)}, u32[]{:S(2)}) async-start(f32[16,48,128]{2,1,0:T(8,128)} %panel_slots.1), calls=%async_computation.2 | async-start | bytes 786432 | tf_op jit(solution)/shard_map/all_to_all | solution.py:432
  224.3 9.7 %copy-start.7 = (f32[4,4,8,128]{3,2,1,0:T(8,128)S(1)}, f32[4,4,8,128]{3,2,1,0:T(8,128)}, u32[]{:S(2)}) copy-start(f32[4,4,8,128]{3,2,1,0:T(8,128)} %place_strip.1) | copy-start | bytes 196612
  226.3 77.3 %all-to-all-start.3 = ((f32[16,4,4,8,128]{4,3,2,1,0:T(8,128)}), f32[16,4,4,8,128]{4,3,2,1,0:T(8,128)}, u32[]{:S(2)}, u32[]{:S(2)}) async-start(f32[16,4,4,8,128]{4,3,2,1,0:T(8,128)} %broadcast_in_dim.73), calls=%async_computation.3 | async-start | bytes 2097152 | tf_op jit(solution)/shard_map/all_to_all | solution.py:437
  234.0 32.3 %collective-permute-start.16 = (f32[4,4,8,128]{3,2,1,0:T(8,128)S(1)}, f32[4,4,8,128]{3,2,1,0:T(8,128)S(1)}, u32[]{:S(2)}, u32[]{:S(2)}) collective-permute-start(f32[4,4,8,128]{3,2,1,0:T(8,128)S(1)} %copy-done.7), channel_id=1, source_target_pairs={{0,0},{1,16},{2,32},{3,48},{4,64},{5,80},{6,96},{7,112},{8,128},{9... | collective-permute-start | bytes 196616 | tf_op jit(solution)/shard_map/ppermute | solution.py:435
  266.3 4.6 %collective-permute-start.17 = (f32[1,4,4,8,128]{4,3,2,1,0:T(8,128)S(1)}, f32[1,4,4,8,128]{4,3,2,1,0:T(8,128)S(1)}, u32[]{:S(2)}, u32[]{:S(2)}) collective-permute-start(f32[1,4,4,8,128]{4,3,2,1,0:T(8,128)S(1)} %bitcast.12), channel_id=1, source_target_pairs={{0,32},{32,0},{1,33},{33,1},{2,34},{34,2},{3,35},{35,3},{4,36},{36... | collective-permute-start | bytes 196616 | tf_op jit(solution)/shard_map/ppermute | solution.py:448
  270.9 5.5 %collective-permute-start.18 = (f32[2,4,4,8,128]{4,3,2,1,0:T(8,128)S(1)}, f32[2,4,4,8,128]{4,3,2,1,0:T(8,128)S(1)}, u32[]{:S(2)}, u32[]{:S(2)}) collective-permute-start(f32[2,4,4,8,128]{4,3,2,1,0:T(8,128)S(1)} %pad_maximum_fusion.3), channel_id=1, source_target_pairs={{0,64},{64,0},{128,192},{192,128},{1,65},{65,1},{129,193},{193,129... | collective-permute-start | bytes 393224 | tf_op jit(solution)/shard_map/ppermute | solution.py:448
  276.4 25.0 %collective-permute-start.19 = (f32[4,4,4,8,128]{4,3,2,1,0:T(8,128)S(1)}, f32[4,4,4,8,128]{4,3,2,1,0:T(8,128)S(1)}, u32[]{:S(2)}, u32[]{:S(2)}) collective-permute-start(f32[4,4,4,8,128]{4,3,2,1,0:T(8,128)S(1)} %pad_maximum_fusion.2), channel_id=1, source_target_pairs={{0,192},{64,128},{128,64},{192,0},{1,193},{65,129},{129,65},{193,1... | collective-permute-start | bytes 786440 | tf_op jit(solution)/shard_map/ppermute | solution.py:448
  284.3 33.5 %collective-permute-start.21 = (f32[2,4,128,128]{3,2,1,0:T(8,128)}, f32[2,4,128,128]{3,2,1,0:T(8,128)S(1)}, u32[]{:S(2)}, u32[]{:S(2)}) collective-permute-start(f32[2,4,128,128]{3,2,1,0:T(8,128)} %get-tuple-element.41), channel_id=1, source_target_pairs={{16,18},{29,19},{22,20},{25,21},{28,22},{26,23},{18,24},{17,25},{2... | collective-permute-start | bytes 1572872 | tf_op jit(solution)/shard_map/ppermute | solution.py:440
  286.2 73.3 %collective-permute-start.23 = (f32[2,4,128,128]{3,2,1,0:T(8,128)}, f32[2,4,128,128]{3,2,1,0:T(8,128)S(1)}, u32[]{:S(2)}, u32[]{:S(2)}) collective-permute-start(f32[2,4,128,128]{3,2,1,0:T(8,128)} %get-tuple-element.41), channel_id=1, source_target_pairs={{16,33},{29,49},{22,65},{25,81},{28,97},{26,113},{18,129},{17,145}... | collective-permute-start | bytes 1572872 | tf_op jit(solution)/shard_map/ppermute | solution.py:440
  291.8 39.5 %collective-permute-start.22 = (f32[2,4,128,128]{3,2,1,0:T(8,128)}, f32[2,4,128,128]{3,2,1,0:T(8,128)S(1)}, u32[]{:S(2)}, u32[]{:S(2)}) collective-permute-start(f32[2,4,128,128]{3,2,1,0:T(8,128)} %get-tuple-element.42), channel_id=1, source_target_pairs={{16,18},{29,19},{22,20},{25,21},{28,22},{26,23},{18,24},{17,25},{2... | collective-permute-start | bytes 1572872 | tf_op jit(solution)/shard_map/ppermute | solution.py:441
  293.7 85.1 %collective-permute-start.24 = (f32[2,4,128,128]{3,2,1,0:T(8,128)}, f32[2,4,128,128]{3,2,1,0:T(8,128)}, u32[]{:S(2)}, u32[]{:S(2)}) collective-permute-start(f32[2,4,128,128]{3,2,1,0:T(8,128)} %get-tuple-element.42), channel_id=1, source_target_pairs={{16,33},{29,49},{22,65},{25,81},{28,97},{26,113},{18,129},{17,145}... | collective-permute-start | bytes 1572872 | tf_op jit(solution)/shard_map/ppermute | solution.py:441
  301.5 2.0 collective-permute-start.20
  303.5 4.1 %copy-start.3 = (f32[16,4,4,8,128]{4,3,2,1,0:T(8,128)}, f32[16,4,4,8,128]{4,3,2,1,0:T(8,128)S(1)}, u32[]{:S(2)}) copy-start(f32[16,4,4,8,128]{4,3,2,1,0:T(8,128)S(1)} %constant_dynamic-update-slice_fusion.right) | copy-start | bytes 3145732
  317.8 61.1 %copy-start.4 = (f32[2,4,128,128]{3,2,1,0:T(8,128)}, f32[2,4,128,128]{3,2,1,0:T(8,128)S(1)}, u32[]{:S(2)}) copy-start(f32[2,4,128,128]{3,2,1,0:T(8,128)S(1)} %collective-permute-done.21.upper) | copy-start | bytes 1572868
  331.3 47.5 %copy-start.6 = (f32[2,4,128,128]{3,2,1,0:T(8,128)}, f32[2,4,128,128]{3,2,1,0:T(8,128)S(1)}, u32[]{:S(2)}) copy-start(f32[2,4,128,128]{3,2,1,0:T(8,128)S(1)} %collective-permute-done.22.lower) | copy-start | bytes 1572868
  359.5 19.4 %copy-start.5 = (f32[2,4,128,128]{3,2,1,0:T(8,128)}, f32[2,4,128,128]{3,2,1,0:T(8,128)S(1)}, u32[]{:S(2)}) copy-start(f32[2,4,128,128]{3,2,1,0:T(8,128)S(1)} %collective-permute-done.23.turned_upper) | copy-start | bytes 1572868

commit v8 on v5

--- a/solution.py
+++ b/solution.py
@@ -198,8 +198,10 @@
     )(meta, picks, slots)
 
 
-def solve_part(ref, inverse, b):
-    rows = jnp.concatenate([ref[:, b, a].reshape(BLK, BLK) for a in range(SPAN)], axis=0)
+def solve_part(ref, inverse, b, order):
+    rows = jnp.concatenate(
+        [ref[order[k], b, a] for a in range(SPAN) for k in range(NWIN)], axis=0
+    )
     solved = lax.dot_general(
         rows, inverse[b], CONTRACT_COLS, precision=HIGH, preferred_element_type=jnp.float32
     )
@@ -210,7 +212,7 @@
 def solve_kernel(left, inverse, out, high, low):
     for b in range(SPAN):
         cols = slice(b * BLK, (b + 1) * BLK)
-        out[:, cols], high[:, cols], low[:, cols] = solve_part(left, inverse, b)
+        out[:, cols], high[:, cols], low[:, cols] = solve_part(left, inverse, b, range(NWIN))
 
 
 def solve_rows(left, inverse):
@@ -249,7 +251,12 @@
 
     @pl.when(inside)
     def _():
-        parts = [solve_part(right, inverse, b) for b in range(SPAN)]
+        gaps = [k ^ i for k in range(NWIN)]
+        order = [
+            ((d >> 1) & 1) | ((((d >> 2) ^ (d >> 3)) & 1) << 1) | ((d >> 3) << 2) | ((d & 1) << 3)
+            for d in gaps
+        ]
+        parts = [solve_part(right, inverse, b, order) for b in range(SPAN)]
         other_high = jnp.concatenate([p[1] for p in parts], axis=1)
         other_low = jnp.concatenate([p[2] for p in parts], axis=1)
 
@@ -352,14 +359,16 @@
     same, diag, piece, flipped = lax.optimization_barrier((same, diag, piece, flipped))
 
     other = lax.ppermute(same, "core", [(0, 1), (1, 0)])
-    diag = diag + lax.ppermute(diag, "yl", swap_pairs(2, 1))
+    across = lax.ppermute(diag, "yl", swap_pairs(2, 1))
+    tiles, late = gram_slots(meta, flipped, same, other)
+    across, late = lax.optimization_barrier((across, late))
+    diag = diag + across
     eye = jnp.eye(BLK, dtype=jnp.float32)
     given_here = lax.dynamic_slice(given_diag, (i * SPAN * BLK,), (SPAN * BLK,))
     diag = diag + given_here.reshape(SPAN, 1, BLK) * eye
     corner = spread(jnp.where(i == 0, diag, 0.0), "core")
     corner = spread(corner, "yh")
     piece = spread(piece, "yh")
-    tiles, late = gram_slots(meta, flipped, same, other)
 
     tiles = lax.all_to_all(tiles, GC, 0, 0, tiled=True)
     chol, inverse = factor(spread(corner, "x"))
@@ -374,12 +383,19 @@
     part = place(place_kernel, meta, block_pick, tiles, (SPAN, SPAN, BLK, BLK))
     slices = lax.all_to_all(slices, GC, 0, 0, tiled=True)
     everywhere = [(r * NWIN + c, c * NWIN + r) for r in range(NWIN) for c in range(NWIN)]
-    mirror = lax.ppermute(part, AXES, everywhere)
     strip = place(strip_kernel, meta, block_pick, slices, (SPAN, SPAN, SLICE, BLK))
-    copies = (NWIN,) + strip.shape
-    turned = lax.ppermute(strip, AXES, everywhere)
-    left = lax.all_to_all(jnp.broadcast_to(strip, copies), GC, 0, 0, tiled=True)
-    right = lax.all_to_all(jnp.broadcast_to(turned, copies), GR, 0, 0, tiled=True)
+    right = lax.ppermute(strip, AXES, everywhere)[None]
+    copies = jnp.broadcast_to(strip, (NWIN,) + strip.shape)
+    left = lax.all_to_all(copies, GC, 0, 0, tiled=True)
+    inner = [(r * NWIN + c, c * NWIN + r) for r in range(1, NWIN) for c in range(1, NWIN) if r != c]
+    mirror = lax.ppermute(part, AXES, inner)
+    for axis, pairs in (
+        ("yh", swap_pairs(2, 1)),
+        ("x", swap_pairs(4, 1)),
+        ("x", swap_pairs(4, 3)),
+        ("core", swap_pairs(2, 1)),
+    ):
+        right = jnp.concatenate([right, lax.ppermute(right, axis, pairs)], axis=0)
     lefts, high, low = solve_rows(left, inverse)
     base = update(meta, part, lefts, high, low, right, diag, chol, inverse)
     return finish(meta, base, mirror)

time: 361 us -> 366 us (1.014); the launches traced: 355 us -> 364 us
  waiting for transfers between devices: 201 us -> 208 us
    ppermute x3 -> x7, waiting for transfers between devices: 63.9 us -> 96.4 us  [the longest x1 56.3 us: body(): mirror = lax.ppermute(part, AXES, inner)]
    all_to_all x2 -> x1, waiting for transfers between devices: 19.8 us -> 0.01 us  [body(): left = lax.all_to_all(copies, GC, 0, 0, tiled=True)]
    ppermute x3 -> x7, starting transfers between devices: 12.1 us -> 17.2 us  [the longest x1 10.7 us: body(): right = lax.ppermute(strip, AXES, everywhere)[None]]
    all_to_all x2 -> x1, starting transfers between devices: 10.4 us -> 5.84 us  [body(): left = lax.all_to_all(copies, GC, 0, 0, tiled=True)]
    ppermute x4, waiting for transfers between devices: 12.9 us -> 8.46 us  [spread(): v = v + lax.ppermute(v, 'x', [(0, 1)]) + lax.ppermute(v, 'x', [(0, 3)])]
  transfers between devices with their start and end apart: 23 -> 26, of which waited for: 15 -> 17; matrix products, arithmetic and copies ran while one was open for 3% -> 3% of each run, Pallas kernels for 12% -> 12%
where the time goes in v8:
time: 366 us; the launch traced here: 364 us
  waiting for transfers between devices  208 us (57%)
  starting transfers between devices  74 us (20%)
  Pallas kernels  60.8 us (17%)
  other arithmetic  15.7 us (4%)
  local copies, waits for them, and re-layouts  4.75 us (1%)
    ppermute x1, waiting for transfers between devices, body(): mirror = lax.ppermute(part, AXES, inner)  56.3 us
    ppermute x3, waiting for transfers between devices, spread(): return v + lax.ppermute(v, step, [(0, 1)])  37 us
    all_to_all x1, waiting for transfers between devices, body(): same = lax.all_to_all(slots, ('x', 'yh'), 0, 0, tiled=True)  28.7 us
    ppermute x1, waiting for transfers between devices, body(): right = lax.ppermute(strip, AXES, everywhere)[None]  24.3 us
    pallas_call x1, Pallas kernels, factor(): pl.pallas_call(factor_kernel, in_specs=[LOCAL], out_specs=[LOCAL] * 2, ou...  21 us
    ppermute x3, waiting for transfers between devices, body(): diag = diag + lax.ppermute(diag, 'z', swap_pairs(8, bit))  18.9 us
    ppermute x4, waiting for transfers between devices, body(): right = jnp.concatenate([right, lax.ppermute(right, axis, pairs)], axis=0)  12.2 us
    ppermute x1, starting transfers between devices, body(): right = lax.ppermute(strip, AXES, everywhere)[None]  10.7 us
  transfers between devices with their start and end apart: 26, of which 17 were waited for; matrix products, arithmetic and copies ran while one was open for 3% of the time, Pallas kernels for 12%

profile of v8, /device:TPU:66, one launch (start us, length us, event | category | flops | bytes accessed | tf_op | source)
XLA Modules:
  0.0 363.9 jit_solution(1740843167988497100)
XLA Ops:
  0.0 0.8 sqrt.3
  0.8 1.9 multiply_convert_fusion.scaled.first
  2.8 2.8 broadcast_select_fusion
  5.6 7.6 %all-to-all-start = ((bf16[8,3,768,128]{3,2,1,0:T(8,128)(2,1)}), bf16[8,3,768,128]{3,2,1,0:T(8,128)(2,1)}, u32[]{:S(2)}, u32[]{:S(2)}) async-start(bf16[8,3,768,128]{3,2,1,0:T(8,128)(2,1)} %broadcast_select_fusion), calls=%async_computation | async-start | bytes 9437184 | tf_op jit(solution)/shard_map/all_to_all | solution.py:354
  13.3 0.5 fusion.1
  13.8 0.2 select_reduce_fusion
  14.0 2.0 collective-permute-start
  16.1 1.3 collective-permute-start.3
  17.4 4.4 %collective-permute-done = f32[4,128,128]{2,1,0:T(8,128)S(1)} collective-permute-done((f32[4,128,128]{2,1,0:T(8,128)S(1)}, f32[4,128,128]{2,1,0:T(8,128)S(1)}, u32[]{:S(2)}, u32[]{:S(2)}) %collective-permute-start) | collective-permute-done | bytes 262176 | tf_op jit(solution)/shard_map/ppermute | solution.py:349
  21.9 10.3 %collective-permute-done.1 = f32[4,128,128]{2,1,0:T(8,128)S(1)} collective-permute-done((f32[4,128,128]{2,1,0:T(8,128)S(1)}, f32[4,128,128]{2,1,0:T(8,128)S(1)}, u32[]{:S(2)}, u32[]{:S(2)}) %collective-permute-start.1) | collective-permute-done | bytes 262176 | tf_op jit(solution)/shard_map/ppermute | solution.py:349
  32.3 6.3 %collective-permute-start.2 = (f32[4,128,128]{2,1,0:T(8,128)S(1)}, f32[4,128,128]{2,1,0:T(8,128)S(1)}, u32[]{:S(2)}, u32[]{:S(2)}) collective-permute-start(f32[4,128,128]{2,1,0:T(8,128)S(1)} %add.75), channel_id=1, source_target_pairs={{0,4},{1,5},{2,6},{3,7},{4,0},{5,1},{6,2},{7,3},{8,12},{9,13},{10,... | collective-permute-start | bytes 786440 | tf_op jit(solution)/shard_map/ppermute | solution.py:349
  38.6 4.6 %flip.1.mine = bf16[6,128,768]{2,1,0:T(8,128)(2,1)} custom-call(bf16[6,768,128]{2,1,0:T(8,128)(2,1)} %copy-done.1), custom_call_target="tpu_custom_call" | custom-call | tf_op jit(solution)/shard_map/flip/pallas_call | solution.py:84
  43.3 4.1 %collective-permute-done.2 = f32[4,128,128]{2,1,0:T(8,128)S(1)} collective-permute-done((f32[4,128,128]{2,1,0:T(8,128)S(1)}, f32[4,128,128]{2,1,0:T(8,128)S(1)}, u32[]{:S(2)}, u32[]{:S(2)}) %collective-permute-start.2) | collective-permute-done | bytes 262176 | tf_op jit(solution)/shard_map/ppermute | solution.py:349
  47.4 0.7 add.76
  48.1 28.7 %all-to-all-done.same = bf16[8,3,768,128]{3,2,1,0:T(8,128)(2,1)} async-done(((bf16[8,3,768,128]{3,2,1,0:T(8,128)(2,1)}), bf16[8,3,768,128]{3,2,1,0:T(8,128)(2,1)}, u32[]{:S(2)}, u32[]{:S(2)}) %all-to-all-start) | async-done | bytes 4718624 | tf_op jit(solution)/shard_map/all_to_all | solution.py:354
  76.8 0.7 pad_add_fusion.meta
  77.5 7.6 %collective-permute-done.4.other = bf16[8,3,768,128]{3,2,1,0:T(8,128)(2,1)} collective-permute-done((bf16[8,3,768,128]{3,2,1,0:T(8,128)(2,1)}, bf16[8,3,768,128]{3,2,1,0:T(8,128)(2,1)}, u32[]{:S(2)}, u32[]{:S(2)}) %collective-permute-start.4) | collective-permute-done | bytes 4718624 | tf_op jit(solution)/shard_map/ppermute | solution.py:361
  85.1 9.8 %gram_slots.1 = (f32[16,384,128]{2,1,0:T(8,128)}, f32[3,128,128]{2,1,0:T(8,128)}) custom-call(s32[4]{0:T(128)} %pad_add_fusion.meta, bf16[6,128,768]{2,1,0:T(8,128)(2,1)} %flip.1.mine, bf16[8,3,768,128]{3,2,1,0:T(8,128)(2,1)} %all-to-all-done.same, bf16[8,3,768,128]{3,2,1,0:T(8,128)(2,1)} %collective-permute-done.4.other), custom_call_target="tpu_custom_call" | custom-call | tf_op jit(solution)/shard_map/gram_slots/pallas_call | solution.py:130
  94.9 8.2 %all-to-all-start.1 = ((f32[16,384,128]{2,1,0:T(8,128)}), f32[16,384,128]{2,1,0:T(8,128)S(1)}, u32[]{:S(2)}, u32[]{:S(2)}) async-start(f32[16,384,128]{2,1,0:T(8,128)} %get-tuple-element.24), calls=%async_computation.1 | async-start | bytes 6291456 | tf_op jit(solution)/shard_map/all_to_all | solution.py:373
  103.2 5.4 %collective-permute-start.5 = (bf16[3,384,128]{2,1,0:T(8,128)(2,1)S(1)}, bf16[3,384,128]{2,1,0:T(8,128)(2,1)}, u32[]{:S(2)}, u32[]{:S(2)}) collective-permute-start(bf16[3,384,128]{2,1,0:T(8,128)(2,1)S(1)} %slice_add_fusion), channel_id=1, source_target_pairs={{0,32},{1,33},{2,34},{3,35},{4,36},{5,37},{6,38},{7,39},{8,40},{9,... | collective-permute-start | bytes 884744 | tf_op jit(solution)/shard_map/ppermute | solution.py:330
  108.6 0.9 collective-permute-start.10
  109.5 18.0 %collective-permute-done.5 = bf16[3,384,128]{2,1,0:T(8,128)(2,1)} collective-permute-done((bf16[3,384,128]{2,1,0:T(8,128)(2,1)S(1)}, bf16[3,384,128]{2,1,0:T(8,128)(2,1)}, u32[]{:S(2)}, u32[]{:S(2)}) %collective-permute-start.5) | collective-permute-done | bytes 294944 | tf_op jit(solution)/shard_map/ppermute | solution.py:330
  127.5 1.0 add.78
  128.6 1.3 collective-permute-start.6
  129.9 0.7 collective-permute-start.7
  130.6 3.6 collective-permute-done.10
  134.2 1.8 broadcast_select_fusion.4
  135.9 1.3 collective-permute-start.11
  137.2 1.1 collective-permute-done.11
  138.4 2.4 collective-permute-start.12
  140.9 2.4 collective-permute-start.8
  143.3 17.8 %collective-permute-done.12 = f32[4,128,128]{2,1,0:T(8,128)S(1)} collective-permute-done((f32[4,128,128]{2,1,0:T(8,128)S(1)}, f32[4,128,128]{2,1,0:T(8,128)S(1)}, u32[]{:S(2)}, u32[]{:S(2)}) %collective-permute-start.12) | collective-permute-done | bytes 262176 | tf_op jit(solution)/shard_map/ppermute | solution.py:330
  161.1 0.7 add.86
  161.9 1.3 collective-permute-start.13
  163.2 1.4 collective-permute-start.14
  164.7 8.5 %collective-permute-done.13 = f32[4,128,128]{2,1,0:T(8,128)} collective-permute-done((f32[4,128,128]{2,1,0:T(8,128)}, f32[4,128,128]{2,1,0:T(8,128)}, u32[]{:S(2)}, u32[]{:S(2)}) %collective-permute-start.13) | collective-permute-done | bytes 262176 | tf_op jit(solution)/shard_map/ppermute | solution.py:331
  173.2 1.8 add_add_fusion.1
  175.0 2.0 collective-permute-start.15
  177.0 1.0 broadcast_select_fusion.3
  178.0 0.9 pad_maximum_fusion.lead
  178.9 2.4 panel_slots.1
  181.3 0.8 collective-permute-done.15
  182.1 1.8 add.89.corner
  183.8 21.0 %factor.1 = (f32[4,128,128]{2,1,0:T(8,128)}, f32[4,128,128]{2,1,0:T(8,128)}) custom-call(f32[4,128,128]{2,1,0:T(8,128)} %add.89.corner), custom_call_target="tpu_custom_call" | custom-call | tf_op jit(solution)/shard_map/factor/pallas_call | solution.py:69
  204.8 7.2 %all-to-all-start.2 = ((f32[16,48,128]{2,1,0:T(8,128)}), f32[16,48,128]{2,1,0:T(8,128)}, u32[]{:S(2)}, u32[]{:S(2)}) async-start(f32[16,48,128]{2,1,0:T(8,128)} %panel_slots.1), calls=%async_computation.2 | async-start | bytes 786432 | tf_op jit(solution)/shard_map/all_to_all | solution.py:384
  212.0 0.7 copy.9.picks
  212.7 10.1 %all-to-all-done.2.slots = f32[16,48,128]{2,1,0:T(8,128)} async-done(((f32[16,48,128]{2,1,0:T(8,128)}), f32[16,48,128]{2,1,0:T(8,128)}, u32[]{:S(2)}, u32[]{:S(2)}) %all-to-all-start.2) | async-done | bytes 393248 | tf_op jit(solution)/shard_map/all_to_all | solution.py:384
  222.8 3.6 shard_map.47
  226.4 2.0 broadcast_in_dim.73
  228.4 5.8 %all-to-all-start.3 = ((f32[16,4,4,8,128]{4,3,2,1,0:T(8,128)}), f32[16,4,4,8,128]{4,3,2,1,0:T(8,128)}, u32[]{:S(2)}, u32[]{:S(2)}) async-start(f32[16,4,4,8,128]{4,3,2,1,0:T(8,128)} %broadcast_in_dim.73), calls=%async_computation.3 | async-start | bytes 2097152 | tf_op jit(solution)/shard_map/all_to_all | solution.py:389
  234.3 10.7 %collective-permute-start.16 = (f32[4,4,8,128]{3,2,1,0:T(8,128)S(1)}, f32[4,4,8,128]{3,2,1,0:T(8,128)S(1)}, u32[]{:S(2)}, u32[]{:S(2)}) collective-permute-start(f32[4,4,8,128]{3,2,1,0:T(8,128)S(1)} %copy-done.5), channel_id=1, source_target_pairs={{0,0},{1,16},{2,32},{3,48},{4,64},{5,80},{6,96},{7,112},{8,128},{9... | collective-permute-start | bytes 196616 | tf_op jit(solution)/shard_map/ppermute | solution.py:387
  245.0 24.3 %collective-permute-done.16 = f32[4,4,8,128]{3,2,1,0:T(8,128)S(1)} collective-permute-done((f32[4,4,8,128]{3,2,1,0:T(8,128)S(1)}, f32[4,4,8,128]{3,2,1,0:T(8,128)S(1)}, u32[]{:S(2)}, u32[]{:S(2)}) %collective-permute-start.16) | collective-permute-done | bytes 65568 | tf_op jit(solution)/shard_map/ppermute | solution.py:387
  269.3 5.8 %collective-permute-done.17 = f32[1,4,4,8,128]{4,3,2,1,0:T(8,128)S(1)} collective-permute-done((f32[1,4,4,8,128]{4,3,2,1,0:T(8,128)S(1)}, f32[1,4,4,8,128]{4,3,2,1,0:T(8,128)S(1)}, u32[]{:S(2)}, u32[]{:S(2)}) %collective-permute-start.17) | collective-permute-done | bytes 65568 | tf_op jit(solution)/shard_map/ppermute | solution.py:398
  275.2 5.0 %collective-permute-done.18 = f32[2,4,4,8,128]{4,3,2,1,0:T(8,128)S(1)} collective-permute-done((f32[2,4,4,8,128]{4,3,2,1,0:T(8,128)S(1)}, f32[2,4,4,8,128]{4,3,2,1,0:T(8,128)S(1)}, u32[]{:S(2)}, u32[]{:S(2)}) %collective-permute-start.18) | collective-permute-done | bytes 131104 | tf_op jit(solution)/shard_map/ppermute | solution.py:398
  280.2 0.7 collective-permute-start.19
  280.9 4.8 %shard_map.46.part = f32[4,4,128,128]{3,2,1,0:T(8,128)} custom-call(s32[4]{0:T(128)} %pad_add_fusion.meta, s32[96,16]{1,0:T(8,128)} %copy.9.picks, f32[16,384,128]{2,1,0:T(8,128)} %copy-done.2), custom_call_target="tpu_custom_call" | custom-call | tf_op jit(solution)/shard_map/pallas_call | solution.py:196
  285.7 3.1 collective-permute-start.21
  288.9 1.6 collective-permute-start.20
  290.6 1.5 collective-permute-done.20
  292.2 4.1 %solve_rows.1 = (f32[512,512]{1,0:T(8,128)}, bf16[512,512]{1,0:T(8,128)(2,1)}, bf16[512,512]{1,0:T(8,128)(2,1)}) custom-call(f32[16,4,4,8,128]{4,3,2,1,0:T(8,128)} %all-to-all-done.3.left, f32[4,128,128]{2,1,0:T(8,128)} %get-tuple-element.34.inverse), custom_call_target="tpu_custom_call" | custom-call | tf_op jit(solution)/shard_map/solve_rows/pallas_call | solution.py:220
  296.3 6.0 %update.1.base = f32[512,512]{1,0:T(8,128)} custom-call(s32[4]{0:T(128)} %pad_add_fusion.meta, f32[4,4,128,128]{3,2,1,0:T(8,128)} %shard_map.46.part, f32[512,512]{1,0:T(8,128)} %get-tuple-element.35.lefts, bf16[512,512]{1,0:T(8,128)(2,1)} %get-tuple-element.36.high, bf16[512,512]{1,0:T(8,128)(2,1)} %get-tuple-element.37.low, ...), custom_call_target="tpu_custom_call" | custom-call | tf_op jit(solution)/shard_map/update/pallas_call | solution.py:284
  302.2 56.3 %collective-permute-done.21.mirror = f32[4,4,128,128]{3,2,1,0:T(8,128)S(1)} collective-permute-done((f32[4,4,128,128]{3,2,1,0:T(8,128)}, f32[4,4,128,128]{3,2,1,0:T(8,128)S(1)}, u32[]{:S(2)}, u32[]{:S(2)}) %collective-permute-start.21) | collective-permute-done | bytes 1048608 | tf_op jit(solution)/shard_map/ppermute | solution.py:391
  358.5 1.0 copy-done.4
  359.5 4.4 %finish.1 = f32[512,512]{1,0:T(8,128)} custom-call(s32[4]{0:T(128)} %pad_add_fusion.meta, f32[512,512]{1,0:T(8,128)} %update.1.base, f32[4,4,128,128]{3,2,1,0:T(8,128)} %copy-done.4), custom_call_target="tpu_custom_call" | custom-call | tf_op jit(solution)/shard_map/finish/pallas_call | solution.py:316
  (48 shorter events, 1.1 us)
Async XLA Ops:
  0.0 109.4 %copy-start = (f32[8192]{0:T(1024)S(1)}, f32[8192]{0:T(1024)}, u32[]{:S(2)}) copy-start(f32[8192]{0:T(1024)} %param.7) | copy-start | bytes 98308
  2.6 10.7 %copy-start.1 = (bf16[6,768,128]{2,1,0:T(8,128)(2,1)}, bf16[6,768,128]{2,1,0:T(8,128)(2,1)S(1)}, u32[]{:S(2)}) copy-start(bf16[6,768,128]{2,1,0:T(8,128)(2,1)S(1)} %multiply_convert_fusion.scaled.first) | copy-start | bytes 3538948
  5.6 7.6 %copy-start.6 = (s32[96,16]{0,1:T(8,128)S(1)}, s32[96,16]{0,1:T(8,128)}, u32[]{:S(2)}) copy-start(s32[96,16]{0,1:T(8,128)} %param.6) | copy-start | bytes 18436
  5.6 71.3 %all-to-all-start = ((bf16[8,3,768,128]{3,2,1,0:T(8,128)(2,1)}), bf16[8,3,768,128]{3,2,1,0:T(8,128)(2,1)}, u32[]{:S(2)}, u32[]{:S(2)}) async-start(bf16[8,3,768,128]{3,2,1,0:T(8,128)(2,1)} %broadcast_select_fusion), calls=%async_computation | async-start | bytes 9437184 | tf_op jit(solution)/shard_map/all_to_all | solution.py:354
  14.0 7.8 %collective-permute-start = (f32[4,128,128]{2,1,0:T(8,128)S(1)}, f32[4,128,128]{2,1,0:T(8,128)S(1)}, u32[]{:S(2)}, u32[]{:S(2)}) collective-permute-start(f32[4,128,128]{2,1,0:T(8,128)S(1)} %select_reduce_fusion), channel_id=1, source_target_pairs={{0,1},{1,0},{2,3},{3,2},{4,5},{5,4},{6,7},{7,6},{8,9},{9,8},{10,11... | collective-permute-start | bytes 786440 | tf_op jit(solution)/shard_map/ppermute | solution.py:349
  16.1 27.2 %collective-permute-start.3 = (bf16[3,384,128]{2,1,0:T(8,128)(2,1)S(1)}, bf16[3,384,128]{2,1,0:T(8,128)(2,1)S(1)}, u32[]{:S(2)}, u32[]{:S(2)}) collective-permute-start(bf16[3,384,128]{2,1,0:T(8,128)(2,1)S(1)} %slice.20), channel_id=1, source_target_pairs={{0,16},{1,17},{2,18},{3,19},{4,20},{5,21},{6,22},{7,23},{8,24},{9,... | collective-permute-start | bytes 884744 | tf_op jit(solution)/shard_map/ppermute | solution.py:357
  21.8 10.4 %collective-permute-start.1 = (f32[4,128,128]{2,1,0:T(8,128)S(1)}, f32[4,128,128]{2,1,0:T(8,128)S(1)}, u32[]{:S(2)}, u32[]{:S(2)}) collective-permute-start(f32[4,128,128]{2,1,0:T(8,128)S(1)} %add.74), channel_id=1, source_target_pairs={{0,2},{1,3},{2,0},{3,1},{4,6},{5,7},{6,4},{7,5},{8,10},{9,11},{10,... | collective-permute-start | bytes 786440 | tf_op jit(solution)/shard_map/ppermute | solution.py:349
  32.3 15.1 %collective-permute-start.2 = (f32[4,128,128]{2,1,0:T(8,128)S(1)}, f32[4,128,128]{2,1,0:T(8,128)S(1)}, u32[]{:S(2)}, u32[]{:S(2)}) collective-permute-start(f32[4,128,128]{2,1,0:T(8,128)S(1)} %add.75), channel_id=1, source_target_pairs={{0,4},{1,5},{2,6},{3,7},{4,0},{5,1},{6,2},{7,3},{8,12},{9,13},{10,... | collective-permute-start | bytes 786440 | tf_op jit(solution)/shard_map/ppermute | solution.py:349
  76.8 8.3 %collective-permute-start.4 = (bf16[8,3,768,128]{3,2,1,0:T(8,128)(2,1)}, bf16[8,3,768,128]{3,2,1,0:T(8,128)(2,1)}, u32[]{:S(2)}, u32[]{:S(2)}) collective-permute-start(bf16[8,3,768,128]{3,2,1,0:T(8,128)(2,1)} %all-to-all-done.same), channel_id=1, source_target_pairs={{0,16},{16,0},{1,17},{17,1},{2,18},{18,2},{3,19},{19,3},{4,20},{20... | collective-permute-start | bytes 14155784 | tf_op jit(solution)/shard_map/ppermute | solution.py:361
  94.9 109.9 %all-to-all-start.1 = ((f32[16,384,128]{2,1,0:T(8,128)}), f32[16,384,128]{2,1,0:T(8,128)S(1)}, u32[]{:S(2)}, u32[]{:S(2)}) async-start(f32[16,384,128]{2,1,0:T(8,128)} %get-tuple-element.24), calls=%async_computation.1 | async-start | bytes 6291456 | tf_op jit(solution)/shard_map/all_to_all | solution.py:373
  103.2 24.4 %collective-permute-start.5 = (bf16[3,384,128]{2,1,0:T(8,128)(2,1)S(1)}, bf16[3,384,128]{2,1,0:T(8,128)(2,1)}, u32[]{:S(2)}, u32[]{:S(2)}) collective-permute-start(bf16[3,384,128]{2,1,0:T(8,128)(2,1)S(1)} %slice_add_fusion), channel_id=1, source_target_pairs={{0,32},{1,33},{2,34},{3,35},{4,36},{5,37},{6,38},{7,39},{8,40},{9,... | collective-permute-start | bytes 884744 | tf_op jit(solution)/shard_map/ppermute | solution.py:330
  108.6 25.6 %collective-permute-start.10 = (f32[4,128,128]{2,1,0:T(8,128)}, f32[4,128,128]{2,1,0:T(8,128)}, u32[]{:S(2)}, u32[]{:S(2)}) collective-permute-start(f32[4,128,128]{2,1,0:T(8,128)} %add.76), channel_id=1, source_target_pairs={{0,8},{8,0},{1,9},{9,1},{2,10},{10,2},{3,11},{11,3},{4,12},{12,4},... | collective-permute-start | bytes 786440 | tf_op jit(solution)/shard_map/ppermute | solution.py:362
  128.6 12.3 %collective-permute-start.6 = (bf16[3,384,128]{2,1,0:T(8,128)(2,1)S(1)}, bf16[3,384,128]{2,1,0:T(8,128)(2,1)S(1)}, u32[]{:S(2)}, u32[]{:S(2)}) collective-permute-start(bf16[3,384,128]{2,1,0:T(8,128)(2,1)S(1)} %add.78), channel_id=1, source_target_pairs={{0,64},{1,65},{2,66},{3,67},{4,68},{5,69},{6,70},{7,71},{8,72},{9,... | collective-permute-start | bytes 884744 | tf_op jit(solution)/shard_map/ppermute | solution.py:331
  129.9 11.0 %collective-permute-start.7 = (bf16[3,384,128]{2,1,0:T(8,128)(2,1)S(1)}, bf16[3,384,128]{2,1,0:T(8,128)(2,1)S(1)}, u32[]{:S(2)}, u32[]{:S(2)}) collective-permute-start(bf16[3,384,128]{2,1,0:T(8,128)(2,1)S(1)} %add.78), channel_id=1, source_target_pairs={{0,192},{1,193},{2,194},{3,195},{4,196},{5,197},{6,198},{7,199},{8... | collective-permute-start | bytes 884744 | tf_op jit(solution)/shard_map/ppermute | solution.py:331
  135.9 2.4 collective-permute-start.11
  138.4 22.7 %collective-permute-start.12 = (f32[4,128,128]{2,1,0:T(8,128)S(1)}, f32[4,128,128]{2,1,0:T(8,128)S(1)}, u32[]{:S(2)}, u32[]{:S(2)}) collective-permute-start(f32[4,128,128]{2,1,0:T(8,128)S(1)} %add.85), channel_id=1, source_target_pairs={{0,32},{1,33},{2,34},{3,35},{4,36},{5,37},{6,38},{7,39},{8,40},{9,... | collective-permute-start | bytes 786440 | tf_op jit(solution)/shard_map/ppermute | solution.py:330
  140.9 23.6 %collective-permute-start.8 = (bf16[3,384,128]{2,1,0:T(8,128)(2,1)S(1)}, bf16[3,384,128]{2,1,0:T(8,128)(2,1)S(1)}, u32[]{:S(2)}, u32[]{:S(2)}) collective-permute-start(bf16[3,384,128]{2,1,0:T(8,128)(2,1)S(1)} %add_add_fusion), channel_id=1, source_target_pairs={{64,128},{65,129},{66,130},{67,131},{68,132},{69,133},{70,134},{71... | collective-permute-start | bytes 884744 | tf_op jit(solution)/shard_map/ppermute | solution.py:332
  161.9 11.3 %collective-permute-start.13 = (f32[4,128,128]{2,1,0:T(8,128)}, f32[4,128,128]{2,1,0:T(8,128)}, u32[]{:S(2)}, u32[]{:S(2)}) collective-permute-start(f32[4,128,128]{2,1,0:T(8,128)} %add.86), channel_id=1, source_target_pairs={{0,64},{1,65},{2,66},{3,67},{4,68},{5,69},{6,70},{7,71},{8,72},{9,... | collective-permute-start | bytes 786440 | tf_op jit(solution)/shard_map/ppermute | solution.py:331
  163.2 10.0 %collective-permute-start.14 = (f32[4,128,128]{2,1,0:T(8,128)}, f32[4,128,128]{2,1,0:T(8,128)}, u32[]{:S(2)}, u32[]{:S(2)}) collective-permute-start(f32[4,128,128]{2,1,0:T(8,128)} %add.86), channel_id=1, source_target_pairs={{0,192},{1,193},{2,194},{3,195},{4,196},{5,197},{6,198},{7,199},{8... | collective-permute-start | bytes 786440 | tf_op jit(solution)/shard_map/ppermute | solution.py:331
  164.6 12.4 %collective-permute-start.9 = (bf16[3,384,128]{2,1,0:T(8,128)(2,1)S(1)}, bf16[3,384,128]{2,1,0:T(8,128)(2,1)}, u32[]{:S(2)}, u32[]{:S(2)}) collective-permute-start(bf16[3,384,128]{2,1,0:T(8,128)(2,1)S(1)} %add.81), channel_id=1, source_target_pairs={{0,16},{16,0},{1,17},{17,1},{2,18},{18,2},{3,19},{19,3},{4,20},{20... | collective-permute-start | bytes 884744 | tf_op jit(solution)/shard_map/ppermute | solution.py:376
  175.0 7.0 %collective-permute-start.15 = (f32[4,128,128]{2,1,0:T(8,128)}, f32[4,128,128]{2,1,0:T(8,128)}, u32[]{:S(2)}, u32[]{:S(2)}) collective-permute-start(f32[4,128,128]{2,1,0:T(8,128)} %add_add_fusion.1), channel_id=1, source_target_pairs={{64,128},{65,129},{66,130},{67,131},{68,132},{69,133},{70,134},{71... | collective-permute-start | bytes 786440 | tf_op jit(solution)/shard_map/ppermute | solution.py:332
  204.8 23.6 %copy-start.2 = (f32[16,384,128]{2,1,0:T(8,128)}, f32[16,384,128]{2,1,0:T(8,128)S(1)}, u32[]{:S(2)}) copy-start(f32[16,384,128]{2,1,0:T(8,128)S(1)} %all-to-all-done.1.slots) | copy-start | bytes 9437188
  204.8 18.0 %all-to-all-start.2 = ((f32[16,48,128]{2,1,0:T(8,128)}), f32[16,48,128]{2,1,0:T(8,128)}, u32[]{:S(2)}, u32[]{:S(2)}) async-start(f32[16,48,128]{2,1,0:T(8,128)} %panel_slots.1), calls=%async_computation.2 | async-start | bytes 786432 | tf_op jit(solution)/shard_map/all_to_all | solution.py:384
  226.4 7.9 %copy-start.5 = (f32[4,4,8,128]{3,2,1,0:T(8,128)S(1)}, f32[4,4,8,128]{3,2,1,0:T(8,128)}, u32[]{:S(2)}) copy-start(f32[4,4,8,128]{3,2,1,0:T(8,128)} %shard_map.47) | copy-start | bytes 196612
  228.4 63.7 %all-to-all-start.3 = ((f32[16,4,4,8,128]{4,3,2,1,0:T(8,128)}), f32[16,4,4,8,128]{4,3,2,1,0:T(8,128)}, u32[]{:S(2)}, u32[]{:S(2)}) async-start(f32[16,4,4,8,128]{4,3,2,1,0:T(8,128)} %broadcast_in_dim.73), calls=%async_computation.3 | async-start | bytes 2097152 | tf_op jit(solution)/shard_map/all_to_all | solution.py:389
  234.3 35.1 %collective-permute-start.16 = (f32[4,4,8,128]{3,2,1,0:T(8,128)S(1)}, f32[4,4,8,128]{3,2,1,0:T(8,128)S(1)}, u32[]{:S(2)}, u32[]{:S(2)}) collective-permute-start(f32[4,4,8,128]{3,2,1,0:T(8,128)S(1)} %copy-done.5), channel_id=1, source_target_pairs={{0,0},{1,16},{2,32},{3,48},{4,64},{5,80},{6,96},{7,112},{8,128},{9... | collective-permute-start | bytes 196616 | tf_op jit(solution)/shard_map/ppermute | solution.py:387
  269.3 5.8 %collective-permute-start.17 = (f32[1,4,4,8,128]{4,3,2,1,0:T(8,128)S(1)}, f32[1,4,4,8,128]{4,3,2,1,0:T(8,128)S(1)}, u32[]{:S(2)}, u32[]{:S(2)}) collective-permute-start(f32[1,4,4,8,128]{4,3,2,1,0:T(8,128)S(1)} %bitcast.12), channel_id=1, source_target_pairs={{0,32},{32,0},{1,33},{33,1},{2,34},{34,2},{3,35},{35,3},{4,36},{36... | collective-permute-start | bytes 196616 | tf_op jit(solution)/shard_map/ppermute | solution.py:398
  275.1 5.1 %collective-permute-start.18 = (f32[2,4,4,8,128]{4,3,2,1,0:T(8,128)S(1)}, f32[2,4,4,8,128]{4,3,2,1,0:T(8,128)S(1)}, u32[]{:S(2)}, u32[]{:S(2)}) collective-permute-start(f32[2,4,4,8,128]{4,3,2,1,0:T(8,128)S(1)} %pad_maximum_fusion.3), channel_id=1, source_target_pairs={{0,64},{64,0},{128,192},{192,128},{1,65},{65,1},{129,193},{193,129... | collective-permute-start | bytes 393224 | tf_op jit(solution)/shard_map/ppermute | solution.py:398
  280.2 8.7 %collective-permute-start.19 = (f32[4,4,4,8,128]{4,3,2,1,0:T(8,128)S(1)}, f32[4,4,4,8,128]{4,3,2,1,0:T(8,128)S(1)}, u32[]{:S(2)}, u32[]{:S(2)}) collective-permute-start(f32[4,4,4,8,128]{4,3,2,1,0:T(8,128)S(1)} %pad_maximum_fusion.2), channel_id=1, source_target_pairs={{0,192},{64,128},{128,64},{192,0},{1,193},{65,129},{129,65},{193,1... | collective-permute-start | bytes 786440 | tf_op jit(solution)/shard_map/ppermute | solution.py:398
  285.7 72.8 %collective-permute-start.21 = (f32[4,4,128,128]{3,2,1,0:T(8,128)}, f32[4,4,128,128]{3,2,1,0:T(8,128)S(1)}, u32[]{:S(2)}, u32[]{:S(2)}) collective-permute-start(f32[4,4,128,128]{3,2,1,0:T(8,128)} %shard_map.46.part), channel_id=1, source_target_pairs={{18,33},{19,49},{20,65},{21,81},{22,97},{23,113},{24,129},{25,145}... | collective-permute-start | bytes 3145736 | tf_op jit(solution)/shard_map/ppermute | solution.py:391
  288.9 3.2 collective-permute-start.20
  292.1 4.1 %copy-start.3 = (f32[16,4,4,8,128]{4,3,2,1,0:T(8,128)}, f32[16,4,4,8,128]{4,3,2,1,0:T(8,128)S(1)}, u32[]{:S(2)}) copy-start(f32[16,4,4,8,128]{4,3,2,1,0:T(8,128)S(1)} %constant_dynamic-update-slice_fusion.right) | copy-start | bytes 3145732
  358.5 1.0 copy-start.4

commit v9 on v6

--- a/solution.py
+++ b/solution.py
@@ -410,8 +410,11 @@
     right = lax.ppermute(strip, AXES, everywhere)[None]
     copies = jnp.broadcast_to(strip, (NWIN,) + strip.shape)
     left = lax.all_to_all(copies, GC, 0, 0, tiled=True)
-    mirror_a = lax.ppermute(upper, AXES, everywhere)
-    mirror_b = lax.ppermute(lower, AXES, everywhere)
+    inner = [
+        (r * NWIN + c, c * NWIN + r) for r in range(1, NWIN) for c in range(1, NWIN) if r != c
+    ]
+    mirror_a = lax.ppermute(upper, AXES, inner)
+    mirror_b = lax.ppermute(lower, AXES, inner)
     for axis, pairs in (
         ("yh", swap_pairs(2, 1)),
         ("x", swap_pairs(4, 1)),

time: 365 us -> 365 us (level)
  no operation moved by 1% of the time
where the time goes in v9:
time: 365 us; the launch traced here: 364 us
  waiting for transfers between devices  201 us (55%)
  starting transfers between devices  80.6 us (22%)
  Pallas kernels  60.8 us (17%)
  other arithmetic  15.7 us (4%)
  local copies, waits for them, and re-layouts  4.54 us (1%)
    ppermute x1, waiting for transfers between devices, body(): mirror_a = lax.ppermute(upper, AXES, inner)  38.2 us
    ppermute x3, waiting for transfers between devices, spread(): return v + lax.ppermute(v, step, [(0, 1)])  37 us
    all_to_all x1, waiting for transfers between devices, body(): same = lax.all_to_all(slots, ('x', 'yh'), 0, 0, tiled=True)  28.7 us
    ppermute x1, waiting for transfers between devices, body(): right = lax.ppermute(strip, AXES, everywhere)[None]  24.3 us
    pallas_call x1, Pallas kernels, factor(): pl.pallas_call(factor_kernel, in_specs=[LOCAL], out_specs=[LOCAL] * 2, ou...  21 us
    ppermute x3, waiting for transfers between devices, body(): diag = diag + lax.ppermute(diag, 'z', swap_pairs(8, bit))  18.9 us
    ppermute x4, waiting for transfers between devices, body(): right = jnp.concatenate([right, lax.ppermute(right, axis, pairs)], axis=0)  12.5 us
    ppermute x1, waiting for transfers between devices, body(): mirror_b = lax.ppermute(lower, AXES, inner)  11.1 us
  transfers between devices with their start and end apart: 27, of which 18 were waited for; matrix products, arithmetic and copies ran while one was open for 3% of the time, Pallas kernels for 12%

profile of v9, /device:TPU:66, one launch (start us, length us, event | category | flops | bytes accessed | tf_op | source)
XLA Modules:
  0.0 363.8 jit_solution(2546433584560395694)
XLA Ops:
  0.0 0.8 sqrt.3
  0.8 1.9 multiply_convert_fusion.scaled.first
  2.8 2.8 broadcast_select_fusion
  5.6 7.6 %all-to-all-start = ((bf16[8,3,768,128]{3,2,1,0:T(8,128)(2,1)}), bf16[8,3,768,128]{3,2,1,0:T(8,128)(2,1)}, u32[]{:S(2)}, u32[]{:S(2)}) async-start(bf16[8,3,768,128]{3,2,1,0:T(8,128)(2,1)} %broadcast_select_fusion), calls=%async_computation | async-start | bytes 9437184 | tf_op jit(solution)/shard_map/all_to_all | solution.py:377
  13.3 0.5 fusion.1
  14.0 2.0 collective-permute-start
  16.0 1.3 collective-permute-start.3
  17.4 4.4 %collective-permute-done = f32[4,128,128]{2,1,0:T(8,128)S(1)} collective-permute-done((f32[4,128,128]{2,1,0:T(8,128)S(1)}, f32[4,128,128]{2,1,0:T(8,128)S(1)}, u32[]{:S(2)}, u32[]{:S(2)}) %collective-permute-start) | collective-permute-done | bytes 262176 | tf_op jit(solution)/shard_map/ppermute | solution.py:372
  21.9 10.3 %collective-permute-done.1 = f32[4,128,128]{2,1,0:T(8,128)S(1)} collective-permute-done((f32[4,128,128]{2,1,0:T(8,128)S(1)}, f32[4,128,128]{2,1,0:T(8,128)S(1)}, u32[]{:S(2)}, u32[]{:S(2)}) %collective-permute-start.1) | collective-permute-done | bytes 262176 | tf_op jit(solution)/shard_map/ppermute | solution.py:372
  32.3 6.3 %collective-permute-start.2 = (f32[4,128,128]{2,1,0:T(8,128)S(1)}, f32[4,128,128]{2,1,0:T(8,128)S(1)}, u32[]{:S(2)}, u32[]{:S(2)}) collective-permute-start(f32[4,128,128]{2,1,0:T(8,128)S(1)} %add.75), channel_id=1, source_target_pairs={{0,4},{1,5},{2,6},{3,7},{4,0},{5,1},{6,2},{7,3},{8,12},{9,13},{10,... | collective-permute-start | bytes 786440 | tf_op jit(solution)/shard_map/ppermute | solution.py:372
  38.5 4.6 %flip.1.mine = bf16[6,128,768]{2,1,0:T(8,128)(2,1)} custom-call(bf16[6,768,128]{2,1,0:T(8,128)(2,1)} %copy-done.1), custom_call_target="tpu_custom_call" | custom-call | tf_op jit(solution)/shard_map/flip/pallas_call | solution.py:84
  43.2 4.2 %collective-permute-done.2 = f32[4,128,128]{2,1,0:T(8,128)S(1)} collective-permute-done((f32[4,128,128]{2,1,0:T(8,128)S(1)}, f32[4,128,128]{2,1,0:T(8,128)S(1)}, u32[]{:S(2)}, u32[]{:S(2)}) %collective-permute-start.2) | collective-permute-done | bytes 262176 | tf_op jit(solution)/shard_map/ppermute | solution.py:372
  47.4 0.7 add.76
  48.1 28.7 %all-to-all-done.same = bf16[8,3,768,128]{3,2,1,0:T(8,128)(2,1)} async-done(((bf16[8,3,768,128]{3,2,1,0:T(8,128)(2,1)}), bf16[8,3,768,128]{3,2,1,0:T(8,128)(2,1)}, u32[]{:S(2)}, u32[]{:S(2)}) %all-to-all-start) | async-done | bytes 4718624 | tf_op jit(solution)/shard_map/all_to_all | solution.py:377
  76.8 0.6 pad_add_fusion.meta
  77.4 7.6 %collective-permute-done.4.other = bf16[8,3,768,128]{3,2,1,0:T(8,128)(2,1)} collective-permute-done((bf16[8,3,768,128]{3,2,1,0:T(8,128)(2,1)}, bf16[8,3,768,128]{3,2,1,0:T(8,128)(2,1)}, u32[]{:S(2)}, u32[]{:S(2)}) %collective-permute-start.4) | collective-permute-done | bytes 4718624 | tf_op jit(solution)/shard_map/ppermute | solution.py:384
  85.1 9.8 %gram_slots.1 = (f32[16,384,128]{2,1,0:T(8,128)}, f32[3,128,128]{2,1,0:T(8,128)}) custom-call(s32[4]{0:T(128)} %pad_add_fusion.meta, bf16[6,128,768]{2,1,0:T(8,128)(2,1)} %flip.1.mine, bf16[8,3,768,128]{3,2,1,0:T(8,128)(2,1)} %all-to-all-done.same, bf16[8,3,768,128]{3,2,1,0:T(8,128)(2,1)} %collective-permute-done.4.other), custom_call_target="tpu_custom_call" | custom-call | tf_op jit(solution)/shard_map/gram_slots/pallas_call | solution.py:130
  94.9 8.2 %all-to-all-start.1 = ((f32[16,384,128]{2,1,0:T(8,128)}), f32[16,384,128]{2,1,0:T(8,128)S(1)}, u32[]{:S(2)}, u32[]{:S(2)}) async-start(f32[16,384,128]{2,1,0:T(8,128)} %get-tuple-element.26), calls=%async_computation.1 | async-start | bytes 6291456 | tf_op jit(solution)/shard_map/all_to_all | solution.py:396
  103.2 5.4 %collective-permute-start.5 = (bf16[3,384,128]{2,1,0:T(8,128)(2,1)S(1)}, bf16[3,384,128]{2,1,0:T(8,128)(2,1)}, u32[]{:S(2)}, u32[]{:S(2)}) collective-permute-start(bf16[3,384,128]{2,1,0:T(8,128)(2,1)S(1)} %slice_add_fusion), channel_id=1, source_target_pairs={{0,32},{1,33},{2,34},{3,35},{4,36},{5,37},{6,38},{7,39},{8,40},{9,... | collective-permute-start | bytes 884744 | tf_op jit(solution)/shard_map/ppermute | solution.py:353
  108.6 0.9 collective-permute-start.10
  109.5 18.0 %collective-permute-done.5 = bf16[3,384,128]{2,1,0:T(8,128)(2,1)} collective-permute-done((bf16[3,384,128]{2,1,0:T(8,128)(2,1)S(1)}, bf16[3,384,128]{2,1,0:T(8,128)(2,1)}, u32[]{:S(2)}, u32[]{:S(2)}) %collective-permute-start.5) | collective-permute-done | bytes 294944 | tf_op jit(solution)/shard_map/ppermute | solution.py:353
  127.5 1.0 add.78
  128.6 1.3 collective-permute-start.6
  129.9 0.7 collective-permute-start.7
  130.6 3.6 collective-permute-done.10
  134.2 1.8 broadcast_select_fusion.4
  136.0 1.3 collective-permute-start.11
  137.3 1.1 collective-permute-done.11
  138.4 2.4 collective-permute-start.12
  140.9 2.4 collective-permute-start.8
  143.3 17.8 %collective-permute-done.12 = f32[4,128,128]{2,1,0:T(8,128)S(1)} collective-permute-done((f32[4,128,128]{2,1,0:T(8,128)S(1)}, f32[4,128,128]{2,1,0:T(8,128)S(1)}, u32[]{:S(2)}, u32[]{:S(2)}) %collective-permute-start.12) | collective-permute-done | bytes 262176 | tf_op jit(solution)/shard_map/ppermute | solution.py:353
  161.1 0.7 add.86
  161.9 1.3 collective-permute-start.13
  163.2 1.4 collective-permute-start.14
  164.7 8.4 %collective-permute-done.13 = f32[4,128,128]{2,1,0:T(8,128)} collective-permute-done((f32[4,128,128]{2,1,0:T(8,128)}, f32[4,128,128]{2,1,0:T(8,128)}, u32[]{:S(2)}, u32[]{:S(2)}) %collective-permute-start.13) | collective-permute-done | bytes 262176 | tf_op jit(solution)/shard_map/ppermute | solution.py:354
  173.2 1.8 add_add_fusion.1
  175.0 2.0 collective-permute-start.15
  177.0 1.0 broadcast_select_fusion.3
  178.0 0.9 pad_maximum_fusion.lead
  178.9 2.4 panel_slots.1
  181.3 0.8 collective-permute-done.15
  182.1 1.8 add.89.corner
  183.8 21.0 %factor.1 = (f32[4,128,128]{2,1,0:T(8,128)}, f32[4,128,128]{2,1,0:T(8,128)}) custom-call(f32[4,128,128]{2,1,0:T(8,128)} %add.89.corner), custom_call_target="tpu_custom_call" | custom-call | tf_op jit(solution)/shard_map/factor/pallas_call | solution.py:69
  204.8 7.4 %all-to-all-start.2 = ((f32[16,48,128]{2,1,0:T(8,128)}), f32[16,48,128]{2,1,0:T(8,128)}, u32[]{:S(2)}, u32[]{:S(2)}) async-start(f32[16,48,128]{2,1,0:T(8,128)} %panel_slots.1), calls=%async_computation.2 | async-start | bytes 786432 | tf_op jit(solution)/shard_map/all_to_all | solution.py:407
  212.2 0.7 copy.9.picks
  212.9 10.0 %all-to-all-done.2.slots = f32[16,48,128]{2,1,0:T(8,128)} async-done(((f32[16,48,128]{2,1,0:T(8,128)}), f32[16,48,128]{2,1,0:T(8,128)}, u32[]{:S(2)}, u32[]{:S(2)}) %all-to-all-start.2) | async-done | bytes 393248 | tf_op jit(solution)/shard_map/all_to_all | solution.py:407
  222.9 3.6 place_strip.1
  226.5 2.0 broadcast_in_dim.73
  228.5 5.8 %all-to-all-start.3 = ((f32[16,4,4,8,128]{4,3,2,1,0:T(8,128)}), f32[16,4,4,8,128]{4,3,2,1,0:T(8,128)}, u32[]{:S(2)}, u32[]{:S(2)}) async-start(f32[16,4,4,8,128]{4,3,2,1,0:T(8,128)} %broadcast_in_dim.73), calls=%async_computation.3 | async-start | bytes 2097152 | tf_op jit(solution)/shard_map/all_to_all | solution.py:412
  234.3 10.6 %collective-permute-start.16 = (f32[4,4,8,128]{3,2,1,0:T(8,128)S(1)}, f32[4,4,8,128]{3,2,1,0:T(8,128)S(1)}, u32[]{:S(2)}, u32[]{:S(2)}) collective-permute-start(f32[4,4,8,128]{3,2,1,0:T(8,128)S(1)} %copy-done.6), channel_id=1, source_target_pairs={{0,0},{1,16},{2,32},{3,48},{4,64},{5,80},{6,96},{7,112},{8,128},{9... | collective-permute-start | bytes 196616 | tf_op jit(solution)/shard_map/ppermute | solution.py:410
  245.0 24.3 %collective-permute-done.16 = f32[4,4,8,128]{3,2,1,0:T(8,128)S(1)} collective-permute-done((f32[4,4,8,128]{3,2,1,0:T(8,128)S(1)}, f32[4,4,8,128]{3,2,1,0:T(8,128)S(1)}, u32[]{:S(2)}, u32[]{:S(2)}) %collective-permute-start.16) | collective-permute-done | bytes 65568 | tf_op jit(solution)/shard_map/ppermute | solution.py:410
  269.3 5.8 %collective-permute-done.17 = f32[1,4,4,8,128]{4,3,2,1,0:T(8,128)S(1)} collective-permute-done((f32[1,4,4,8,128]{4,3,2,1,0:T(8,128)S(1)}, f32[1,4,4,8,128]{4,3,2,1,0:T(8,128)S(1)}, u32[]{:S(2)}, u32[]{:S(2)}) %collective-permute-start.17) | collective-permute-done | bytes 65568 | tf_op jit(solution)/shard_map/ppermute | solution.py:424
  275.2 5.0 %collective-permute-done.18 = f32[2,4,4,8,128]{4,3,2,1,0:T(8,128)S(1)} collective-permute-done((f32[2,4,4,8,128]{4,3,2,1,0:T(8,128)S(1)}, f32[2,4,4,8,128]{4,3,2,1,0:T(8,128)S(1)}, u32[]{:S(2)}, u32[]{:S(2)}) %collective-permute-start.18) | collective-permute-done | bytes 131104 | tf_op jit(solution)/shard_map/ppermute | solution.py:424
  280.1 0.7 collective-permute-start.19
  280.8 4.9 %place_tiles.1 = (f32[2,4,128,128]{3,2,1,0:T(8,128)}, f32[2,4,128,128]{3,2,1,0:T(8,128)}) custom-call(s32[4]{0:T(128)} %pad_add_fusion.meta, s32[96,16]{1,0:T(8,128)} %copy.9.picks, f32[16,384,128]{2,1,0:T(8,128)} %copy-done.2), custom_call_target="tpu_custom_call" | custom-call | tf_op jit(solution)/shard_map/place_tiles/pallas_call | solution.py:193
  285.8 3.1 collective-permute-start.21
  288.9 8.1 %collective-permute-start.22 = (f32[2,4,128,128]{3,2,1,0:T(8,128)}, f32[2,4,128,128]{3,2,1,0:T(8,128)S(1)}, u32[]{:S(2)}, u32[]{:S(2)}) collective-permute-start(f32[2,4,128,128]{3,2,1,0:T(8,128)} %get-tuple-element.36.lower), channel_id=1, source_target_pairs={{18,33},{19,49},{20,65},{21,81},{22,97},{23,113},{24,129},{25,145}... | collective-permute-start | bytes 1572872 | tf_op jit(solution)/shard_map/ppermute | solution.py:417
  297.2 1.8 collective-permute-done.20
  299.1 4.0 %solve_rows.1 = (f32[512,512]{1,0:T(8,128)}, bf16[512,512]{1,0:T(8,128)(2,1)}, bf16[512,512]{1,0:T(8,128)(2,1)}) custom-call(f32[16,4,4,8,128]{4,3,2,1,0:T(8,128)} %all-to-all-done.3.left, f32[4,128,128]{2,1,0:T(8,128)} %get-tuple-element.38.inverse), custom_call_target="tpu_custom_call" | custom-call | tf_op jit(solution)/shard_map/solve_rows/pallas_call | solution.py:242
  303.2 6.0 %update.1.base = f32[512,512]{1,0:T(8,128)} custom-call(s32[4]{0:T(128)} %pad_add_fusion.meta, f32[2,4,128,128]{3,2,1,0:T(8,128)} %get-tuple-element.35.upper, f32[2,4,128,128]{3,2,1,0:T(8,128)} %get-tuple-element.36.lower, f32[512,512]{1,0:T(8,128)} %get-tuple-element.39.lefts, bf16[512,512]{1,0:T(8,128)(2,1)} %get-tuple-element.40.high, ...), custom_call_target="tpu_custom_call" | custom-call | tf_op jit(solution)/shard_map/update/pallas_call | solution.py:307
  309.2 38.2 %collective-permute-done.21.upper = f32[2,4,128,128]{3,2,1,0:T(8,128)S(1)} collective-permute-done((f32[2,4,128,128]{3,2,1,0:T(8,128)}, f32[2,4,128,128]{3,2,1,0:T(8,128)S(1)}, u32[]{:S(2)}, u32[]{:S(2)}) %collective-permute-start.21) | collective-permute-done | bytes 524320 | tf_op jit(solution)/shard_map/ppermute | solution.py:416
  347.4 11.1 %collective-permute-done.22.lower = f32[2,4,128,128]{3,2,1,0:T(8,128)S(1)} collective-permute-done((f32[2,4,128,128]{3,2,1,0:T(8,128)}, f32[2,4,128,128]{3,2,1,0:T(8,128)S(1)}, u32[]{:S(2)}, u32[]{:S(2)}) %collective-permute-start.22) | collective-permute-done | bytes 524320 | tf_op jit(solution)/shard_map/ppermute | solution.py:417
  358.5 0.8 copy-done.5
  359.3 4.5 %finish.1 = f32[512,512]{1,0:T(8,128)} custom-call(s32[4]{0:T(128)} %pad_add_fusion.meta, f32[512,512]{1,0:T(8,128)} %update.1.base, f32[2,4,128,128]{3,2,1,0:T(8,128)} %copy-done.4, f32[2,4,128,128]{3,2,1,0:T(8,128)} %copy-done.5), custom_call_target="tpu_custom_call" | custom-call | tf_op jit(solution)/shard_map/finish/pallas_call | solution.py:339
  (52 shorter events, 1.4 us)
Async XLA Ops:
  0.0 109.4 %copy-start = (f32[8192]{0:T(1024)S(1)}, f32[8192]{0:T(1024)}, u32[]{:S(2)}) copy-start(f32[8192]{0:T(1024)} %param.7) | copy-start | bytes 98308
  2.6 10.7 %copy-start.1 = (bf16[6,768,128]{2,1,0:T(8,128)(2,1)}, bf16[6,768,128]{2,1,0:T(8,128)(2,1)S(1)}, u32[]{:S(2)}) copy-start(bf16[6,768,128]{2,1,0:T(8,128)(2,1)S(1)} %multiply_convert_fusion.scaled.first) | copy-start | bytes 3538948
  5.6 7.6 %copy-start.7 = (s32[96,16]{0,1:T(8,128)S(1)}, s32[96,16]{0,1:T(8,128)}, u32[]{:S(2)}) copy-start(s32[96,16]{0,1:T(8,128)} %param.6) | copy-start | bytes 18436
  5.6 71.3 %all-to-all-start = ((bf16[8,3,768,128]{3,2,1,0:T(8,128)(2,1)}), bf16[8,3,768,128]{3,2,1,0:T(8,128)(2,1)}, u32[]{:S(2)}, u32[]{:S(2)}) async-start(bf16[8,3,768,128]{3,2,1,0:T(8,128)(2,1)} %broadcast_select_fusion), calls=%async_computation | async-start | bytes 9437184 | tf_op jit(solution)/shard_map/all_to_all | solution.py:377
  14.0 7.7 %collective-permute-start = (f32[4,128,128]{2,1,0:T(8,128)S(1)}, f32[4,128,128]{2,1,0:T(8,128)S(1)}, u32[]{:S(2)}, u32[]{:S(2)}) collective-permute-start(f32[4,128,128]{2,1,0:T(8,128)S(1)} %select_reduce_fusion), channel_id=1, source_target_pairs={{0,1},{1,0},{2,3},{3,2},{4,5},{5,4},{6,7},{7,6},{8,9},{9,8},{10,11... | collective-permute-start | bytes 786440 | tf_op jit(solution)/shard_map/ppermute | solution.py:372
  16.0 27.1 %collective-permute-start.3 = (bf16[3,384,128]{2,1,0:T(8,128)(2,1)S(1)}, bf16[3,384,128]{2,1,0:T(8,128)(2,1)S(1)}, u32[]{:S(2)}, u32[]{:S(2)}) collective-permute-start(bf16[3,384,128]{2,1,0:T(8,128)(2,1)S(1)} %slice.20), channel_id=1, source_target_pairs={{0,16},{1,17},{2,18},{3,19},{4,20},{5,21},{6,22},{7,23},{8,24},{9,... | collective-permute-start | bytes 884744 | tf_op jit(solution)/shard_map/ppermute | solution.py:380
  21.8 10.4 %collective-permute-start.1 = (f32[4,128,128]{2,1,0:T(8,128)S(1)}, f32[4,128,128]{2,1,0:T(8,128)S(1)}, u32[]{:S(2)}, u32[]{:S(2)}) collective-permute-start(f32[4,128,128]{2,1,0:T(8,128)S(1)} %add.74), channel_id=1, source_target_pairs={{0,2},{1,3},{2,0},{3,1},{4,6},{5,7},{6,4},{7,5},{8,10},{9,11},{10,... | collective-permute-start | bytes 786440 | tf_op jit(solution)/shard_map/ppermute | solution.py:372
  32.3 15.1 %collective-permute-start.2 = (f32[4,128,128]{2,1,0:T(8,128)S(1)}, f32[4,128,128]{2,1,0:T(8,128)S(1)}, u32[]{:S(2)}, u32[]{:S(2)}) collective-permute-start(f32[4,128,128]{2,1,0:T(8,128)S(1)} %add.75), channel_id=1, source_target_pairs={{0,4},{1,5},{2,6},{3,7},{4,0},{5,1},{6,2},{7,3},{8,12},{9,13},{10,... | collective-permute-start | bytes 786440 | tf_op jit(solution)/shard_map/ppermute | solution.py:372
  76.8 8.3 %collective-permute-start.4 = (bf16[8,3,768,128]{3,2,1,0:T(8,128)(2,1)}, bf16[8,3,768,128]{3,2,1,0:T(8,128)(2,1)}, u32[]{:S(2)}, u32[]{:S(2)}) collective-permute-start(bf16[8,3,768,128]{3,2,1,0:T(8,128)(2,1)} %all-to-all-done.same), channel_id=1, source_target_pairs={{0,16},{16,0},{1,17},{17,1},{2,18},{18,2},{3,19},{19,3},{4,20},{20... | collective-permute-start | bytes 14155784 | tf_op jit(solution)/shard_map/ppermute | solution.py:384
  94.9 109.9 %all-to-all-start.1 = ((f32[16,384,128]{2,1,0:T(8,128)}), f32[16,384,128]{2,1,0:T(8,128)S(1)}, u32[]{:S(2)}, u32[]{:S(2)}) async-start(f32[16,384,128]{2,1,0:T(8,128)} %get-tuple-element.26), calls=%async_computation.1 | async-start | bytes 6291456 | tf_op jit(solution)/shard_map/all_to_all | solution.py:396
  103.2 24.4 %collective-permute-start.5 = (bf16[3,384,128]{2,1,0:T(8,128)(2,1)S(1)}, bf16[3,384,128]{2,1,0:T(8,128)(2,1)}, u32[]{:S(2)}, u32[]{:S(2)}) collective-permute-start(bf16[3,384,128]{2,1,0:T(8,128)(2,1)S(1)} %slice_add_fusion), channel_id=1, source_target_pairs={{0,32},{1,33},{2,34},{3,35},{4,36},{5,37},{6,38},{7,39},{8,40},{9,... | collective-permute-start | bytes 884744 | tf_op jit(solution)/shard_map/ppermute | solution.py:353
  108.6 25.6 %collective-permute-start.10 = (f32[4,128,128]{2,1,0:T(8,128)}, f32[4,128,128]{2,1,0:T(8,128)}, u32[]{:S(2)}, u32[]{:S(2)}) collective-permute-start(f32[4,128,128]{2,1,0:T(8,128)} %add.76), channel_id=1, source_target_pairs={{0,8},{8,0},{1,9},{9,1},{2,10},{10,2},{3,11},{11,3},{4,12},{12,4},... | collective-permute-start | bytes 786440 | tf_op jit(solution)/shard_map/ppermute | solution.py:385
  128.6 12.3 %collective-permute-start.6 = (bf16[3,384,128]{2,1,0:T(8,128)(2,1)S(1)}, bf16[3,384,128]{2,1,0:T(8,128)(2,1)S(1)}, u32[]{:S(2)}, u32[]{:S(2)}) collective-permute-start(bf16[3,384,128]{2,1,0:T(8,128)(2,1)S(1)} %add.78), channel_id=1, source_target_pairs={{0,64},{1,65},{2,66},{3,67},{4,68},{5,69},{6,70},{7,71},{8,72},{9,... | collective-permute-start | bytes 884744 | tf_op jit(solution)/shard_map/ppermute | solution.py:354
  129.9 11.0 %collective-permute-start.7 = (bf16[3,384,128]{2,1,0:T(8,128)(2,1)S(1)}, bf16[3,384,128]{2,1,0:T(8,128)(2,1)S(1)}, u32[]{:S(2)}, u32[]{:S(2)}) collective-permute-start(bf16[3,384,128]{2,1,0:T(8,128)(2,1)S(1)} %add.78), channel_id=1, source_target_pairs={{0,192},{1,193},{2,194},{3,195},{4,196},{5,197},{6,198},{7,199},{8... | collective-permute-start | bytes 884744 | tf_op jit(solution)/shard_map/ppermute | solution.py:354
  136.0 2.4 collective-permute-start.11
  138.4 22.7 %collective-permute-start.12 = (f32[4,128,128]{2,1,0:T(8,128)S(1)}, f32[4,128,128]{2,1,0:T(8,128)S(1)}, u32[]{:S(2)}, u32[]{:S(2)}) collective-permute-start(f32[4,128,128]{2,1,0:T(8,128)S(1)} %add.85), channel_id=1, source_target_pairs={{0,32},{1,33},{2,34},{3,35},{4,36},{5,37},{6,38},{7,39},{8,40},{9,... | collective-permute-start | bytes 786440 | tf_op jit(solution)/shard_map/ppermute | solution.py:353
  140.9 23.6 %collective-permute-start.8 = (bf16[3,384,128]{2,1,0:T(8,128)(2,1)S(1)}, bf16[3,384,128]{2,1,0:T(8,128)(2,1)S(1)}, u32[]{:S(2)}, u32[]{:S(2)}) collective-permute-start(bf16[3,384,128]{2,1,0:T(8,128)(2,1)S(1)} %add_add_fusion), channel_id=1, source_target_pairs={{64,128},{65,129},{66,130},{67,131},{68,132},{69,133},{70,134},{71... | collective-permute-start | bytes 884744 | tf_op jit(solution)/shard_map/ppermute | solution.py:355
  161.9 11.3 %collective-permute-start.13 = (f32[4,128,128]{2,1,0:T(8,128)}, f32[4,128,128]{2,1,0:T(8,128)}, u32[]{:S(2)}, u32[]{:S(2)}) collective-permute-start(f32[4,128,128]{2,1,0:T(8,128)} %add.86), channel_id=1, source_target_pairs={{0,64},{1,65},{2,66},{3,67},{4,68},{5,69},{6,70},{7,71},{8,72},{9,... | collective-permute-start | bytes 786440 | tf_op jit(solution)/shard_map/ppermute | solution.py:354
  163.2 10.0 %collective-permute-start.14 = (f32[4,128,128]{2,1,0:T(8,128)}, f32[4,128,128]{2,1,0:T(8,128)}, u32[]{:S(2)}, u32[]{:S(2)}) collective-permute-start(f32[4,128,128]{2,1,0:T(8,128)} %add.86), channel_id=1, source_target_pairs={{0,192},{1,193},{2,194},{3,195},{4,196},{5,197},{6,198},{7,199},{8... | collective-permute-start | bytes 786440 | tf_op jit(solution)/shard_map/ppermute | solution.py:354
  164.6 12.4 %collective-permute-start.9 = (bf16[3,384,128]{2,1,0:T(8,128)(2,1)S(1)}, bf16[3,384,128]{2,1,0:T(8,128)(2,1)}, u32[]{:S(2)}, u32[]{:S(2)}) collective-permute-start(bf16[3,384,128]{2,1,0:T(8,128)(2,1)S(1)} %add.81), channel_id=1, source_target_pairs={{0,16},{16,0},{1,17},{17,1},{2,18},{18,2},{3,19},{19,3},{4,20},{20... | collective-permute-start | bytes 884744 | tf_op jit(solution)/shard_map/ppermute | solution.py:399
  175.0 7.0 %collective-permute-start.15 = (f32[4,128,128]{2,1,0:T(8,128)}, f32[4,128,128]{2,1,0:T(8,128)}, u32[]{:S(2)}, u32[]{:S(2)}) collective-permute-start(f32[4,128,128]{2,1,0:T(8,128)} %add_add_fusion.1), channel_id=1, source_target_pairs={{64,128},{65,129},{66,130},{67,131},{68,132},{69,133},{70,134},{71... | collective-permute-start | bytes 786440 | tf_op jit(solution)/shard_map/ppermute | solution.py:355
  204.8 23.7 %copy-start.2 = (f32[16,384,128]{2,1,0:T(8,128)}, f32[16,384,128]{2,1,0:T(8,128)S(1)}, u32[]{:S(2)}) copy-start(f32[16,384,128]{2,1,0:T(8,128)S(1)} %all-to-all-done.1.slots) | copy-start | bytes 9437188
  204.8 18.1 %all-to-all-start.2 = ((f32[16,48,128]{2,1,0:T(8,128)}), f32[16,48,128]{2,1,0:T(8,128)}, u32[]{:S(2)}, u32[]{:S(2)}) async-start(f32[16,48,128]{2,1,0:T(8,128)} %panel_slots.1), calls=%async_computation.2 | async-start | bytes 786432 | tf_op jit(solution)/shard_map/all_to_all | solution.py:407
  226.5 7.8 %copy-start.6 = (f32[4,4,8,128]{3,2,1,0:T(8,128)S(1)}, f32[4,4,8,128]{3,2,1,0:T(8,128)}, u32[]{:S(2)}) copy-start(f32[4,4,8,128]{3,2,1,0:T(8,128)} %place_strip.1) | copy-start | bytes 196612
  228.5 70.6 %all-to-all-start.3 = ((f32[16,4,4,8,128]{4,3,2,1,0:T(8,128)}), f32[16,4,4,8,128]{4,3,2,1,0:T(8,128)}, u32[]{:S(2)}, u32[]{:S(2)}) async-start(f32[16,4,4,8,128]{4,3,2,1,0:T(8,128)} %broadcast_in_dim.73), calls=%async_computation.3 | async-start | bytes 2097152 | tf_op jit(solution)/shard_map/all_to_all | solution.py:412
  234.3 35.0 %collective-permute-start.16 = (f32[4,4,8,128]{3,2,1,0:T(8,128)S(1)}, f32[4,4,8,128]{3,2,1,0:T(8,128)S(1)}, u32[]{:S(2)}, u32[]{:S(2)}) collective-permute-start(f32[4,4,8,128]{3,2,1,0:T(8,128)S(1)} %copy-done.6), channel_id=1, source_target_pairs={{0,0},{1,16},{2,32},{3,48},{4,64},{5,80},{6,96},{7,112},{8,128},{9... | collective-permute-start | bytes 196616 | tf_op jit(solution)/shard_map/ppermute | solution.py:410
  269.3 5.8 %collective-permute-start.17 = (f32[1,4,4,8,128]{4,3,2,1,0:T(8,128)S(1)}, f32[1,4,4,8,128]{4,3,2,1,0:T(8,128)S(1)}, u32[]{:S(2)}, u32[]{:S(2)}) collective-permute-start(f32[1,4,4,8,128]{4,3,2,1,0:T(8,128)S(1)} %bitcast.12), channel_id=1, source_target_pairs={{0,32},{32,0},{1,33},{33,1},{2,34},{34,2},{3,35},{35,3},{4,36},{36... | collective-permute-start | bytes 196616 | tf_op jit(solution)/shard_map/ppermute | solution.py:424
  275.1 5.1 %collective-permute-start.18 = (f32[2,4,4,8,128]{4,3,2,1,0:T(8,128)S(1)}, f32[2,4,4,8,128]{4,3,2,1,0:T(8,128)S(1)}, u32[]{:S(2)}, u32[]{:S(2)}) collective-permute-start(f32[2,4,4,8,128]{4,3,2,1,0:T(8,128)S(1)} %pad_maximum_fusion.3), channel_id=1, source_target_pairs={{0,64},{64,0},{128,192},{192,128},{1,65},{65,1},{129,193},{193,129... | collective-permute-start | bytes 393224 | tf_op jit(solution)/shard_map/ppermute | solution.py:424
  280.1 16.9 %collective-permute-start.19 = (f32[4,4,4,8,128]{4,3,2,1,0:T(8,128)S(1)}, f32[4,4,4,8,128]{4,3,2,1,0:T(8,128)S(1)}, u32[]{:S(2)}, u32[]{:S(2)}) collective-permute-start(f32[4,4,4,8,128]{4,3,2,1,0:T(8,128)S(1)} %pad_maximum_fusion.2), channel_id=1, source_target_pairs={{0,192},{64,128},{128,64},{192,0},{1,193},{65,129},{129,65},{193,1... | collective-permute-start | bytes 786440 | tf_op jit(solution)/shard_map/ppermute | solution.py:424
  285.8 61.6 %collective-permute-start.21 = (f32[2,4,128,128]{3,2,1,0:T(8,128)}, f32[2,4,128,128]{3,2,1,0:T(8,128)S(1)}, u32[]{:S(2)}, u32[]{:S(2)}) collective-permute-start(f32[2,4,128,128]{3,2,1,0:T(8,128)} %get-tuple-element.35.upper), channel_id=1, source_target_pairs={{18,33},{19,49},{20,65},{21,81},{22,97},{23,113},{24,129},{25,145}... | collective-permute-start | bytes 1572872 | tf_op jit(solution)/shard_map/ppermute | solution.py:416
  288.9 69.6 %collective-permute-start.22 = (f32[2,4,128,128]{3,2,1,0:T(8,128)}, f32[2,4,128,128]{3,2,1,0:T(8,128)S(1)}, u32[]{:S(2)}, u32[]{:S(2)}) collective-permute-start(f32[2,4,128,128]{3,2,1,0:T(8,128)} %get-tuple-element.36.lower), channel_id=1, source_target_pairs={{18,33},{19,49},{20,65},{21,81},{22,97},{23,113},{24,129},{25,145}... | collective-permute-start | bytes 1572872 | tf_op jit(solution)/shard_map/ppermute | solution.py:417
  297.1 2.0 collective-permute-start.20
  299.1 4.1 %copy-start.3 = (f32[16,4,4,8,128]{4,3,2,1,0:T(8,128)}, f32[16,4,4,8,128]{4,3,2,1,0:T(8,128)S(1)}, u32[]{:S(2)}) copy-start(f32[16,4,4,8,128]{4,3,2,1,0:T(8,128)S(1)} %constant_dynamic-update-slice_fusion.right) | copy-start | bytes 3145732
  347.4 11.1 %copy-start.4 = (f32[2,4,128,128]{3,2,1,0:T(8,128)}, f32[2,4,128,128]{3,2,1,0:T(8,128)S(1)}, u32[]{:S(2)}) copy-start(f32[2,4,128,128]{3,2,1,0:T(8,128)S(1)} %collective-permute-done.21.upper) | copy-start | bytes 1572868
  358.5 0.8 copy-start.5
